TPU v7x, 32 devices: a whole 2x2x4 slice. The times are simulated.
32 devices in a mesh: dp: 8 (over y, x, core), mp: 4 (over z).
Axes of the slice: x: 2, y: 2, z: 4, core: 2. Of those that a mesh axis runs over, the one named last changes fastest.
Arguments:
- tokens: bfloat16 [16384, 1024], P(('dp', 'mp')), may hold values from -6 to 6
- segments: int32 [16384], P('dp'), may hold values from 0 to 68, as said below
- ln1_gain: bfloat16 [1024], replicated, may hold values from 0.5 to 1.5
- ln1_bias: bfloat16 [1024], replicated, may hold values from -1.75 to 1.75
- w_query: bfloat16 [1024, 1024], P(None, 'mp'), may hold values from -0.1875 to 0.1875
- b_query: bfloat16 [1024], P('mp'), may hold values from -3 to 3
- w_key: bfloat16 [1024, 1024], P(None, 'mp'), may hold values from -0.1875 to 0.1875
- w_value: bfloat16 [1024, 1024], P(None, 'mp'), may hold values from -0.1875 to 0.1875
- b_value: bfloat16 [1024], P('mp'), may hold values from -3 to 3
- w_out: bfloat16 [1024, 1024], P('mp'), may hold values from -0.5 to 0.5
- b_out: bfloat16 [1024], replicated, may hold values from -1.75 to 1.75
- ln2_gain: bfloat16 [1024], replicated, may hold values from 0.5 to 1.5
- ln2_bias: bfloat16 [1024], replicated, may hold values from -1.75 to 1.75
- w_up: bfloat16 [1024, 4096], P(None, 'mp'), may hold values from -0.1875 to 0.1875
- b_up: bfloat16 [4096], P('mp'), may hold values from -3 to 3
- w_down: bfloat16 [4096, 1024], P('mp'), may hold values from -0.09375 to 0.09375
- b_down: bfloat16 [1024], replicated, may hold values from -1.75 to 1.75
- cotangent: bfloat16 [16384, 1024], P(('dp', 'mp')), may hold values from -6 to 6
Outputs:
- output: bfloat16 [16384, 1024], P(('dp', 'mp'))
- grad_tokens: float32 [16384, 1024], P(('dp', 'mp'))
- grad_ln1_gain: float32 [1024], replicated
- grad_ln1_bias: float32 [1024], replicated
- grad_w_query: float32 [1024, 1024], P(None, 'mp')
- grad_b_query: float32 [1024], P('mp')
- grad_w_key: float32 [1024, 1024], P(None, 'mp')
- grad_w_value: float32 [1024, 1024], P(None, 'mp')
- grad_b_value: float32 [1024], P('mp')
- grad_w_out: float32 [1024, 1024], P('mp')
- grad_b_out: float32 [1024], replicated
- grad_ln2_gain: float32 [1024], replicated
- grad_ln2_bias: float32 [1024], replicated
- grad_w_up: float32 [1024, 4096], P(None, 'mp')
- grad_b_up: float32 [4096], P('mp')
- grad_w_down: float32 [4096, 1024], P('mp')
- grad_b_down: float32 [1024], replicated
Inputs may be any that keep to these rules, and one draw needn't show every extreme that they name: `segments`: within each group of 2048 rows the ids start at 0 and rise by one from image to image, so an image's patches are consecutive rows. Small images have 30 to 48 patches; in some groups, and always in at least one, the first image has exactly 900 patches; in at least one other group every image has exactly 30 patches; the last image of a group may have fewer patches. No image has more than 900 patches.
All inputs are finite; a program needn't handle non-finite values.
Results may differ from a plain program's by a relative error of at most 0.019.
Values may be sent and summed in bfloat16 or wider, within the bound.
A program may use at most 128 MiB of HBM per device.

v0:
```python
import jax
import jax.numpy as jnp
from jax import lax
from jax.sharding import PartitionSpec as P

HEAD_DIM = 64


epsilon = 1e-06
minus_big = -1e30


def matmul(left, right):
    return jnp.dot(left, right, preferred_element_type=jnp.float32)


def times_transposed(left, right):
    return lax.dot_general(
        left, right, (((1,), (1,)), ((), ())), preferred_element_type=jnp.float32
    )


def transposed_times(left, right):
    return lax.dot_general(
        left, right, (((0,), (0,)), ((), ())), preferred_element_type=jnp.float32
    )


def normalize(values):
    average = jnp.mean(values, axis=1, keepdims=True)
    centered = values - average
    spread = jnp.mean(centered * centered, axis=1, keepdims=True)
    inv_std = lax.rsqrt(spread + epsilon)
    return (centered * inv_std, inv_std)


def norm_back(grad_norm, x_hat, inv_std, gain_vec):
    grad_hat = grad_norm * gain_vec
    first = jnp.mean(grad_hat, axis=1, keepdims=True)
    second = jnp.mean(grad_hat * x_hat, axis=1, keepdims=True)
    grad_input = inv_std * (grad_hat - first - x_hat * second)
    return (grad_input, jnp.sum(grad_norm * x_hat, axis=0), jnp.sum(grad_norm, axis=0))


def gelu_slope(values):
    cdf_part = 0.5 * (1.0 + lax.erf(values * 0.7071067811865476))
    return cdf_part + values * jnp.exp(-0.5 * values * values) * 0.3989422804014327


def local(
    tokens,
    segments,
    ln1_gain,
    ln1_bias,
    w_query,
    b_query,
    w_key,
    w_value,
    b_value,
    w_out,
    b_out,
    ln2_gain,
    ln2_bias,
    w_up,
    b_up,
    w_down,
    b_down,
    cotangent,
):
    all_rows = segments.shape[0]
    local_width = w_query.shape[1]
    head_count = local_width // HEAD_DIM
    score_scale = HEAD_DIM ** (-0.5)
    block_rows = min(512, all_rows)
    block_count = all_rows // block_rows
    gain_one = ln1_gain.astype(jnp.float32)
    bias_one = ln1_bias.astype(jnp.float32)
    gain_two = ln2_gain.astype(jnp.float32)
    bias_two = ln2_bias.astype(jnp.float32)
    resid_in = tokens.astype(jnp.float32)
    hat_one, inv_one = normalize(resid_in)
    normed_one = (hat_one * gain_one + bias_one).astype(jnp.bfloat16)
    gathered_one = lax.all_gather(normed_one, "mp", axis=0, tiled=True)
    query = (matmul(gathered_one, w_query) + b_query.astype(jnp.float32)).astype(jnp.bfloat16)
    keys = matmul(gathered_one, w_key).astype(jnp.bfloat16)
    values = (matmul(gathered_one, w_value) + b_value.astype(jnp.float32)).astype(jnp.bfloat16)
    query_blocks = query.reshape(block_count, block_rows, head_count, HEAD_DIM)
    segment_blocks = segments.reshape(block_count, block_rows)
    keys_heads = keys.reshape(all_rows, head_count, HEAD_DIM)
    values_heads = values.reshape(all_rows, head_count, HEAD_DIM)

    def scores_of(query_block, segment_block):
        raw_scores = (
            jnp.einsum("qhd,khd->hqk", query_block, keys_heads, preferred_element_type=jnp.float32)
            * score_scale
        )
        same_image = (segment_block[:, None] == segments[None, :])[None]
        return jnp.where(same_image, raw_scores, minus_big)

    def forward_block(pieces):
        query_block, segment_block = pieces
        scores = scores_of(query_block, segment_block)
        row_max = jnp.max(scores, axis=2, keepdims=True)
        exp_scores = jnp.exp(scores - row_max)
        row_sum = jnp.sum(exp_scores, axis=2, keepdims=True)
        probabilities = (exp_scores / row_sum).astype(jnp.bfloat16)
        head_out = jnp.einsum(
            "hqk,khd->qhd", probabilities, values_heads, preferred_element_type=jnp.float32
        )
        return (head_out.astype(jnp.bfloat16), row_max[:, :, 0] + jnp.log(row_sum[:, :, 0]))

    attn_blocks, log_totals = lax.map(forward_block, (query_blocks, segment_blocks))
    attn_out = attn_blocks.reshape(all_rows, local_width)
    attn_branch = lax.psum_scatter(
        matmul(attn_out, w_out).astype(jnp.bfloat16), "mp", scatter_dimension=0, tiled=True
    ).astype(jnp.float32)
    hidden_one = resid_in + attn_branch + b_out.astype(jnp.float32)
    hat_two, inv_two = normalize(hidden_one)
    normed_two = (hat_two * gain_two + bias_two).astype(jnp.bfloat16)
    gathered_two = lax.all_gather(normed_two, "mp", axis=0, tiled=True)
    upper = matmul(gathered_two, w_up) + b_up.astype(jnp.float32)
    active = jax.nn.gelu(upper, approximate=False).astype(jnp.bfloat16)
    mlp_branch = lax.psum_scatter(
        matmul(active, w_down).astype(jnp.bfloat16), "mp", scatter_dimension=0, tiled=True
    ).astype(jnp.float32)
    output = (hidden_one + mlp_branch + b_down.astype(jnp.float32)).astype(jnp.bfloat16)
    grad_out = cotangent.astype(jnp.float32)
    grad_b_down = jnp.sum(grad_out, axis=0)
    grad_rows = lax.all_gather(cotangent, "mp", axis=0, tiled=True)
    grad_w_down = transposed_times(active, grad_rows)
    grad_active = times_transposed(grad_rows, w_down)
    grad_upper = (grad_active * gelu_slope(upper)).astype(jnp.bfloat16)
    grad_b_up = jnp.sum(grad_upper, axis=0, dtype=jnp.float32)
    grad_w_up = transposed_times(gathered_two, grad_upper)
    grad_normed_two = lax.psum_scatter(
        times_transposed(grad_upper, w_up).astype(jnp.bfloat16),
        "mp",
        scatter_dimension=0,
        tiled=True,
    ).astype(jnp.float32)
    grad_hidden, grad_ln2_gain, grad_ln2_bias = norm_back(
        grad_normed_two, hat_two, inv_two, gain_two
    )
    grad_hidden = grad_hidden + grad_out
    grad_b_out = jnp.sum(grad_hidden, axis=0)
    hidden_rows = lax.all_gather(grad_hidden.astype(jnp.bfloat16), "mp", axis=0, tiled=True)
    grad_w_out = transposed_times(attn_out, hidden_rows)
    grad_attn = times_transposed(hidden_rows, w_out).astype(jnp.bfloat16)
    grad_attn_blocks = grad_attn.reshape(block_count, block_rows, head_count, HEAD_DIM)

    def backward_block(carry, pieces):
        grad_keys_sum, grad_values_sum = carry
        query_block, segment_block, log_block, grad_block = pieces
        scores = scores_of(query_block, segment_block)
        probabilities = jnp.exp(scores - log_block[:, :, None])
        grad_probs = jnp.einsum(
            "qhd,khd->hqk", grad_block, values_heads, preferred_element_type=jnp.float32
        )
        inner = jnp.sum(probabilities * grad_probs, axis=2, keepdims=True)
        grad_scores = (probabilities * (grad_probs - inner)).astype(jnp.bfloat16)
        grad_query_block = (
            jnp.einsum("hqk,khd->qhd", grad_scores, keys_heads, preferred_element_type=jnp.float32)
            * score_scale
        )
        grad_keys_sum = (
            grad_keys_sum
            + jnp.einsum(
                "hqk,qhd->khd", grad_scores, query_block, preferred_element_type=jnp.float32
            )
            * score_scale
        )
        grad_values_sum = grad_values_sum + jnp.einsum(
            "hqk,qhd->khd",
            probabilities.astype(jnp.bfloat16),
            grad_block,
            preferred_element_type=jnp.float32,
        )
        return ((grad_keys_sum, grad_values_sum), grad_query_block.astype(jnp.bfloat16))

    zeros_heads = jnp.zeros((all_rows, head_count, HEAD_DIM), jnp.float32)
    (grad_keys_sum, grad_values_sum), grad_query_blocks = lax.scan(
        backward_block,
        (zeros_heads, zeros_heads),
        (query_blocks, segment_blocks, log_totals, grad_attn_blocks),
    )
    grad_query = grad_query_blocks.reshape(all_rows, local_width)
    grad_keys = grad_keys_sum.reshape(all_rows, local_width).astype(jnp.bfloat16)
    grad_values = grad_values_sum.reshape(all_rows, local_width).astype(jnp.bfloat16)
    grad_w_query = transposed_times(gathered_one, grad_query)
    grad_b_query = jnp.sum(grad_query, axis=0, dtype=jnp.float32)
    grad_w_key = transposed_times(gathered_one, grad_keys)
    grad_w_value = transposed_times(gathered_one, grad_values)
    grad_b_value = jnp.sum(grad_values, axis=0, dtype=jnp.float32)
    term = times_transposed(grad_query, w_query)
    term = term + times_transposed(grad_keys, w_key)
    grad_normed_one = lax.psum_scatter(
        (term + times_transposed(grad_values, w_value)).astype(jnp.bfloat16),
        "mp",
        scatter_dimension=0,
        tiled=True,
    ).astype(jnp.float32)
    grad_input, grad_ln1_gain, grad_ln1_bias = norm_back(
        grad_normed_one, hat_one, inv_one, gain_one
    )
    grad_tokens = grad_input + grad_hidden
    (
        grad_w_query,
        grad_b_query,
        grad_w_key,
        grad_w_value,
        grad_b_value,
        grad_w_out,
        grad_w_up,
        grad_b_up,
        grad_w_down,
    ) = (
        lax.psum(grad_w_query.astype(jnp.bfloat16), "dp").astype(jnp.float32),
        lax.psum(grad_b_query.astype(jnp.bfloat16), "dp").astype(jnp.float32),
        lax.psum(grad_w_key.astype(jnp.bfloat16), "dp").astype(jnp.float32),
        lax.psum(grad_w_value.astype(jnp.bfloat16), "dp").astype(jnp.float32),
        lax.psum(grad_b_value.astype(jnp.bfloat16), "dp").astype(jnp.float32),
        lax.psum(grad_w_out.astype(jnp.bfloat16), "dp").astype(jnp.float32),
        lax.psum(grad_w_up.astype(jnp.bfloat16), "dp").astype(jnp.float32),
        lax.psum(grad_b_up.astype(jnp.bfloat16), "dp").astype(jnp.float32),
        lax.psum(grad_w_down.astype(jnp.bfloat16), "dp").astype(jnp.float32),
    )
    grad_ln1_gain, grad_ln1_bias, grad_b_out, grad_ln2_gain, grad_ln2_bias, grad_b_down = lax.psum(
        (grad_ln1_gain, grad_ln1_bias, grad_b_out, grad_ln2_gain, grad_ln2_bias, grad_b_down),
        ("dp", "mp"),
    )
    return (
        output,
        grad_tokens,
        grad_ln1_gain,
        grad_ln1_bias,
        grad_w_query,
        grad_b_query,
        grad_w_key,
        grad_w_value,
        grad_b_value,
        grad_w_out,
        grad_b_out,
        grad_ln2_gain,
        grad_ln2_bias,
        grad_w_up,
        grad_b_up,
        grad_w_down,
        grad_b_down,
    )


def solution(mesh):
    in_specs = (
        P(("dp", "mp"), None),
        P("dp"),
        P(),
        P(),
        P(None, "mp"),
        P("mp"),
        P(None, "mp"),
        P(None, "mp"),
        P("mp"),
        P("mp", None),
        P(),
        P(),
        P(),
        P(None, "mp"),
        P("mp"),
        P("mp", None),
        P(),
        P(("dp", "mp"), None),
    )
    out_specs = (
        P(("dp", "mp"), None),
        P(("dp", "mp"), None),
        P(),
        P(),
        P(None, "mp"),
        P("mp"),
        P(None, "mp"),
        P(None, "mp"),
        P("mp"),
        P("mp", None),
        P(),
        P(),
        P(),
        P(None, "mp"),
        P("mp"),
        P("mp", None),
        P(),
    )
    return jax.shard_map(local, mesh=mesh, in_specs=in_specs, out_specs=out_specs, check_vma=False)
```

profile of v0, /device:TPU:0, one launch (start us, length us, event | category | flops | bytes accessed | tf_op | source)
XLA Modules:
  0.0 1142.3 jit_solution(16438787603620042261)
XLA Ops:
  14.7 83.5 %all-gather.5.cloned.1.call-done = bf16[2048,1024]{1,0:T(8,128)(2,1)} async-done(((bf16[512,1024]{1,0:T(8,128)(2,1)}), bf16[2048,1024]{1,0:T(8,128)(2,1)}) %all-gather.5.cloned.1.call-update) | async-done | bytes 4194320 | tf_op jit(solution)/shard_map/all_gather | solution.py:83
  98.2 3.6 fusion.65
  103.6 4.0 copy.39
  107.6 4.7 convolution_convert_fusion.4
  114.7 64.4 %while.27 = (s32[]{:T(128)}, bf16[4,512,4,64]{1,3,2,0:T(8,128)(2,1)}, f32[4,4,512]{2,1,0:T(4,128)}, s32[4,512]{1,0:T(4,128)S(1)}, s32[2048]{0:T(1024)S(1)}, /*in...) while((s32[]{:T(128)}, ...), condition=%wide.region_5.6_spmd, body=%wide.region_2.5_spmd.sunk | while | flops 1125251072 | bytes 57227380 | solution.py:112
  115.4 4.5 fusion.153
  119.9 4.3 fusion.154
  124.2 5.9 fusion.155
  131.5 4.5 fusion.153
  136.0 4.3 fusion.154
  140.3 5.9 fusion.155
  147.6 4.5 fusion.153
  152.1 4.3 fusion.154
  156.5 5.9 fusion.155
  163.7 4.5 fusion.153
  168.2 4.3 fusion.154
  172.6 5.9 fusion.155
  182.8 3.3 convolution_convert_fusion
  186.8 74.8 %reduce-scatter.5.cloned.1.call-done = bf16[512,1024]{1,0:T(8,128)(2,1)} async-done(((bf16[2048,1024]{1,0:T(8,128)(2,1)}), bf16[512,1024]{1,0:T(8,128)(2,1)}) %reduce-scatter.5.cloned.1.call-update) | async-done | bytes 1048592 | tf_op jit(solution)/shard_map/reduce_scatter | solution.py:114
  267.4 80.8 %all-gather.7.cloned.1.call-done = bf16[2048,1024]{1,0:T(8,128)(2,1)} async-done(((bf16[512,1024]{1,0:T(8,128)(2,1)}), bf16[2048,1024]{1,0:T(8,128)(2,1)}) %all-gather.7.cloned.1.call-update) | async-done | bytes 4194320 | tf_op jit(solution)/shard_map/all_gather | solution.py:120
  348.2 25.0 %fusion.45 = (bf16[2048,1024]{1,0:T(8,128)(2,1)}, f32[2048,1024]{1,0:T(8,128)}) fusion(f32[1024]{0:T(1024)S(1)} %convert_element_type.187, bf16[2048,1024]{1,0:T(8,128)(2,1)} %all-gather.7.cloned.1.call-done, bf16[1024,1024]{1,0:T(8,128)(2,1)S(1)} %copy-done), kind=kOutput, calls=%fused_computation.56 | convolution fusion | flops 4433379328 | bytes 18878464 | tf_op jit(solution)/shard_map/dot_general | solution.py:14
  373.2 55.6 %all-gather.9.cloned.1.call-done = bf16[2048,1024]{1,0:T(8,128)(2,1)} async-done(((bf16[512,1024]{1,0:T(8,128)(2,1)}), bf16[2048,1024]{1,0:T(8,128)(2,1)}) %all-gather.9.cloned.1.call-update) | async-done | bytes 4194320 | tf_op jit(solution)/shard_map/all_gather | solution.py:129
  428.9 11.9 %fusion.87 = (bf16[1024]{0:T(1024)(128)(2,1)}, bf16[2048,1024]{1,0:T(8,128)(2,1)S(1)}) fusion(f32[2048,1024]{1,0:T(8,128)} %get-tuple-element.270, f32[1024]{0:T(1024)S(1)} %convert_element_type.187, bf16[2048,1024]{1,0:T(8,128)(2,1)} %all-gather.9.cloned.1.call-done, bf16[1024,1024]{1,0:T(8,128)(2,1)} %param.37), kind=kOutput, calls=%fused_computation.143 | convolution fusion | flops 4320132096 | bytes 18880512 | tf_op jit(solution)/shard_map/dot_general | solution.py:18
  442.7 6.3 convolution_convert_fusion.1
  450.5 8.3 convolution_convert_fusion.2
  459.5 64.9 %reduce-scatter.9.cloned.1.call-done = bf16[512,1024]{1,0:T(8,128)(2,1)} async-done(((bf16[2048,1024]{1,0:T(8,128)(2,1)}), bf16[512,1024]{1,0:T(8,128)(2,1)}) %reduce-scatter.9.cloned.1.call-update) | async-done | bytes 1048592 | tf_op jit(solution)/shard_map/reduce_scatter | solution.py:135
  524.4 3.0 fusion.82
  527.4 76.5 %reduce-scatter.7.cloned.1.call-done = bf16[512,1024]{1,0:T(8,128)(2,1)} async-done(((bf16[2048,1024]{1,0:T(8,128)(2,1)}), bf16[512,1024]{1,0:T(8,128)(2,1)}) %reduce-scatter.7.cloned.1.call-update) | async-done | bytes 1048592 | tf_op jit(solution)/shard_map/reduce_scatter | solution.py:123
  603.9 4.2 fusion.86
  610.6 9.5 convolution_convert_fusion.5
  620.2 5.8 convolution_convert_fusion.6
  625.9 66.0 %all-gather.11.cloned.1.call-done = bf16[2048,1024]{1,0:T(8,128)(2,1)} async-done(((bf16[512,1024]{1,0:T(8,128)(2,1)}), bf16[2048,1024]{1,0:T(8,128)(2,1)}) %all-gather.11.cloned.1.call-update) | async-done | bytes 4194320 | tf_op jit(solution)/shard_map/all_gather | solution.py:146
  692.0 3.5 convolution_convert_fusion.3
  699.7 191.3 %while.28 = (s32[]{:T(128)}, f32[2048,4,64]{0,2,1:T(8,128)}, f32[2048,4,64]{0,2,1:T(8,128)}, bf16[4,512,4,64]{1,3,2,0:T(8,128)(2,1)}, bf16[4,512,4,64]{1,3,2,0:T...) while((s32[]{:T(128)}, f32[2048,4,64]{0,2,1:T(8,128)}, ...), condition=%wide.region_15.16_spmd.clone, body=%wide.region_13.15_spmd.clone.sunk | while | flops 2751199232 | bytes 176625968 | solution.py:181
  702.6 3.7 fusion.165
  706.3 7.3 fusion.167
  713.5 11.3 multiply_reduce_fusion.3
  724.8 10.8 multiply_convert_fusion.2
  735.7 7.1 fusion.168
  742.8 3.9 fusion.166
  749.4 3.7 fusion.165
  753.1 7.7 fusion.167
  760.7 11.3 multiply_reduce_fusion.3
  772.0 10.8 multiply_convert_fusion.2
  782.9 7.1 fusion.168
  790.0 4.7 fusion.166
  797.3 3.7 fusion.165
  801.0 7.7 fusion.167
  808.7 11.3 multiply_reduce_fusion.3
  820.0 10.8 multiply_convert_fusion.2
  830.8 7.1 fusion.168
  838.0 4.7 fusion.166
  845.3 3.7 fusion.165
  849.0 7.7 fusion.167
  856.6 11.3 multiply_reduce_fusion.3
  867.9 10.8 multiply_convert_fusion.2
  878.8 7.1 fusion.168
  885.9 4.7 fusion.166
  909.4 3.4 add_convert_fusion
  914.5 14.5 %all-reduce.1 = (bf16[256]{0:T(256)(128)(2,1)S(1)}, bf16[256]{0:T(256)(128)(2,1)S(1)}, bf16[1024]{0:T(1024)(128)(2,1)S(1)}) all-reduce(bf16[256]{0:T(256)(128)(2,1)S(1)} %reduce_sum.195, bf16[256]{0:T(256)(128)(2,1)S(1)} %reduce_sum.197, bf16[1024]{0:T(1024)(128)(2,1)S(1)} %copy-done.41), channel_id=1, replica_groups=mesh['dp'=8,'mp'=4] {'dp'}, use_global_device_ids=true, to_apply=%region_25.26 | all-reduce | flops 1536 | bytes 6144 | tf_op jit(solution)/shard_map/psum | solution.py:218
  930.7 78.0 %all-reduce.5.cloned.1.call-done = (bf16[1024,256]{1,0:T(8,128)(2,1)}, bf16[1024,256]{1,0:T(8,128)(2,1)}, bf16[1024,256]{1,0:T(8,128)(2,1)}, bf16[256,1024]{1,0:...) async-done(((bf16[1024,256]{1,0:T(8,128)(2,1)}, bf16[1024,256]{1,0:T(8,128)(2,1)}, bf16[1024,256]{1,0:T(8,128)(2,1)}, bf16[256,1024]{1,0:T(8,128)(2,1)}, ...) | async-done | bytes 6291472 | tf_op jit(solution)/shard_map/psum | solution.py:217
  1021.3 66.7 %reduce-scatter.11.cloned.1.call-done = bf16[512,1024]{1,0:T(8,128)(2,1)} async-done(((bf16[2048,1024]{1,0:T(8,128)(2,1)}), bf16[512,1024]{1,0:T(8,128)(2,1)}) %reduce-scatter.11.cloned.1.call-update) | async-done | bytes 1048592 | tf_op jit(solution)/shard_map/reduce_scatter | solution.py:196
  1090.3 41.4 %all-reduce = (f32[1024]{0:T(1024)}, f32[1024]{0:T(1024)}, f32[1024]{0:T(1024)}, f32[1024]{0:T(1024)}, f32[1024]{0:T(1024)}, /*index=5*/f32[1024]{0:T(1024)}) all-reduce(f32[1024]{0:T(1024)S(1)} %get-tuple-element.200, f32[1024]{0:T(1024)S(1)} %get-tuple-element.205, ...), channel_id=1, replica_groups=mesh['dp'=8,'mp'=4] {'dp','mp'}, use_global_device_ids=true, to_apply=%region_20.21 | all-reduce | flops 6144 | bytes 49152 | tf_op jit(solution)/shard_map/psum | solution.py:227
  1131.7 3.9 fusion.75
  (232 shorter events, 84.7 us)
Async XLA Ops:
  7.2 341.0 %copy-start = (bf16[1024,1024]{1,0:T(8,128)(2,1)S(1)}, bf16[1024,1024]{1,0:T(8,128)(2,1)}, u32[]{:S(2)}) copy-start(bf16[1024,1024]{1,0:T(8,128)(2,1)} %param.35) | copy-start | bytes 6291460
  7.2 7.4 copy-start.47
  7.2 7.4 copy-start.48
  7.2 7.4 copy-start.15
  7.2 91.0 %all-gather.5.cloned.1.call-start = ((), (), s32[]{:S(2)}) async-start(), calls=%async_computation.4 | async-start | bytes 5242880 | tf_op jit(solution)/shard_map/all_gather | solution.py:83
  8.9 5.8 copy-start.28
  10.5 4.2 copy-start.30
  11.2 3.5 copy-start.26
  14.6 247.0 %reduce-scatter.5.cloned.1.call-start = ((), (), s32[]{:S(2)}) async-start(), calls=%async_computation.5 | async-start | bytes 5242880 | tf_op jit(solution)/shard_map/reduce_scatter | solution.py:114
  107.6 4.7 copy-start.21
  107.6 4.7 copy-start.42
  179.1 2.7 copy-start.5
  179.1 3.7 copy-start.18
  181.8 1.0 copy-start.10
  186.1 0.7 copy-start.38
  186.1 75.5 %copy-start.3 = (bf16[512,1024]{1,0:T(8,128)(2,1)S(1)}, bf16[512,1024]{1,0:T(8,128)(2,1)}, u32[]{:S(2)}) copy-start(bf16[512,1024]{1,0:T(8,128)(2,1)} %param.22) | copy-start | bytes 3145732
  186.2 162.0 %all-gather.7.cloned.1.call-start = ((), (), s32[]{:S(2)}) async-start(), calls=%async_computation.6 | async-start | bytes 5242880 | tf_op jit(solution)/shard_map/all_gather | solution.py:120
  261.6 3.6 copy-start.6
  263.3 4.1 copy-start.39
  266.8 162.1 %all-gather.9.cloned.1.call-start = ((), (), s32[]{:S(2)}) async-start(), calls=%async_computation.8 | async-start | bytes 5242880 | tf_op jit(solution)/shard_map/all_gather | solution.py:129
  267.4 257.0 %reduce-scatter.9.cloned.1.call-start = ((), (), s32[]{:S(2)}) async-start(), calls=%async_computation.9 | async-start | bytes 5242880 | tf_op jit(solution)/shard_map/reduce_scatter | solution.py:135
  440.7 2.0 copy-start.49
  448.9 1.6 copy-start.46
  449.0 154.9 %reduce-scatter.7.cloned.1.call-start = ((), (), s32[]{:S(2)}) async-start(), calls=%async_computation.7 | async-start | bytes 5242880 | tf_op jit(solution)/shard_map/reduce_scatter | solution.py:123
  458.9 65.5 %copy-start.7 = (bf16[512,1024]{1,0:T(8,128)(2,1)S(1)}, bf16[512,1024]{1,0:T(8,128)(2,1)}, u32[]{:S(2)}) copy-start(bf16[512,1024]{1,0:T(8,128)(2,1)} %reduce-scatter.5.cloned.1.call-done) | copy-start | bytes 3145732
  458.9 145.0 %copy-start.12 = (bf16[512,1024]{1,0:T(8,128)(2,1)S(1)}, bf16[512,1024]{1,0:T(8,128)(2,1)}, u32[]{:S(2)}) copy-start(bf16[512,1024]{1,0:T(8,128)(2,1)} %param.39) | copy-start | bytes 3145732
  458.9 233.1 %all-gather.11.cloned.1.call-start = ((), (), s32[]{:S(2)}) async-start(), calls=%async_computation.10 | async-start | bytes 5242880 | tf_op jit(solution)/shard_map/all_gather | solution.py:146
  608.1 1.3 copy-start.8
  610.6 398.2 %all-reduce.5.cloned.1.call-start = ((), (), s32[]{:S(2)}) async-start(), calls=%async_computation.12 | async-start | bytes 12582912 | tf_op jit(solution)/shard_map/psum | solution.py:217
  610.6 9.5 copy-start.45
  610.6 9.5 copy-start.50
  620.2 71.8 %copy-start.19 = (bf16[256,1024]{1,0:T(8,128)(2,1)S(1)}, bf16[256,1024]{1,0:T(8,128)(2,1)}, u32[]{:S(2)}) copy-start(bf16[256,1024]{1,0:T(8,128)(2,1)} %param.31) | copy-start | bytes 1572868
  735.7 7.1 copy-start.2
  742.8 3.9 copy-start.17
  742.8 3.9 copy-start.25
  782.9 7.1 copy-start.2
  790.0 4.7 copy-start.17
  790.0 4.7 copy-start.25
  830.8 7.1 copy-start.2
  838.0 4.7 copy-start.17
  838.0 4.7 copy-start.25
  878.8 7.1 copy-start.2
  885.9 4.7 copy-start.17
  885.9 4.7 copy-start.25
  892.7 4.3 copy-start.11
  892.7 4.3 copy-start.44
  897.0 2.2 copy-start.43
  905.6 182.4 %reduce-scatter.11.cloned.1.call-start = ((), (), s32[]{:S(2)}) async-start(), calls=%async_computation.11 | async-start | bytes 5242880 | tf_op jit(solution)/shard_map/reduce_scatter | solution.py:196
  905.7 2.4 copy-start.20
  908.1 1.3 copy-start.22
  912.8 1.2 copy-start.9
  912.8 1.6 copy-start.41
  1008.7 6.4 copy-start.23
  1008.7 7.5 copy-start.14
  1015.1 3.6 copy-start.13
  1018.7 69.3 %copy-start.4 = (bf16[512,1024]{1,0:T(8,128)(2,1)S(1)}, bf16[512,1024]{1,0:T(8,128)(2,1)}, u32[]{:S(2)}) copy-start(bf16[512,1024]{1,0:T(8,128)(2,1)} %param.22) | copy-start | bytes 3145732
  1018.7 69.3 %copy-start.27 = (f32[1024]{0:T(1024)S(1)}, f32[1024]{0:T(1024)}, u32[]{:S(2)}) copy-start(f32[1024]{0:T(1024)} %copy-done.26) | copy-start | bytes 12292
  1018.7 69.3 %copy-start.29 = (f32[512]{0:T(512)S(1)}, f32[512]{0:T(512)}, u32[]{:S(2)}) copy-start(f32[512]{0:T(512)} %copy-done.28) | copy-start | bytes 6148
  1018.7 69.3 %copy-start.31 = (f32[512]{0:T(512)S(1)}, f32[512]{0:T(512)}, u32[]{:S(2)}) copy-start(f32[512]{0:T(512)} %copy-done.30) | copy-start | bytes 6148
  1018.7 71.5 %copy-start.32 = (f32[1024]{0:T(1024)S(1)}, f32[1024]{0:T(1024)}, u32[]{:S(2)}) copy-start(f32[1024]{0:T(1024)} %get-tuple-element.198) | copy-start | bytes 12292
  1018.7 71.5 %copy-start.33 = (f32[1024]{0:T(1024)S(1)}, f32[1024]{0:T(1024)}, u32[]{:S(2)}) copy-start(f32[1024]{0:T(1024)} %get-tuple-element.204) | copy-start | bytes 12292
  1018.8 71.5 %copy-start.34 = (f32[1024]{0:T(1024)S(1)}, f32[1024]{0:T(1024)}, u32[]{:S(2)}) copy-start(f32[1024]{0:T(1024)} %get-tuple-element.261) | copy-start | bytes 12292
  1018.8 71.5 %copy-start.35 = (f32[1024]{0:T(1024)S(1)}, f32[1024]{0:T(1024)}, u32[]{:S(2)}) copy-start(f32[1024]{0:T(1024)} %get-tuple-element.268) | copy-start | bytes 12292
  1018.8 116.8 %copy-start.1 = (bf16[1024,1024]{1,0:T(8,128)(2,1)S(1)}, bf16[1024,1024]{1,0:T(8,128)(2,1)}, u32[]{:S(2)}) copy-start(bf16[1024,1024]{1,0:T(8,128)(2,1)} %param.35) | copy-start | bytes 6291460
  (11 other events, 6.8 us)
Sparse Core Ops, SparseCore 0:
  14.7 83.4 all-gather.4
  186.3 75.2 reduce-scatter.4
  266.9 81.2 all-gather.6
  349.6 79.2 all-gather.8
  449.1 75.2 reduce-scatter.8
  526.5 77.2 reduce-scatter.6
  610.7 81.2 all-gather.10
  905.7 102.9 all-reduce.4
  1011.0 76.9 reduce-scatter.10
where the time goes:
time: 1150 us; the launch traced here: 1140 us
  waiting for transfers between devices  647 us (56%)
  matrix products  277 us (24%)
  other arithmetic  116 us (10%)
  blocking collectives  55.9 us (5%)
  local copies, waits for them, and re-layouts  29.5 us (3%)
  between operations  14.6 us (1%)
    all_gather x1, waiting for transfers between devices, local(): gathered_one = lax.all_gather(normed_one, 'mp', axis=0, tiled=True)  83.5 us
    all_gather x1, waiting for transfers between devices, local(): gathered_two = lax.all_gather(normed_two, 'mp', axis=0, tiled=True)  80.8 us
    psum x1, waiting for transfers between devices, local(): lax.psum(grad_w_query.astype(jnp.bfloat16), 'dp').astype(jnp.float32)  78 us
    reduce_scatter x1, waiting for transfers between devices, local(): lax.psum_scatter(matmul(active, w_down).astype(jnp.bfloat16), 'mp', scatt...  76.5 us
    reduce_scatter x1, waiting for transfers between devices, local(): lax.psum_scatter(matmul(attn_out, w_out).astype(jnp.bfloat16), 'mp', scat...  74.8 us
    reduce_scatter x1, waiting for transfers between devices, local(): lax.psum_scatter((term + times_transposed(grad_values, w_value)).astype(j...  66.7 us
    all_gather x1, waiting for transfers between devices, local(): lax.all_gather(grad_hidden.astype(jnp.bfloat16), 'mp', axis=0, tiled=True)  66 us
    reduce_scatter x1, waiting for transfers between devices, local(): lax.psum_scatter(times_transposed(grad_upper, w_up).astype(jnp.bfloat16),...  64.9 us
  transfers between devices with their start and end apart: 9, of which 9 were waited for; matrix products, arithmetic and copies ran while one was open for 6% of the time, Pallas kernels for 0%

commit v1 on v0

v1 whole, which is shorter than its diff:
```python
import functools

import jax
import jax.numpy as jnp
from jax import lax
from jax.experimental import pallas as pl
from jax.experimental.pallas import tpu as pltpu
from jax.sharding import PartitionSpec as P

HEAD_DIM = 64
LONGEST = 900
HALO = 64
PAIR = 128
EPS = 1e-06
NEG = -1e30
VMEM = 60 * 1024 * 1024
F32 = jnp.float32
BF16 = jnp.bfloat16


def dot_nn(a, b):
    return lax.dot_general(a, b, (((1,), (0,)), ((), ())), preferred_element_type=F32)


def dot_nt(a, b):
    return lax.dot_general(a, b, (((1,), (1,)), ((), ())), preferred_element_type=F32)


def dot_tn(a, b):
    return lax.dot_general(a, b, (((0,), (0,)), ((), ())), preferred_element_type=F32)


def barrier(*xs):
    return lax.optimization_barrier(xs)


def params(*sem, **kw):
    return pltpu.CompilerParams(dimension_semantics=sem, vmem_limit_bytes=VMEM, **kw)


def norm_rows(x):
    mean = jnp.mean(x, axis=1, keepdims=True)
    cent = x - mean
    inv = lax.rsqrt(jnp.mean(cent * cent, axis=1, keepdims=True) + EPS)
    return cent * inv, inv


def qkv_call(n1w, packed, b_q, b_v, own, rows, cw):
    n, dm, _ = packed.shape
    win = n1w.shape[0]

    def body(x_ref, w_ref, bq_ref, bv_ref, q_ref, k_ref, v_ref):
        x = x_ref[...]
        q_ref[0] = (dot_nn(x[own : own + rows], w_ref[0, :, 0:cw]) + bq_ref[0].astype(F32)).astype(BF16)
        k_ref[0] = dot_nn(x, w_ref[0, :, cw : 2 * cw]).astype(BF16)
        v_ref[0] = (dot_nn(x, w_ref[0, :, 2 * cw : 3 * cw]) + bv_ref[0].astype(F32)).astype(BF16)

    return pl.pallas_call(
        body,
        grid=(n,),
        in_specs=[
            pl.BlockSpec((win, dm), lambda d: (0, 0)),
            pl.BlockSpec((1, dm, 4 * cw), lambda d: (d, 0, 0)),
            pl.BlockSpec((1, 1, cw), lambda d: (d, 0, 0)),
            pl.BlockSpec((1, 1, cw), lambda d: (d, 0, 0)),
        ],
        out_specs=[
            pl.BlockSpec((1, rows, cw), lambda d: (d, 0, 0)),
            pl.BlockSpec((1, win, cw), lambda d: (d, 0, 0)),
            pl.BlockSpec((1, win, cw), lambda d: (d, 0, 0)),
        ],
        out_shape=[
            jax.ShapeDtypeStruct((n, rows, cw), BF16),
            jax.ShapeDtypeStruct((n, win, cw), BF16),
            jax.ShapeDtypeStruct((n, win, cw), BF16),
        ],
        compiler_params=params("arbitrary"),
        cost_estimate=pl.CostEstimate(
            flops=2 * n * dm * cw * (rows + 2 * win), bytes_accessed=2 * (n * dm * 4 * cw + win * dm), transcendentals=0
        ),
    )(n1w, packed, b_q[:, None, :], b_v[:, None, :])


def blocks_of(rows, own, win, big):
    if big:
        step = min(256, rows)
        return [(s, step, 0, win) for s in range(0, rows, step)]
    return [(s, 128, own + s - 128, 384) for s in range(0, rows, 128)]


def attn_fwd_call(is_big, q, k, v, qseg, kseg, own):
    n, rows, cw = q.shape
    win = k.shape[1]
    pairs = cw // PAIR

    def work(big, q_ref, k_ref, v_ref, qs_ref, ks_ref, o_ref, l_ref):
        for qs, qn, ks, kn in blocks_of(rows, own, win, big):
            mask = qs_ref[qs : qs + qn, :] == ks_ref[:, ks : ks + kn]
            for h in range(2):
                lanes = slice(h * HEAD_DIM, (h + 1) * HEAD_DIM)
                qh = q_ref[0, qs : qs + qn, lanes] * BF16(HEAD_DIM**-0.5)
                s = jnp.where(mask, dot_nt(qh, k_ref[0, ks : ks + kn, lanes]), NEG)
                top = jnp.max(s, axis=1, keepdims=True)
                p = jnp.exp(s - top)
                total = jnp.sum(p, axis=1, keepdims=True)
                o = dot_nn(p.astype(BF16), v_ref[0, ks : ks + kn, lanes])
                o_ref[0, qs : qs + qn, lanes] = (o / total).astype(BF16)
                l_ref[0, qs : qs + qn, h : h + 1] = top + jnp.log(total)

    def body(big_ref, *refs):
        @pl.when(big_ref[0] == 1)
        def _():
            work(True, *refs)

        @pl.when(big_ref[0] == 0)
        def _():
            work(False, *refs)

    return pl.pallas_call(
        body,
        grid_spec=pltpu.PrefetchScalarGridSpec(
            num_scalar_prefetch=1,
            grid=(n, pairs),
            in_specs=[
                pl.BlockSpec((1, rows, PAIR), lambda d, p, *_: (d, 0, p)),
                pl.BlockSpec((1, win, PAIR), lambda d, p, *_: (d, 0, p)),
                pl.BlockSpec((1, win, PAIR), lambda d, p, *_: (d, 0, p)),
                pl.BlockSpec((rows, 1), lambda d, p, *_: (0, 0)),
                pl.BlockSpec((1, win), lambda d, p, *_: (0, 0)),
            ],
            out_specs=[
                pl.BlockSpec((1, rows, PAIR), lambda d, p, *_: (d, 0, p)),
                pl.BlockSpec((1, rows, 2), lambda d, p, *_: (d * pairs + p, 0, 0)),
            ],
        ),
        out_shape=[
            jax.ShapeDtypeStruct((n, rows, cw), BF16),
            jax.ShapeDtypeStruct((n * pairs, rows, 2), F32),
        ],
        compiler_params=params("arbitrary", "arbitrary"),
        cost_estimate=pl.CostEstimate(
            flops=16 * n * rows * win * cw, bytes_accessed=2 * n * cw * (2 * rows + 2 * win), transcendentals=n * rows * win * 4
        ),
    )(is_big, q, k, v, qseg, kseg)


def attn_bwd_call(info, q, k, v, attn, gattn, lse, qseg, kseg, own):
    n, rows, cw = q.shape
    win = k.shape[1]
    pairs = cw // PAIR
    scale = HEAD_DIM**-0.5

    def work(big, q_ref, k_ref, v_ref, a_ref, g_ref, l_ref, qs_ref, ks_ref, dq_ref, dk_ref, dv_ref, dkt, dvt):
        if not big:
            dkt[...] = jnp.zeros_like(dkt)
            dvt[...] = jnp.zeros_like(dvt)
        for i, (qs, qn, ks, kn) in enumerate(blocks_of(rows, own, win, big)):
            mask = qs_ref[qs : qs + qn, :] == ks_ref[:, ks : ks + kn]
            for h in range(2):
                lanes = slice(h * HEAD_DIM, (h + 1) * HEAD_DIM)
                qh = q_ref[0, qs : qs + qn, lanes] * BF16(scale)
                kh = k_ref[0, ks : ks + kn, lanes]
                gh = g_ref[0, qs : qs + qn, lanes]
                s = jnp.where(mask, dot_nt(qh, kh) - l_ref[0, qs : qs + qn, h : h + 1], NEG)
                p = jnp.exp(s)
                dp = dot_nt(gh, v_ref[0, ks : ks + kn, lanes])
                delta = jnp.sum(
                    gh.astype(F32) * a_ref[0, qs : qs + qn, lanes].astype(F32), axis=1, keepdims=True
                )
                ds = (p * (dp - delta)).astype(BF16)
                dq_ref[0, qs : qs + qn, lanes] = (dot_nn(ds, kh) * scale).astype(BF16)
                dk = dot_tn(qh, ds)
                dv = dot_tn(gh, p.astype(BF16))
                if big and i == 0:
                    dkt[lanes, :] = dk
                    dvt[lanes, :] = dv
                else:
                    dkt[lanes, ks : ks + kn] += dk
                    dvt[lanes, ks : ks + kn] += dv
        dk_ref[0] = dkt[...].T.astype(BF16)
        dv_ref[0] = dvt[...].T.astype(BF16)

    def body(info_ref, *refs):
        @pl.when(info_ref[0] == 1)
        def _():
            work(True, *refs)

        @pl.when(info_ref[0] == 0)
        def _():
            work(False, *refs)

    if pairs > 1:

        def put(d, p, info):
            rel = lax.bitwise_xor(p // (pairs // 2), info[1])
            return (rel, 0, d * (pairs // 2) + p % (pairs // 2))

        half_shape = (2, rows, n * cw // 2)
        half_win = (2, win, n * cw // 2)
    else:

        def put(d, p, info):
            return (0, 0, d)

        half_shape = (1, rows, n * cw)
        half_win = (1, win, n * cw)
    return pl.pallas_call(
        body,
        grid_spec=pltpu.PrefetchScalarGridSpec(
            num_scalar_prefetch=1,
            grid=(n, pairs),
            in_specs=[
                pl.BlockSpec((1, rows, PAIR), lambda d, p, *_: (d, 0, p)),
                pl.BlockSpec((1, win, PAIR), lambda d, p, *_: (d, 0, p)),
                pl.BlockSpec((1, win, PAIR), lambda d, p, *_: (d, 0, p)),
                pl.BlockSpec((1, rows, PAIR), lambda d, p, *_: (d, 0, p)),
                pl.BlockSpec((1, rows, PAIR), lambda d, p, *_: (d, 0, p)),
                pl.BlockSpec((1, rows, 2), lambda d, p, *_: (d * pairs + p, 0, 0)),
                pl.BlockSpec((rows, 1), lambda d, p, *_: (0, 0)),
                pl.BlockSpec((1, win), lambda d, p, *_: (0, 0)),
            ],
            out_specs=[
                pl.BlockSpec((1, rows, PAIR), put),
                pl.BlockSpec((1, win, PAIR), put),
                pl.BlockSpec((1, win, PAIR), put),
            ],
            scratch_shapes=[pltpu.VMEM((PAIR, win), F32), pltpu.VMEM((PAIR, win), F32)],
        ),
        out_shape=[
            jax.ShapeDtypeStruct(half_shape, BF16),
            jax.ShapeDtypeStruct(half_win, BF16),
            jax.ShapeDtypeStruct(half_win, BF16),
        ],
        compiler_params=params("arbitrary", "arbitrary"),
        cost_estimate=pl.CostEstimate(
            flops=40 * n * rows * win * cw, bytes_accessed=2 * n * cw * (4 * rows + 4 * win), transcendentals=n * rows * win * 4
        ),
    )(info, q, k, v, attn, gattn, lse, qseg, kseg)


def out_call(attn, packed, resid, b_out, gain, bias):
    n, rows, cw = attn.shape
    dm = packed.shape[1]

    def body(a_ref, w_ref, x_ref, bo_ref, g_ref, b_ref, h_ref, n_ref):
        d = pl.program_id(0)
        part = dot_nt(a_ref[0], w_ref[0])

        @pl.when(d == 0)
        def _():
            h_ref[...] = part + x_ref[...].astype(F32) + bo_ref[...].astype(F32)

        @pl.when(d > 0)
        def _():
            h_ref[...] += part

        @pl.when(d == n - 1)
        def _():
            hat, _ = norm_rows(h_ref[...])
            n_ref[...] = (hat * g_ref[...].astype(F32) + b_ref[...].astype(F32)).astype(BF16)

    full = lambda d: (0, 0)
    return pl.pallas_call(
        body,
        grid=(n,),
        in_specs=[
            pl.BlockSpec((1, rows, cw), lambda d: (d, 0, 0)),
            pl.BlockSpec((1, dm, cw), lambda d: (d, 0, 3)),
            pl.BlockSpec((rows, dm), full),
            pl.BlockSpec((1, dm), full),
            pl.BlockSpec((1, dm), full),
            pl.BlockSpec((1, dm), full),
        ],
        out_specs=[pl.BlockSpec((rows, dm), full), pl.BlockSpec((rows, dm), full)],
        out_shape=[jax.ShapeDtypeStruct((rows, dm), F32), jax.ShapeDtypeStruct((rows, dm), BF16)],
        compiler_params=params("arbitrary"),
        cost_estimate=pl.CostEstimate(flops=2 * n * rows * cw * dm, bytes_accessed=2 * n * dm * cw, transcendentals=0),
    )(attn, packed, resid, b_out[None], gain[None], bias[None])


def up_call(n2, w_up, b_up):
    rows, dm = n2.shape
    ff = w_up.shape[1]
    tile = 512

    def body(x_ref, w_ref, b_ref, a_ref, s_ref):
        u = dot_nn(x_ref[...], w_ref[...]) + b_ref[...].astype(F32)
        cdf = 0.5 * (1.0 + lax.erf(u * 0.7071067811865476))
        a_ref[...] = (u * cdf).astype(BF16)
        s_ref[...] = (cdf + u * jnp.exp(-0.5 * u * u) * 0.3989422804014327).astype(BF16)

    return pl.pallas_call(
        body,
        grid=(ff // tile,),
        in_specs=[
            pl.BlockSpec((rows, dm), lambda t: (0, 0)),
            pl.BlockSpec((dm, tile), lambda t: (0, t)),
            pl.BlockSpec((1, tile), lambda t: (0, t)),
        ],
        out_specs=[pl.BlockSpec((rows, tile), lambda t: (0, t)), pl.BlockSpec((rows, tile), lambda t: (0, t))],
        out_shape=[jax.ShapeDtypeStruct((rows, ff), BF16), jax.ShapeDtypeStruct((rows, ff), BF16)],
        compiler_params=params("arbitrary"),
        cost_estimate=pl.CostEstimate(flops=2 * rows * dm * ff, bytes_accessed=2 * dm * ff, transcendentals=2 * rows * ff),
    )(n2, w_up, b_up[None])


def norm1_back_call(dq, dk, dv, packed, info, own):
    halves, rows, _ = dq.shape
    n, dm, four = packed.shape
    cw = four // 4
    win = dk.shape[1]
    width = cw // halves

    def body(info_ref, dq_ref, dk_ref, dv_ref, wq_ref, wk_ref, wv_ref, o_ref, h_ref, t_ref, acc):
        step = pl.program_id(0)
        part = dot_nt(dk_ref[0], wk_ref[0]) + dot_nt(dv_ref[0], wv_ref[0])
        mine = dot_nt(dq_ref[0], wq_ref[0])

        @pl.when(step == 0)
        def _():
            acc[...] = part

        @pl.when(step > 0)
        def _():
            acc[...] += part

        acc[own : own + rows, :] += mine

        @pl.when(step == n * halves - 1)
        def _():
            o_ref[...] = acc[own : own + rows, :]
            h_ref[...] = acc[0:own, :].astype(BF16)
            t_ref[...] = acc[own + rows : own + rows + HALO, :].astype(BF16)

    def grad_map(s, info):
        return (s // n, 0, s % n)

    def weight_map(which):
        def f(s, info):
            part = lax.bitwise_xor(s // n, info[1]) if halves > 1 else 0
            return (s % n, 0, which * halves + part)

        return f

    full = lambda s, info: (0, 0)
    return pl.pallas_call(
        body,
        grid_spec=pltpu.PrefetchScalarGridSpec(
            num_scalar_prefetch=1,
            grid=(n * halves,),
            in_specs=[
                pl.BlockSpec((1, rows, width), grad_map),
                pl.BlockSpec((1, win, width), grad_map),
                pl.BlockSpec((1, win, width), grad_map),
                pl.BlockSpec((1, dm, width), weight_map(0)),
                pl.BlockSpec((1, dm, width), weight_map(1)),
                pl.BlockSpec((1, dm, width), weight_map(2)),
            ],
            out_specs=[
                pl.BlockSpec((rows, dm), full),
                pl.BlockSpec((own, dm), full),
                pl.BlockSpec((HALO, dm), full),
            ],
            scratch_shapes=[pltpu.VMEM((win, dm), F32)],
        ),
        out_shape=[
            jax.ShapeDtypeStruct((rows, dm), F32),
            jax.ShapeDtypeStruct((own, dm), BF16),
            jax.ShapeDtypeStruct((HALO, dm), BF16),
        ],
        compiler_params=params("arbitrary"),
        cost_estimate=pl.CostEstimate(
            flops=2 * n * cw * dm * (rows + 2 * win), bytes_accessed=2 * n * cw * (3 * dm + rows + 2 * win), transcendentals=0
        ),
    )(info, dq, dk, dv, packed, packed, packed)


def swap(v, bit):
    return lax.ppermute(v, "dp", [(i, i ^ bit) for i in range(8)])


def plane_spread(v, axis):
    half = v.shape[axis] // 2
    first = lambda a: lax.slice_in_dim(a, 0, half, axis=axis)
    second = lambda a: lax.slice_in_dim(a, half, 2 * half, axis=axis)
    by_x = swap(v, 2)
    by_y = swap(v, 4)
    diag_a = swap(first(by_x), 4)
    diag_b = swap(second(by_y), 2)
    own = [v, by_x, by_y, diag_a, diag_b]
    return own + [swap(a, 1) for a in own]


def gather_shards(shard, me, after=None):
    step = shard.shape[0] // 8
    piece = lax.dynamic_slice_in_dim(shard, me * step, step, axis=0)
    if after is not None:
        piece, _ = barrier(piece, after)
    got = [lax.ppermute(piece, "mp", [((i + d) % 4, i) for i in range(4)]) for d in (1, 2, 3)]
    stack = jnp.stack(got)
    return stack, plane_spread(stack, 1)


def assemble(idx, shard, parts, mode):
    rows, cols = shard.shape
    step = rows // 8
    half = step // 2

    def body(idx_ref, l_ref, *refs):
        ins, out = refs[:-1], refs[-1]
        o = pl.program_id(0)

        def put(d, a, b, x):
            if mode == "stack":
                out[d, 0, a:b, :] = x
            elif mode == "rows":
                out[0, 0, d, 0, a:b, :] = x
            else:
                for j in range(2):
                    rel = lax.bitwise_xor(j, idx_ref[0])
                    for ab in range(2):
                        at = pl.multiple_of(rel * (cols * 2) + ab * cols + d * (cols // 4), 128)
                        src = (2 * j + ab) * (cols // 4)
                        out[a:b, pl.ds(at, cols // 4)] = x[:, src : src + cols // 4]

        put(0, 0, step, l_ref[...])
        for off in range(8):
            base = 5 * (off & 1)

            @pl.when(o == off)
            def _():
                for d in range(3):
                    if off // 2 < 3:
                        put(d + 1, 0, step, ins[base + off // 2][d])
                    else:
                        put(d + 1, 0, half, ins[base + 3][d])
                        put(d + 1, half, step, ins[base + 4][d])

    if mode == "stack":
        shape = (4, 8, step, cols)
        out_spec = pl.BlockSpec((4, 1, step, cols), lambda o, idx: (0, idx[1 + o], 0, 0))
        final = (4, rows, cols)
    elif mode == "rows":
        shape = (2, 2, 4, 2, step, cols)
        out_spec = pl.BlockSpec(
            (1, 1, 4, 1, step, cols),
            lambda o, idx: (
                lax.bitwise_xor(idx[1 + o] // 4, idx[0]),
                lax.rem(idx[1 + o] // 2, 2),
                0,
                lax.rem(idx[1 + o], 2),
                0,
                0,
            ),
        )
        final = (4 * rows, cols)
    else:
        shape = (rows, 4 * cols)
        out_spec = pl.BlockSpec((step, 4 * cols), lambda o, idx: (idx[1 + o], 0))
        final = shape
    once = pl.Buffered(1)
    in_specs = [pl.BlockSpec((step, cols), lambda o, idx: (idx[1 + o], 0))]
    for a in parts:
        in_specs.append(pl.BlockSpec(a.shape, lambda o, idx: (0, 0, 0), pipeline_mode=once))
    out = pl.pallas_call(
        body,
        grid_spec=pltpu.PrefetchScalarGridSpec(
            num_scalar_prefetch=1, grid=(8,), in_specs=in_specs, out_specs=out_spec
        ),
        out_shape=jax.ShapeDtypeStruct(shape, BF16),
        compiler_params=params("arbitrary"),
        cost_estimate=pl.CostEstimate(flops=0, bytes_accessed=16 * rows * cols, transcendentals=0),
    )(idx, shard, *parts)
    return out.reshape(final)


def reduce_grad(a, b, y, x):
    rows, cols = a.shape
    half, quarter = rows // 2, rows // 4
    w = cols // 4

    def cut(v, at, size):
        return lax.dynamic_slice_in_dim(v, at * size, size, axis=0)

    def add(u, v):
        return (u.astype(F32) + v.astype(F32)).astype(BF16)

    a1 = swap(cut(a, 1 - x, half), 2)
    b1 = swap(cut(b, 1 - y, half), 4)
    a = add(cut(a, x, half), a1)
    b = add(cut(b, y, half), b1)
    a2 = swap(cut(a, 1 - y, quarter), 4)
    b2 = swap(cut(b, 1 - x, quarter), 2)
    both = jnp.concatenate([add(cut(a, y, quarter), a2), add(cut(b, x, quarter), b2)], axis=0)
    total = both[:, :w].astype(F32)
    for d in (1, 2, 3):
        got = lax.ppermute(both[:, d * w : (d + 1) * w], "mp", [(i, (i + d) % 4) for i in range(4)])
        total = total + got.astype(F32)
    return plane_spread(total.astype(BF16), 0)


def place_grads(coords, parts, mode):
    two_q, w = parts[0].shape
    q = two_q // 2
    dm = 4 * q

    def body(c_ref, *refs):
        ins, outs = refs[:10], refs[10:]
        for off in range(8):
            y = lax.bitwise_xor(c_ref[0], off >> 2)
            x = lax.bitwise_xor(c_ref[1], (off >> 1) & 1)
            k = lax.bitwise_xor(c_ref[2], off & 1)
            base = 5 * (off & 1)
            for part in range(2):
                if off // 2 < 3:
                    val = ins[base + off // 2][part * q : (part + 1) * q, :]
                else:
                    val = ins[base + 3 + part][...]
                val = val.astype(F32)
                rows = pl.ds(pl.multiple_of((x * 2 + y if part == 0 else y * 2 + x) * q, q), q)
                if mode == "up":
                    outs[0][rows, pl.ds(pl.multiple_of((k * 2 + part) * w, w), w)] = val
                elif mode == "down":
                    outs[0][pl.ds(pl.multiple_of((k * 2 + part) * w, w), w), rows] = val.T
                else:
                    at = pl.ds(pl.multiple_of(k * (w // 2), w // 2), w // 2)
                    if part == 0:
                        outs[0][rows, at] = val[:, : w // 2]
                        outs[1][rows, at] = val[:, w // 2 :]
                    else:
                        outs[2][rows, at] = val[:, : w // 2]
                        outs[3][at, rows] = val[:, w // 2 :].T

    if mode == "up":
        shapes = [(dm, 4 * w)]
    elif mode == "down":
        shapes = [(4 * w, dm)]
    else:
        shapes = [(dm, w), (dm, w), (dm, w), (w, dm)]
    return pl.pallas_call(
        body,
        in_specs=[pl.BlockSpec(memory_space=pltpu.SMEM)] + [pl.BlockSpec(memory_space=pltpu.VMEM)] * 10,
        out_specs=[pl.BlockSpec(memory_space=pltpu.VMEM)] * len(shapes),
        out_shape=[jax.ShapeDtypeStruct(s, F32) for s in shapes],
        compiler_params=pltpu.CompilerParams(vmem_limit_bytes=VMEM),
        cost_estimate=pl.CostEstimate(flops=0, bytes_accessed=6 * 4 * dm * w, transcendentals=0),
    )(coords, *parts)


def relative(stack, z):
    return jnp.roll(stack, -z, axis=0)


def core_first(v, core, axis):
    return jnp.where(core == 0, v, jnp.flip(v, axis))


def gather_any(shard, z, core, mode):
    mp = lax.axis_size("mp")
    whole = relative(lax.all_gather(shard, "mp", axis=0, tiled=False), z)
    if mode == "stack":
        return whole
    if mode == "rows":
        v = whole.reshape(mp, 2, 2, shard.shape[0] // 4, shard.shape[1])
        v = core_first(v.transpose(1, 2, 0, 3, 4), core, 0)
        return v.reshape(mp * shard.shape[0], shard.shape[1])
    v = whole.reshape(mp, shard.shape[0], 2, 2, shard.shape[1] // 4).transpose(1, 2, 3, 0, 4)
    return core_first(v, core, 1).reshape(shard.shape[0], mp * shard.shape[1])


def reduce_any(half, z, core):
    mp = lax.axis_size("mp")
    zero = jnp.zeros_like(half)
    v = jnp.stack([jnp.where(core == 0, half, zero), jnp.where(core == 1, half, zero)], axis=1)
    v = jnp.roll(jnp.moveaxis(v, 3, 0), z, axis=0).astype(BF16)
    v = lax.psum_scatter(v, "mp", scatter_dimension=0, tiled=True)[0]
    return lax.psum(v.astype(BF16), "dp").astype(F32)


def local(
    tokens,
    segments,
    ln1_gain,
    ln1_bias,
    w_query,
    b_query,
    w_key,
    w_value,
    b_value,
    w_out,
    b_out,
    ln2_gain,
    ln2_bias,
    w_up,
    b_up,
    w_down,
    b_down,
    cotangent,
):
    rows, dm = tokens.shape
    cw = w_query.shape[1]
    ffw = w_up.shape[1]
    mp = lax.axis_size("mp")
    dp = lax.axis_size("dp")
    fast = mp == 4 and dp == 8 and rows % 128 == 0
    z = lax.axis_index("mp")
    me = lax.axis_index("dp")
    core = lax.rem(me, 2)
    x = lax.rem(me // 2, 2)
    y = me // 4
    f32 = lambda v: v.astype(F32)

    near = -(-LONGEST // rows)
    own = (near - 1) * rows
    win = own + rows + 2 * HALO
    halo = [
        lax.ppermute(tokens, "mp", [((i + j) % near, i) for i in range(near)]) for j in range(1, near)
    ]
    before = lax.ppermute(tokens[-HALO:], "mp", [(i - 1, i) for i in range(near, mp)])
    behind = lax.ppermute(tokens[:HALO], "mp", [(i + 1, i) for i in range(near - 1, mp - 1)])
    small_vec = jnp.concatenate([b_query, b_value, b_up])
    if fast:
        vecs = [small_vec] + [
            lax.ppermute(small_vec, "mp", [((i + d) % mp, i) for i in range(mp)]) for d in range(1, mp)
        ]
        vecs = jnp.stack(vecs)
    else:
        vecs = relative(lax.all_gather(small_vec, "mp", axis=0, tiled=False), z)
    bq_all, bv_all = vecs[:, :cw], vecs[:, cw : 2 * cw]
    bu_all = vecs[:, 2 * cw :].reshape(mp, 2, 2, ffw // 4).transpose(1, 2, 0, 3)
    bu_all = core_first(bu_all, core, 0).reshape(mp * ffw)

    is_near = z < near
    seg_parts = [
        jnp.where(is_near, lax.dynamic_slice_in_dim(segments, lax.rem(z + j, near) * rows, rows), -1)
        for j in range(1, near)
    ]
    seg_own = lax.dynamic_slice_in_dim(segments, z * rows, rows)
    seg_prev = lax.dynamic_slice_in_dim(segments, jnp.maximum(z * rows - HALO, 0), HALO)
    seg_next = lax.dynamic_slice_in_dim(segments, jnp.minimum((z + 1) * rows, segments.shape[0] - HALO), HALO)
    seg_far = jnp.concatenate(seg_parts)
    seg_far = jnp.concatenate([seg_far[:-HALO], jnp.where(is_near, seg_far[-HALO:], seg_prev)])
    has_next = jnp.logical_and(z >= near - 1, z < mp - 1)
    seg_win = jnp.concatenate(
        [seg_far, seg_own, jnp.where(has_next, seg_next, -1), jnp.full((HALO,), -1, segments.dtype)]
    )
    kseg, qseg = seg_win[None, :], seg_own[:, None]
    info = jnp.stack([is_near.astype(jnp.int32), core]).astype(jnp.int32)

    pack = jnp.concatenate([w_query, w_key, w_value, w_out.T], axis=1)
    if fast:
        idx = jnp.concatenate([core[None], jnp.bitwise_xor(me, jnp.arange(8, dtype=jnp.int32))]).astype(jnp.int32)
        mark1, parts1 = gather_shards(pack, me)
        mark2, parts2 = gather_shards(w_up, me, mark1)
        _, parts3 = gather_shards(w_down, me, mark2)
        packed = assemble(idx, pack, parts1, "stack")
        up_all = assemble(idx, w_up, parts2, "cols")
        down_all = assemble(idx, w_down, parts3, "rows")
    else:
        packed = gather_any(pack, z, core, "stack")
        up_all = gather_any(w_up, z, core, "cols")
        down_all = gather_any(w_down, z, core, "rows")

    far = jnp.concatenate(halo, axis=0)
    far = jnp.concatenate([far[:-HALO], far[-HALO:] + before], axis=0)
    tok_win = jnp.concatenate([far, tokens, behind, jnp.zeros((HALO, dm), tokens.dtype)], axis=0)
    hat_win, inv_win = norm_rows(f32(tok_win))
    n1w = (hat_win * f32(ln1_gain) + f32(ln1_bias)).astype(BF16)
    q, k, v = qkv_call(n1w, packed, bq_all, bv_all, own, rows, cw)
    attn, lse = attn_fwd_call(info, q, k, v, qseg, kseg, own)
    hidden, n2 = out_call(attn, packed, tokens, b_out, ln2_gain, ln2_bias)
    active, slope = up_call(n2, up_all, bu_all)
    output = (hidden + dot_nn(active, down_all) + f32(b_down)).astype(BF16)

    other = lambda v: lax.ppermute(v, "dp", [(i, i ^ 1) for i in range(dp)])
    hw = mp * ffw // 2
    cot_o = other(cotangent)
    act_o = other(active[:, hw:])
    gout = f32(cotangent)

    def pair_grad(left, right, left_o, right_o):
        return (dot_tn(left, right) + dot_tn(left_o, right_o)).astype(BF16)

    gd_a = pair_grad(cotangent, active[:, : hw // 2], cot_o, act_o[:, : hw // 2])
    gd_b = pair_grad(cotangent, active[:, hw // 2 : hw], cot_o, act_o[:, hw // 2 :])
    g_upper = (dot_nt(cotangent, down_all) * f32(slope)).astype(BF16)
    n2_o = other(n2)
    gup_o = other(g_upper[:, hw:])
    gu_a = pair_grad(n2, g_upper[:, : hw // 2], n2_o, gup_o[:, : hw // 2])
    gu_b = pair_grad(n2, g_upper[:, hw // 2 : hw], n2_o, gup_o[:, hw // 2 :])
    g_b_up = jnp.sum(f32(g_upper), axis=0)
    g_n2 = dot_nt(g_upper, up_all)
    hat2, inv2 = norm_rows(hidden)

    def norm_back(g, hat, inv, gain):
        gg = g * gain
        first = jnp.mean(gg, axis=1, keepdims=True)
        second = jnp.mean(gg * hat, axis=1, keepdims=True)
        return inv * (gg - first - hat * second), jnp.sum(g * hat, axis=0), jnp.sum(g, axis=0)

    g_hidden, g_gain2, g_bias2 = norm_back(g_n2, hat2, inv2, f32(ln2_gain))
    g_hidden = g_hidden + gout
    ghb = g_hidden.astype(BF16)

    g_attn = jnp.stack([dot_nn(ghb, packed[d, :, 3 * cw :]).astype(BF16) for d in range(mp)])
    dq, dk, dv = attn_bwd_call(info, q, k, v, attn, g_attn, lse, qseg, kseg, own)
    halves = dq.shape[0]
    g_own, g_far, g_next = norm1_back_call(dq, dk, dv, packed, info, own)
    back = g_own
    for j in range(1, near):
        part = g_far[(j - 1) * rows : j * rows]
        back = back + f32(lax.ppermute(part, "mp", [(i, (i + j) % near) for i in range(near)]))
    to_prev = f32(lax.ppermute(g_far[-HALO:], "mp", [(i, i - 1) for i in range(near, mp)]))
    to_next = f32(lax.ppermute(g_next, "mp", [(i, i + 1) for i in range(near - 1, mp - 1)]))
    back = jnp.concatenate([back[:HALO] + to_next, back[HALO:-HALO], back[-HALO:] + to_prev], axis=0)
    hat1 = hat_win[own : own + rows]
    inv1 = inv_win[own : own + rows]
    g_in, g_gain1, g_bias1 = norm_back(back, hat1, inv1, f32(ln1_gain))
    g_tokens = g_in + g_hidden

    n1 = n1w[own : own + rows]
    if fast:
        n1w_o = other(n1w)
        ghb_o = other(ghb)
        attn_h = attn.reshape(mp, rows, 2, cw // 2).transpose(2, 1, 0, 3).reshape(2, rows, mp * cw // 2)
        attn_m = lax.dynamic_index_in_dim(attn_h, core, 0, keepdims=False)
        attn_t = lax.dynamic_index_in_dim(attn_h, 1 - core, 0, keepdims=False)
        dq_o, dk_o, dv_o, at_o = other(dq[1]), other(dk[1]), other(dv[1]), other(attn_t)
        n1_o = n1w_o[own : own + rows]
        half = cw // 2
        by_shard = lambda v: v.reshape(dm, mp, half)
        gq = by_shard(pair_grad(n1, dq[0], n1_o, dq_o))
        gk = by_shard(pair_grad(n1w, dk[0], n1w_o, dk_o))
        gv = by_shard(pair_grad(n1w, dv[0], n1w_o, dv_o))
        go = by_shard(pair_grad(ghb, attn_m, ghb_o, at_o))
        gp_a = jnp.concatenate([gq, gk], axis=2).reshape(dm, mp * cw)
        gp_b = jnp.concatenate([gv, go], axis=2).reshape(dm, mp * cw)
        coords = jnp.stack([y, x, core]).astype(jnp.int32)
        (g_w_down,) = place_grads(coords, reduce_grad(gd_a, gd_b, y, x), "down")
        (g_w_up,) = place_grads(coords, reduce_grad(gu_a, gu_b, y, x), "up")
        g_w_query, g_w_key, g_w_value, g_w_out = place_grads(coords, reduce_grad(gp_a, gp_b, y, x), "pack")
    else:
        two = lambda a, b: jnp.stack([a, b], axis=1).reshape(dm, 2, mp, ffw // 4)
        g_w_up = reduce_any(two(gu_a, gu_b), z, core).reshape(dm, ffw)
        g_w_down = reduce_any(two(gd_a, gd_b), z, core).reshape(dm, ffw).T

        def whole_grad(left, right, name=None):
            v = dot_tn(left, right).astype(BF16).reshape(dm, mp, cw)
            v = jnp.roll(jnp.moveaxis(v, 1, 0), z, axis=0)
            v = lax.psum_scatter(v, "mp", scatter_dimension=0, tiled=True)[0]
            return lax.psum(v, "dp").astype(F32)

        def whole(v):
            if halves == 1:
                return v[0]
            v = v.reshape(2, v.shape[1], mp, cw // 2).transpose(1, 2, 0, 3)
            return core_first(v, core, 2).reshape(v.shape[0], mp * cw)

        g_w_query = whole_grad(n1, whole(dq))
        g_w_key = whole_grad(n1w, whole(dk))
        g_w_value = whole_grad(n1w, whole(dv))
        g_w_out = whole_grad(ghb, attn.transpose(1, 0, 2).reshape(rows, mp * cw)).T

    def shards(v, width):
        if v.shape[0] == 2:
            v = core_first(v.reshape(2, mp, width // 2), core, 0).transpose(1, 0, 2)
        return jnp.roll(v.reshape(mp, width), z, axis=0).reshape(mp * width)

    gbq = shards(jnp.sum(f32(dq), axis=1), cw)
    gbv = shards(jnp.sum(f32(dv), axis=1), cw)
    gbu = core_first(g_b_up.reshape(2, 2, mp, ffw // 4), core, 0).transpose(2, 0, 1, 3)
    gbu = jnp.roll(gbu.reshape(mp, ffw), z, axis=0).reshape(-1)
    vec = jnp.concatenate(
        [g_gain1, g_bias1, jnp.sum(g_hidden, axis=0), g_gain2, g_bias2, jnp.sum(gout, axis=0), gbq, gbv, gbu]
    )
    vec = lax.psum(vec, ("dp", "mp"))
    g_gain1, g_bias1, g_b_out, g_gain2, g_bias2, g_b_down = (vec[i * dm : (i + 1) * dm] for i in range(6))
    at = 6 * dm
    g_b_query = lax.dynamic_slice_in_dim(vec, at + z * cw, cw)
    g_b_value = lax.dynamic_slice_in_dim(vec, at + mp * cw + z * cw, cw)
    g_b_up = lax.dynamic_slice_in_dim(vec, at + 2 * mp * cw + z * ffw, ffw)
    return (
        output,
        g_tokens,
        g_gain1,
        g_bias1,
        g_w_query,
        g_b_query,
        g_w_key,
        g_w_value,
        g_b_value,
        g_w_out,
        g_b_out,
        g_gain2,
        g_bias2,
        g_w_up,
        g_b_up,
        g_w_down,
        g_b_down,
    )


def solution(mesh):
    in_specs = (
        P(("dp", "mp"), None),
        P("dp"),
        P(),
        P(),
        P(None, "mp"),
        P("mp"),
        P(None, "mp"),
        P(None, "mp"),
        P("mp"),
        P("mp", None),
        P(),
        P(),
        P(),
        P(None, "mp"),
        P("mp"),
        P("mp", None),
        P(),
        P(("dp", "mp"), None),
    )
    out_specs = (
        P(("dp", "mp"), None),
        P(("dp", "mp"), None),
        P(),
        P(),
        P(None, "mp"),
        P("mp"),
        P(None, "mp"),
        P(None, "mp"),
        P("mp"),
        P("mp", None),
        P(),
        P(),
        P(),
        P(None, "mp"),
        P("mp"),
        P("mp", None),
        P(),
    )
    return jax.shard_map(local, mesh=mesh, in_specs=in_specs, out_specs=out_specs, check_vma=False)
```

time: 1150 us -> 690 us (0.60)
  waiting for transfers between devices: 647 us -> 191 us
  matrix products: 277 us -> 83.7 us
  Pallas kernels: 0 us -> 150 us
  starting transfers between devices: 1.01 us -> 109 us
  other arithmetic: 116 us -> 46 us
  local copies, waits for them, and re-layouts: 29.5 us -> 61 us
  blocking collectives: 55.9 us -> 38.9 us
  between operations: 14.6 us -> 2.57 us
    all_gather x4 -> x0, waiting for transfers between devices: 286 us -> none  [the longest x1 83.5 us: local(): gathered_one = lax.all_gather(normed_one, 'mp', axis=0, tiled=True)]
    reduce_scatter x4 -> x0, waiting for transfers between devices: 283 us -> none  [the longest x1 76.5 us: local(): lax.psum_scatter(matmul(active, w_down).astype(jnp.bfloat16), 'mp', scatt...]
    dot_general x46 -> x23, matrix products: 277 us -> 83.7 us  [the longest x16 47.1 us: dot_tn(): lax.dot_general(a, b, (((0,), (0,)), ((), ())), preferred_element_type=F32)]
    ppermute x0 -> x103, waiting for transfers between devices: none -> 191 us  [the longest x66 117 us: swap(): return lax.ppermute(v, 'dp', [(i, i ^ bit) for i in range(8)])]
    pallas_call x0 -> x12, Pallas kernels: none -> 150 us  [the longest x1 30.5 us: attn_bwd_call(): pl.pallas_call(body, grid_spec=pltpu.PrefetchScalarGridSpec(num_scalar_pr...]
    ppermute x0 -> x103, starting transfers between devices: none -> 109 us  [the longest x66 51.4 us: swap(): return lax.ppermute(v, 'dp', [(i, i ^ bit) for i in range(8)])]
    psum x1 -> x0, waiting for transfers between devices: 78 us -> none  [local(): lax.psum(grad_w_query.astype(jnp.bfloat16), 'dp').astype(jnp.float32)]
    convert_element_type x26 -> x20, other arithmetic: 66 us -> 7.72 us  [the longest x12 4.85 us: add(): return (u.astype(F32) + v.astype(F32)).astype(BF16)]
  transfers between devices with their start and end apart: 9 -> 103, of which waited for: 9 -> 24; matrix products, arithmetic and copies ran while one was open for 6% -> 27% of each run, Pallas kernels for 0% -> 21%
where the time goes in v1:
time: 690 us; the launch traced here: 681 us
  waiting for transfers between devices  191 us (28%)
  Pallas kernels  150 us (22%)
  starting transfers between devices  109 us (16%)
  matrix products  83.7 us (12%)
  local copies, waits for them, and re-layouts  61 us (9%)
  other arithmetic  46 us (7%)
  blocking collectives  38.9 us (6%)
    ppermute x66, waiting for transfers between devices, swap(): return lax.ppermute(v, 'dp', [(i, i ^ bit) for i in range(8)])  117 us
    ppermute x66, starting transfers between devices, swap(): return lax.ppermute(v, 'dp', [(i, i ^ bit) for i in range(8)])  51.4 us
    dot_general x16, matrix products, dot_tn(): lax.dot_general(a, b, (((0,), (0,)), ((), ())), preferred_element_type=F32)  47.1 us
    psum x1, blocking collectives, local(): vec = lax.psum(vec, ('dp', 'mp'))  38.9 us
    ppermute x9, waiting for transfers between devices, reduce_grad(): lax.ppermute(both[:, d * w:(d + 1) * w], 'mp', [(i, (i + d) % 4) for i in...  30.9 us
    pallas_call x1, Pallas kernels, attn_bwd_call(): pl.pallas_call(body, grid_spec=pltpu.PrefetchScalarGridSpec(num_scalar_pr...  30.5 us
    pallas_call x3, Pallas kernels, assemble(): pl.pallas_call(body, grid_spec=pltpu.PrefetchScalarGridSpec(num_scalar_pr...  29 us
    pallas_call x1, Pallas kernels, attn_fwd_call(): pl.pallas_call(body, grid_spec=pltpu.PrefetchScalarGridSpec(num_scalar_pr...  25.2 us
  transfers between devices with their start and end apart: 103, of which 24 were waited for; matrix products, arithmetic and copies ran while one was open for 27% of the time, Pallas kernels for 21%

profile of v1, /device:TPU:0, one launch (start us, length us, event | category | flops | bytes accessed | tf_op | source)
XLA Modules:
  0.0 681.4 jit_solution(10549636152376598472)
XLA Ops:
  5.4 3.1 collective-permute-start.5
  8.5 2.6 collective-permute-start.4
  12.4 2.6 collective-permute-start
  21.3 7.3 %collective-permute-done.4 = bf16[128,1024]{1,0:T(8,128)(2,1)} collective-permute-done((bf16[128,1024]{1,0:T(8,128)(2,1)}, bf16[128,1024]{1,0:T(8,128)(2,1)}, u32[]{:S(2)}, u32[]{:S(2)}) %collective-permute-start.4) | collective-permute-done | bytes 262176 | tf_op jit(solution)/shard_map/ppermute | solution.py:399
  30.7 6.1 collective-permute-start.20
  39.8 9.5 %collective-permute-done.17 = bf16[1536]{0:T(1024)(128)(2,1)S(1)} collective-permute-done((bf16[1536]{0:T(1024)(128)(2,1)S(1)}, bf16[1536]{0:T(1024)(128)(2,1)S(1)}, u32[]{:S(2)}, u32[]{:S(2)}) %collective-permute-start.17) | collective-permute-done | bytes 3104 | tf_op jit(solution)/shard_map/ppermute | solution.py:624
  50.5 14.6 %collective-permute-done.16 = bf16[1536]{0:T(1024)(128)(2,1)S(1)} collective-permute-done((bf16[1536]{0:T(1024)(128)(2,1)S(1)}, bf16[1536]{0:T(1024)(128)(2,1)S(1)}, u32[]{:S(2)}, u32[]{:S(2)}) %collective-permute-start.16) | collective-permute-done | bytes 3104 | tf_op jit(solution)/shard_map/ppermute | solution.py:624
  72.4 5.2 collective-permute-start.32
  79.1 2.8 collective-permute-start.30
  85.7 8.2 %collective-permute-done.31 = bf16[128,1024]{1,0:T(8,128)(2,1)S(1)} collective-permute-done((bf16[128,1024]{1,0:T(8,128)(2,1)S(1)}, bf16[128,1024]{1,0:T(8,128)(2,1)S(1)}, u32[]{:S(2)}, u32[]{:S(2)}) %collective-permute-start.31) | collective-permute-done | bytes 262176 | tf_op jit(solution)/shard_map/ppermute | solution.py:399
  102.4 12.2 %collective-permute-done.6.refs_1_ = bf16[3,128,1024]{2,1,0:T(8,128)(2,1)S(1)} collective-permute-done((bf16[3,128,1024]{2,1,0:T(8,128)(2,1)}, bf16[3,128,1024]{2,1,0:T(8,128)(2,1)S(1)}, u32[]{:S(2)}, u32[]{:S(2)}) %collective-permute-start.6) | collective-permute-done | bytes 786464 | tf_op jit(solution)/shard_map/ppermute | solution.py:379
  118.7 12.9 %collective-permute-done.21.refs_1_ = bf16[3,128,1024]{2,1,0:T(8,128)(2,1)} collective-permute-done((bf16[3,128,1024]{2,1,0:T(8,128)(2,1)S(1)}, bf16[3,128,1024]{2,1,0:T(8,128)(2,1)}, u32[]{:S(2)}, u32[]{:S(2)}) %collective-permute-start.21) | collective-permute-done | bytes 786464 | tf_op jit(solution)/shard_map/ppermute | solution.py:379
  133.9 23.0 %collective-permute-done.8.refs_3_ = bf16[3,64,1024]{2,1,0:T(8,128)(2,1)S(1)} collective-permute-done((bf16[3,64,1024]{2,1,0:T(8,128)(2,1)S(1)}, bf16[3,64,1024]{2,1,0:T(8,128)(2,1)S(1)}, u32[]{:S(2)}, u32[]{:S(2)}) %collective-permute-start.8) | collective-permute-done | bytes 393248 | tf_op jit(solution)/shard_map/ppermute | solution.py:379
  158.0 3.9 fusion.1
  170.8 9.6 %shard_map.305 = bf16[4,8,128,1024]{3,2,1,0:T(8,128)(2,1)} custom-call(s32[9]{0:T(128)} %pad_add_fusion.1.idx_ref, bf16[1024,1024]{1,0:T(8,128)(2,1)} %copy-done.5, bf16[3,128,1024]{2,1,0:T(8,128)(2,1)} %pad_maximum_fusion.5.refs_0_, bf16[3,128,1024]{2,1,0:T(8,128)(2,1)} %copy-done.19, bf16[3,128,1024]{2,1,0:T(8,128)(2,1)} %copy-done.20, ...), custom_call_target="tpu_custom_call" | custom-call | bytes 16777216 | tf_op jit(solution)/shard_map/pallas_call | solution.py:465
  180.4 10.2 %shard_map.306 = (bf16[4,512,256]{2,1,0:T(8,128)(2,1)}, bf16[4,1152,256]{2,1,0:T(8,128)(2,1)}, bf16[4,1152,256]{2,1,0:T(8,128)(2,1)}) custom-call(bf16[1152,1024]{1,0:T(8,128)(2,1)} %get-tuple-element.74.x_ref, bf16[4,1024,1024]{2,1,0:T(8,128)(2,1)} %bitcast.145, bf16[4,1,256]{2,1,0:T(2,128)(2,1)} %copy.53.bq_ref, bf16[4,1,256]{2,1,0:T(2,128)(2,1)} %copy.54.bv_ref), custom_call_target="tpu_custom_call" | custom-call | flops 5905580032 | bytes 10747904 | tf_op jit(solution)/shard_map/pallas_call | solution.py:58
  192.7 25.2 %shard_map.307 = (bf16[4,512,256]{2,1,0:T(8,128)(2,1)}, f32[8,512,2]{2,1,0:T(8,128)}) custom-call(s32[2]{0:T(128)} %pad_add_fusion.big_ref.info_ref, bf16[4,512,256]{2,1,0:T(8,128)(2,1)} %get-tuple-element.39.refs_0_, bf16[4,1152,256]{2,1,0:T(8,128)(2,1)} %get-tuple-element.40.refs_1_, bf16[4,1152,256]{2,1,0:T(8,128)(2,1)} %get-tuple-element.41.refs_2_, ...), custom_call_target="tpu_custom_call" | custom-call | flops 9663676416 | bytes 6815744 | tf_op jit(solution)/shard_map/pallas_call | solution.py:119
  217.8 7.1 %shard_map.308 = (f32[512,1024]{1,0:T(8,128)}, bf16[512,1024]{1,0:T(8,128)(2,1)}) custom-call(bf16[4,512,256]{2,1,0:T(8,128)(2,1)} %get-tuple-element.42.a_ref.refs_3_, bf16[4,1024,1024]{2,1,0:T(8,128)(2,1)} %bitcast.146, bf16[512,1024]{1,0:T(8,128)(2,1)} %x_ref.1, bf16[1,1024]{1,0:T(2,128)(2,1)} %broadcast_in_dim.54.bo_ref, ...), custom_call_target="tpu_custom_call" | custom-call | flops 1073741824 | bytes 2097152 | tf_op jit(solution)/shard_map/pallas_call | solution.py:263
  234.4 9.7 %shard_map.309.w_ref = bf16[1024,4096]{1,0:T(8,128)(2,1)} custom-call(s32[9]{0:T(128)} %pad_add_fusion.1.idx_ref, bf16[1024,1024]{1,0:T(8,128)(2,1)} %l_ref.2, bf16[3,128,1024]{2,1,0:T(8,128)(2,1)} %copy-done.16, bf16[3,128,1024]{2,1,0:T(8,128)(2,1)} %collective-permute-done.21.refs_1_, bf16[3,128,1024]{2,1,0:T(8,128)(2,1)} %copy-done.18, ...), custom_call_target="tpu_custom_call" | custom-call | bytes 16777216 | tf_op jit(solution)/shard_map/pallas_call | solution.py:465
  244.1 13.1 %shard_map.310 = (bf16[512,4096]{1,0:T(8,128)(2,1)}, bf16[512,4096]{1,0:T(8,128)(2,1)}) custom-call(bf16[512,1024]{1,0:T(8,128)(2,1)} %get-tuple-element.44.x_ref, bf16[1024,4096]{1,0:T(8,128)(2,1)} %shard_map.309.w_ref, bf16[1,4096]{1,0:T(2,128)(2,1)} %broadcast_in_dim_reshape.3.b_ref), custom_call_target="tpu_custom_call" | custom-call | flops 4294967296 | bytes 8388608 | tf_op jit(solution)/shard_map/pallas_call | solution.py:292
  257.2 3.2 slice.258
  262.5 9.6 %shard_map.311 = bf16[2,2,4,2,128,1024]{5,4,3,2,1,0:T(8,128)(2,1)} custom-call(s32[9]{0:T(128)} %pad_add_fusion.1.idx_ref, bf16[1024,1024]{1,0:T(8,128)(2,1)} %l_ref.3, bf16[3,128,1024]{2,1,0:T(8,128)(2,1)} %pad_maximum_fusion.7.refs_0_, bf16[3,128,1024]{2,1,0:T(8,128)(2,1)} %collective-permute-done.33.refs_1_, ...), custom_call_target="tpu_custom_call" | custom-call | bytes 16777216 | tf_op jit(solution)/shard_map/pallas_call | solution.py:465
  272.2 9.5 %convert_reduce_fusion = (f32[4096]{0:T(1024)S(1)}, bf16[512,4096]{1,0:T(8,128)(2,1)S(1)}) fusion(bf16[512,4096]{1,0:T(8,128)(2,1)} %get-tuple-element.48, bf16[4096,1024]{1,0:T(8,128)(2,1)} %bitcast.154, bf16[512,1024]{1,0:T(8,128)(2,1)} %param.37), kind=kOutput, calls=%fused_computation.2 | convolution fusion | flops 4305448960 | bytes 17842176 | tf_op jit(solution)/shard_map/dot_general | solution.py:26
  281.6 9.7 %multiply_reduce_fusion = (f32[1024]{0:T(1024)}, f32[512]{0:T(512)S(1)}, f32[512]{0:T(512)S(1)}, f32[1024]{0:T(1024)}, f32[512,1024]{1,0:T(8,128)S(1)}) fusion(f32[512,1024]{1,0:T(8,128)S(1)} %copy-done, f32[512]{0:T(512)S(1)} %add_rsqrt_fusion.1, f32[512]{0:T(512)S(1)} %broadcast_multiply_fusion.5, f32[1024]{0:T(1024)S(1)} %convert_element_type.258, ...), kind=kOutput, calls=%fused_computation.33 | convolution fusion | flops 4299682816 | bytes 16797696 | tf_op jit(solution)/shard_map/dot_general | solution.py:26
  303.1 30.5 %shard_map.312 = (bf16[2,512,512]{2,1,0:T(8,128)(2,1)}, bf16[2,1152,512]{2,1,0:T(8,128)(2,1)}, bf16[2,1152,512]{2,1,0:T(8,128)(2,1)}) custom-call(s32[2]{0:T(128)} %pad_add_fusion.big_ref.info_ref, bf16[4,512,256]{2,1,0:T(8,128)(2,1)} %get-tuple-element.39.refs_0_, bf16[4,1152,256]{2,1,0:T(8,128)(2,1)} %get-tuple-element.40.refs_1_, ...), custom_call_target="tpu_custom_call" | custom-call | flops 24159191040 | bytes 13631488 | tf_op jit(solution)/shard_map/pallas_call | solution.py:207
  337.1 23.1 %shard_map.313 = (f32[512,1024]{1,0:T(8,128)}, bf16[512,1024]{1,0:T(8,128)(2,1)}, bf16[64,1024]{1,0:T(8,128)(2,1)}) custom-call(s32[2]{0:T(128)} %pad_add_fusion.big_ref.info_ref, bf16[2,512,512]{2,1,0:T(8,128)(2,1)} %get-tuple-element.50.dq_ref, bf16[2,1152,512]{2,1,0:T(8,128)(2,1)} %get-tuple-element.51.dk_ref, ...), custom_call_target="tpu_custom_call" | custom-call | flops 5905580032 | bytes 12058624 | tf_op jit(solution)/shard_map/pallas_call | solution.py:346
  360.2 2.5 slice_bitcast_fusion.1
  365.0 7.3 %collective-permute-start.42 = (bf16[512,1024]{1,0:T(8,128)(2,1)}, bf16[512,1024]{1,0:T(8,128)(2,1)}, u32[]{:S(2)}, u32[]{:S(2)}) collective-permute-start(bf16[512,1024]{1,0:T(8,128)(2,1)} %get-tuple-element.54), channel_id=1, source_target_pairs={{0,1},{1,0},{4,5},{5,4},{8,9},{9,8},{12,13},{13,12},{16,17},{17,16... | collective-permute-start | bytes 3145736 | tf_op jit(solution)/shard_map/ppermute | solution.py:712
  374.6 10.3 %add_convert_fusion.13 = bf16[512,1024]{1,0:T(8,128)(2,1)} fusion(f32[512,1024]{1,0:T(8,128)S(1)} %copy-done, bf16[512,4096]{1,0:T(8,128)(2,1)} %get-tuple-element.46, bf16[4096,1024]{1,0:T(8,128)(2,1)} %bitcast.155, f32[1024]{0:T(1024)S(1)} %copy-done.64), kind=kOutput, calls=%fused_computation.40 | convolution fusion | flops 4296540160 | bytes 15732736 | tf_op jit(solution)/shard_map/dot_general | solution.py:22
  391.3 3.0 add_convert_fusion.12
  399.4 2.9 add_convert_fusion.8
  412.6 3.4 multiply_add_fusion
  416.5 3.5 fusion.65
  419.9 4.2 add_convert_fusion.11
  430.1 3.5 fusion.66
  433.7 4.2 add_convert_fusion.9
  437.9 2.5 copy.61
  440.4 2.7 pad_maximum_fusion.3
  445.2 2.9 fusion.22
  448.1 2.6 add_convert_fusion.2
  451.6 2.9 fusion.20
  454.4 2.6 add_convert_fusion.1
  458.2 2.7 fusion.27
  461.0 2.6 add_convert_fusion.4
  465.0 2.5 fusion.24
  471.5 2.8 add_convert_fusion.3
  474.4 27.8 %collective-permute-done.49 = bf16[256,1024]{1,0:T(8,128)(2,1)S(1)} collective-permute-done((bf16[256,1024]{1,0:T(8,128)(2,1)S(1)}, bf16[256,1024]{1,0:T(8,128)(2,1)S(1)}, u32[]{:S(2)}, u32[]{:S(2)}) %collective-permute-start.49) | collective-permute-done | bytes 524320 | tf_op jit(solution)/shard_map/ppermute | solution.py:379
  503.9 6.2 collective-permute-done.54
  510.4 5.1 collective-permute-start.56
  520.5 17.6 %collective-permute-done.56 = bf16[512,256]{1,0:T(8,128)(2,1)S(1)} collective-permute-done((bf16[512,256]{1,0:T(8,128)(2,1)S(1)}, bf16[512,256]{1,0:T(8,128)(2,1)S(1)}, u32[]{:S(2)}, u32[]{:S(2)}) %collective-permute-start.56) | collective-permute-done | bytes 262176 | tf_op jit(solution)/shard_map/ppermute | solution.py:497
  543.0 13.5 %collective-permute-done.58.refs_1_ = bf16[512,256]{1,0:T(8,128)(2,1)S(1)} collective-permute-done((bf16[512,256]{1,0:T(8,128)(2,1)S(1)}, bf16[512,256]{1,0:T(8,128)(2,1)S(1)}, u32[]{:S(2)}, u32[]{:S(2)}) %collective-permute-start.58) | collective-permute-done | bytes 262176 | tf_op jit(solution)/shard_map/ppermute | solution.py:379
  560.0 8.3 %collective-permute-done.70 = bf16[256,1024]{1,0:T(8,128)(2,1)S(1)} collective-permute-done((bf16[256,1024]{1,0:T(8,128)(2,1)S(1)}, bf16[256,1024]{1,0:T(8,128)(2,1)S(1)}, u32[]{:S(2)}, u32[]{:S(2)}) %collective-permute-start.70) | collective-permute-done | bytes 524320 | tf_op jit(solution)/shard_map/ppermute | solution.py:379
  570.6 3.9 collective-permute-start.75
  576.8 2.5 collective-permute-start.73
  580.0 6.3 collective-permute-done.92
  586.3 8.6 %collective-permute-start.61 = (bf16[256,256]{1,0:T(8,128)(2,1)S(1)}, bf16[256,256]{1,0:T(8,128)(2,1)S(1)}, u32[]{:S(2)}, u32[]{:S(2)}) collective-permute-start(bf16[256,256]{1,0:T(8,128)(2,1)S(1)} %slice.297), channel_id=1, source_target_pairs={{0,8},{4,12},{8,0},{12,4},{16,24},{20,28},{24,16},{28,20},{1,9},{5... | collective-permute-start | bytes 393224 | tf_op jit(solution)/shard_map/ppermute | solution.py:379
  595.1 2.8 collective-permute-done.61.refs_4_
  598.4 6.3 collective-permute-done.74
  610.3 3.6 collective-permute-done.94.refs_1_
  615.8 2.8 collective-permute-done.76.refs_1_
  625.1 38.9 %psum.7 = f32[12288]{0:T(1024)} all-reduce(f32[12288]{0:T(1024)} %bitcast_dynamic-update-slice_fusion), channel_id=1, replica_groups=mesh['dp'=8,'mp'=4] {'dp','mp'}, use_global_device_ids=true, to_apply=%region_19.21 | all-reduce | flops 12288 | bytes 98304 | tf_op jit(solution)/shard_map/psum | solution.py:776
  668.5 3.8 shard_map.314
  672.3 4.2 shard_map.316
  677.4 3.8 shard_map.315
  (482 shorter events, 166.7 us)
Async XLA Ops:
  8.5 20.1 %collective-permute-start.4 = (bf16[128,1024]{1,0:T(8,128)(2,1)}, bf16[128,1024]{1,0:T(8,128)(2,1)}, u32[]{:S(2)}, u32[]{:S(2)}) collective-permute-start(bf16[128,1024]{1,0:T(8,128)(2,1)} %constant_dynamic-slice_fusion.16), channel_id=1, source_target_pairs={{2,0},{3,1},{0,2},{1,3},{6,4},{7,5},{4,6},{5,7},{10,8},{11,9},{8,1... | collective-permute-start | bytes 786440 | tf_op jit(solution)/shard_map/ppermute | solution.py:399
  11.1 17.5 %collective-permute-start.3 = (bf16[128,1024]{1,0:T(8,128)(2,1)}, bf16[128,1024]{1,0:T(8,128)(2,1)}, u32[]{:S(2)}, u32[]{:S(2)}) collective-permute-start(bf16[128,1024]{1,0:T(8,128)(2,1)} %constant_dynamic-slice_fusion.16), channel_id=1, source_target_pairs={{1,0},{2,1},{3,2},{0,3},{5,4},{6,5},{7,6},{4,7},{9,8},{10,9},{11,1... | collective-permute-start | bytes 786440 | tf_op jit(solution)/shard_map/ppermute | solution.py:399
  12.4 86.5 %collective-permute-start = (bf16[512,1024]{1,0:T(8,128)(2,1)S(1)}, bf16[512,1024]{1,0:T(8,128)(2,1)}, u32[]{:S(2)}, u32[]{:S(2)}) collective-permute-start(bf16[512,1024]{1,0:T(8,128)(2,1)S(1)} %copy-done.9), channel_id=1, source_target_pairs={{1,0},{0,1},{5,4},{4,5},{9,8},{8,9},{13,12},{12,13},{17,16},{16,17... | collective-permute-start | bytes 3145736 | tf_op jit(solution)/shard_map/ppermute | solution.py:617
  15.7 33.5 %collective-permute-start.17 = (bf16[1536]{0:T(1024)(128)(2,1)S(1)}, bf16[1536]{0:T(1024)(128)(2,1)S(1)}, u32[]{:S(2)}, u32[]{:S(2)}) collective-permute-start(bf16[1536]{0:T(1024)(128)(2,1)S(1)} %dynamic-update-slice.11), channel_id=1, source_target_pairs={{3,0},{0,1},{1,2},{2,3},{7,4},{4,5},{5,6},{6,7},{11,8},{8,9},{9,10... | collective-permute-start | bytes 9224 | tf_op jit(solution)/shard_map/ppermute | solution.py:624
  30.7 40.4 %collective-permute-start.20 = (bf16[128,1024]{1,0:T(8,128)(2,1)}, bf16[128,1024]{1,0:T(8,128)(2,1)}, u32[]{:S(2)}, u32[]{:S(2)}) collective-permute-start(bf16[128,1024]{1,0:T(8,128)(2,1)} %constant_dynamic-slice_fusion.15), channel_id=1, source_target_pairs={{3,0},{0,1},{1,2},{2,3},{7,4},{4,5},{5,6},{6,7},{11,8},{8,9},{9,10... | collective-permute-start | bytes 786440 | tf_op jit(solution)/shard_map/ppermute | solution.py:399
  36.8 34.3 %collective-permute-start.19 = (bf16[128,1024]{1,0:T(8,128)(2,1)}, bf16[128,1024]{1,0:T(8,128)(2,1)}, u32[]{:S(2)}, u32[]{:S(2)}) collective-permute-start(bf16[128,1024]{1,0:T(8,128)(2,1)} %constant_dynamic-slice_fusion.15), channel_id=1, source_target_pairs={{2,0},{3,1},{0,2},{1,3},{6,4},{7,5},{4,6},{5,7},{10,8},{11,9},{8,1... | collective-permute-start | bytes 786440 | tf_op jit(solution)/shard_map/ppermute | solution.py:399
  38.3 32.8 %collective-permute-start.18 = (bf16[128,1024]{1,0:T(8,128)(2,1)}, bf16[128,1024]{1,0:T(8,128)(2,1)}, u32[]{:S(2)}, u32[]{:S(2)}) collective-permute-start(bf16[128,1024]{1,0:T(8,128)(2,1)} %constant_dynamic-slice_fusion.15), channel_id=1, source_target_pairs={{1,0},{2,1},{3,2},{0,3},{5,4},{6,5},{7,6},{4,7},{9,8},{10,9},{11,1... | collective-permute-start | bytes 786440 | tf_op jit(solution)/shard_map/ppermute | solution.py:399
  69.7 30.5 %collective-permute-start.1 = (bf16[64,1024]{1,0:T(8,128)(2,1)}, bf16[64,1024]{1,0:T(8,128)(2,1)S(1)}, u32[]{:S(2)}, u32[]{:S(2)}) collective-permute-start(bf16[64,1024]{1,0:T(8,128)(2,1)} %get-tuple-element.90), channel_id=1, source_target_pairs={{1,2},{2,3},{5,6},{6,7},{9,10},{10,11},{13,14},{14,15},{17,18},{18... | collective-permute-start | bytes 393224 | tf_op jit(solution)/shard_map/ppermute | solution.py:619
  85.1 16.8 %collective-permute-start.2 = (bf16[64,1024]{1,0:T(8,128)(2,1)}, bf16[64,1024]{1,0:T(8,128)(2,1)S(1)}, u32[]{:S(2)}, u32[]{:S(2)}) collective-permute-start(bf16[64,1024]{1,0:T(8,128)(2,1)} %get-tuple-element.89), channel_id=1, source_target_pairs={{2,1},{3,2},{6,5},{7,6},{10,9},{11,10},{14,13},{15,14},{18,17},{19... | collective-permute-start | bytes 393224 | tf_op jit(solution)/shard_map/ppermute | solution.py:620
  94.0 20.6 %collective-permute-start.6 = (bf16[3,128,1024]{2,1,0:T(8,128)(2,1)}, bf16[3,128,1024]{2,1,0:T(8,128)(2,1)S(1)}, u32[]{:S(2)}, u32[]{:S(2)}) collective-permute-start(bf16[3,128,1024]{2,1,0:T(8,128)(2,1)} %pad_maximum_fusion.5.refs_0_), channel_id=1, source_target_pairs={{0,8},{4,12},{8,0},{12,4},{16,24},{20,28},{24,16},{28,20},{1,9},{5... | collective-permute-start | bytes 2359304 | tf_op jit(solution)/shard_map/ppermute | solution.py:379
  95.5 20.6 %collective-permute-start.7 = (bf16[3,128,1024]{2,1,0:T(8,128)(2,1)}, bf16[3,128,1024]{2,1,0:T(8,128)(2,1)S(1)}, u32[]{:S(2)}, u32[]{:S(2)}) collective-permute-start(bf16[3,128,1024]{2,1,0:T(8,128)(2,1)} %pad_maximum_fusion.5.refs_0_), channel_id=1, source_target_pairs={{0,16},{4,20},{8,24},{12,28},{16,0},{20,4},{24,8},{28,12},{1,17},{... | collective-permute-start | bytes 2359304 | tf_op jit(solution)/shard_map/ppermute | solution.py:379
  98.9 19.1 %collective-permute-start.10 = (bf16[3,128,1024]{2,1,0:T(8,128)(2,1)S(1)}, bf16[3,128,1024]{2,1,0:T(8,128)(2,1)S(1)}, u32[]{:S(2)}, u32[]{:S(2)}) collective-permute-start(bf16[3,128,1024]{2,1,0:T(8,128)(2,1)S(1)} %copy-done.15), channel_id=1, source_target_pairs={{0,4},{4,0},{8,12},{12,8},{16,20},{20,16},{24,28},{28,24},{1,5},{5... | collective-permute-start | bytes 2359304 | tf_op jit(solution)/shard_map/ppermute | solution.py:379
  100.2 31.4 %collective-permute-start.21 = (bf16[3,128,1024]{2,1,0:T(8,128)(2,1)S(1)}, bf16[3,128,1024]{2,1,0:T(8,128)(2,1)}, u32[]{:S(2)}, u32[]{:S(2)}) collective-permute-start(bf16[3,128,1024]{2,1,0:T(8,128)(2,1)S(1)} %pad_maximum_fusion.6.refs_0_), channel_id=1, source_target_pairs={{0,8},{4,12},{8,0},{12,4},{16,24},{20,28},{24,16},{28,20},{1,9},{5... | collective-permute-start | bytes 2359304 | tf_op jit(solution)/shard_map/ppermute | solution.py:379
  101.8 32.0 %collective-permute-start.22 = (bf16[3,128,1024]{2,1,0:T(8,128)(2,1)S(1)}, bf16[3,128,1024]{2,1,0:T(8,128)(2,1)S(1)}, u32[]{:S(2)}, u32[]{:S(2)}) collective-permute-start(bf16[3,128,1024]{2,1,0:T(8,128)(2,1)S(1)} %pad_maximum_fusion.6.refs_0_), channel_id=1, source_target_pairs={{0,16},{4,20},{8,24},{12,28},{16,0},{20,4},{24,8},{28,12},{1,17},{... | collective-permute-start | bytes 2359304 | tf_op jit(solution)/shard_map/ppermute | solution.py:379
  114.6 42.9 %collective-permute-start.33 = (bf16[3,128,1024]{2,1,0:T(8,128)(2,1)}, bf16[3,128,1024]{2,1,0:T(8,128)(2,1)}, u32[]{:S(2)}, u32[]{:S(2)}) collective-permute-start(bf16[3,128,1024]{2,1,0:T(8,128)(2,1)} %pad_maximum_fusion.7.refs_0_), channel_id=1, source_target_pairs={{0,8},{4,12},{8,0},{12,4},{16,24},{20,28},{24,16},{28,20},{1,9},{5... | collective-permute-start | bytes 2359304 | tf_op jit(solution)/shard_map/ppermute | solution.py:379
  116.1 41.5 %collective-permute-start.34 = (bf16[3,128,1024]{2,1,0:T(8,128)(2,1)}, bf16[3,128,1024]{2,1,0:T(8,128)(2,1)}, u32[]{:S(2)}, u32[]{:S(2)}) collective-permute-start(bf16[3,128,1024]{2,1,0:T(8,128)(2,1)} %pad_maximum_fusion.7.refs_0_), channel_id=1, source_target_pairs={{0,16},{4,20},{8,24},{12,28},{16,0},{20,4},{24,8},{28,12},{1,17},{... | collective-permute-start | bytes 2359304 | tf_op jit(solution)/shard_map/ppermute | solution.py:379
  118.1 38.8 %collective-permute-start.8 = (bf16[3,64,1024]{2,1,0:T(8,128)(2,1)S(1)}, bf16[3,64,1024]{2,1,0:T(8,128)(2,1)S(1)}, u32[]{:S(2)}, u32[]{:S(2)}) collective-permute-start(bf16[3,64,1024]{2,1,0:T(8,128)(2,1)S(1)} %slice.271), channel_id=1, source_target_pairs={{0,16},{4,20},{8,24},{12,28},{16,0},{20,4},{24,8},{28,12},{1,17},{... | collective-permute-start | bytes 1179656 | tf_op jit(solution)/shard_map/ppermute | solution.py:379
  131.6 25.4 %collective-permute-start.9 = (bf16[3,64,1024]{2,1,0:T(8,128)(2,1)S(1)}, bf16[3,64,1024]{2,1,0:T(8,128)(2,1)S(1)}, u32[]{:S(2)}, u32[]{:S(2)}) collective-permute-start(bf16[3,64,1024]{2,1,0:T(8,128)(2,1)S(1)} %slice.272), channel_id=1, source_target_pairs={{0,8},{4,12},{8,0},{12,4},{16,24},{20,28},{24,16},{28,20},{1,9},{5... | collective-permute-start | bytes 1179656 | tf_op jit(solution)/shard_map/ppermute | solution.py:379
  133.8 56.8 %collective-permute-start.25 = (bf16[3,128,1024]{2,1,0:T(8,128)(2,1)S(1)}, bf16[3,128,1024]{2,1,0:T(8,128)(2,1)S(1)}, u32[]{:S(2)}, u32[]{:S(2)}) collective-permute-start(bf16[3,128,1024]{2,1,0:T(8,128)(2,1)S(1)} %pad_maximum_fusion.6.refs_0_), channel_id=1, source_target_pairs={{0,4},{4,0},{8,12},{12,8},{16,20},{20,16},{24,28},{28,24},{1,5},{5... | collective-permute-start | bytes 2359304 | tf_op jit(solution)/shard_map/ppermute | solution.py:379
  167.2 23.9 %collective-permute-start.23 = (bf16[3,64,1024]{2,1,0:T(8,128)(2,1)S(1)}, bf16[3,64,1024]{2,1,0:T(8,128)(2,1)S(1)}, u32[]{:S(2)}, u32[]{:S(2)}) collective-permute-start(bf16[3,64,1024]{2,1,0:T(8,128)(2,1)S(1)} %slice.273), channel_id=1, source_target_pairs={{0,16},{4,20},{8,24},{12,28},{16,0},{20,4},{24,8},{28,12},{1,17},{... | collective-permute-start | bytes 1179656 | tf_op jit(solution)/shard_map/ppermute | solution.py:379
  168.8 58.1 %collective-permute-start.24 = (bf16[3,64,1024]{2,1,0:T(8,128)(2,1)}, bf16[3,64,1024]{2,1,0:T(8,128)(2,1)}, u32[]{:S(2)}, u32[]{:S(2)}) collective-permute-start(bf16[3,64,1024]{2,1,0:T(8,128)(2,1)} %slice.274), channel_id=1, source_target_pairs={{0,8},{4,12},{8,0},{12,4},{16,24},{20,28},{24,16},{28,20},{1,9},{5... | collective-permute-start | bytes 1179656 | tf_op jit(solution)/shard_map/ppermute | solution.py:379
  169.3 58.2 %collective-permute-start.26 = (bf16[3,128,1024]{2,1,0:T(8,128)(2,1)}, bf16[3,128,1024]{2,1,0:T(8,128)(2,1)}, u32[]{:S(2)}, u32[]{:S(2)}) collective-permute-start(bf16[3,128,1024]{2,1,0:T(8,128)(2,1)} %collective-permute-done.21.refs_1_), channel_id=1, source_target_pairs={{0,4},{4,0},{8,12},{12,8},{16,20},{20,16},{24,28},{28,24},{1,5},{5... | collective-permute-start | bytes 2359304 | tf_op jit(solution)/shard_map/ppermute | solution.py:379
  170.8 57.1 %collective-permute-start.27 = (bf16[3,128,1024]{2,1,0:T(8,128)(2,1)S(1)}, bf16[3,128,1024]{2,1,0:T(8,128)(2,1)}, u32[]{:S(2)}, u32[]{:S(2)}) collective-permute-start(bf16[3,128,1024]{2,1,0:T(8,128)(2,1)S(1)} %collective-permute-done.22.refs_2_), channel_id=1, source_target_pairs={{0,4},{4,0},{8,12},{12,8},{16,20},{20,16},{24,28},{28,24},{1,5},{5... | collective-permute-start | bytes 2359304 | tf_op jit(solution)/shard_map/ppermute | solution.py:379
  190.6 36.3 %collective-permute-start.35 = (bf16[3,64,1024]{2,1,0:T(8,128)(2,1)}, bf16[3,64,1024]{2,1,0:T(8,128)(2,1)}, u32[]{:S(2)}, u32[]{:S(2)}) collective-permute-start(bf16[3,64,1024]{2,1,0:T(8,128)(2,1)} %slice.275), channel_id=1, source_target_pairs={{0,16},{4,20},{8,24},{12,28},{16,0},{20,4},{24,8},{28,12},{1,17},{... | collective-permute-start | bytes 1179656 | tf_op jit(solution)/shard_map/ppermute | solution.py:379
  191.1 36.4 %collective-permute-start.36 = (bf16[3,64,1024]{2,1,0:T(8,128)(2,1)S(1)}, bf16[3,64,1024]{2,1,0:T(8,128)(2,1)}, u32[]{:S(2)}, u32[]{:S(2)}) collective-permute-start(bf16[3,64,1024]{2,1,0:T(8,128)(2,1)S(1)} %slice.276), channel_id=1, source_target_pairs={{0,8},{4,12},{8,0},{12,4},{16,24},{20,28},{24,16},{28,20},{1,9},{5... | collective-permute-start | bytes 1179656 | tf_op jit(solution)/shard_map/ppermute | solution.py:379
  226.9 33.5 %collective-permute-start.37 = (bf16[3,128,1024]{2,1,0:T(8,128)(2,1)}, bf16[3,128,1024]{2,1,0:T(8,128)(2,1)}, u32[]{:S(2)}, u32[]{:S(2)}) collective-permute-start(bf16[3,128,1024]{2,1,0:T(8,128)(2,1)} %pad_maximum_fusion.7.refs_0_), channel_id=1, source_target_pairs={{0,4},{4,0},{8,12},{12,8},{16,20},{20,16},{24,28},{28,24},{1,5},{5... | collective-permute-start | bytes 2359304 | tf_op jit(solution)/shard_map/ppermute | solution.py:379
  227.0 34.0 %collective-permute-start.38 = (bf16[3,128,1024]{2,1,0:T(8,128)(2,1)}, bf16[3,128,1024]{2,1,0:T(8,128)(2,1)}, u32[]{:S(2)}, u32[]{:S(2)}) collective-permute-start(bf16[3,128,1024]{2,1,0:T(8,128)(2,1)} %collective-permute-done.33.refs_1_), channel_id=1, source_target_pairs={{0,4},{4,0},{8,12},{12,8},{16,20},{20,16},{24,28},{28,24},{1,5},{5... | collective-permute-start | bytes 2359304 | tf_op jit(solution)/shard_map/ppermute | solution.py:379
  227.4 33.6 %collective-permute-start.39 = (bf16[3,128,1024]{2,1,0:T(8,128)(2,1)}, bf16[3,128,1024]{2,1,0:T(8,128)(2,1)}, u32[]{:S(2)}, u32[]{:S(2)}) collective-permute-start(bf16[3,128,1024]{2,1,0:T(8,128)(2,1)} %collective-permute-done.34.refs_2_), channel_id=1, source_target_pairs={{0,4},{4,0},{8,12},{12,8},{16,20},{20,16},{24,28},{28,24},{1,5},{5... | collective-permute-start | bytes 2359304 | tf_op jit(solution)/shard_map/ppermute | solution.py:379
  233.6 27.4 %collective-permute-start.40 = (bf16[3,64,1024]{2,1,0:T(8,128)(2,1)}, bf16[3,64,1024]{2,1,0:T(8,128)(2,1)S(1)}, u32[]{:S(2)}, u32[]{:S(2)}) collective-permute-start(bf16[3,64,1024]{2,1,0:T(8,128)(2,1)} %collective-permute-done.35.refs_3_), channel_id=1, source_target_pairs={{0,4},{4,0},{8,12},{12,8},{16,20},{20,16},{24,28},{28,24},{1,5},{5... | collective-permute-start | bytes 1179656 | tf_op jit(solution)/shard_map/ppermute | solution.py:379
  234.1 26.9 %collective-permute-start.41 = (bf16[3,64,1024]{2,1,0:T(8,128)(2,1)}, bf16[3,64,1024]{2,1,0:T(8,128)(2,1)S(1)}, u32[]{:S(2)}, u32[]{:S(2)}) collective-permute-start(bf16[3,64,1024]{2,1,0:T(8,128)(2,1)} %collective-permute-done.36.refs_4_), channel_id=1, source_target_pairs={{0,4},{4,0},{8,12},{12,8},{16,20},{20,16},{24,28},{28,24},{1,5},{5... | collective-permute-start | bytes 1179656 | tf_op jit(solution)/shard_map/ppermute | solution.py:379
  260.4 183.3 %collective-permute-start.86 = (bf16[512,1024]{1,0:T(8,128)(2,1)}, bf16[512,1024]{1,0:T(8,128)(2,1)}, u32[]{:S(2)}, u32[]{:S(2)}) collective-permute-start(bf16[512,1024]{1,0:T(8,128)(2,1)} %param.37), channel_id=1, source_target_pairs={{0,4},{4,0},{8,12},{12,8},{16,20},{20,16},{24,28},{28,24},{1,5},{5... | collective-permute-start | bytes 3145736 | tf_op jit(solution)/shard_map/ppermute | solution.py:675
  260.9 130.2 %collective-permute-start.45 = (bf16[1152,1024]{1,0:T(8,128)(2,1)}, bf16[1152,1024]{1,0:T(8,128)(2,1)}, u32[]{:S(2)}, u32[]{:S(2)}) collective-permute-start(bf16[1152,1024]{1,0:T(8,128)(2,1)} %get-tuple-element.74.x_ref), channel_id=1, source_target_pairs={{0,4},{4,0},{8,12},{12,8},{16,20},{20,16},{24,28},{28,24},{1,5},{5... | collective-permute-start | bytes 7077896 | tf_op jit(solution)/shard_map/ppermute | solution.py:675
  363.5 34.8 %collective-permute-start.51 = (bf16[512,1024]{1,0:T(8,128)(2,1)}, bf16[512,1024]{1,0:T(8,128)(2,1)}, u32[]{:S(2)}, u32[]{:S(2)}) collective-permute-start(bf16[512,1024]{1,0:T(8,128)(2,1)} %convert_element_type.260), channel_id=1, source_target_pairs={{0,4},{4,0},{8,12},{12,8},{16,20},{20,16},{24,28},{28,24},{1,5},{5... | collective-permute-start | bytes 3145736 | tf_op jit(solution)/shard_map/ppermute | solution.py:675
  365.0 30.9 %collective-permute-start.42 = (bf16[512,1024]{1,0:T(8,128)(2,1)}, bf16[512,1024]{1,0:T(8,128)(2,1)}, u32[]{:S(2)}, u32[]{:S(2)}) collective-permute-start(bf16[512,1024]{1,0:T(8,128)(2,1)} %get-tuple-element.54), channel_id=1, source_target_pairs={{0,1},{1,0},{4,5},{5,4},{8,9},{9,8},{12,13},{13,12},{16,17},{17,16... | collective-permute-start | bytes 3145736 | tf_op jit(solution)/shard_map/ppermute | solution.py:712
  372.4 18.3 %collective-permute-start.46 = (bf16[512,512]{1,0:T(8,128)(2,1)}, bf16[512,512]{1,0:T(8,128)(2,1)S(1)}, u32[]{:S(2)}, u32[]{:S(2)}) collective-permute-start(bf16[512,512]{1,0:T(8,128)(2,1)} %slice_bitcast_fusion.10), channel_id=1, source_target_pairs={{0,4},{4,0},{8,12},{12,8},{16,20},{20,16},{24,28},{28,24},{1,5},{5... | collective-permute-start | bytes 1572872 | tf_op jit(solution)/shard_map/ppermute | solution.py:675
  390.6 66.6 %collective-permute-start.67 = (bf16[512,1024]{1,0:T(8,128)(2,1)}, bf16[512,1024]{1,0:T(8,128)(2,1)S(1)}, u32[]{:S(2)}, u32[]{:S(2)}) collective-permute-start(bf16[512,1024]{1,0:T(8,128)(2,1)} %get-tuple-element.44.x_ref), channel_id=1, source_target_pairs={{0,4},{4,0},{8,12},{12,8},{16,20},{20,16},{24,28},{28,24},{1,5},{5... | collective-permute-start | bytes 3145736 | tf_op jit(solution)/shard_map/ppermute | solution.py:675
  395.8 49.4 %collective-permute-start.85 = (bf16[512,2048]{1,0:T(8,128)(2,1)}, bf16[512,2048]{1,0:T(8,128)(2,1)}, u32[]{:S(2)}, u32[]{:S(2)}) collective-permute-start(bf16[512,2048]{1,0:T(8,128)(2,1)} %slice.258), channel_id=1, source_target_pairs={{0,4},{4,0},{8,12},{12,8},{16,20},{20,16},{24,28},{28,24},{1,5},{5... | collective-permute-start | bytes 6291464 | tf_op jit(solution)/shard_map/ppermute | solution.py:675
  407.9 20.8 %collective-permute-start.50 = (bf16[1152,512]{1,0:T(8,128)(2,1)}, bf16[1152,512]{1,0:T(8,128)(2,1)}, u32[]{:S(2)}, u32[]{:S(2)}) collective-permute-start(bf16[1152,512]{1,0:T(8,128)(2,1)} %slice_bitcast_fusion), channel_id=1, source_target_pairs={{0,4},{4,0},{8,12},{12,8},{16,20},{20,16},{24,28},{28,24},{1,5},{5... | collective-permute-start | bytes 3538952 | tf_op jit(solution)/shard_map/ppermute | solution.py:675
  416.0 42.2 %collective-permute-start.68 = (bf16[512,2048]{1,0:T(8,128)(2,1)}, bf16[512,2048]{1,0:T(8,128)(2,1)}, u32[]{:S(2)}, u32[]{:S(2)}) collective-permute-start(bf16[512,2048]{1,0:T(8,128)(2,1)} %slice.302), channel_id=1, source_target_pairs={{0,4},{4,0},{8,12},{12,8},{16,20},{20,16},{24,28},{28,24},{1,5},{5... | collective-permute-start | bytes 6291464 | tf_op jit(solution)/shard_map/ppermute | solution.py:675
  428.6 38.9 %collective-permute-start.48 = (bf16[512,1024]{1,0:T(8,128)(2,1)}, bf16[512,1024]{1,0:T(8,128)(2,1)}, u32[]{:S(2)}, u32[]{:S(2)}) collective-permute-start(bf16[512,1024]{1,0:T(8,128)(2,1)} %constant_dynamic-slice_fusion.11), channel_id=1, source_target_pairs={{0,8},{4,12},{8,0},{12,4},{16,24},{20,28},{24,16},{28,20},{1,9},{5... | collective-permute-start | bytes 3145736 | tf_op jit(solution)/shard_map/ppermute | solution.py:379
  443.7 26.6 %collective-permute-start.53 = (bf16[512,1024]{1,0:T(8,128)(2,1)S(1)}, bf16[512,1024]{1,0:T(8,128)(2,1)S(1)}, u32[]{:S(2)}, u32[]{:S(2)}) collective-permute-start(bf16[512,1024]{1,0:T(8,128)(2,1)S(1)} %constant_dynamic-slice_fusion.9), channel_id=1, source_target_pairs={{0,16},{4,20},{8,24},{12,28},{16,0},{20,4},{24,8},{28,12},{1,17},{... | collective-permute-start | bytes 3145736 | tf_op jit(solution)/shard_map/ppermute | solution.py:379
  450.8 59.6 %collective-permute-start.87 = (bf16[512,1024]{1,0:T(8,128)(2,1)S(1)}, bf16[512,1024]{1,0:T(8,128)(2,1)S(1)}, u32[]{:S(2)}, u32[]{:S(2)}) collective-permute-start(bf16[512,1024]{1,0:T(8,128)(2,1)S(1)} %dynamic-slice_bitcast_fusion.1), channel_id=1, source_target_pairs={{0,8},{4,12},{8,0},{12,4},{16,24},{20,28},{24,16},{28,20},{1,9},{5... | collective-permute-start | bytes 3145736 | tf_op jit(solution)/shard_map/ppermute | solution.py:379
  457.2 58.7 %collective-permute-start.89 = (bf16[512,1024]{1,0:T(8,128)(2,1)S(1)}, bf16[512,1024]{1,0:T(8,128)(2,1)S(1)}, u32[]{:S(2)}, u32[]{:S(2)}) collective-permute-start(bf16[512,1024]{1,0:T(8,128)(2,1)S(1)} %dynamic-slice_bitcast_fusion), channel_id=1, source_target_pairs={{0,16},{4,20},{8,24},{12,28},{16,0},{20,4},{24,8},{28,12},{1,17},{... | collective-permute-start | bytes 3145736 | tf_op jit(solution)/shard_map/ppermute | solution.py:379
  463.7 76.8 %collective-permute-start.69 = (bf16[512,1024]{1,0:T(8,128)(2,1)S(1)}, bf16[512,1024]{1,0:T(8,128)(2,1)S(1)}, u32[]{:S(2)}, u32[]{:S(2)}) collective-permute-start(bf16[512,1024]{1,0:T(8,128)(2,1)S(1)} %constant_dynamic-slice_fusion.7), channel_id=1, source_target_pairs={{0,8},{4,12},{8,0},{12,4},{16,24},{20,28},{24,16},{28,20},{1,9},{5... | collective-permute-start | bytes 3145736 | tf_op jit(solution)/shard_map/ppermute | solution.py:379
  469.3 33.0 %collective-permute-start.49 = (bf16[256,1024]{1,0:T(8,128)(2,1)S(1)}, bf16[256,1024]{1,0:T(8,128)(2,1)S(1)}, u32[]{:S(2)}, u32[]{:S(2)}) collective-permute-start(bf16[256,1024]{1,0:T(8,128)(2,1)S(1)} %constant_dynamic-slice_fusion.10), channel_id=1, source_target_pairs={{0,16},{4,20},{8,24},{12,28},{16,0},{20,4},{24,8},{28,12},{1,17},{... | collective-permute-start | bytes 1572872 | tf_op jit(solution)/shard_map/ppermute | solution.py:379
  470.7 39.3 %collective-permute-start.54 = (bf16[256,1024]{1,0:T(8,128)(2,1)S(1)}, bf16[256,1024]{1,0:T(8,128)(2,1)S(1)}, u32[]{:S(2)}, u32[]{:S(2)}) collective-permute-start(bf16[256,1024]{1,0:T(8,128)(2,1)S(1)} %constant_dynamic-slice_fusion.8), channel_id=1, source_target_pairs={{0,8},{4,12},{8,0},{12,4},{16,24},{20,28},{24,16},{28,20},{1,9},{5... | collective-permute-start | bytes 1572872 | tf_op jit(solution)/shard_map/ppermute | solution.py:379
  502.2 40.1 %collective-permute-start.71 = (bf16[512,1024]{1,0:T(8,128)(2,1)S(1)}, bf16[512,1024]{1,0:T(8,128)(2,1)S(1)}, u32[]{:S(2)}, u32[]{:S(2)}) collective-permute-start(bf16[512,1024]{1,0:T(8,128)(2,1)S(1)} %constant_dynamic-slice_fusion.5), channel_id=1, source_target_pairs={{0,16},{4,20},{8,24},{12,28},{16,0},{20,4},{24,8},{28,12},{1,17},{... | collective-permute-start | bytes 3145736 | tf_op jit(solution)/shard_map/ppermute | solution.py:379
  510.4 27.7 %collective-permute-start.56 = (bf16[512,256]{1,0:T(8,128)(2,1)S(1)}, bf16[512,256]{1,0:T(8,128)(2,1)S(1)}, u32[]{:S(2)}, u32[]{:S(2)}) collective-permute-start(bf16[512,256]{1,0:T(8,128)(2,1)S(1)} %get-tuple-element.87), channel_id=1, source_target_pairs={{0,2},{1,3},{2,0},{3,1},{4,6},{5,7},{6,4},{7,5},{8,10},{9,11},{10,... | collective-permute-start | bytes 786440 | tf_op jit(solution)/shard_map/ppermute | solution.py:497
  515.9 23.7 %collective-permute-start.55 = (bf16[512,256]{1,0:T(8,128)(2,1)S(1)}, bf16[512,256]{1,0:T(8,128)(2,1)S(1)}, u32[]{:S(2)}, u32[]{:S(2)}) collective-permute-start(bf16[512,256]{1,0:T(8,128)(2,1)S(1)} %get-tuple-element.85), channel_id=1, source_target_pairs={{0,1},{1,2},{2,3},{3,0},{4,5},{5,6},{6,7},{7,4},{8,9},{9,10},{10,1... | collective-permute-start | bytes 786440 | tf_op jit(solution)/shard_map/ppermute | solution.py:497
  519.0 39.1 %collective-permute-start.88 = (bf16[256,1024]{1,0:T(8,128)(2,1)S(1)}, bf16[256,1024]{1,0:T(8,128)(2,1)S(1)}, u32[]{:S(2)}, u32[]{:S(2)}) collective-permute-start(bf16[256,1024]{1,0:T(8,128)(2,1)S(1)} %constant_dynamic-slice_fusion.3), channel_id=1, source_target_pairs={{0,16},{4,20},{8,24},{12,28},{16,0},{20,4},{24,8},{28,12},{1,17},{... | collective-permute-start | bytes 1572872 | tf_op jit(solution)/shard_map/ppermute | solution.py:379
  538.2 21.5 %collective-permute-start.90 = (bf16[256,1024]{1,0:T(8,128)(2,1)S(1)}, bf16[256,1024]{1,0:T(8,128)(2,1)S(1)}, u32[]{:S(2)}, u32[]{:S(2)}) collective-permute-start(bf16[256,1024]{1,0:T(8,128)(2,1)S(1)} %constant_dynamic-slice_fusion.2), channel_id=1, source_target_pairs={{0,8},{4,12},{8,0},{12,4},{16,24},{20,28},{24,16},{28,20},{1,9},{5... | collective-permute-start | bytes 1572872 | tf_op jit(solution)/shard_map/ppermute | solution.py:379
  540.4 29.5 %collective-permute-start.59 = (bf16[512,256]{1,0:T(8,128)(2,1)S(1)}, bf16[512,256]{1,0:T(8,128)(2,1)S(1)}, u32[]{:S(2)}, u32[]{:S(2)}) collective-permute-start(bf16[512,256]{1,0:T(8,128)(2,1)S(1)} %add_convert_fusion.22.refs_0_), channel_id=1, source_target_pairs={{0,16},{4,20},{8,24},{12,28},{16,0},{20,4},{24,8},{28,12},{1,17},{... | collective-permute-start | bytes 786440 | tf_op jit(solution)/shard_map/ppermute | solution.py:379
  542.4 28.2 %collective-permute-start.62 = (bf16[512,256]{1,0:T(8,128)(2,1)S(1)}, bf16[512,256]{1,0:T(8,128)(2,1)S(1)}, u32[]{:S(2)}, u32[]{:S(2)}) collective-permute-start(bf16[512,256]{1,0:T(8,128)(2,1)S(1)} %add_convert_fusion.22.refs_0_), channel_id=1, source_target_pairs={{0,4},{4,0},{8,12},{12,8},{16,20},{20,16},{24,28},{28,24},{1,5},{5... | collective-permute-start | bytes 786440 | tf_op jit(solution)/shard_map/ppermute | solution.py:379
  560.0 16.9 %collective-permute-start.93 = (bf16[512,256]{1,0:T(8,128)(2,1)S(1)}, bf16[512,256]{1,0:T(8,128)(2,1)S(1)}, u32[]{:S(2)}, u32[]{:S(2)}) collective-permute-start(bf16[512,256]{1,0:T(8,128)(2,1)S(1)} %get-tuple-element.80), channel_id=1, source_target_pairs={{0,3},{1,0},{2,1},{3,2},{4,7},{5,4},{6,5},{7,6},{8,11},{9,8},{10,9... | collective-permute-start | bytes 786440 | tf_op jit(solution)/shard_map/ppermute | solution.py:497
  568.4 18.0 %collective-permute-start.92 = (bf16[512,256]{1,0:T(8,128)(2,1)S(1)}, bf16[512,256]{1,0:T(8,128)(2,1)S(1)}, u32[]{:S(2)}, u32[]{:S(2)}) collective-permute-start(bf16[512,256]{1,0:T(8,128)(2,1)S(1)} %get-tuple-element.81), channel_id=1, source_target_pairs={{0,2},{1,3},{2,0},{3,1},{4,6},{5,7},{6,4},{7,5},{8,10},{9,11},{10,... | collective-permute-start | bytes 786440 | tf_op jit(solution)/shard_map/ppermute | solution.py:497
  569.7 25.2 %collective-permute-start.91 = (bf16[512,256]{1,0:T(8,128)(2,1)S(1)}, bf16[512,256]{1,0:T(8,128)(2,1)S(1)}, u32[]{:S(2)}, u32[]{:S(2)}) collective-permute-start(bf16[512,256]{1,0:T(8,128)(2,1)S(1)} %get-tuple-element.79), channel_id=1, source_target_pairs={{0,1},{1,2},{2,3},{3,0},{4,5},{5,6},{6,7},{7,4},{8,9},{9,10},{10,1... | collective-permute-start | bytes 786440 | tf_op jit(solution)/shard_map/ppermute | solution.py:497
  570.6 27.3 %collective-permute-start.75 = (bf16[512,256]{1,0:T(8,128)(2,1)S(1)}, bf16[512,256]{1,0:T(8,128)(2,1)S(1)}, u32[]{:S(2)}, u32[]{:S(2)}) collective-permute-start(bf16[512,256]{1,0:T(8,128)(2,1)S(1)} %get-tuple-element.83), channel_id=1, source_target_pairs={{0,3},{1,0},{2,1},{3,2},{4,7},{5,4},{6,5},{7,6},{8,11},{9,8},{10,9... | collective-permute-start | bytes 786440 | tf_op jit(solution)/shard_map/ppermute | solution.py:497
  575.0 29.7 %collective-permute-start.74 = (bf16[512,256]{1,0:T(8,128)(2,1)S(1)}, bf16[512,256]{1,0:T(8,128)(2,1)S(1)}, u32[]{:S(2)}, u32[]{:S(2)}) collective-permute-start(bf16[512,256]{1,0:T(8,128)(2,1)S(1)} %get-tuple-element.84), channel_id=1, source_target_pairs={{0,2},{1,3},{2,0},{3,1},{4,6},{5,7},{6,4},{7,5},{8,10},{9,11},{10,... | collective-permute-start | bytes 786440 | tf_op jit(solution)/shard_map/ppermute | solution.py:497
  576.8 28.6 %collective-permute-start.73 = (bf16[512,256]{1,0:T(8,128)(2,1)S(1)}, bf16[512,256]{1,0:T(8,128)(2,1)S(1)}, u32[]{:S(2)}, u32[]{:S(2)}) collective-permute-start(bf16[512,256]{1,0:T(8,128)(2,1)S(1)} %get-tuple-element.82), channel_id=1, source_target_pairs={{0,1},{1,2},{2,3},{3,0},{4,5},{5,6},{6,7},{7,4},{8,9},{9,10},{10,1... | collective-permute-start | bytes 786440 | tf_op jit(solution)/shard_map/ppermute | solution.py:497
  619.5 44.5 %collective-permute-start.100 = (bf16[512,256]{1,0:T(8,128)(2,1)S(1)}, bf16[512,256]{1,0:T(8,128)(2,1)S(1)}, u32[]{:S(2)}, u32[]{:S(2)}) collective-permute-start(bf16[512,256]{1,0:T(8,128)(2,1)S(1)} %collective-permute-done.95.refs_2_), channel_id=1, source_target_pairs={{0,4},{4,0},{8,12},{12,8},{16,20},{20,16},{24,28},{28,24},{1,5},{5... | collective-permute-start | bytes 786440 | tf_op jit(solution)/shard_map/ppermute | solution.py:379
  621.5 42.5 %collective-permute-start.101 = (bf16[256,256]{1,0:T(8,128)(2,1)S(1)}, bf16[256,256]{1,0:T(8,128)(2,1)S(1)}, u32[]{:S(2)}, u32[]{:S(2)}) collective-permute-start(bf16[256,256]{1,0:T(8,128)(2,1)S(1)} %collective-permute-done.96.refs_3_), channel_id=1, source_target_pairs={{0,4},{4,0},{8,12},{12,8},{16,20},{20,16},{24,28},{28,24},{1,5},{5... | collective-permute-start | bytes 393224 | tf_op jit(solution)/shard_map/ppermute | solution.py:379
  623.6 41.1 %collective-permute-start.102 = (bf16[256,256]{1,0:T(8,128)(2,1)S(1)}, bf16[256,256]{1,0:T(8,128)(2,1)}, u32[]{:S(2)}, u32[]{:S(2)}) collective-permute-start(bf16[256,256]{1,0:T(8,128)(2,1)S(1)} %collective-permute-done.97.refs_4_), channel_id=1, source_target_pairs={{0,4},{4,0},{8,12},{12,8},{16,20},{20,16},{24,28},{28,24},{1,5},{5... | collective-permute-start | bytes 393224 | tf_op jit(solution)/shard_map/ppermute | solution.py:379
  623.6 41.6 %collective-permute-start.78 = (bf16[256,256]{1,0:T(8,128)(2,1)}, bf16[256,256]{1,0:T(8,128)(2,1)}, u32[]{:S(2)}, u32[]{:S(2)}) collective-permute-start(bf16[256,256]{1,0:T(8,128)(2,1)} %slice.312), channel_id=1, source_target_pairs={{0,16},{4,20},{8,24},{12,28},{16,0},{20,4},{24,8},{28,12},{1,17},{... | collective-permute-start | bytes 393224 | tf_op jit(solution)/shard_map/ppermute | solution.py:379
  624.2 41.0 %collective-permute-start.79 = (bf16[256,256]{1,0:T(8,128)(2,1)}, bf16[256,256]{1,0:T(8,128)(2,1)}, u32[]{:S(2)}, u32[]{:S(2)}) collective-permute-start(bf16[256,256]{1,0:T(8,128)(2,1)} %slice.313), channel_id=1, source_target_pairs={{0,8},{4,12},{8,0},{12,4},{16,24},{20,28},{24,16},{28,20},{1,9},{5... | collective-permute-start | bytes 393224 | tf_op jit(solution)/shard_map/ppermute | solution.py:379
  (117 other events, 2466.2 us)

commit v2 on v1

--- a/solution.py
+++ b/solution.py
@@ -278,30 +278,79 @@
     )(attn, packed, resid, b_out[None], gain[None], bias[None])
 
 
-def up_call(n2, w_up, b_up):
+def ffn_call(core, n2, hidden, cot, w_up, w_down, b_up, b_down, halves):
     rows, dm = n2.shape
-    ff = w_up.shape[1]
-    tile = 512
-
-    def body(x_ref, w_ref, b_ref, a_ref, s_ref):
-        u = dot_nn(x_ref[...], w_ref[...]) + b_ref[...].astype(F32)
+    n, _, ffw = w_up.shape
+    tile = ffw // halves
+
+    def body(core_ref, x_ref, h_ref, c_ref, wu_ref, wd_ref, bu_ref, bd_ref, o_ref, gn_ref, a_ref, gu_ref, gb_ref, acc):
+        t = pl.program_id(0)
+        u = dot_nn(x_ref[...], wu_ref[0]) + bu_ref[...].astype(F32)
         cdf = 0.5 * (1.0 + lax.erf(u * 0.7071067811865476))
-        a_ref[...] = (u * cdf).astype(BF16)
-        s_ref[...] = (cdf + u * jnp.exp(-0.5 * u * u) * 0.3989422804014327).astype(BF16)
+        act = (u * cdf).astype(BF16)
+        slope = cdf + u * jnp.exp(-0.5 * u * u) * 0.3989422804014327
+        a_ref[...] = act
+        grad = dot_nt(c_ref[...], wd_ref[0]) * slope
+        gu = grad.astype(BF16)
+        gu_ref[...] = gu
+        gb_ref[...] = jnp.sum(gu.astype(F32), axis=0, keepdims=True)
+        out = dot_nn(act, wd_ref[0])
+        gn = dot_nt(gu, wu_ref[0])
+
+        @pl.when(t == 0)
+        def _():
+            acc[...] = h_ref[...] + bd_ref[...].astype(F32) + out
+            gn_ref[...] = gn
+
+        @pl.when(t > 0)
+        def _():
+            acc[...] += out
+            gn_ref[...] += gn
+
+        @pl.when(t == n * halves - 1)
+        def _():
+            o_ref[...] = acc[...].astype(BF16)
+
+    full = lambda t, c: (0, 0)
+
+    def part(t, c):
+        return lax.bitwise_xor(t // n, c[0]) if halves > 1 else 0
 
     return pl.pallas_call(
         body,
-        grid=(ff // tile,),
-        in_specs=[
-            pl.BlockSpec((rows, dm), lambda t: (0, 0)),
-            pl.BlockSpec((dm, tile), lambda t: (0, t)),
-            pl.BlockSpec((1, tile), lambda t: (0, t)),
+        grid_spec=pltpu.PrefetchScalarGridSpec(
+            num_scalar_prefetch=1,
+            grid=(n * halves,),
+            in_specs=[
+                pl.BlockSpec((rows, dm), full),
+                pl.BlockSpec((rows, dm), full),
+                pl.BlockSpec((rows, dm), full),
+                pl.BlockSpec((1, dm, tile), lambda t, c: (t % n, 0, part(t, c))),
+                pl.BlockSpec((1, tile, dm), lambda t, c: (t % n, part(t, c), 0)),
+                pl.BlockSpec((1, tile), lambda t, c: (0, t)),
+                pl.BlockSpec((1, dm), full),
+            ],
+            out_specs=[
+                pl.BlockSpec((rows, dm), full),
+                pl.BlockSpec((rows, dm), full),
+                pl.BlockSpec((rows, tile), lambda t, c: (0, t)),
+                pl.BlockSpec((rows, tile), lambda t, c: (0, t)),
+                pl.BlockSpec((1, tile), lambda t, c: (0, t)),
+            ],
+            scratch_shapes=[pltpu.VMEM((rows, dm), F32)],
+        ),
+        out_shape=[
+            jax.ShapeDtypeStruct((rows, dm), BF16),
+            jax.ShapeDtypeStruct((rows, dm), F32),
+            jax.ShapeDtypeStruct((rows, n * ffw), BF16),
+            jax.ShapeDtypeStruct((rows, n * ffw), BF16),
+            jax.ShapeDtypeStruct((1, n * ffw), F32),
         ],
-        out_specs=[pl.BlockSpec((rows, tile), lambda t: (0, t)), pl.BlockSpec((rows, tile), lambda t: (0, t))],
-        out_shape=[jax.ShapeDtypeStruct((rows, ff), BF16), jax.ShapeDtypeStruct((rows, ff), BF16)],
         compiler_params=params("arbitrary"),
-        cost_estimate=pl.CostEstimate(flops=2 * rows * dm * ff, bytes_accessed=2 * dm * ff, transcendentals=2 * rows * ff),
-    )(n2, w_up, b_up[None])
+        cost_estimate=pl.CostEstimate(
+            flops=8 * rows * dm * n * ffw, bytes_accessed=4 * n * dm * ffw, transcendentals=2 * rows * n * ffw
+        ),
+    )(core, n2, hidden, cot, w_up, w_down, b_up[None], b_down[None])
 
 
 def norm1_back_call(dq, dk, dv, packed, info, own):
@@ -311,10 +360,19 @@
     win = dk.shape[1]
     width = cw // halves
 
-    def body(info_ref, dq_ref, dk_ref, dv_ref, wq_ref, wk_ref, wv_ref, o_ref, h_ref, t_ref, acc):
+    def body(info_ref, dq_ref, dk_ref, dv_ref, w_ref, o_ref, h_ref, t_ref, acc):
         step = pl.program_id(0)
-        part = dot_nt(dk_ref[0], wk_ref[0]) + dot_nt(dv_ref[0], wv_ref[0])
-        mine = dot_nt(dq_ref[0], wq_ref[0])
+
+        def weight(which, j):
+            at = lax.bitwise_xor(j, info_ref[1]) if halves > 1 else 0
+            return w_ref[0, :, pl.ds(pl.multiple_of(which * cw + at * width, width), width)]
+
+        left = jnp.concatenate([r[j] for r in (dk_ref, dv_ref) for j in range(halves)], axis=1)
+        right = jnp.concatenate([weight(m, j) for m in (1, 2) for j in range(halves)], axis=1)
+        part = dot_nt(left, right)
+        left = jnp.concatenate([dq_ref[j] for j in range(halves)], axis=1)
+        right = jnp.concatenate([weight(0, j) for j in range(halves)], axis=1)
+        mine = dot_nt(left, right)
 
         @pl.when(step == 0)
         def _():
@@ -326,35 +384,23 @@
 
         acc[own : own + rows, :] += mine
 
-        @pl.when(step == n * halves - 1)
+        @pl.when(step == n - 1)
         def _():
             o_ref[...] = acc[own : own + rows, :]
             h_ref[...] = acc[0:own, :].astype(BF16)
             t_ref[...] = acc[own + rows : own + rows + HALO, :].astype(BF16)
-
-    def grad_map(s, info):
-        return (s // n, 0, s % n)
-
-    def weight_map(which):
-        def f(s, info):
-            part = lax.bitwise_xor(s // n, info[1]) if halves > 1 else 0
-            return (s % n, 0, which * halves + part)
-
-        return f
 
     full = lambda s, info: (0, 0)
     return pl.pallas_call(
         body,
         grid_spec=pltpu.PrefetchScalarGridSpec(
             num_scalar_prefetch=1,
-            grid=(n * halves,),
+            grid=(n,),
             in_specs=[
-                pl.BlockSpec((1, rows, width), grad_map),
-                pl.BlockSpec((1, win, width), grad_map),
-                pl.BlockSpec((1, win, width), grad_map),
-                pl.BlockSpec((1, dm, width), weight_map(0)),
-                pl.BlockSpec((1, dm, width), weight_map(1)),
-                pl.BlockSpec((1, dm, width), weight_map(2)),
+                pl.BlockSpec((halves, rows, width), lambda s, info: (0, 0, s)),
+                pl.BlockSpec((halves, win, width), lambda s, info: (0, 0, s)),
+                pl.BlockSpec((halves, win, width), lambda s, info: (0, 0, s)),
+                pl.BlockSpec((1, dm, four), lambda s, info: (s, 0, 0)),
             ],
             out_specs=[
                 pl.BlockSpec((rows, dm), full),
@@ -372,179 +418,339 @@
         cost_estimate=pl.CostEstimate(
             flops=2 * n * cw * dm * (rows + 2 * win), bytes_accessed=2 * n * cw * (3 * dm + rows + 2 * win), transcendentals=0
         ),
-    )(info, dq, dk, dv, packed, packed, packed)
-
-
-def swap(v, bit):
-    return lax.ppermute(v, "dp", [(i, i ^ bit) for i in range(8)])
-
-
-def plane_spread(v, axis):
-    half = v.shape[axis] // 2
-    first = lambda a: lax.slice_in_dim(a, 0, half, axis=axis)
-    second = lambda a: lax.slice_in_dim(a, half, 2 * half, axis=axis)
-    by_x = swap(v, 2)
-    by_y = swap(v, 4)
-    diag_a = swap(first(by_x), 4)
-    diag_b = swap(second(by_y), 2)
-    own = [v, by_x, by_y, diag_a, diag_b]
-    return own + [swap(a, 1) for a in own]
-
-
-def gather_shards(shard, me, after=None):
+    )(info, dq, dk, dv, packed)
+
+
+MESH = pl.DeviceIdType.MESH
+
+
+class Place:
+    def __init__(self):
+        self.me = lax.axis_index("dp")
+        self.z = lax.axis_index("mp")
+        self.k = lax.rem(self.me, 2)
+        self.x = lax.rem(self.me // 2, 2)
+        self.y = self.me // 4
+        self.me_k = self.me + 1 - 2 * self.k
+        self.me_x = self.me + 2 - 4 * self.x
+        self.me_y = self.me + 4 - 8 * self.y
+        self.me_xy = self.me_x + 4 - 8 * self.y
+        self.core = {"dp": self.me_k, "mp": self.z}
+        self.by_x = {"dp": self.me_x, "mp": self.z}
+        self.by_y = {"dp": self.me_y, "mp": self.z}
+
+    def along(self, d):
+        return {"dp": self.me, "mp": lax.rem(self.z + d, 4)}
+
+    def meet(self):
+        sem = pltpu.get_barrier_semaphore()
+        for dev in (self.core, self.by_x, self.by_y, self.along(1), self.along(2), self.along(3)):
+            pl.semaphore_signal(sem, inc=1, device_id=dev, device_id_type=MESH)
+        pl.semaphore_wait(sem, 6)
+
+
+class Wire:
+    def __init__(self, send, recv):
+        self.send, self.recv = send, recv
+        self.open = []
+
+    def start(self, slot, src, dst, dev):
+        copy = pltpu.make_async_remote_copy(
+            src_ref=src, dst_ref=dst, send_sem=self.send.at[slot], recv_sem=self.recv.at[slot],
+            device_id=dev, device_id_type=MESH,
+        )
+        copy.start()
+        self.open.append(copy)
+
+    def landed(self, slot, ref, dev):
+        pltpu.make_async_remote_copy(
+            src_ref=ref, dst_ref=ref, send_sem=self.send.at[slot], recv_sem=self.recv.at[slot],
+            device_id=dev, device_id_type=MESH,
+        ).wait_recv()
+
+    def drain(self):
+        for copy in self.open:
+            copy.wait_send()
+
+
+def gather_steps(place, wire, base, shard, whole):
     step = shard.shape[0] // 8
-    piece = lax.dynamic_slice_in_dim(shard, me * step, step, axis=0)
-    if after is not None:
-        piece, _ = barrier(piece, after)
-    got = [lax.ppermute(piece, "mp", [((i + d) % 4, i) for i in range(4)]) for d in (1, 2, 3)]
-    stack = jnp.stack(got)
-    return stack, plane_spread(stack, 1)
-
-
-def assemble(idx, shard, parts, mode):
-    rows, cols = shard.shape
-    step = rows // 8
     half = step // 2
 
-    def body(idx_ref, l_ref, *refs):
-        ins, out = refs[:-1], refs[-1]
-        o = pl.program_id(0)
-
-        def put(d, a, b, x):
-            if mode == "stack":
-                out[d, 0, a:b, :] = x
-            elif mode == "rows":
-                out[0, 0, d, 0, a:b, :] = x
-            else:
-                for j in range(2):
-                    rel = lax.bitwise_xor(j, idx_ref[0])
-                    for ab in range(2):
-                        at = pl.multiple_of(rel * (cols * 2) + ab * cols + d * (cols // 4), 128)
-                        src = (2 * j + ab) * (cols // 4)
-                        out[a:b, pl.ds(at, cols // 4)] = x[:, src : src + cols // 4]
-
-        put(0, 0, step, l_ref[...])
-        for off in range(8):
-            base = 5 * (off & 1)
-
-            @pl.when(o == off)
-            def _():
-                for d in range(3):
-                    if off // 2 < 3:
-                        put(d + 1, 0, step, ins[base + off // 2][d])
-                    else:
-                        put(d + 1, 0, half, ins[base + 3][d])
-                        put(d + 1, half, step, ins[base + 4][d])
-
-    if mode == "stack":
-        shape = (4, 8, step, cols)
-        out_spec = pl.BlockSpec((4, 1, step, cols), lambda o, idx: (0, idx[1 + o], 0, 0))
-        final = (4, rows, cols)
-    elif mode == "rows":
-        shape = (2, 2, 4, 2, step, cols)
-        out_spec = pl.BlockSpec(
-            (1, 1, 4, 1, step, cols),
-            lambda o, idx: (
-                lax.bitwise_xor(idx[1 + o] // 4, idx[0]),
-                lax.rem(idx[1 + o] // 2, 2),
-                0,
-                lax.rem(idx[1 + o], 2),
-                0,
-                0,
-            ),
+    def rows(who, at=0, size=step):
+        return pl.ds(pl.multiple_of(who * step + at, half), size)
+
+    def slot(d, kind):
+        return base + (d - 1) * 9 + kind
+
+    def begin():
+        for d in (1, 2, 3):
+            wire.start(slot(d, 0), shard.at[rows(place.me)], whole.at[d, rows(place.me)], place.along(4 - d))
+
+    def first(d):
+        mine = whole.at[d, rows(place.me)]
+        wire.landed(slot(d, 0), mine, place.along(d))
+        wire.start(slot(d, 2), mine, mine, place.by_x)
+        wire.start(slot(d, 3), mine, mine, place.by_y)
+        wire.start(slot(d, 1), mine, mine, place.core)
+
+    def second(d):
+        got = whole.at[d, rows(place.me_x)]
+        wire.landed(slot(d, 2), got, place.by_x)
+        part = whole.at[d, rows(place.me_x, 0, half)]
+        wire.start(slot(d, 4), part, part, place.by_y)
+        wire.start(slot(d, 6), got, got, place.core)
+        got = whole.at[d, rows(place.me_y)]
+        wire.landed(slot(d, 3), got, place.by_y)
+        part = whole.at[d, rows(place.me_y, half, half)]
+        wire.start(slot(d, 5), part, part, place.by_x)
+        wire.start(slot(d, 7), got, got, place.core)
+
+    def third(d):
+        wire.landed(slot(d, 4), whole.at[d, rows(place.me_xy, 0, half)], place.by_y)
+        wire.landed(slot(d, 5), whole.at[d, rows(place.me_xy, half, half)], place.by_x)
+        got = whole.at[d, rows(place.me_xy)]
+        wire.start(slot(d, 8), got, got, place.core)
+
+    def finish():
+        flip = 1 - 2 * place.k
+        for d in (1, 2, 3):
+            for kind, who in ((1, place.me), (6, place.me_x), (7, place.me_y), (8, place.me_xy)):
+                wire.landed(slot(d, kind), whole.at[d, rows(who + flip)], place.core)
+
+    return begin, first, second, third, finish
+
+
+def gather_call(shards):
+    count = len(shards)
+
+    def body(*refs):
+        ins, outs = refs[:count], refs[count : 2 * count]
+        send, recv, local_sem = refs[2 * count :]
+        place = Place()
+        wire = Wire(send, recv)
+        copies = [pltpu.make_async_copy(ins[g], outs[g].at[0], local_sem.at[g]) for g in range(count)]
+        place.meet()
+        groups = [gather_steps(place, wire, g * 27, ins[g], outs[g]) for g in range(count)]
+        for begin, *_ in groups:
+            begin()
+        for c in copies:
+            c.start()
+        order = [(g, d) for g in range(count) for d in (1, 3, 2)]
+        for i in range(len(order) + 2):
+            for lag in range(3):
+                if 0 <= i - lag < len(order):
+                    g, d = order[i - lag]
+                    groups[g][1 + lag](d)
+        for *_, finish in groups:
+            finish()
+        for c in copies:
+            c.wait()
+        wire.drain()
+
+    return pl.pallas_call(
+        body,
+        in_specs=[pl.BlockSpec(memory_space=pltpu.VMEM)] * count,
+        out_specs=[pl.BlockSpec(memory_space=pl.ANY)] * count,
+        out_shape=[jax.ShapeDtypeStruct((4,) + s.shape, s.dtype) for s in shards],
+        scratch_shapes=[
+            pltpu.SemaphoreType.DMA((27 * count,)),
+            pltpu.SemaphoreType.DMA((27 * count,)),
+            pltpu.SemaphoreType.DMA((count,)),
+        ],
+        compiler_params=pltpu.CompilerParams(collective_id=0, has_side_effects=True, vmem_limit_bytes=VMEM),
+    )(*shards)
+
+
+class Reduce:
+    SLOTS = 32
+
+    @staticmethod
+    def scratch(dm, w):
+        q = dm // 4
+        e = q // 2
+        return [
+            pltpu.VMEM((4, q, w), BF16),
+            pltpu.VMEM((4, q, w), BF16),
+            pltpu.VMEM((4, e, w), BF16),
+            pltpu.VMEM((4, e, w), BF16),
+            pltpu.VMEM((4, e, w), BF16),
+            pltpu.VMEM((4, e, w), BF16),
+            pltpu.VMEM((4, q, w), BF16),
+            pltpu.VMEM((3, q, w), BF16),
+            pltpu.SemaphoreType.DMA((Reduce.SLOTS,)),
+            pltpu.SemaphoreType.DMA((Reduce.SLOTS,)),
+        ]
+
+    def __init__(self, place, grad, landing, scratch):
+        self.place, self.g, self.f = place, grad, landing
+        self.ra1, self.rb1, self.ra2, self.rb2, self.sa, self.sb, self.t, self.zb = scratch[:8]
+        self.wire = Wire(scratch[8], scratch[9])
+        self.q = grad.shape[0] // 4
+        self.e = self.q // 2
+        self.w = grad.shape[1] // 4
+
+    def at(self, base, big, small=None):
+        start = base * 2 * self.q + big * self.q + (0 if small is None else small * self.e)
+        return pl.ds(pl.multiple_of(start, self.e), self.q if small is None else self.e)
+
+    def eighth(self, small):
+        return pl.ds(pl.multiple_of(small * self.e, self.e), self.e)
+
+    def cols(self, d):
+        return slice(d * self.w, (d + 1) * self.w)
+
+    def one(self, d):
+        p, wire = self.place, self.wire
+        wire.start(d, self.g.at[self.at(0, 1 - p.x), self.cols(d)], self.ra1.at[d], p.by_x)
+        wire.start(4 + d, self.g.at[self.at(1, 1 - p.y), self.cols(d)], self.rb1.at[d], p.by_y)
+
+    def two(self, d):
+        p, wire, c = self.place, self.wire, self.cols(d)
+        wire.landed(d, self.ra1.at[d], p.by_x)
+        self.sa[d] = (
+            self.g[self.at(0, p.x, 1 - p.y), c].astype(F32) + self.ra1[d, self.eighth(1 - p.y), :].astype(F32)
+        ).astype(BF16)
+        wire.start(8 + d, self.sa.at[d], self.ra2.at[d], p.by_y)
+        wire.landed(4 + d, self.rb1.at[d], p.by_y)
+        self.sb[d] = (
+            self.g[self.at(1, p.y, 1 - p.x), c].astype(F32) + self.rb1[d, self.eighth(1 - p.x), :].astype(F32)
+        ).astype(BF16)
+        wire.start(12 + d, self.sb.at[d], self.rb2.at[d], p.by_x)
+
+    def three(self, d):
+        p, wire, c, e = self.place, self.wire, self.cols(d), self.e
+        wire.landed(8 + d, self.ra2.at[d], p.by_y)
+        wire.landed(12 + d, self.rb2.at[d], p.by_x)
+        up = (
+            self.g[self.at(0, p.x, p.y), c].astype(F32)
+            + self.ra1[d, self.eighth(p.y), :].astype(F32)
+            + self.ra2[d].astype(F32)
         )
-        final = (4 * rows, cols)
-    else:
-        shape = (rows, 4 * cols)
-        out_spec = pl.BlockSpec((step, 4 * cols), lambda o, idx: (idx[1 + o], 0))
-        final = shape
-    once = pl.Buffered(1)
-    in_specs = [pl.BlockSpec((step, cols), lambda o, idx: (idx[1 + o], 0))]
-    for a in parts:
-        in_specs.append(pl.BlockSpec(a.shape, lambda o, idx: (0, 0, 0), pipeline_mode=once))
-    out = pl.pallas_call(
+        low = (
+            self.g[self.at(1, p.y, p.x), c].astype(F32)
+            + self.rb1[d, self.eighth(p.x), :].astype(F32)
+            + self.rb2[d].astype(F32)
+        )
+        if d:
+            self.t[d, 0:e] = up.astype(BF16)
+            self.t[d, e : 2 * e] = low.astype(BF16)
+            wire.start(16 + d, self.t.at[d], self.zb.at[d - 1], p.along(d))
+        else:
+            for s in (1, 2, 3):
+                wire.landed(16 + s, self.zb.at[s - 1], p.along(4 - s))
+                up = up + self.zb[s - 1, 0:e].astype(F32)
+                low = low + self.zb[s - 1, e : 2 * e].astype(F32)
+            self.f[0, 0:e] = up.astype(BF16)
+            self.f[0, e : 2 * e] = low.astype(BF16)
+            wire.start(20, self.f.at[0], self.f.at[2], p.by_x)
+            wire.start(21, self.f.at[0], self.f.at[4], p.by_y)
+            wire.start(22, self.f.at[0], self.f.at[1], p.core)
+
+    def four(self):
+        p, wire, e = self.place, self.wire, self.e
+        wire.landed(20, self.f.at[2], p.by_x)
+        wire.start(23, self.f.at[2, 0:e], self.f.at[6, 0:e], p.by_y)
+        wire.start(25, self.f.at[2], self.f.at[3], p.core)
+        wire.landed(21, self.f.at[4], p.by_y)
+        wire.start(24, self.f.at[4, e : 2 * e], self.f.at[6, e : 2 * e], p.by_x)
+        wire.start(26, self.f.at[4], self.f.at[5], p.core)
+
+    def five(self):
+        p, wire, e = self.place, self.wire, self.e
+        wire.landed(23, self.f.at[6, 0:e], p.by_y)
+        wire.landed(24, self.f.at[6, e : 2 * e], p.by_x)
+        wire.start(27, self.f.at[6], self.f.at[7], p.core)
+
+    def six(self):
+        for slot, to in ((22, 1), (25, 3), (26, 5), (27, 7)):
+            self.wire.landed(slot, self.f.at[to], self.place.core)
+        self.wire.drain()
+
+    def steps(self):
+        out = [functools.partial(self.one, d) for d in (1, 2, 3, 0)]
+        lagged = [(self.two, d) for d in (1, 2, 3, 0)]
+        last = [(self.three, d) for d in (1, 2, 3, 0)]
+        for i in range(6):
+            if i < 4:
+                out.append(functools.partial(*lagged[i]))
+            if i >= 1 and i - 1 < 4:
+                out.append(functools.partial(*last[i - 1]))
+        return out + [self.four, self.five, self.six]
+
+
+def reduce_call(grads, cid):
+    count = len(grads)
+    dm, cols = grads[0].shape
+    w = cols // 4
+    each = len(Reduce.scratch(dm, w))
+
+    def body(*refs):
+        ins, outs, scr = refs[:count], refs[count : 2 * count], refs[2 * count :]
+        place = Place()
+        place.meet()
+        todo = [Reduce(place, ins[i], outs[i], scr[each * i : each * (i + 1)]).steps() for i in range(count)]
+        for steps in todo:
+            for s in steps[:4]:
+                s()
+        tails = [steps[4:] for steps in todo]
+        if count == 1:
+            order = tails[0]
+        else:
+            a, b = tails
+            order = a[:-4] + b[:-4] + [a[-4], a[-3], b[-4], a[-2], b[-3], a[-1], b[-2], b[-1]]
+        for s in order:
+            s()
+
+    return pl.pallas_call(
         body,
-        grid_spec=pltpu.PrefetchScalarGridSpec(
-            num_scalar_prefetch=1, grid=(8,), in_specs=in_specs, out_specs=out_spec
-        ),
-        out_shape=jax.ShapeDtypeStruct(shape, BF16),
-        compiler_params=params("arbitrary"),
-        cost_estimate=pl.CostEstimate(flops=0, bytes_accessed=16 * rows * cols, transcendentals=0),
-    )(idx, shard, *parts)
-    return out.reshape(final)
-
-
-def reduce_grad(a, b, y, x):
-    rows, cols = a.shape
-    half, quarter = rows // 2, rows // 4
-    w = cols // 4
-
-    def cut(v, at, size):
-        return lax.dynamic_slice_in_dim(v, at * size, size, axis=0)
-
-    def add(u, v):
-        return (u.astype(F32) + v.astype(F32)).astype(BF16)
-
-    a1 = swap(cut(a, 1 - x, half), 2)
-    b1 = swap(cut(b, 1 - y, half), 4)
-    a = add(cut(a, x, half), a1)
-    b = add(cut(b, y, half), b1)
-    a2 = swap(cut(a, 1 - y, quarter), 4)
-    b2 = swap(cut(b, 1 - x, quarter), 2)
-    both = jnp.concatenate([add(cut(a, y, quarter), a2), add(cut(b, x, quarter), b2)], axis=0)
-    total = both[:, :w].astype(F32)
-    for d in (1, 2, 3):
-        got = lax.ppermute(both[:, d * w : (d + 1) * w], "mp", [(i, (i + d) % 4) for i in range(4)])
-        total = total + got.astype(F32)
-    return plane_spread(total.astype(BF16), 0)
-
-
-def place_grads(coords, parts, mode):
-    two_q, w = parts[0].shape
-    q = two_q // 2
+        in_specs=[pl.BlockSpec(memory_space=pltpu.VMEM)] * count,
+        out_specs=[pl.BlockSpec(memory_space=pltpu.VMEM)] * count,
+        out_shape=[jax.ShapeDtypeStruct((8, dm // 4, w), BF16) for _ in grads],
+        scratch_shapes=Reduce.scratch(dm, w) * count,
+        compiler_params=pltpu.CompilerParams(collective_id=cid, has_side_effects=True, vmem_limit_bytes=VMEM),
+    )(*grads)
+
+
+def place_grads(coords, done, mode):
+    _, q, w = done.shape
+    e = q // 2
     dm = 4 * q
-
-    def body(c_ref, *refs):
-        ins, outs = refs[:10], refs[10:]
+    lanes = w // 4
+
+    def body(c_ref, f_ref, *outs):
         for off in range(8):
             y = lax.bitwise_xor(c_ref[0], off >> 2)
             x = lax.bitwise_xor(c_ref[1], (off >> 1) & 1)
             k = lax.bitwise_xor(c_ref[2], off & 1)
-            base = 5 * (off & 1)
             for part in range(2):
-                if off // 2 < 3:
-                    val = ins[base + off // 2][part * q : (part + 1) * q, :]
+                val = f_ref[off, part * e : (part + 1) * e, :].astype(F32)
+                block = x * 2 + y if part == 0 else 4 + y * 2 + x
+                rows = pl.ds(pl.multiple_of(block * e, e), e)
+                if mode == "up":
+                    outs[0][rows, pl.ds(pl.multiple_of(k * w, w), w)] = val
+                elif mode == "down":
+                    outs[0][pl.ds(pl.multiple_of(k * w, w), w), rows] = val.T
                 else:
-                    val = ins[base + 3 + part][...]
-                val = val.astype(F32)
-                rows = pl.ds(pl.multiple_of((x * 2 + y if part == 0 else y * 2 + x) * q, q), q)
-                if mode == "up":
-                    outs[0][rows, pl.ds(pl.multiple_of((k * 2 + part) * w, w), w)] = val
-                elif mode == "down":
-                    outs[0][pl.ds(pl.multiple_of((k * 2 + part) * w, w), w), rows] = val.T
-                else:
-                    at = pl.ds(pl.multiple_of(k * (w // 2), w // 2), w // 2)
-                    if part == 0:
-                        outs[0][rows, at] = val[:, : w // 2]
-                        outs[1][rows, at] = val[:, w // 2 :]
-                    else:
-                        outs[2][rows, at] = val[:, : w // 2]
-                        outs[3][at, rows] = val[:, w // 2 :].T
+                    at = pl.ds(pl.multiple_of(k * lanes, lanes), lanes)
+                    for m in range(3):
+                        outs[m][rows, at] = val[:, m * lanes : (m + 1) * lanes]
+                    outs[3][at, rows] = val[:, 3 * lanes :].T
 
     if mode == "up":
-        shapes = [(dm, 4 * w)]
+        shapes = [(dm, 2 * w)]
     elif mode == "down":
-        shapes = [(4 * w, dm)]
+        shapes = [(2 * w, dm)]
     else:
-        shapes = [(dm, w), (dm, w), (dm, w), (w, dm)]
+        shapes = [(dm, w // 2)] * 3 + [(w // 2, dm)]
     return pl.pallas_call(
         body,
-        in_specs=[pl.BlockSpec(memory_space=pltpu.SMEM)] + [pl.BlockSpec(memory_space=pltpu.VMEM)] * 10,
+        in_specs=[pl.BlockSpec(memory_space=pltpu.SMEM), pl.BlockSpec(memory_space=pltpu.VMEM)],
         out_specs=[pl.BlockSpec(memory_space=pltpu.VMEM)] * len(shapes),
         out_shape=[jax.ShapeDtypeStruct(s, F32) for s in shapes],
         compiler_params=pltpu.CompilerParams(vmem_limit_bytes=VMEM),
-        cost_estimate=pl.CostEstimate(flops=0, bytes_accessed=6 * 4 * dm * w, transcendentals=0),
-    )(coords, *parts)
+        cost_estimate=pl.CostEstimate(flops=0, bytes_accessed=12 * dm * w, transcendentals=0),
+    )(coords, done)
 
 
 def relative(stack, z):
@@ -555,26 +761,16 @@
     return jnp.where(core == 0, v, jnp.flip(v, axis))
 
 
-def gather_any(shard, z, core, mode):
-    mp = lax.axis_size("mp")
-    whole = relative(lax.all_gather(shard, "mp", axis=0, tiled=False), z)
-    if mode == "stack":
-        return whole
-    if mode == "rows":
-        v = whole.reshape(mp, 2, 2, shard.shape[0] // 4, shard.shape[1])
-        v = core_first(v.transpose(1, 2, 0, 3, 4), core, 0)
-        return v.reshape(mp * shard.shape[0], shard.shape[1])
-    v = whole.reshape(mp, shard.shape[0], 2, 2, shard.shape[1] // 4).transpose(1, 2, 3, 0, 4)
-    return core_first(v, core, 1).reshape(shard.shape[0], mp * shard.shape[1])
+def gather_any(shard, z):
+    return relative(lax.all_gather(shard, "mp", axis=0, tiled=False), z)
 
 
 def reduce_any(half, z, core):
-    mp = lax.axis_size("mp")
     zero = jnp.zeros_like(half)
-    v = jnp.stack([jnp.where(core == 0, half, zero), jnp.where(core == 1, half, zero)], axis=1)
-    v = jnp.roll(jnp.moveaxis(v, 3, 0), z, axis=0).astype(BF16)
+    v = jnp.stack([jnp.where(core == 0, half, zero), jnp.where(core == 1, half, zero)], axis=2)
+    v = jnp.roll(jnp.moveaxis(v, 1, 0), z, axis=0)
     v = lax.psum_scatter(v, "mp", scatter_dimension=0, tiled=True)[0]
-    return lax.psum(v.astype(BF16), "dp").astype(F32)
+    return lax.psum(v, "dp").astype(F32).reshape(half.shape[0], -1)
 
 
 def local(
@@ -627,7 +823,7 @@
     else:
         vecs = relative(lax.all_gather(small_vec, "mp", axis=0, tiled=False), z)
     bq_all, bv_all = vecs[:, :cw], vecs[:, cw : 2 * cw]
-    bu_all = vecs[:, 2 * cw :].reshape(mp, 2, 2, ffw // 4).transpose(1, 2, 0, 3)
+    bu_all = vecs[:, 2 * cw :].reshape(mp, 2, ffw // 2).transpose(1, 0, 2)
     bu_all = core_first(bu_all, core, 0).reshape(mp * ffw)
 
     is_near = z < near
@@ -649,17 +845,9 @@
 
     pack = jnp.concatenate([w_query, w_key, w_value, w_out.T], axis=1)
     if fast:
-        idx = jnp.concatenate([core[None], jnp.bitwise_xor(me, jnp.arange(8, dtype=jnp.int32))]).astype(jnp.int32)
-        mark1, parts1 = gather_shards(pack, me)
-        mark2, parts2 = gather_shards(w_up, me, mark1)
-        _, parts3 = gather_shards(w_down, me, mark2)
-        packed = assemble(idx, pack, parts1, "stack")
-        up_all = assemble(idx, w_up, parts2, "cols")
-        down_all = assemble(idx, w_down, parts3, "rows")
+        packed, up_all, down_all = gather_call([pack, w_up, w_down])
     else:
-        packed = gather_any(pack, z, core, "stack")
-        up_all = gather_any(w_up, z, core, "cols")
-        down_all = gather_any(w_down, z, core, "rows")
+        packed, up_all, down_all = (gather_any(w, z) for w in (pack, w_up, w_down))
 
     far = jnp.concatenate(halo, axis=0)
     far = jnp.concatenate([far[:-HALO], far[-HALO:] + before], axis=0)
@@ -669,27 +857,23 @@
     q, k, v = qkv_call(n1w, packed, bq_all, bv_all, own, rows, cw)
     attn, lse = attn_fwd_call(info, q, k, v, qseg, kseg, own)
     hidden, n2 = out_call(attn, packed, tokens, b_out, ln2_gain, ln2_bias)
-    active, slope = up_call(n2, up_all, bu_all)
-    output = (hidden + dot_nn(active, down_all) + f32(b_down)).astype(BF16)
-
-    other = lambda v: lax.ppermute(v, "dp", [(i, i ^ 1) for i in range(dp)])
+    output, g_n2, active, g_upper, g_b_up = ffn_call(
+        info[1:], n2, hidden, cotangent, up_all, down_all, bu_all, b_down, 2
+    )
+
+    other = lambda v: lax.ppermute(v, "dp", [(i, i - i % 2 + (i + 1) % 2) for i in range(dp)])
     hw = mp * ffw // 2
     cot_o = other(cotangent)
     act_o = other(active[:, hw:])
+    n2_o = other(n2)
+    gup_o = other(g_upper[:, hw:])
     gout = f32(cotangent)
 
     def pair_grad(left, right, left_o, right_o):
         return (dot_tn(left, right) + dot_tn(left_o, right_o)).astype(BF16)
 
-    gd_a = pair_grad(cotangent, active[:, : hw // 2], cot_o, act_o[:, : hw // 2])
-    gd_b = pair_grad(cotangent, active[:, hw // 2 : hw], cot_o, act_o[:, hw // 2 :])
-    g_upper = (dot_nt(cotangent, down_all) * f32(slope)).astype(BF16)
-    n2_o = other(n2)
-    gup_o = other(g_upper[:, hw:])
-    gu_a = pair_grad(n2, g_upper[:, : hw // 2], n2_o, gup_o[:, : hw // 2])
-    gu_b = pair_grad(n2, g_upper[:, hw // 2 : hw], n2_o, gup_o[:, hw // 2 :])
-    g_b_up = jnp.sum(f32(g_upper), axis=0)
-    g_n2 = dot_nt(g_upper, up_all)
+    gd = pair_grad(cotangent, active[:, :hw], cot_o, act_o)
+    gu = pair_grad(n2, g_upper[:, :hw], n2_o, gup_o)
     hat2, inv2 = norm_rows(hidden)
 
     def norm_back(g, hat, inv, gain):
@@ -728,21 +912,22 @@
         dq_o, dk_o, dv_o, at_o = other(dq[1]), other(dk[1]), other(dv[1]), other(attn_t)
         n1_o = n1w_o[own : own + rows]
         half = cw // 2
-        by_shard = lambda v: v.reshape(dm, mp, half)
-        gq = by_shard(pair_grad(n1, dq[0], n1_o, dq_o))
-        gk = by_shard(pair_grad(n1w, dk[0], n1w_o, dk_o))
-        gv = by_shard(pair_grad(n1w, dv[0], n1w_o, dv_o))
-        go = by_shard(pair_grad(ghb, attn_m, ghb_o, at_o))
-        gp_a = jnp.concatenate([gq, gk], axis=2).reshape(dm, mp * cw)
-        gp_b = jnp.concatenate([gv, go], axis=2).reshape(dm, mp * cw)
+        gs = [
+            pair_grad(n1, dq[0], n1_o, dq_o),
+            pair_grad(n1w, dk[0], n1w_o, dk_o),
+            pair_grad(n1w, dv[0], n1w_o, dv_o),
+            pair_grad(ghb, attn_m, ghb_o, at_o),
+        ]
+        gp = jnp.concatenate([g[:, d * half : (d + 1) * half] for d in range(mp) for g in gs], axis=1)
         coords = jnp.stack([y, x, core]).astype(jnp.int32)
-        (g_w_down,) = place_grads(coords, reduce_grad(gd_a, gd_b, y, x), "down")
-        (g_w_up,) = place_grads(coords, reduce_grad(gu_a, gu_b, y, x), "up")
-        g_w_query, g_w_key, g_w_value, g_w_out = place_grads(coords, reduce_grad(gp_a, gp_b, y, x), "pack")
+        done_d, done_u = reduce_call([gd, gu], 1)
+        (done_p,) = reduce_call([gp], 2)
+        (g_w_down,) = place_grads(coords, done_d, "down")
+        (g_w_up,) = place_grads(coords, done_u, "up")
+        g_w_query, g_w_key, g_w_value, g_w_out = place_grads(coords, done_p, "pack")
     else:
-        two = lambda a, b: jnp.stack([a, b], axis=1).reshape(dm, 2, mp, ffw // 4)
-        g_w_up = reduce_any(two(gu_a, gu_b), z, core).reshape(dm, ffw)
-        g_w_down = reduce_any(two(gd_a, gd_b), z, core).reshape(dm, ffw).T
+        g_w_up = reduce_any(gu.reshape(dm, mp, ffw // 2), z, core)
+        g_w_down = reduce_any(gd.reshape(dm, mp, ffw // 2), z, core).T
 
         def whole_grad(left, right, name=None):
             v = dot_tn(left, right).astype(BF16).reshape(dm, mp, cw)
@@ -768,7 +953,7 @@
 
     gbq = shards(jnp.sum(f32(dq), axis=1), cw)
     gbv = shards(jnp.sum(f32(dv), axis=1), cw)
-    gbu = core_first(g_b_up.reshape(2, 2, mp, ffw // 4), core, 0).transpose(2, 0, 1, 3)
+    gbu = core_first(g_b_up.reshape(2, mp, ffw // 2), core, 0).transpose(1, 0, 2)
     gbu = jnp.roll(gbu.reshape(mp, ffw), z, axis=0).reshape(-1)
     vec = jnp.concatenate(
         [g_gain1, g_bias1, jnp.sum(g_hidden, axis=0), g_gain2, g_bias2, jnp.sum(gout, axis=0), gbq, gbv, gbu]

time: 690 us -> 631 us (0.914)
  Pallas kernels: 150 us -> 415 us
  waiting for transfers between devices: 191 us -> 7.52 us
  starting transfers between devices: 109 us -> 31.5 us
  matrix products: 83.7 us -> 60.6 us
  local copies, waits for them, and re-layouts: 61 us -> 38.3 us
  other arithmetic: 46 us -> 26.5 us
    pallas_call x7, Pallas kernels: 53.8 us -> 328 us  [the longest x2 184 us: reduce_call(): pl.pallas_call(body, in_specs=[pl.BlockSpec(memory_space=pltpu.VMEM)] * c...]
    ppermute x94 -> x10, waiting for transfers between devices: 165 us -> 2.02 us  [local(): lax.ppermute(v, 'dp', [(i, i - i % 2 + (i + 1) % 2) for i in range(dp)])]
    ppermute x94 -> x10, starting transfers between devices: 94.5 us -> 2.72 us  [local(): lax.ppermute(v, 'dp', [(i, i - i % 2 + (i + 1) % 2) for i in range(dp)])]
    ppermute x3, waiting for transfers between devices: 24.1 us -> 0.01 us  [local(): lax.ppermute(small_vec, 'mp', [((i + d) % mp, i) for i in range(mp)])]
    dot_general x2 -> x0, matrix products: 19.1 us -> none  [dot_nt(): lax.dot_general(a, b, (((1,), (1,)), ((), ())), preferred_element_type=F32)]
    dot_general x5 -> x4, matrix products: 17.4 us -> 5.97 us  [dot_nn(): lax.dot_general(a, b, (((1,), (0,)), ((), ())), preferred_element_type=F32)]
    reshape x5 -> x1, local copies, waits for them, and re-layouts: 9.13 us -> 0.01 us  [local(): g_b_up.reshape(2, mp, ffw // 2)]
    pallas_call x1, Pallas kernels: 23.1 us -> 14.2 us  [norm1_back_call(): pl.pallas_call(body, grid_spec=pltpu.PrefetchScalarGridSpec(num_scalar_pr...]
  transfers between devices with their start and end apart: 103 -> 19, of which waited for: 24 -> 2; matrix products, arithmetic and copies ran while one was open for 27% -> 17% of each run, Pallas kernels for 21% -> 55%
where the time goes in v2:
time: 631 us; the launch traced here: 622 us
  Pallas kernels  415 us (66%)
  matrix products  60.6 us (10%)
  blocking collectives  40.8 us (6%)
  local copies, waits for them, and re-layouts  38.3 us (6%)
  starting transfers between devices  31.5 us (5%)
  other arithmetic  26.5 us (4%)
  waiting for transfers between devices  7.52 us (1%)
    pallas_call x2, Pallas kernels, reduce_call(): pl.pallas_call(body, in_specs=[pl.BlockSpec(memory_space=pltpu.VMEM)] * c...  184 us
    pallas_call x1, Pallas kernels, gather_call(): pl.pallas_call(body, in_specs=[pl.BlockSpec(memory_space=pltpu.VMEM)] * c...  104 us
    dot_general x12, matrix products, dot_tn(): lax.dot_general(a, b, (((0,), (0,)), ((), ())), preferred_element_type=F32)  54.6 us
    psum x1, blocking collectives, local(): vec = lax.psum(vec, ('dp', 'mp'))  40.8 us
    pallas_call x1, Pallas kernels, attn_bwd_call(): pl.pallas_call(body, grid_spec=pltpu.PrefetchScalarGridSpec(num_scalar_pr...  30.4 us
    pallas_call x1, Pallas kernels, ffn_call(): pl.pallas_call(body, grid_spec=pltpu.PrefetchScalarGridSpec(num_scalar_pr...  28.7 us
    pallas_call x1, Pallas kernels, attn_fwd_call(): pl.pallas_call(body, grid_spec=pltpu.PrefetchScalarGridSpec(num_scalar_pr...  25.2 us
    unnamed x86, local copies, waits for them, and re-layouts  16.1 us
  transfers between devices with their start and end apart: 19, of which 2 were waited for; matrix products, arithmetic and copies ran while one was open for 17% of the time, Pallas kernels for 55%

profile of v2, /device:TPU:0, one launch (start us, length us, event | category | flops | bytes accessed | tf_op | source)
XLA Modules:
  0.0 622.2 jit_solution(17844545088295616564)
XLA Ops:
  0.7 0.9 dynamic-update-slice.25
  1.5 0.8 dynamic-update-slice.26
  2.4 0.8 dynamic-update-slice.27
  3.2 5.1 collective-permute-start.3
  8.3 1.0 collective-permute-start.5
  9.3 4.4 collective-permute-start
  13.7 1.0 fusion.51
  15.4 1.3 broadcast_in_dim.56.g_ref
  17.4 1.2 copy.64
  19.9 0.8 dynamic-slice_select_fusion
  20.8 3.0 pad_maximum_fusion.refs_0_
  23.7 0.8 broadcast_select_fusion
  25.3 0.9 copy.67.refs_3_.refs_6_
  27.9 103.5 %shard_map.305 = (bf16[4,1024,1024]{2,1,0:T(8,128)(2,1)}, bf16[4,1024,1024]{2,1,0:T(8,128)(2,1)}, bf16[4,1024,1024]{2,1,0:T(8,128)(2,1)}) custom-call(bf16[1024,1024]{1,0:T(8,128)(2,1)} %pad_maximum_fusion.refs_0_, bf16[1024,1024]{1,0:T(8,128)(2,1)} %refs_1_.1, bf16[1024,1024]{1,0:T(8,128)(2,1)} %refs_2_.1), custom_call_target="tpu_custom_call" | custom-call | tf_op jit(solution)/shard_map/pallas_call | solution.py:551
  131.5 0.8 collective-permute-start.2
  136.3 4.0 fusion
  140.3 10.2 %shard_map.306 = (bf16[4,512,256]{2,1,0:T(8,128)(2,1)}, bf16[4,1152,256]{2,1,0:T(8,128)(2,1)}, bf16[4,1152,256]{2,1,0:T(8,128)(2,1)}) custom-call(bf16[1152,1024]{1,0:T(8,128)(2,1)} %get-tuple-element.86.x_ref, bf16[4,1024,1024]{2,1,0:T(8,128)(2,1)} %get-tuple-element.45.w_ref, bf16[4,1,256]{2,1,0:T(2,128)(2,1)} %copy.65.bq_ref, bf16[4,1,256]{2,1,0:T(2,128)(2,1)} %copy.66.bv_ref), custom_call_target="tpu_custom_call" | custom-call | flops 5905580032 | bytes 10747904 | tf_op jit(solution)/shard_map/pallas_call | solution.py:58
  150.4 25.2 %shard_map.307 = (bf16[4,512,256]{2,1,0:T(8,128)(2,1)}, f32[8,512,2]{2,1,0:T(8,128)}) custom-call(s32[2]{0:T(128)} %pad_add_fusion.big_ref.info_ref, bf16[4,512,256]{2,1,0:T(8,128)(2,1)} %get-tuple-element.46.refs_0_, bf16[4,1152,256]{2,1,0:T(8,128)(2,1)} %get-tuple-element.47.refs_1_, bf16[4,1152,256]{2,1,0:T(8,128)(2,1)} %get-tuple-element.48.refs_2_, ...), custom_call_target="tpu_custom_call" | custom-call | flops 9663676416 | bytes 6815744 | tf_op jit(solution)/shard_map/pallas_call | solution.py:119
  175.7 7.1 %shard_map.308 = (f32[512,1024]{1,0:T(8,128)}, bf16[512,1024]{1,0:T(8,128)(2,1)}) custom-call(bf16[4,512,256]{2,1,0:T(8,128)(2,1)} %get-tuple-element.49.a_ref.refs_3_, bf16[4,1024,1024]{2,1,0:T(8,128)(2,1)} %get-tuple-element.45.w_ref, bf16[512,1024]{1,0:T(8,128)(2,1)} %x_ref.1, bf16[1,1024]{1,0:T(2,128)(2,1)} %broadcast_in_dim.55.bo_ref, ...), custom_call_target="tpu_custom_call" | custom-call | flops 1073741824 | bytes 2097152 | tf_op jit(solution)/shard_map/pallas_call | solution.py:263
  182.7 28.7 %shard_map.309 = (bf16[512,1024]{1,0:T(8,128)(2,1)}, f32[512,1024]{1,0:T(8,128)}, bf16[512,4096]{1,0:T(8,128)(2,1)}, bf16[512,4096]{1,0:T(8,128)(2,1)}, f32[1,4096]{1,0:T(1,128)}) custom-call(s32[1]{0:T(128)} %bitcast.core_ref, bf16[512,1024]{1,0:T(8,128)(2,1)} %get-tuple-element.50.x_ref, f32[512,1024]{1,0:T(8,128)} %get-tuple-element.51.h_ref, ...), custom_call_target="tpu_custom_call" | custom-call | flops 17179869184 | bytes 16777216 | tf_op jit(solution)/shard_map/pallas_call | solution.py:319
  211.5 7.7 %fusion.4 = f32[1024,2048]{1,0:T(8,128)} fusion(bf16[512,1024]{1,0:T(8,128)(2,1)} %get-tuple-element.50.x_ref, bf16[512,4096]{1,0:T(8,128)(2,1)} %get-tuple-element.69), kind=kOutput, calls=%fused_computation.14 | convolution fusion | flops 2147483648 | bytes 11534336 | tf_op jit(solution)/shard_map/dot_general | solution.py:30
  219.2 1.5 slice.211
  220.8 1.1 reshape.138
  222.5 1.2 copy-done.4
  223.7 1.0 multiply_reduce_fusion
  224.7 2.3 fusion.48
  227.7 1.5 fusion.18
  229.2 1.5 fusion.19
  230.7 1.5 fusion.20
  232.2 1.5 fusion.21
  233.7 1.1 pad_maximum_fusion.2.refs_4_
  234.8 30.4 %shard_map.310 = (bf16[2,512,512]{2,1,0:T(8,128)(2,1)}, bf16[2,1152,512]{2,1,0:T(8,128)(2,1)}, bf16[2,1152,512]{2,1,0:T(8,128)(2,1)}) custom-call(s32[2]{0:T(128)} %pad_add_fusion.big_ref.info_ref, bf16[4,512,256]{2,1,0:T(8,128)(2,1)} %get-tuple-element.46.refs_0_, bf16[4,1152,256]{2,1,0:T(8,128)(2,1)} %get-tuple-element.47.refs_1_, ...), custom_call_target="tpu_custom_call" | custom-call | flops 24159191040 | bytes 13631488 | tf_op jit(solution)/shard_map/pallas_call | solution.py:207
  265.2 3.5 fusion.23
  268.7 0.8 slice_bitcast_fusion.2
  269.8 1.1 slice_bitcast_fusion
  271.2 14.2 %shard_map.311 = (f32[512,1024]{1,0:T(8,128)}, bf16[512,1024]{1,0:T(8,128)(2,1)}, bf16[64,1024]{1,0:T(8,128)(2,1)}) custom-call(s32[2]{0:T(128)} %pad_add_fusion.big_ref.info_ref, bf16[2,512,512]{2,1,0:T(8,128)(2,1)} %get-tuple-element.57.dq_ref, bf16[2,1152,512]{2,1,0:T(8,128)(2,1)} %get-tuple-element.58.dk_ref, ...), custom_call_target="tpu_custom_call" | custom-call | flops 5905580032 | bytes 12058624 | tf_op jit(solution)/shard_map/pallas_call | solution.py:394
  285.4 15.5 %collective-permute-start.6 = (bf16[512,1024]{1,0:T(8,128)(2,1)}, bf16[512,1024]{1,0:T(8,128)(2,1)}, u32[]{:S(2)}, u32[]{:S(2)}) collective-permute-start(bf16[512,1024]{1,0:T(8,128)(2,1)} %get-tuple-element.61), channel_id=1, source_target_pairs={{0,1},{1,0},{4,5},{5,4},{8,9},{9,8},{12,13},{13,12},{16,17},{17,16... | collective-permute-start | bytes 3145736 | tf_op jit(solution)/shard_map/ppermute | solution.py:896
  301.0 0.9 slice.177
  301.9 3.2 slice.209
  305.1 0.8 copy.76
  305.9 2.1 fusion.25
  308.0 0.8 dynamic-slice_bitcast_fusion
  310.8 7.6 %fusion.6 = f32[2048,1024]{0,1:T(8,128)} fusion(bf16[512,1024]{1,0:T(8,128)(2,1)} %c_ref.1, bf16[512,4096]{1,0:T(8,128)(2,1)} %get-tuple-element.68), kind=kOutput, calls=%fused_computation.16 | convolution fusion | flops 2147483648 | bytes 11534336 | tf_op jit(solution)/shard_map/dot_general | solution.py:30
  318.5 1.1 slice_bitcast_fusion.1
  319.5 5.5 collective-permute-done.6
  325.7 1.7 convert_add_fusion.1
  328.3 2.4 multiply_reduce_fusion.1
  330.8 2.0 collective-permute-done.14
  333.3 2.0 add_convert_fusion.3
  335.4 40.8 %psum.7 = f32[12288]{0:T(1024)S(1)} all-reduce(f32[12288]{0:T(1024)S(1)} %bitcast_dynamic-update-slice_fusion), channel_id=1, replica_groups=mesh['dp'=8,'mp'=4] {'dp','mp'}, use_global_device_ids=true, to_apply=%region_18.20 | all-reduce | flops 12288 | bytes 98304 | tf_op jit(solution)/shard_map/psum | solution.py:961
  376.2 3.9 multiply_add_fusion
  382.0 9.3 %add_convert_fusion.refs_1_ = bf16[1024,2048]{1,0:T(8,128)(2,1)} fusion(f32[1024,2048]{1,0:T(8,128)} %fusion.4, bf16[512,1024]{1,0:T(8,128)(2,1)} %collective-permute-done.17, bf16[512,2048]{1,0:T(8,128)(2,1)} %collective-permute-done.18), kind=kOutput, calls=%fused_computation | convolution fusion | flops 2151677952 | bytes 15728640 | tf_op jit(solution)/shard_map/dot_general | solution.py:30
  391.4 6.6 %fusion.3.refs_0_ = bf16[1024,2048]{1,0:T(8,128)(2,1)} fusion(f32[2048,1024]{0,1:T(8,128)S(1)} %bitcast.114, bf16[512,2048]{1,0:T(8,128)(2,1)} %collective-permute-done.15, bf16[512,1024]{1,0:T(8,128)(2,1)} %collective-permute-done.16), kind=kOutput, calls=%fused_computation.9 | convolution fusion | flops 2151677952 | bytes 15728640 | tf_op jit(solution)/shard_map/dot_general | solution.py:30
  398.0 114.2 %shard_map.314 = (bf16[8,256,512]{2,1,0:T(8,128)(2,1)}, bf16[8,256,512]{2,1,0:T(8,128)(2,1)}) custom-call(bf16[1024,2048]{1,0:T(8,128)(2,1)} %fusion.3.refs_0_, bf16[1024,2048]{1,0:T(8,128)(2,1)} %add_convert_fusion.refs_1_), custom_call_target="tpu_custom_call" | custom-call | tf_op jit(solution)/shard_map/pallas_call | solution.py:705
  512.2 4.3 shard_map.316
  516.5 3.9 shard_map.315
  520.4 3.7 fusion.55
  524.1 3.2 add_convert_fusion.4
  527.4 3.6 fusion.54
  530.9 3.4 add_convert_fusion.5
  534.3 2.0 add_convert_fusion.6
  537.9 0.8 slice_dynamic-update-slice_fusion.14
  548.6 69.5 %shard_map.312.f_ref = bf16[8,256,512]{2,1,0:T(8,128)(2,1)} custom-call(bf16[1024,2048]{1,0:T(8,128)(2,1)} %slice_dynamic-update-slice_fusion.1.refs_0_), custom_call_target="tpu_custom_call" | custom-call | tf_op jit(solution)/shard_map/pallas_call | solution.py:705
  618.1 3.9 shard_map.313
  (169 shorter events, 28.2 us)
Async XLA Ops:
  3.2 128.3 %collective-permute-start.3 = (bf16[1536]{0:T(1024)(128)(2,1)S(1)}, bf16[1536]{0:T(1024)(128)(2,1)S(1)}, u32[]{:S(2)}, u32[]{:S(2)}) collective-permute-start(bf16[1536]{0:T(1024)(128)(2,1)S(1)} %dynamic-update-slice.27), channel_id=1, source_target_pairs={{1,0},{2,1},{3,2},{0,3},{5,4},{6,5},{7,6},{4,7},{9,8},{10,9},{11,1... | collective-permute-start | bytes 9224 | tf_op jit(solution)/shard_map/ppermute | solution.py:820
  8.3 124.0 %collective-permute-start.4 = (bf16[1536]{0:T(1024)(128)(2,1)S(1)}, bf16[1536]{0:T(1024)(128)(2,1)S(1)}, u32[]{:S(2)}, u32[]{:S(2)}) collective-permute-start(bf16[1536]{0:T(1024)(128)(2,1)S(1)} %dynamic-update-slice.27), channel_id=1, source_target_pairs={{2,0},{3,1},{0,2},{1,3},{6,4},{7,5},{4,6},{5,7},{10,8},{11,9},{8,1... | collective-permute-start | bytes 9224 | tf_op jit(solution)/shard_map/ppermute | solution.py:820
  8.3 124.6 %collective-permute-start.5 = (bf16[1536]{0:T(1024)(128)(2,1)S(1)}, bf16[1536]{0:T(1024)(128)(2,1)S(1)}, u32[]{:S(2)}, u32[]{:S(2)}) collective-permute-start(bf16[1536]{0:T(1024)(128)(2,1)S(1)} %dynamic-update-slice.27), channel_id=1, source_target_pairs={{3,0},{0,1},{1,2},{2,3},{7,4},{4,5},{5,6},{6,7},{11,8},{8,9},{9,10... | collective-permute-start | bytes 9224 | tf_op jit(solution)/shard_map/ppermute | solution.py:820
  9.3 125.5 %collective-permute-start = (bf16[512,1024]{1,0:T(8,128)(2,1)}, bf16[512,1024]{1,0:T(8,128)(2,1)S(1)}, u32[]{:S(2)}, u32[]{:S(2)}) collective-permute-start(bf16[512,1024]{1,0:T(8,128)(2,1)} %x_ref.1), channel_id=1, source_target_pairs={{1,0},{0,1},{5,4},{4,5},{9,8},{8,9},{13,12},{12,13},{17,16},{16,17... | collective-permute-start | bytes 3145736 | tf_op jit(solution)/shard_map/ppermute | solution.py:813
  14.7 120.2 %collective-permute-start.1 = (bf16[64,1024]{1,0:T(8,128)(2,1)S(1)}, bf16[64,1024]{1,0:T(8,128)(2,1)S(1)}, u32[]{:S(2)}, u32[]{:S(2)}) collective-permute-start(bf16[64,1024]{1,0:T(8,128)(2,1)S(1)} %get-tuple-element.93), channel_id=1, source_target_pairs={{1,2},{2,3},{5,6},{6,7},{9,10},{10,11},{13,14},{14,15},{17,18},{18... | collective-permute-start | bytes 393224 | tf_op jit(solution)/shard_map/ppermute | solution.py:815
  18.6 7.5 %copy-start.20 = (bf16[1024]{0:T(1024)(128)(2,1)S(1)}, bf16[1024]{0:T(1024)(128)(2,1)}, u32[]{:S(2)}) copy-start(bf16[1024]{0:T(1024)(128)(2,1)} %param.22) | copy-start | bytes 6148
  18.6 7.5 %copy-start.21 = (bf16[1024]{0:T(1024)(128)(2,1)S(1)}, bf16[1024]{0:T(1024)(128)(2,1)}, u32[]{:S(2)}) copy-start(bf16[1024]{0:T(1024)(128)(2,1)} %param.23) | copy-start | bytes 6148
  18.6 7.5 %copy-start.22 = (bf16[1024]{0:T(1024)(128)(2,1)S(1)}, bf16[1024]{0:T(1024)(128)(2,1)}, u32[]{:S(2)}) copy-start(bf16[1024]{0:T(1024)(128)(2,1)} %param.30) | copy-start | bytes 6148
  18.7 8.1 %copy-start.23 = (bf16[1024]{0:T(1024)(128)(2,1)S(1)}, bf16[1024]{0:T(1024)(128)(2,1)}, u32[]{:S(2)}) copy-start(bf16[1024]{0:T(1024)(128)(2,1)} %param.32) | copy-start | bytes 6148
  18.7 8.7 %copy-start.24 = (bf16[1024]{0:T(1024)(128)(2,1)S(1)}, bf16[1024]{0:T(1024)(128)(2,1)}, u32[]{:S(2)}) copy-start(bf16[1024]{0:T(1024)(128)(2,1)} %param.36) | copy-start | bytes 6148
  131.5 3.5 copy-start.8
  131.5 3.5 collective-permute-start.2
  132.3 259.0 %collective-permute-start.16 = (bf16[512,1024]{1,0:T(8,128)(2,1)}, bf16[512,1024]{1,0:T(8,128)(2,1)}, u32[]{:S(2)}, u32[]{:S(2)}) collective-permute-start(bf16[512,1024]{1,0:T(8,128)(2,1)} %c_ref.1), channel_id=1, source_target_pairs={{0,4},{4,0},{8,12},{12,8},{16,20},{20,16},{24,28},{28,24},{1,5},{5... | collective-permute-start | bytes 3145736 | tf_op jit(solution)/shard_map/ppermute | solution.py:864
  211.5 7.7 %copy-start.15 = (bf16[512,4096]{1,0:T(8,128)(2,1)S(1)}, bf16[512,4096]{1,0:T(8,128)(2,1)}, u32[]{:S(2)}) copy-start(bf16[512,4096]{1,0:T(8,128)(2,1)} %get-tuple-element.69) | copy-start | bytes 12582916
  219.2 1.6 copy-start.10
  219.2 2.7 copy-start
  220.7 160.7 %collective-permute-start.17 = (bf16[512,1024]{1,0:T(8,128)(2,1)}, bf16[512,1024]{1,0:T(8,128)(2,1)}, u32[]{:S(2)}, u32[]{:S(2)}) collective-permute-start(bf16[512,1024]{1,0:T(8,128)(2,1)} %get-tuple-element.50.x_ref), channel_id=1, source_target_pairs={{0,4},{4,0},{8,12},{12,8},{16,20},{20,16},{24,28},{28,24},{1,5},{5... | collective-permute-start | bytes 3145736 | tf_op jit(solution)/shard_map/ppermute | solution.py:864
  222.1 1.6 copy-start.4
  227.0 2.2 copy-start.1
  227.2 105.8 %collective-permute-start.13 = (bf16[512,1024]{1,0:T(8,128)(2,1)S(1)}, bf16[512,1024]{1,0:T(8,128)(2,1)}, u32[]{:S(2)}, u32[]{:S(2)}) collective-permute-start(bf16[512,1024]{1,0:T(8,128)(2,1)S(1)} %convert_element_type.76), channel_id=1, source_target_pairs={{0,4},{4,0},{8,12},{12,8},{16,20},{20,16},{24,28},{28,24},{1,5},{5... | collective-permute-start | bytes 3145736 | tf_op jit(solution)/shard_map/ppermute | solution.py:864
  265.2 3.6 copy-start.12
  265.2 4.6 copy-start.6
  285.4 19.6 %copy-start.9 = (bf16[4,512,2,128]{3,2,1,0:T(2,128)(2,1)S(1)}, bf16[4,512,2,128]{3,2,1,0:T(2,128)(2,1)}, u32[]{:S(2)}) copy-start(bf16[4,512,2,128]{3,2,1,0:T(2,128)(2,1)} %reshape.138) | copy-start | bytes 3145732
  285.4 39.6 %collective-permute-start.6 = (bf16[512,1024]{1,0:T(8,128)(2,1)}, bf16[512,1024]{1,0:T(8,128)(2,1)}, u32[]{:S(2)}, u32[]{:S(2)}) collective-permute-start(bf16[512,1024]{1,0:T(8,128)(2,1)} %get-tuple-element.61), channel_id=1, source_target_pairs={{0,1},{1,0},{4,5},{5,4},{8,9},{9,8},{12,13},{13,12},{16,17},{17,16... | collective-permute-start | bytes 3145736 | tf_op jit(solution)/shard_map/ppermute | solution.py:896
  305.9 4.2 copy-start.19
  308.9 18.7 %collective-permute-start.8 = (bf16[64,1024]{1,0:T(8,128)(2,1)S(1)}, bf16[64,1024]{1,0:T(8,128)(2,1)S(1)}, u32[]{:S(2)}, u32[]{:S(2)}) collective-permute-start(bf16[64,1024]{1,0:T(8,128)(2,1)S(1)} %slice.177), channel_id=1, source_target_pairs={{2,1},{3,2},{6,5},{7,6},{10,9},{11,10},{14,13},{15,14},{18,17},{19... | collective-permute-start | bytes 393224 | tf_op jit(solution)/shard_map/ppermute | solution.py:897
  310.8 7.6 %copy-start.16 = (bf16[2,1152,512]{2,1,0:T(8,128)(2,1)S(1)}, bf16[2,1152,512]{2,1,0:T(8,128)(2,1)}, u32[]{:S(2)}) copy-start(bf16[2,1152,512]{2,1,0:T(8,128)(2,1)} %get-tuple-element.58.dk_ref) | copy-start | bytes 7077892
  318.4 6.6 %copy-start.25 = (bf16[64,1024]{1,0:T(8,128)(2,1)S(1)}, bf16[64,1024]{1,0:T(8,128)(2,1)}, u32[]{:S(2)}) copy-start(bf16[64,1024]{1,0:T(8,128)(2,1)} %get-tuple-element.62) | copy-start | bytes 393220
  318.4 7.2 %copy-start.14 = (f32[512,1024]{1,0:T(8,128)S(1)}, f32[512,1024]{1,0:T(8,128)}, u32[]{:S(2)}) copy-start(f32[512,1024]{1,0:T(8,128)} %get-tuple-element.60) | copy-start | bytes 6291460
  325.0 2.7 collective-permute-start.7
  327.6 3.1 copy-start.3
  327.6 53.9 %collective-permute-start.18 = (bf16[512,2048]{1,0:T(8,128)(2,1)}, bf16[512,2048]{1,0:T(8,128)(2,1)}, u32[]{:S(2)}, u32[]{:S(2)}) collective-permute-start(bf16[512,2048]{1,0:T(8,128)(2,1)} %slice.211), channel_id=1, source_target_pairs={{0,4},{4,0},{8,12},{12,8},{16,20},{20,16},{24,28},{28,24},{1,5},{5... | collective-permute-start | bytes 6291464 | tf_op jit(solution)/shard_map/ppermute | solution.py:864
  327.7 5.1 collective-permute-start.14
  328.3 7.0 %copy-start.11 = (f32[64,1024]{1,0:T(8,128)}, f32[64,1024]{1,0:T(8,128)S(1)}, u32[]{:S(2)}) copy-start(f32[64,1024]{1,0:T(8,128)S(1)} %get-tuple-element.90) | copy-start | bytes 786436
  328.3 5.0 copy-start.5
  330.8 45.4 %copy-start.2 = (f32[512,1024]{1,0:T(8,128)S(1)}, f32[512,1024]{1,0:T(8,128)}, u32[]{:S(2)}) copy-start(f32[512,1024]{1,0:T(8,128)} %copy-done.1) | copy-start | bytes 6291460
  332.8 187.6 %collective-permute-start.9 = (bf16[1152,1024]{1,0:T(8,128)(2,1)}, bf16[1152,1024]{1,0:T(8,128)(2,1)}, u32[]{:S(2)}, u32[]{:S(2)}) collective-permute-start(bf16[1152,1024]{1,0:T(8,128)(2,1)} %get-tuple-element.86.x_ref), channel_id=1, source_target_pairs={{0,4},{4,0},{8,12},{12,8},{16,20},{20,16},{24,28},{28,24},{1,5},{5... | collective-permute-start | bytes 7077896 | tf_op jit(solution)/shard_map/ppermute | solution.py:864
  333.0 58.4 %collective-permute-start.15 = (bf16[512,2048]{1,0:T(8,128)(2,1)}, bf16[512,2048]{1,0:T(8,128)(2,1)}, u32[]{:S(2)}, u32[]{:S(2)}) collective-permute-start(bf16[512,2048]{1,0:T(8,128)(2,1)} %slice.209), channel_id=1, source_target_pairs={{0,4},{4,0},{8,12},{12,8},{16,20},{20,16},{24,28},{28,24},{1,5},{5... | collective-permute-start | bytes 6291464 | tf_op jit(solution)/shard_map/ppermute | solution.py:864
  380.8 10.5 %slice-start = ((s8[8388608]{0:T(1024)(128)(4,1)}), s8[4194304]{0:T(1024)(128)(4,1)S(1)}, s32[]{:S(2)}) async-start(s8[8388608]{0:T(1024)(128)(4,1)} %bitcast.113), calls=%async_computation | async-start | bytes 8388608
  381.4 9.9 %copy-start.18 = (bf16[512,512]{1,0:T(8,128)(2,1)S(1)}, bf16[512,512]{1,0:T(8,128)(2,1)}, u32[]{:S(2)}) copy-start(bf16[512,512]{1,0:T(8,128)(2,1)} %slice_bitcast_fusion.2) | copy-start | bytes 1572868
  381.4 9.9 %slice-start.1 = ((s8[8388608]{0:T(1024)(128)(4,1)}), s8[4194304]{0:T(1024)(128)(4,1)S(1)}, s32[]{:S(2)}) async-start(s8[8388608]{0:T(1024)(128)(4,1)} %bitcast.113), calls=%async_computation.1 | async-start | bytes 8388608
  381.4 139.0 %collective-permute-start.12 = (bf16[1152,512]{1,0:T(8,128)(2,1)}, bf16[1152,512]{1,0:T(8,128)(2,1)}, u32[]{:S(2)}, u32[]{:S(2)}) collective-permute-start(bf16[1152,512]{1,0:T(8,128)(2,1)} %slice_bitcast_fusion), channel_id=1, source_target_pairs={{0,4},{4,0},{8,12},{12,8},{16,20},{20,16},{24,28},{28,24},{1,5},{5... | collective-permute-start | bytes 3538952 | tf_op jit(solution)/shard_map/ppermute | solution.py:864
  381.5 145.8 %collective-permute-start.11 = (bf16[1152,512]{1,0:T(8,128)(2,1)}, bf16[1152,512]{1,0:T(8,128)(2,1)S(1)}, u32[]{:S(2)}, u32[]{:S(2)}) collective-permute-start(bf16[1152,512]{1,0:T(8,128)(2,1)} %slice_bitcast_fusion.1), channel_id=1, source_target_pairs={{0,4},{4,0},{8,12},{12,8},{16,20},{20,16},{24,28},{28,24},{1,5},{5... | collective-permute-start | bytes 3538952 | tf_op jit(solution)/shard_map/ppermute | solution.py:864
  391.3 143.0 %collective-permute-start.10 = (bf16[512,512]{1,0:T(8,128)(2,1)S(1)}, bf16[512,512]{1,0:T(8,128)(2,1)S(1)}, u32[]{:S(2)}, u32[]{:S(2)}) collective-permute-start(bf16[512,512]{1,0:T(8,128)(2,1)S(1)} %copy-done.18), channel_id=1, source_target_pairs={{0,4},{4,0},{8,12},{12,8},{16,20},{20,16},{24,28},{28,24},{1,5},{5... | collective-permute-start | bytes 1572872 | tf_op jit(solution)/shard_map/ppermute | solution.py:864
  520.4 3.7 copy-start.7
  527.3 3.6 copy-start.17
  530.9 3.4 copy-start.13

commit v3 on v2

--- a/solution.py
+++ b/solution.py
@@ -14,6 +14,7 @@
 EPS = 1e-06
 NEG = -1e30
 VMEM = 60 * 1024 * 1024
+VMEM_ALL = 67043328
 F32 = jnp.float32
 BF16 = jnp.bfloat16
 
@@ -450,9 +451,8 @@
 
 
 class Wire:
-    def __init__(self, send, recv):
-        self.send, self.recv = send, recv
-        self.open = []
+    def __init__(self, send, recv, dev):
+        self.send, self.recv, self.dev = send, recv, dev
 
     def start(self, slot, src, dst, dev):
         copy = pltpu.make_async_remote_copy(
@@ -460,17 +460,18 @@
             device_id=dev, device_id_type=MESH,
         )
         copy.start()
-        self.open.append(copy)
+
+    def sent(self, slot, ref):
+        pltpu.make_async_remote_copy(
+            src_ref=ref, dst_ref=ref, send_sem=self.send.at[slot], recv_sem=self.recv.at[slot],
+            device_id=dict(self.dev), device_id_type=MESH,
+        ).wait_send()
 
     def landed(self, slot, ref, dev):
         pltpu.make_async_remote_copy(
             src_ref=ref, dst_ref=ref, send_sem=self.send.at[slot], recv_sem=self.recv.at[slot],
             device_id=dev, device_id_type=MESH,
         ).wait_recv()
-
-    def drain(self):
-        for copy in self.open:
-            copy.wait_send()
 
 
 def gather_steps(place, wire, base, shard, whole):
@@ -517,6 +518,8 @@
         for d in (1, 2, 3):
             for kind, who in ((1, place.me), (6, place.me_x), (7, place.me_y), (8, place.me_xy)):
                 wire.landed(slot(d, kind), whole.at[d, rows(who + flip)], place.core)
+            for kind in range(9):
+                wire.sent(slot(d, kind), whole.at[d, pl.ds(0, half if kind in (4, 5) else step)])
 
     return begin, first, second, third, finish
 
@@ -528,7 +531,7 @@
         ins, outs = refs[:count], refs[count : 2 * count]
         send, recv, local_sem = refs[2 * count :]
         place = Place()
-        wire = Wire(send, recv)
+        wire = Wire(send, recv, place.core)
         copies = [pltpu.make_async_copy(ins[g], outs[g].at[0], local_sem.at[g]) for g in range(count)]
         place.meet()
         groups = [gather_steps(place, wire, g * 27, ins[g], outs[g]) for g in range(count)]
@@ -546,7 +549,6 @@
             finish()
         for c in copies:
             c.wait()
-        wire.drain()
 
     return pl.pallas_call(
         body,
@@ -574,9 +576,6 @@
             pltpu.VMEM((4, q, w), BF16),
             pltpu.VMEM((4, e, w), BF16),
             pltpu.VMEM((4, e, w), BF16),
-            pltpu.VMEM((4, e, w), BF16),
-            pltpu.VMEM((4, e, w), BF16),
-            pltpu.VMEM((4, q, w), BF16),
             pltpu.VMEM((3, q, w), BF16),
             pltpu.SemaphoreType.DMA((Reduce.SLOTS,)),
             pltpu.SemaphoreType.DMA((Reduce.SLOTS,)),
@@ -584,8 +583,8 @@
 
     def __init__(self, place, grad, landing, scratch):
         self.place, self.g, self.f = place, grad, landing
-        self.ra1, self.rb1, self.ra2, self.rb2, self.sa, self.sb, self.t, self.zb = scratch[:8]
-        self.wire = Wire(scratch[8], scratch[9])
+        self.ra1, self.rb1, self.ra2, self.rb2, self.zb = scratch[:5]
+        self.wire = Wire(scratch[5], scratch[6], place.core)
         self.q = grad.shape[0] // 4
         self.e = self.q // 2
         self.w = grad.shape[1] // 4
@@ -598,7 +597,7 @@
         return pl.ds(pl.multiple_of(small * self.e, self.e), self.e)
 
     def cols(self, d):
-        return slice(d * self.w, (d + 1) * self.w)
+        return pl.ds(pl.multiple_of(d * self.w, self.w), self.w)
 
     def one(self, d):
         p, wire = self.place, self.wire
@@ -607,19 +606,16 @@
 
     def two(self, d):
         p, wire, c = self.place, self.wire, self.cols(d)
-        wire.landed(d, self.ra1.at[d], p.by_x)
-        self.sa[d] = (
-            self.g[self.at(0, p.x, 1 - p.y), c].astype(F32) + self.ra1[d, self.eighth(1 - p.y), :].astype(F32)
-        ).astype(BF16)
-        wire.start(8 + d, self.sa.at[d], self.ra2.at[d], p.by_y)
-        wire.landed(4 + d, self.rb1.at[d], p.by_y)
-        self.sb[d] = (
-            self.g[self.at(1, p.y, 1 - p.x), c].astype(F32) + self.rb1[d, self.eighth(1 - p.x), :].astype(F32)
-        ).astype(BF16)
-        wire.start(12 + d, self.sb.at[d], self.rb2.at[d], p.by_x)
-
-    def three(self, d):
-        p, wire, c, e = self.place, self.wire, self.cols(d), self.e
+        for slot, buf, to, at, mine, dev, nxt in (
+            (0, self.ra1, self.ra2, self.at(0, p.x, 1 - p.y), self.eighth(1 - p.y), p.by_x, p.by_y),
+            (4, self.rb1, self.rb2, self.at(1, p.y, 1 - p.x), self.eighth(1 - p.x), p.by_y, p.by_x),
+        ):
+            wire.landed(slot + d, buf.at[d], dev)
+            self.g[at, c] = (self.g[at, c].astype(F32) + buf[d, mine, :].astype(F32)).astype(BF16)
+            wire.start(8 + slot + d, self.g.at[at, c], to.at[d], nxt)
+
+    def sums(self, d):
+        p, wire, c = self.place, self.wire, self.cols(d)
         wire.landed(8 + d, self.ra2.at[d], p.by_y)
         wire.landed(12 + d, self.rb2.at[d], p.by_x)
         up = (
@@ -632,20 +628,30 @@
             + self.rb1[d, self.eighth(p.x), :].astype(F32)
             + self.rb2[d].astype(F32)
         )
-        if d:
-            self.t[d, 0:e] = up.astype(BF16)
-            self.t[d, e : 2 * e] = low.astype(BF16)
-            wire.start(16 + d, self.t.at[d], self.zb.at[d - 1], p.along(d))
-        else:
-            for s in (1, 2, 3):
-                wire.landed(16 + s, self.zb.at[s - 1], p.along(4 - s))
-                up = up + self.zb[s - 1, 0:e].astype(F32)
-                low = low + self.zb[s - 1, e : 2 * e].astype(F32)
-            self.f[0, 0:e] = up.astype(BF16)
-            self.f[0, e : 2 * e] = low.astype(BF16)
-            wire.start(20, self.f.at[0], self.f.at[2], p.by_x)
-            wire.start(21, self.f.at[0], self.f.at[4], p.by_y)
-            wire.start(22, self.f.at[0], self.f.at[1], p.core)
+        return up, low
+
+    def three(self, d):
+        p, wire, c, e = self.place, self.wire, self.cols(d), self.e
+        up, low = self.sums(d)
+        for part, (at, val) in enumerate(((self.at(0, p.x, p.y), up), (self.at(1, p.y, p.x), low))):
+            self.g[at, c] = val.astype(BF16)
+            wire.start(
+                16 + 12 * part + d, self.g.at[at, c], self.zb.at[d - 1, part * e : (part + 1) * e], p.along(d)
+            )
+
+    def last(self):
+        p, wire, e = self.place, self.wire, self.e
+        up, low = self.sums(0)
+        for s in (1, 2, 3):
+            wire.landed(16 + s, self.zb.at[s - 1, 0:e], p.along(4 - s))
+            wire.landed(28 + s, self.zb.at[s - 1, e : 2 * e], p.along(4 - s))
+            up = up + self.zb[s - 1, 0:e].astype(F32)
+            low = low + self.zb[s - 1, e : 2 * e].astype(F32)
+        self.f[0, 0:e] = up.astype(BF16)
+        self.f[0, e : 2 * e] = low.astype(BF16)
+        wire.start(20, self.f.at[0], self.f.at[2], p.by_x)
+        wire.start(21, self.f.at[0], self.f.at[4], p.by_y)
+        wire.start(22, self.f.at[0], self.f.at[1], p.core)
 
     def four(self):
         p, wire, e = self.place, self.wire, self.e
@@ -665,18 +671,30 @@
     def six(self):
         for slot, to in ((22, 1), (25, 3), (26, 5), (27, 7)):
             self.wire.landed(slot, self.f.at[to], self.place.core)
-        self.wire.drain()
-
-    def steps(self):
-        out = [functools.partial(self.one, d) for d in (1, 2, 3, 0)]
-        lagged = [(self.two, d) for d in (1, 2, 3, 0)]
-        last = [(self.three, d) for d in (1, 2, 3, 0)]
-        for i in range(6):
-            if i < 4:
-                out.append(functools.partial(*lagged[i]))
-            if i >= 1 and i - 1 < 4:
-                out.append(functools.partial(*last[i - 1]))
-        return out + [self.four, self.five, self.six]
+        e, sent = self.e, self.wire.sent
+        for d in range(4):
+            sent(d, self.ra1.at[d])
+            sent(4 + d, self.rb1.at[d])
+            sent(8 + d, self.ra2.at[d])
+            sent(12 + d, self.rb2.at[d])
+        for d in range(1, 4):
+            sent(16 + d, self.zb.at[d - 1, 0:e])
+            sent(28 + d, self.zb.at[d - 1, 0:e])
+        for slot in (20, 21, 22, 25, 26, 27):
+            sent(slot, self.f.at[0])
+        for slot in (23, 24):
+            sent(slot, self.f.at[0, 0:e])
+
+    def sweep(self):
+        return [
+            functools.partial(f, d)
+            for f, d in (
+                (self.two, 1), (self.two, 2), (self.three, 1), (self.two, 3), (self.three, 2), (self.two, 0), (self.three, 3)
+            )
+        ]
+
+    def tail(self):
+        return [self.last, self.four, self.five, self.six]
 
 
 def reduce_call(grads, cid):
@@ -689,27 +707,224 @@
         ins, outs, scr = refs[:count], refs[count : 2 * count], refs[2 * count :]
         place = Place()
         place.meet()
-        todo = [Reduce(place, ins[i], outs[i], scr[each * i : each * (i + 1)]).steps() for i in range(count)]
-        for steps in todo:
-            for s in steps[:4]:
-                s()
-        tails = [steps[4:] for steps in todo]
-        if count == 1:
-            order = tails[0]
-        else:
-            a, b = tails
-            order = a[:-4] + b[:-4] + [a[-4], a[-3], b[-4], a[-2], b[-3], a[-1], b[-2], b[-1]]
-        for s in order:
-            s()
+        work = scr[each * count :]
+        for i in range(count):
+            work[i][...] = ins[i][...]
+        todo = [Reduce(place, work[i], outs[i], scr[each * i : each * (i + 1)]) for i in range(count)]
+        for r in todo:
+            for d in (1, 2, 3, 0):
+                r.one(d)
+        for r in todo:
+            for f in r.sweep() + r.tail():
+                f()
 
     return pl.pallas_call(
         body,
         in_specs=[pl.BlockSpec(memory_space=pltpu.VMEM)] * count,
         out_specs=[pl.BlockSpec(memory_space=pltpu.VMEM)] * count,
         out_shape=[jax.ShapeDtypeStruct((8, dm // 4, w), BF16) for _ in grads],
-        scratch_shapes=Reduce.scratch(dm, w) * count,
+        scratch_shapes=Reduce.scratch(dm, w) * count + [pltpu.VMEM((dm, cols), BF16)] * count,
         compiler_params=pltpu.CompilerParams(collective_id=cid, has_side_effects=True, vmem_limit_bytes=VMEM),
     )(*grads)
+
+
+def back_call(cot, act, n2, gup, ghb, n1w, q, k, v, attn, gattn, lse, qseg, kseg, own, near):
+    n, rows, cw = q.shape
+    win = k.shape[1]
+    dm = cot.shape[0]
+    hw = act.shape[1] // 2
+    half = n * cw // 2
+    w = hw // 4
+    pairs = cw // PAIR
+    scale = HEAD_DIM**-0.5
+    each = len(Reduce.scratch(dm, w))
+
+    def body(
+        cot_ref, act_ref, n2_ref, gup_ref, ghb_ref, n1_ref, q_ref, k_ref, v_ref, a_ref, g_ref, l_ref, qs_ref, ks_ref,
+        fd, fu, gp_ref, dq, dk, dv,
+        cot2, act2, n22, gup2, ghb2, n12, gd, gu, dq_o, dk_o, dv_o, at2, dkt, dvt, xs, xr, ls, *scr,
+    ):
+        place = Place()
+        core = place.k
+        big_z = place.z < near
+        wire = Wire(xs, xr, place.core)
+        whole = (
+            (cot_ref, cot2, rows), (n2_ref, n22, rows), (ghb_ref, ghb2, rows), (n1_ref, n12, win)
+        )
+        mixed = ((act_ref, act2), (gup_ref, gup2))
+        local = [pltpu.make_async_copy(src, dst.at[:, 0:wide], ls.at[i]) for i, (src, dst, wide) in enumerate(whole)]
+        local += [pltpu.make_async_copy(src.at[:, 0:hw], dst.at[0:rows], ls.at[4 + i]) for i, (src, dst) in enumerate(mixed)]
+        for i in (0, 4, 1, 5, 2, 3):
+            local[i].start()
+        place.meet()
+
+        def give_whole(i):
+            src, dst, wide = whole[i]
+            wire.start(i, src, dst.at[:, wide : 2 * wide], place.core)
+
+        def give_mixed(i):
+            src, dst = mixed[i]
+            wire.start(4 + i, src.at[:, hw : 2 * hw], dst.at[rows : 2 * rows], place.core)
+
+        def take(*which):
+            for i in which:
+                local[i].wait()
+                if i < 4:
+                    dst, wide = whole[i][1:]
+                    wire.landed(i, dst.at[:, wide : 2 * wide], place.core)
+                else:
+                    wire.landed(i, mixed[i - 4][1].at[rows : 2 * rows], place.core)
+
+        give_whole(0)
+        give_mixed(0)
+        give_whole(1)
+        give_mixed(1)
+        give_whole(2)
+        give_whole(3)
+        for d in range(n):
+            to = slice(d * PAIR, (d + 1) * PAIR)
+            theirs = pl.ds(pl.multiple_of((1 - core) * PAIR, PAIR), PAIR)
+            mine = pl.ds(pl.multiple_of(core * PAIR, PAIR), PAIR)
+            wire.start(6 + d, a_ref.at[d, :, theirs], at2.at[rows : 2 * rows, to], place.core)
+            at2[0:rows, to] = a_ref[d, :, mine]
+
+        down = Reduce(place, gd, fd, scr[:each])
+        up = Reduce(place, gu, fu, scr[each : 2 * each])
+
+        def make(red, grad, left, right):
+            def step(i, carry):
+                d = lax.rem(i + 1, 4)
+                c = pl.ds(pl.multiple_of(d * w, w), w)
+                grad[:, c] = dot_nn(left[...], right[:, c]).astype(BF16)
+                red.one(d)
+                return carry
+
+            lax.fori_loop(0, 4, step, 0)
+
+        take(0, 4)
+        make(down, gd, cot2, act2)
+        take(1, 5)
+        make(up, gu, n22, gup2)
+
+        def work(big, d, p):
+            at = pl.ds(pl.multiple_of(p * PAIR, PAIR), PAIR)
+            to = pl.ds(pl.multiple_of(d * PAIR, PAIR), PAIR)
+            rel = lax.rem(p + core, 2)
+            if not big:
+                dkt[...] = jnp.zeros_like(dkt)
+                dvt[...] = jnp.zeros_like(dvt)
+            for i, (qs, qn, ks, kn) in enumerate(blocks_of(rows, own, win, big)):
+                mask = qs_ref[qs : qs + qn, :] == ks_ref[:, ks : ks + kn]
+                qq, kk, vv = q_ref[d, qs : qs + qn, at], k_ref[d, ks : ks + kn, at], v_ref[d, ks : ks + kn, at]
+                gg = g_ref[d, qs : qs + qn, at]
+                prod = gg.astype(F32) * a_ref[d, qs : qs + qn, at].astype(F32)
+                dqs = []
+                for h in range(2):
+                    lanes = slice(h * HEAD_DIM, (h + 1) * HEAD_DIM)
+                    qh, kh, gh = qq[:, lanes] * BF16(scale), kk[:, lanes], gg[:, lanes]
+                    s = jnp.where(mask, dot_nt(qh, kh) - l_ref[d * pairs + p, qs : qs + qn, h : h + 1], NEG)
+                    pr = jnp.exp(s)
+                    dp = dot_nt(gh, vv[:, lanes])
+                    delta = jnp.sum(prod[:, lanes], axis=1, keepdims=True)
+                    ds = (pr * (dp - delta)).astype(BF16)
+                    dqs.append(dot_nn(ds, kh) * scale)
+                    gk = dot_tn(qh, ds)
+                    gv = dot_tn(gh, pr.astype(BF16))
+                    if big and i == 0:
+                        dkt[lanes, :] = gk
+                        dvt[lanes, :] = gv
+                    else:
+                        dkt[lanes, ks : ks + kn] += gk
+                        dvt[lanes, ks : ks + kn] += gv
+                dq[rel, qs : qs + qn, to] = jnp.concatenate(dqs, axis=1).astype(BF16)
+            dk[rel, :, to] = dkt[...].T.astype(BF16)
+            dv[rel, :, to] = dvt[...].T.astype(BF16)
+
+        todo = down.sweep() + up.sweep()
+        turns = [todo[2 * i : 2 * i + 2] for i in range(n * pairs)]
+        turns[-1] = todo[2 * (n * pairs - 1) :]
+
+        def head_pair(i, carry):
+            d, p = i // pairs, lax.rem(i, pairs)
+
+            @pl.when(big_z)
+            def _():
+                work(True, d, p)
+
+            @pl.when(jnp.logical_not(big_z))
+            def _():
+                work(False, d, p)
+
+            for t, steps in enumerate(turns):
+                if steps:
+
+                    @pl.when(i == t)
+                    def _():
+                        for f in steps:
+                            f()
+
+            return carry
+
+        lax.fori_loop(0, n * pairs, head_pair, 0)
+        halves = ((dq, dq_o), (dk, dk_o), (dv, dv_o))
+        for i, (src, dst) in enumerate(halves):
+            wire.start(10 + i, src.at[1], dst, place.core)
+        down.last()
+        take(2, 3)
+        for d in range(n):
+            wire.landed(6 + d, at2.at[rows : 2 * rows, d * PAIR : (d + 1) * PAIR], place.core)
+
+        def put(m, val):
+            for d in range(n):
+                at = d * w + m * PAIR
+                act2[:, at : at + PAIR] = val[:, d * PAIR : (d + 1) * PAIR].astype(BF16)
+
+        put(3, dot_nn(ghb2[...], at2[...]))
+        up.last()
+        down.four()
+        wire.landed(10, dq_o, place.core)
+        put(0, dot_nn(n12[:, own : own + rows], dq[0]) + dot_nn(n12[:, win + own : win + own + rows], dq_o[...]))
+        down.five()
+        up.four()
+        wire.landed(11, dk_o, place.core)
+        put(1, dot_nn(n12[:, 0:win], dk[0]) + dot_nn(n12[:, win : 2 * win], dk_o[...]))
+        up.five()
+        wire.landed(12, dv_o, place.core)
+        put(2, dot_nn(n12[:, 0:win], dv[0]) + dot_nn(n12[:, win : 2 * win], dv_o[...]))
+        out = pltpu.make_async_copy(act2, gp_ref, ls.at[6])
+        out.start()
+        down.six()
+        up.six()
+        for i in range(4):
+            wire.sent(i, whole[i][0])
+        for i in range(2):
+            wire.sent(4 + i, act2.at[0:rows])
+        for d in range(n):
+            wire.sent(6 + d, at2.at[0:rows, 0:PAIR])
+        for i in range(3):
+            wire.sent(10 + i, halves[i][1])
+        out.wait()
+
+    hbm = pl.BlockSpec(memory_space=pl.ANY)
+    vmem = pl.BlockSpec(memory_space=pltpu.VMEM)
+    shaped = lambda *shape: jax.ShapeDtypeStruct(shape, BF16)
+    buf = lambda *shape: pltpu.VMEM(shape, BF16)
+    return pl.pallas_call(
+        body,
+        in_specs=[hbm] * 6 + [vmem] * 8,
+        out_specs=[vmem, vmem, hbm, vmem, vmem, vmem],
+        out_shape=[
+            shaped(8, dm // 4, w), shaped(8, dm // 4, w), shaped(dm, hw), shaped(2, rows, half), shaped(2, win, half), shaped(2, win, half)
+        ],
+        scratch_shapes=[
+            buf(dm, 2 * rows), buf(2 * rows, hw), buf(dm, 2 * rows), buf(2 * rows, hw), buf(dm, 2 * rows), buf(dm, 2 * win),
+            buf(dm, hw), buf(dm, hw), buf(rows, half), buf(win, half), buf(win, half), buf(2 * rows, half),
+            pltpu.VMEM((PAIR, win), F32), pltpu.VMEM((PAIR, win), F32),
+            pltpu.SemaphoreType.DMA((13,)), pltpu.SemaphoreType.DMA((13,)), pltpu.SemaphoreType.DMA((7,)),
+        ]
+        + Reduce.scratch(dm, w) * 2,
+        compiler_params=pltpu.CompilerParams(collective_id=1, has_side_effects=True, vmem_limit_bytes=VMEM_ALL),
+    )(cot, act, n2, gup, ghb, n1w, q, k, v, attn, gattn, lse, qseg, kseg)
 
 
 def place_grads(coords, done, mode):
@@ -798,7 +1013,7 @@
     ffw = w_up.shape[1]
     mp = lax.axis_size("mp")
     dp = lax.axis_size("dp")
-    fast = mp == 4 and dp == 8 and rows % 128 == 0
+    fast = mp == 4 and dp == 8 and rows % 256 == 0 and cw == 2 * PAIR
     z = lax.axis_index("mp")
     me = lax.axis_index("dp")
     core = lax.rem(me, 2)
@@ -861,19 +1076,7 @@
         info[1:], n2, hidden, cotangent, up_all, down_all, bu_all, b_down, 2
     )
 
-    other = lambda v: lax.ppermute(v, "dp", [(i, i - i % 2 + (i + 1) % 2) for i in range(dp)])
-    hw = mp * ffw // 2
-    cot_o = other(cotangent)
-    act_o = other(active[:, hw:])
-    n2_o = other(n2)
-    gup_o = other(g_upper[:, hw:])
     gout = f32(cotangent)
-
-    def pair_grad(left, right, left_o, right_o):
-        return (dot_tn(left, right) + dot_tn(left_o, right_o)).astype(BF16)
-
-    gd = pair_grad(cotangent, active[:, :hw], cot_o, act_o)
-    gu = pair_grad(n2, g_upper[:, :hw], n2_o, gup_o)
     hat2, inv2 = norm_rows(hidden)
 
     def norm_back(g, hat, inv, gain):
@@ -887,7 +1090,12 @@
     ghb = g_hidden.astype(BF16)
 
     g_attn = jnp.stack([dot_nn(ghb, packed[d, :, 3 * cw :]).astype(BF16) for d in range(mp)])
-    dq, dk, dv = attn_bwd_call(info, q, k, v, attn, g_attn, lse, qseg, kseg, own)
+    if fast:
+        done_d, done_u, gp, dq, dk, dv = back_call(
+            cotangent.T, active, n2.T, g_upper, ghb.T, n1w.T, q, k, v, attn, g_attn, lse, qseg, kseg, own, near
+        )
+    else:
+        dq, dk, dv = attn_bwd_call(info, q, k, v, attn, g_attn, lse, qseg, kseg, own)
     halves = dq.shape[0]
     g_own, g_far, g_next = norm1_back_call(dq, dk, dv, packed, info, own)
     back = g_own
@@ -904,28 +1112,20 @@
 
     n1 = n1w[own : own + rows]
     if fast:
-        n1w_o = other(n1w)
-        ghb_o = other(ghb)
-        attn_h = attn.reshape(mp, rows, 2, cw // 2).transpose(2, 1, 0, 3).reshape(2, rows, mp * cw // 2)
-        attn_m = lax.dynamic_index_in_dim(attn_h, core, 0, keepdims=False)
-        attn_t = lax.dynamic_index_in_dim(attn_h, 1 - core, 0, keepdims=False)
-        dq_o, dk_o, dv_o, at_o = other(dq[1]), other(dk[1]), other(dv[1]), other(attn_t)
-        n1_o = n1w_o[own : own + rows]
-        half = cw // 2
-        gs = [
-            pair_grad(n1, dq[0], n1_o, dq_o),
-            pair_grad(n1w, dk[0], n1w_o, dk_o),
-            pair_grad(n1w, dv[0], n1w_o, dv_o),
-            pair_grad(ghb, attn_m, ghb_o, at_o),
-        ]
-        gp = jnp.concatenate([g[:, d * half : (d + 1) * half] for d in range(mp) for g in gs], axis=1)
         coords = jnp.stack([y, x, core]).astype(jnp.int32)
-        done_d, done_u = reduce_call([gd, gu], 1)
         (done_p,) = reduce_call([gp], 2)
         (g_w_down,) = place_grads(coords, done_d, "down")
         (g_w_up,) = place_grads(coords, done_u, "up")
         g_w_query, g_w_key, g_w_value, g_w_out = place_grads(coords, done_p, "pack")
     else:
+        other = lambda v: lax.ppermute(v, "dp", [(i, i - i % 2 + (i + 1) % 2) for i in range(dp)])
+        hw = mp * ffw // 2
+
+        def pair_grad(left, right):
+            return (dot_tn(left, right[:, :hw]) + dot_tn(other(left), other(right[:, hw:]))).astype(BF16)
+
+        gd = pair_grad(cotangent, active)
+        gu = pair_grad(n2, g_upper)
         g_w_up = reduce_any(gu.reshape(dm, mp, ffw // 2), z, core)
         g_w_down = reduce_any(gd.reshape(dm, mp, ffw // 2), z, core).T
 

time: 631 us -> 561 us (0.89)
  matrix products: 60.6 us -> 8.94 us
  starting transfers between devices: 31.5 us -> 21 us
  local copies, waits for them, and re-layouts: 38.3 us -> 30.7 us
  waiting for transfers between devices: 7.52 us -> 0.02 us
    pallas_call x2 -> x1, Pallas kernels: 184 us -> 65 us  [reduce_call(): pl.pallas_call(body, in_specs=[pl.BlockSpec(memory_space=pltpu.VMEM)] * c...]
    pallas_call x1, Pallas kernels: 30.4 us -> 145 us  [back_call(): pl.pallas_call(body, in_specs=[hbm] * 6 + [vmem] * 8, out_specs=[vmem, vm...]
    dot_general x12 -> x0, matrix products: 54.6 us -> none  [dot_tn(): lax.dot_general(a, b, (((0,), (0,)), ((), ())), preferred_element_type=F32)]
    unnamed x86 -> x68, local copies, waits for them, and re-layouts: 16.1 us -> 7.08 us
    ppermute x1, starting transfers between devices: 15.5 us -> 8.02 us  [local(): lax.ppermute(part, 'mp', [(i, (i + j) % near) for i in range(near)])]
  transfers between devices with their start and end apart: 19 -> 9, of which waited for: 2 -> 0; matrix products, arithmetic and copies ran while one was open for 17% -> 5% of each run, Pallas kernels for 55% -> 33%
where the time goes in v3:
time: 561 us; the launch traced here: 550 us
  Pallas kernels  413 us (74%)
  blocking collectives  42.5 us (8%)
  other arithmetic  32.5 us (6%)
  local copies, waits for them, and re-layouts  30.7 us (5%)
  starting transfers between devices  21 us (4%)
  matrix products  8.94 us (2%)
    pallas_call x1, Pallas kernels, back_call(): pl.pallas_call(body, in_specs=[hbm] * 6 + [vmem] * 8, out_specs=[vmem, vm...  145 us
    pallas_call x1, Pallas kernels, gather_call(): pl.pallas_call(body, in_specs=[pl.BlockSpec(memory_space=pltpu.VMEM)] * c...  104 us
    pallas_call x1, Pallas kernels, reduce_call(): pl.pallas_call(body, in_specs=[pl.BlockSpec(memory_space=pltpu.VMEM)] * c...  65 us
    psum x1, blocking collectives, local(): vec = lax.psum(vec, ('dp', 'mp'))  42.5 us
    pallas_call x1, Pallas kernels, ffn_call(): pl.pallas_call(body, grid_spec=pltpu.PrefetchScalarGridSpec(num_scalar_pr...  29.1 us
    pallas_call x1, Pallas kernels, attn_fwd_call(): pl.pallas_call(body, grid_spec=pltpu.PrefetchScalarGridSpec(num_scalar_pr...  25.2 us
    pallas_call x1, Pallas kernels, norm1_back_call(): pl.pallas_call(body, grid_spec=pltpu.PrefetchScalarGridSpec(num_scalar_pr...  14.5 us
    pallas_call x3, Pallas kernels, place_grads(): pl.pallas_call(body, in_specs=[pl.BlockSpec(memory_space=pltpu.SMEM), pl....  12.3 us
  transfers between devices with their start and end apart: 9, of which 0 were waited for; matrix products, arithmetic and copies ran while one was open for 5% of the time, Pallas kernels for 33%

profile of v3, /device:TPU:0, one launch (start us, length us, event | category | flops | bytes accessed | tf_op | source)
XLA Modules:
  0.0 549.7 jit_solution(8779364772387858824)
XLA Ops:
  0.7 1.5 dynamic-update-slice.9
  2.2 1.4 dynamic-update-slice.10
  3.6 1.4 dynamic-update-slice.11
  5.0 3.1 collective-permute-start.5
  8.1 2.6 collective-permute-start.4
  10.7 1.3 collective-permute-start.3
  12.0 2.6 collective-permute-start
  14.6 1.0 fusion.27
  15.6 0.7 collective-permute-start.1
  16.3 0.7 stack.56
  17.0 1.3 broadcast_in_dim.56.g_ref
  18.3 0.7 convert_element_type.54
  18.9 1.2 copy.51
  21.4 0.8 dynamic-slice_select_fusion
  22.3 2.9 pad_maximum_fusion.refs_0_
  25.2 0.8 broadcast_select_fusion
  26.1 0.7 convert_element_type.52
  26.7 0.7 convert_element_type.51
  27.4 0.8 copy.54.refs_3_.qs_ref
  28.3 0.8 concatenate.28
  29.6 1.3 broadcast_in_dim.55.bo_ref
  30.9 1.3 broadcast_in_dim.57.b_ref
  32.2 1.3 broadcast_in_dim.58.bd_ref
  33.5 1.3 copy.56
  34.8 103.9 %shard_map.305 = (bf16[4,1024,1024]{2,1,0:T(8,128)(2,1)}, bf16[4,1024,1024]{2,1,0:T(8,128)(2,1)}, bf16[4,1024,1024]{2,1,0:T(8,128)(2,1)}) custom-call(bf16[1024,1024]{1,0:T(8,128)(2,1)} %pad_maximum_fusion.refs_0_, bf16[1024,1024]{1,0:T(8,128)(2,1)} %refs_1_.1, bf16[1024,1024]{1,0:T(8,128)(2,1)} %refs_2_.1), custom_call_target="tpu_custom_call" | custom-call | tf_op jit(solution)/shard_map/pallas_call | solution.py:553
  138.7 0.8 collective-permute-start.2
  139.6 0.7 stack.59
  140.2 0.7 stack.58
  140.9 0.7 stack.57
  144.1 0.8 fusion.2
  144.9 3.7 fusion
  148.6 10.2 %shard_map.306 = (bf16[4,512,256]{2,1,0:T(8,128)(2,1)}, bf16[4,1152,256]{2,1,0:T(8,128)(2,1)}, bf16[4,1152,256]{2,1,0:T(8,128)(2,1)}) custom-call(bf16[1152,1024]{1,0:T(8,128)(2,1)} %get-tuple-element.88.x_ref, bf16[4,1024,1024]{2,1,0:T(8,128)(2,1)} %get-tuple-element.46.w_ref, bf16[4,1,256]{2,1,0:T(2,128)(2,1)} %copy.52.bq_ref, bf16[4,1,256]{2,1,0:T(2,128)(2,1)} %copy.53.bv_ref), custom_call_target="tpu_custom_call" | custom-call | flops 5905580032 | bytes 10747904 | tf_op jit(solution)/shard_map/pallas_call | solution.py:59
  158.8 25.2 %shard_map.307 = (bf16[4,512,256]{2,1,0:T(8,128)(2,1)}, f32[8,512,2]{2,1,0:T(8,128)}) custom-call(s32[2]{0:T(128)} %pad_add_fusion.big_ref.info_ref, bf16[4,512,256]{2,1,0:T(8,128)(2,1)} %get-tuple-element.47.refs_0_.q_ref, bf16[4,1152,256]{2,1,0:T(8,128)(2,1)} %get-tuple-element.48.refs_1_.k_ref, bf16[4,1152,256]{2,1,0:T(8,128)(2,1)} %get-tuple-element.49.refs_2_.v_ref, ...), custom_call_target="tpu_custom_call" | custom-call | flops 9663676416 | bytes 6815744 | tf_op jit(solution)/shard_map/pallas_call | solution.py:120
  184.0 7.1 %shard_map.308 = (f32[512,1024]{1,0:T(8,128)}, bf16[512,1024]{1,0:T(8,128)(2,1)}) custom-call(bf16[4,512,256]{2,1,0:T(8,128)(2,1)} %get-tuple-element.50.a_ref, bf16[4,1024,1024]{2,1,0:T(8,128)(2,1)} %get-tuple-element.46.w_ref, bf16[512,1024]{1,0:T(8,128)(2,1)} %x_ref.1, bf16[1,1024]{1,0:T(2,128)(2,1)} %broadcast_in_dim.55.bo_ref, ...), custom_call_target="tpu_custom_call" | custom-call | flops 1073741824 | bytes 2097152 | tf_op jit(solution)/shard_map/pallas_call | solution.py:264
  191.1 1.9 reduce_sum.162
  193.6 1.3 copy.57
  195.0 29.1 %shard_map.309 = (bf16[512,1024]{1,0:T(8,128)(2,1)}, f32[512,1024]{1,0:T(8,128)}, bf16[512,4096]{1,0:T(8,128)(2,1)}, bf16[512,4096]{1,0:T(8,128)(2,1)}, f32[1,4096]{1,0:T(1,128)}) custom-call(s32[1]{0:T(128)} %bitcast.core_ref, bf16[512,1024]{1,0:T(8,128)(2,1)} %get-tuple-element.51.x_ref, f32[512,1024]{1,0:T(8,128)} %get-tuple-element.52.h_ref, ...), custom_call_target="tpu_custom_call" | custom-call | flops 17179869184 | bytes 16777216 | tf_op jit(solution)/shard_map/pallas_call | solution.py:320
  224.1 3.2 multiply_reduce_fusion
  227.3 1.5 fusion.24
  229.2 1.0 copy-done.2
  230.2 2.2 fusion.6
  232.4 2.2 fusion.5
  234.6 2.2 fusion.4
  236.8 2.4 fusion.3
  239.2 1.3 copy.58.ghb_ref
  240.5 2.6 copy.59.n1_ref
  243.1 1.2 pad_maximum_fusion.2.g_ref
  244.3 145.3 %shard_map.310 = (bf16[8,256,512]{2,1,0:T(8,128)(2,1)}, bf16[8,256,512]{2,1,0:T(8,128)(2,1)}, bf16[1024,2048]{1,0:T(8,128)(2,1)}, bf16[2,512,512]{2,1,0:T(8,128)...) custom-call(bf16[1024,512]{1,0:T(8,128)(2,1)} %bitcast.65, ...), custom_call_target="tpu_custom_call" | custom-call | tf_op jit(solution)/shard_map/pallas_call | solution.py:912
  389.6 14.5 %shard_map.311 = (f32[512,1024]{1,0:T(8,128)}, bf16[512,1024]{1,0:T(8,128)(2,1)}, bf16[64,1024]{1,0:T(8,128)(2,1)}) custom-call(s32[2]{0:T(128)} %pad_add_fusion.big_ref.info_ref, bf16[2,512,512]{2,1,0:T(8,128)(2,1)} %get-tuple-element.60.dq_ref, bf16[2,1152,512]{2,1,0:T(8,128)(2,1)} %get-tuple-element.61.dk_ref, ...), custom_call_target="tpu_custom_call" | custom-call | flops 5905580032 | bytes 12058624 | tf_op jit(solution)/shard_map/pallas_call | solution.py:395
  404.0 8.0 %collective-permute-start.6 = (bf16[512,1024]{1,0:T(8,128)(2,1)}, bf16[512,1024]{1,0:T(8,128)(2,1)S(1)}, u32[]{:S(2)}, u32[]{:S(2)}) collective-permute-start(bf16[512,1024]{1,0:T(8,128)(2,1)} %get-tuple-element.64), channel_id=1, source_target_pairs={{0,1},{1,0},{4,5},{5,4},{8,9},{9,8},{12,13},{13,12},{16,17},{17,16... | collective-permute-start | bytes 3145736 | tf_op jit(solution)/shard_map/ppermute | solution.py:1104
  412.1 1.4 convert_reduce_fusion.3
  413.5 1.6 slice.93
  415.0 0.7 slice.103
  415.7 0.7 collective-permute-start.7
  416.4 1.3 collective-permute-start.8
  418.7 1.4 reduce.6
  420.1 65.0 %shard_map.312.f_ref = bf16[8,256,512]{2,1,0:T(8,128)(2,1)} custom-call(bf16[1024,2048]{1,0:T(8,128)(2,1)} %get-tuple-element.67.refs_0_), custom_call_target="tpu_custom_call" | custom-call | tf_op jit(solution)/shard_map/pallas_call | solution.py:721
  485.2 3.9 shard_map.313
  489.1 3.9 shard_map.314
  493.0 4.5 shard_map.315
  498.1 1.2 fusion.25
  499.3 2.4 multiply_reduce_fusion.1
  501.9 42.5 %psum.7 = f32[12288]{0:T(1024)S(1)} all-reduce(f32[12288]{0:T(1024)S(1)} %bitcast_dynamic-update-slice_fusion), channel_id=1, replica_groups=mesh['dp'=8,'mp'=4] {'dp','mp'}, use_global_device_ids=true, to_apply=%region_18.20 | all-reduce | flops 12288 | bytes 98304 | tf_op jit(solution)/shard_map/psum | solution.py:1161
  545.7 3.9 multiply_add_fusion
  (112 shorter events, 8.2 us)
Async XLA Ops:
  0.7 21.6 %copy-start.13 = (bf16[1024,256]{1,0:T(8,128)(2,1)S(1)}, bf16[1024,256]{1,0:T(8,128)(2,1)}, u32[]{:S(2)}) copy-start(bf16[1024,256]{1,0:T(8,128)(2,1)} %param.27) | copy-start | bytes 1572868
  5.0 133.7 %collective-permute-start.5 = (bf16[1536]{0:T(1024)(128)(2,1)}, bf16[1536]{0:T(1024)(128)(2,1)}, u32[]{:S(2)}, u32[]{:S(2)}) collective-permute-start(bf16[1536]{0:T(1024)(128)(2,1)} %dynamic-update-slice.11), channel_id=1, source_target_pairs={{3,0},{0,1},{1,2},{2,3},{7,4},{4,5},{5,6},{6,7},{11,8},{8,9},{9,10... | collective-permute-start | bytes 9224 | tf_op jit(solution)/shard_map/ppermute | solution.py:1035
  8.1 132.2 %collective-permute-start.4 = (bf16[1536]{0:T(1024)(128)(2,1)}, bf16[1536]{0:T(1024)(128)(2,1)}, u32[]{:S(2)}, u32[]{:S(2)}) collective-permute-start(bf16[1536]{0:T(1024)(128)(2,1)} %dynamic-update-slice.11), channel_id=1, source_target_pairs={{2,0},{3,1},{0,2},{1,3},{6,4},{7,5},{4,6},{5,7},{10,8},{11,9},{8,1... | collective-permute-start | bytes 9224 | tf_op jit(solution)/shard_map/ppermute | solution.py:1035
  10.7 130.3 %collective-permute-start.3 = (bf16[1536]{0:T(1024)(128)(2,1)}, bf16[1536]{0:T(1024)(128)(2,1)}, u32[]{:S(2)}, u32[]{:S(2)}) collective-permute-start(bf16[1536]{0:T(1024)(128)(2,1)} %dynamic-update-slice.11), channel_id=1, source_target_pairs={{1,0},{2,1},{3,2},{0,3},{5,4},{6,5},{7,6},{4,7},{9,8},{10,9},{11,1... | collective-permute-start | bytes 9224 | tf_op jit(solution)/shard_map/ppermute | solution.py:1035
  12.0 131.5 %collective-permute-start = (bf16[512,1024]{1,0:T(8,128)(2,1)}, bf16[512,1024]{1,0:T(8,128)(2,1)S(1)}, u32[]{:S(2)}, u32[]{:S(2)}) collective-permute-start(bf16[512,1024]{1,0:T(8,128)(2,1)} %x_ref.1), channel_id=1, source_target_pairs={{1,0},{0,1},{5,4},{4,5},{9,8},{8,9},{13,12},{12,13},{17,16},{16,17... | collective-permute-start | bytes 3145736 | tf_op jit(solution)/shard_map/ppermute | solution.py:1028
  15.6 128.0 %collective-permute-start.1 = (bf16[64,1024]{1,0:T(8,128)(2,1)S(1)}, bf16[64,1024]{1,0:T(8,128)(2,1)S(1)}, u32[]{:S(2)}, u32[]{:S(2)}) collective-permute-start(bf16[64,1024]{1,0:T(8,128)(2,1)S(1)} %get-tuple-element.95), channel_id=1, source_target_pairs={{1,2},{2,3},{5,6},{6,7},{9,10},{10,11},{13,14},{14,15},{17,18},{18... | collective-permute-start | bytes 393224 | tf_op jit(solution)/shard_map/ppermute | solution.py:1030
  22.3 2.9 copy-start.25
  22.3 11.2 %copy-start.8 = (bf16[512,1024]{1,0:T(8,128)(2,1)S(1)}, bf16[512,1024]{1,0:T(8,128)(2,1)}, u32[]{:S(2)}) copy-start(bf16[512,1024]{1,0:T(8,128)(2,1)} %c_ref.1) | copy-start | bytes 3145732
  27.4 117.5 %copy-start.18 = (f32[1024]{0:T(1024)}, f32[1024]{0:T(1024)S(1)}, u32[]{:S(2)}) copy-start(f32[1024]{0:T(1024)S(1)} %convert_element_type.51) | copy-start | bytes 12292
  138.7 4.9 copy-start.7
  138.7 5.0 collective-permute-start.2
  144.9 3.7 copy-start.20
  191.1 2.2 copy-start
  191.1 2.6 copy-start.12
  195.0 29.1 %copy-start.1 = (f32[512,1024]{1,0:T(8,128)S(1)}, f32[512,1024]{1,0:T(8,128)}, u32[]{:S(2)}) copy-start(f32[512,1024]{1,0:T(8,128)} %get-tuple-element.52.h_ref) | copy-start | bytes 6291460
  224.1 3.2 copy-start.6
  224.1 3.2 copy-start.9
  228.9 1.3 copy-start.2
  236.8 3.7 copy-start.5
  240.5 2.6 copy-start.14
  240.5 2.6 copy-start.15
  240.5 2.6 copy-start.16
  240.5 2.6 copy-start.17
  389.5 28.2 %copy-start.10 = (bf16[2,1152,512]{2,1,0:T(8,128)(2,1)S(1)}, bf16[2,1152,512]{2,1,0:T(8,128)(2,1)}, u32[]{:S(2)}) copy-start(bf16[2,1152,512]{2,1,0:T(8,128)(2,1)} %get-tuple-element.62.dv_ref) | copy-start | bytes 7077892
  404.0 93.5 %collective-permute-start.6 = (bf16[512,1024]{1,0:T(8,128)(2,1)}, bf16[512,1024]{1,0:T(8,128)(2,1)S(1)}, u32[]{:S(2)}, u32[]{:S(2)}) collective-permute-start(bf16[512,1024]{1,0:T(8,128)(2,1)} %get-tuple-element.64), channel_id=1, source_target_pairs={{0,1},{1,0},{4,5},{5,4},{8,9},{9,8},{12,13},{13,12},{16,17},{17,16... | collective-permute-start | bytes 3145736 | tf_op jit(solution)/shard_map/ppermute | solution.py:1104
  415.7 82.3 %collective-permute-start.7 = (bf16[64,1024]{1,0:T(8,128)(2,1)}, bf16[64,1024]{1,0:T(8,128)(2,1)S(1)}, u32[]{:S(2)}, u32[]{:S(2)}) collective-permute-start(bf16[64,1024]{1,0:T(8,128)(2,1)} %get-tuple-element.65), channel_id=1, source_target_pairs={{1,2},{2,3},{5,6},{6,7},{9,10},{10,11},{13,14},{14,15},{17,18},{18... | collective-permute-start | bytes 393224 | tf_op jit(solution)/shard_map/ppermute | solution.py:1106
  416.4 81.7 %collective-permute-start.8 = (bf16[64,1024]{1,0:T(8,128)(2,1)}, bf16[64,1024]{1,0:T(8,128)(2,1)}, u32[]{:S(2)}, u32[]{:S(2)}) collective-permute-start(bf16[64,1024]{1,0:T(8,128)(2,1)} %slice.93), channel_id=1, source_target_pairs={{2,1},{3,2},{6,5},{7,6},{10,9},{11,10},{14,13},{15,14},{18,17},{19... | collective-permute-start | bytes 393224 | tf_op jit(solution)/shard_map/ppermute | solution.py:1105
  493.0 4.5 copy-start.11
  497.8 1.4 copy-start.19
  498.1 3.7 copy-start.4
  499.3 2.5 copy-start.24
  499.3 2.5 copy-start.22
  499.3 2.5 copy-start.21
  499.3 2.5 copy-start.23
  499.3 46.4 %copy-start.3 = (f32[512,1024]{1,0:T(8,128)S(1)}, f32[512,1024]{1,0:T(8,128)}, u32[]{:S(2)}) copy-start(f32[512,1024]{1,0:T(8,128)} %copy-done.2) | copy-start | bytes 6291460

commit v4 on v3

--- a/solution.py
+++ b/solution.py
@@ -697,37 +697,6 @@
         return [self.last, self.four, self.five, self.six]
 
 
-def reduce_call(grads, cid):
-    count = len(grads)
-    dm, cols = grads[0].shape
-    w = cols // 4
-    each = len(Reduce.scratch(dm, w))
-
-    def body(*refs):
-        ins, outs, scr = refs[:count], refs[count : 2 * count], refs[2 * count :]
-        place = Place()
-        place.meet()
-        work = scr[each * count :]
-        for i in range(count):
-            work[i][...] = ins[i][...]
-        todo = [Reduce(place, work[i], outs[i], scr[each * i : each * (i + 1)]) for i in range(count)]
-        for r in todo:
-            for d in (1, 2, 3, 0):
-                r.one(d)
-        for r in todo:
-            for f in r.sweep() + r.tail():
-                f()
-
-    return pl.pallas_call(
-        body,
-        in_specs=[pl.BlockSpec(memory_space=pltpu.VMEM)] * count,
-        out_specs=[pl.BlockSpec(memory_space=pltpu.VMEM)] * count,
-        out_shape=[jax.ShapeDtypeStruct((8, dm // 4, w), BF16) for _ in grads],
-        scratch_shapes=Reduce.scratch(dm, w) * count + [pltpu.VMEM((dm, cols), BF16)] * count,
-        compiler_params=pltpu.CompilerParams(collective_id=cid, has_side_effects=True, vmem_limit_bytes=VMEM),
-    )(*grads)
-
-
 def back_call(cot, act, n2, gup, ghb, n1w, q, k, v, attn, gattn, lse, qseg, kseg, own, near):
     n, rows, cw = q.shape
     win = k.shape[1]
@@ -927,6 +896,181 @@
     )(cot, act, n2, gup, ghb, n1w, q, k, v, attn, gattn, lse, qseg, kseg)
 
 
+def finish_call(gp, dq, dk, dv, packed, tokens, gain, vec, own):
+    n, dm, four = packed.shape
+    cw = four // 4
+    rows = tokens.shape[0]
+    win = dk.shape[1]
+    cols = gp.shape[1]
+    w = cols // 4
+    length = vec.shape[1]
+    each = len(Reduce.scratch(dm, w))
+    strip = 128
+
+    def body(
+        gp_ref, dq_ref, dk_ref, dv_ref, w_ref, x_ref, gain_ref, vec_ref,
+        fp, gi_ref, sum_ref,
+        g, acc, far_out, next_out, far_in, prev_in, next_in, va, vr, vz, xs, xr, ls, *scr,
+    ):
+        place = Place()
+        core, z = place.k, place.z
+        load = pltpu.make_async_copy(gp_ref, g, ls)
+        load.start()
+        place.meet()
+        wire = Wire(xs, xr, place.core)
+        red = Reduce(place, g, fp, scr)
+        load.wait()
+        for d in (1, 2, 3, 0):
+            red.one(d)
+
+        def dots(d, carry):
+            def weight(which, j):
+                at = which * cw + lax.rem(j + core, 2) * PAIR
+                return w_ref[d, :, pl.ds(pl.multiple_of(at, PAIR), PAIR)]
+
+            to = pl.ds(pl.multiple_of(d * PAIR, PAIR), PAIR)
+            left = jnp.concatenate([r[j, :, to] for r in (dk_ref, dv_ref) for j in range(2)], axis=1)
+            right = jnp.concatenate([weight(m, j) for m in (1, 2) for j in range(2)], axis=1)
+            part = dot_nt(left, right)
+            left = jnp.concatenate([dq_ref[j, :, to] for j in range(2)], axis=1)
+            right = jnp.concatenate([weight(0, j) for j in range(2)], axis=1)
+            mine = dot_nt(left, right)
+
+            @pl.when(d == 0)
+            def _():
+                acc[...] = part
+
+            @pl.when(d > 0)
+            def _():
+                acc[...] += part
+
+            acc[own : own + rows, :] += mine
+            for t, f in ((2, red.sweep()[0]), (3, red.sweep()[1])):
+
+                @pl.when(d == t)
+                def _():
+                    f()
+
+            return carry
+
+        lax.fori_loop(0, n, dots, 0)
+
+        long, gives_prev, gives_next = z < 2, z >= 2, jnp.logical_and(z >= 1, z < 3)
+        swap = {"dp": place.me, "mp": lax.rem(z + 1, 2)}
+        left_dev = {"dp": place.me, "mp": lax.rem(z + 3, 4)}
+        right_dev = {"dp": place.me, "mp": lax.rem(z + 1, 4)}
+        far_out[...] = acc[0:own, :].astype(BF16)
+        next_out[...] = acc[own + rows : own + rows + HALO, :].astype(BF16)
+
+        @pl.when(long)
+        def _():
+            wire.start(0, far_out, far_in, swap)
+
+        @pl.when(gives_prev)
+        def _():
+            wire.start(1, far_out.at[own - HALO : own], prev_in, left_dev)
+
+        @pl.when(gives_next)
+        def _():
+            wire.start(2, next_out, next_in, right_dev)
+
+        for f in red.sweep()[2:]:
+            f()
+
+        @pl.when(long)
+        def _():
+            wire.landed(0, far_in, swap)
+            acc[own : own + rows, :] += far_in[...].astype(F32)
+
+        @pl.when(gives_next)
+        def _():
+            wire.landed(1, prev_in, right_dev)
+            acc[own + rows - HALO : own + rows, :] += prev_in[...].astype(F32)
+
+        @pl.when(gives_prev)
+        def _():
+            wire.landed(2, next_in, left_dev)
+            acc[own : own + HALO, :] += next_in[...].astype(F32)
+
+        va[0] = vec_ref[...]
+        va[0, :, 0 : 2 * dm] = jnp.zeros((1, 2 * dm), F32)
+        gains = gain_ref[...].astype(F32)
+
+        def norm(i, carry):
+            at = pl.ds(pl.multiple_of(i * strip, strip), strip)
+            hat, inv = norm_rows(x_ref[at, :].astype(F32))
+            back = acc[pl.ds(pl.multiple_of(own + i * strip, strip), strip), :]
+            gg = back * gains
+            first = jnp.mean(gg, axis=1, keepdims=True)
+            second = jnp.mean(gg * hat, axis=1, keepdims=True)
+            gi_ref[at, :] = inv * (gg - first - hat * second)
+            va[0, :, 0:dm] += jnp.sum(back * hat, axis=0, keepdims=True)
+            va[0, :, dm : 2 * dm] += jnp.sum(back, axis=0, keepdims=True)
+            return carry
+
+        lax.fori_loop(0, rows // strip, norm, 0)
+
+        hops = (place.core, place.by_x, place.by_y)
+        between = (red.last, red.four, red.five)
+        for i, dev in enumerate(hops):
+            wire.start(3 + i, va.at[i], vr.at[i], dev)
+            if i == 0:
+                between[0]()
+            wire.landed(3 + i, vr.at[i], dev)
+            if i < 2:
+                va[i + 1] = va[i] + vr[i]
+            else:
+                vz[0] = va[i] + vr[i]
+        for d in (1, 2, 3):
+            wire.start(5 + d, vz.at[0], vz.at[d], place.along(d))
+        between[1]()
+        between[2]()
+        for d in (1, 2, 3):
+            wire.landed(5 + d, vz.at[d], place.along(4 - d))
+        terms = [vz[lax.rem(z - a + 4, 4)] for a in range(4)]
+        sum_ref[...] = (terms[0] + terms[1]) + (terms[2] + terms[3])
+        red.six()
+
+        @pl.when(long)
+        def _():
+            wire.sent(0, far_out)
+
+        @pl.when(gives_prev)
+        def _():
+            wire.sent(1, prev_in)
+
+        @pl.when(gives_next)
+        def _():
+            wire.sent(2, next_out)
+
+        for i in range(3):
+            wire.sent(3 + i, va.at[i])
+        for d in (1, 2, 3):
+            wire.sent(5 + d, vz.at[0])
+
+    hbm = pl.BlockSpec(memory_space=pl.ANY)
+    vmem = pl.BlockSpec(memory_space=pltpu.VMEM)
+    buf = lambda *shape: pltpu.VMEM(shape, BF16)
+    return pl.pallas_call(
+        body,
+        in_specs=[hbm] + [vmem] * 7,
+        out_specs=[vmem] * 3,
+        out_shape=[
+            jax.ShapeDtypeStruct((8, dm // 4, w), BF16),
+            jax.ShapeDtypeStruct((rows, dm), F32),
+            jax.ShapeDtypeStruct((1, length), F32),
+        ],
+        scratch_shapes=[
+            buf(dm, cols), pltpu.VMEM((win, dm), F32),
+            buf(own, dm), buf(HALO, dm), buf(own, dm), buf(HALO, dm), buf(HALO, dm),
+            pltpu.VMEM((3, 1, length), F32), pltpu.VMEM((3, 1, length), F32), pltpu.VMEM((4, 1, length), F32),
+            pltpu.SemaphoreType.DMA((9,)), pltpu.SemaphoreType.DMA((9,)), pltpu.SemaphoreType.DMA(()),
+        ]
+        + Reduce.scratch(dm, w),
+        compiler_params=pltpu.CompilerParams(collective_id=2, has_side_effects=True, vmem_limit_bytes=VMEM),
+    )(gp, dq, dk, dv, packed, tokens, gain[None], vec)
+
+
 def place_grads(coords, done, mode):
     _, q, w = done.shape
     e = q // 2
@@ -1013,7 +1157,7 @@
     ffw = w_up.shape[1]
     mp = lax.axis_size("mp")
     dp = lax.axis_size("dp")
-    fast = mp == 4 and dp == 8 and rows % 256 == 0 and cw == 2 * PAIR
+    fast = mp == 4 and dp == 8 and rows % 256 == 0 and cw == 2 * PAIR and rows < LONGEST <= 2 * rows
     z = lax.axis_index("mp")
     me = lax.axis_index("dp")
     core = lax.rem(me, 2)
@@ -1097,27 +1241,40 @@
     else:
         dq, dk, dv = attn_bwd_call(info, q, k, v, attn, g_attn, lse, qseg, kseg, own)
     halves = dq.shape[0]
-    g_own, g_far, g_next = norm1_back_call(dq, dk, dv, packed, info, own)
-    back = g_own
-    for j in range(1, near):
-        part = g_far[(j - 1) * rows : j * rows]
-        back = back + f32(lax.ppermute(part, "mp", [(i, (i + j) % near) for i in range(near)]))
-    to_prev = f32(lax.ppermute(g_far[-HALO:], "mp", [(i, i - 1) for i in range(near, mp)]))
-    to_next = f32(lax.ppermute(g_next, "mp", [(i, i + 1) for i in range(near - 1, mp - 1)]))
-    back = jnp.concatenate([back[:HALO] + to_next, back[HALO:-HALO], back[-HALO:] + to_prev], axis=0)
-    hat1 = hat_win[own : own + rows]
-    inv1 = inv_win[own : own + rows]
-    g_in, g_gain1, g_bias1 = norm_back(back, hat1, inv1, f32(ln1_gain))
-    g_tokens = g_in + g_hidden
-
+    def shards(v, width):
+        if v.shape[0] == 2:
+            v = core_first(v.reshape(2, mp, width // 2), core, 0).transpose(1, 0, 2)
+        return jnp.roll(v.reshape(mp, width), z, axis=0).reshape(mp * width)
+
+    gbq = shards(jnp.sum(f32(dq), axis=1), cw)
+    gbv = shards(jnp.sum(f32(dv), axis=1), cw)
+    gbu = core_first(g_b_up.reshape(2, mp, ffw // 2), core, 0).transpose(1, 0, 2)
+    gbu = jnp.roll(gbu.reshape(mp, ffw), z, axis=0).reshape(-1)
+    sums = [jnp.sum(g_hidden, axis=0), g_gain2, g_bias2, jnp.sum(gout, axis=0), gbq, gbv, gbu]
     n1 = n1w[own : own + rows]
     if fast:
+        vec = jnp.concatenate([jnp.zeros((2 * dm,), F32)] + sums)[None]
+        done_p, g_in, vec = finish_call(gp, dq, dk, dv, packed, tokens, ln1_gain, vec, own)
+        vec = vec[0]
+        g_tokens = g_in + g_hidden
         coords = jnp.stack([y, x, core]).astype(jnp.int32)
-        (done_p,) = reduce_call([gp], 2)
         (g_w_down,) = place_grads(coords, done_d, "down")
         (g_w_up,) = place_grads(coords, done_u, "up")
         g_w_query, g_w_key, g_w_value, g_w_out = place_grads(coords, done_p, "pack")
     else:
+        g_own, g_far, g_next = norm1_back_call(dq, dk, dv, packed, info, own)
+        back = g_own
+        for j in range(1, near):
+            part = g_far[(j - 1) * rows : j * rows]
+            back = back + f32(lax.ppermute(part, "mp", [(i, (i + j) % near) for i in range(near)]))
+        to_prev = f32(lax.ppermute(g_far[-HALO:], "mp", [(i, i - 1) for i in range(near, mp)]))
+        to_next = f32(lax.ppermute(g_next, "mp", [(i, i + 1) for i in range(near - 1, mp - 1)]))
+        back = jnp.concatenate([back[:HALO] + to_next, back[HALO:-HALO], back[-HALO:] + to_prev], axis=0)
+        hat1 = hat_win[own : own + rows]
+        inv1 = inv_win[own : own + rows]
+        g_in, g_gain1, g_bias1 = norm_back(back, hat1, inv1, f32(ln1_gain))
+        g_tokens = g_in + g_hidden
+
         other = lambda v: lax.ppermute(v, "dp", [(i, i - i % 2 + (i + 1) % 2) for i in range(dp)])
         hw = mp * ffw // 2
 
@@ -1146,19 +1303,7 @@
         g_w_value = whole_grad(n1w, whole(dv))
         g_w_out = whole_grad(ghb, attn.transpose(1, 0, 2).reshape(rows, mp * cw)).T
 
-    def shards(v, width):
-        if v.shape[0] == 2:
-            v = core_first(v.reshape(2, mp, width // 2), core, 0).transpose(1, 0, 2)
-        return jnp.roll(v.reshape(mp, width), z, axis=0).reshape(mp * width)
-
-    gbq = shards(jnp.sum(f32(dq), axis=1), cw)
-    gbv = shards(jnp.sum(f32(dv), axis=1), cw)
-    gbu = core_first(g_b_up.reshape(2, mp, ffw // 2), core, 0).transpose(1, 0, 2)
-    gbu = jnp.roll(gbu.reshape(mp, ffw), z, axis=0).reshape(-1)
-    vec = jnp.concatenate(
-        [g_gain1, g_bias1, jnp.sum(g_hidden, axis=0), g_gain2, g_bias2, jnp.sum(gout, axis=0), gbq, gbv, gbu]
-    )
-    vec = lax.psum(vec, ("dp", "mp"))
+        vec = lax.psum(jnp.concatenate([g_gain1, g_bias1] + sums), ("dp", "mp"))
     g_gain1, g_bias1, g_b_out, g_gain2, g_bias2, g_b_down = (vec[i * dm : (i + 1) * dm] for i in range(6))
     at = 6 * dm
     g_b_query = lax.dynamic_slice_in_dim(vec, at + z * cw, cw)

time: 561 us -> 493 us (0.88); the launches traced: 550 us -> 489 us
  blocking collectives: 42.5 us -> 0 us
  starting transfers between devices: 21 us -> 11.1 us
  other arithmetic: 32.5 us -> 26.2 us
    psum x1 -> x0, blocking collectives: 42.5 us -> none  [local(): vec = lax.psum(vec, ('dp', 'mp'))]
    ppermute x3 -> x0, starting transfers between devices: 9.99 us -> none  [the longest x1 8.02 us: local(): lax.ppermute(part, 'mp', [(i, (i + j) % near) for i in range(near)])]
    pallas_call x2 -> x1, Pallas kernels: 79.5 us -> 82 us  [finish_call(): pl.pallas_call(body, in_specs=[hbm] + [vmem] * 7, out_specs=[vmem] * 3, o...]
  transfers between devices with their start and end apart: 9 -> 6, of which waited for: 0 -> 0; matrix products, arithmetic and copies ran while one was open for 5% -> 3% of each run, Pallas kernels for 33% -> 21%
where the time goes in v4:
time: 493 us; the launch traced here: 489 us
  Pallas kernels  414 us (84%)
  local copies, waits for them, and re-layouts  30.2 us (6%)
  other arithmetic  26.2 us (5%)
  starting transfers between devices  11.1 us (2%)
  matrix products  5.92 us (1%)
    pallas_call x1, Pallas kernels, back_call(): pl.pallas_call(body, in_specs=[hbm] * 6 + [vmem] * 8, out_specs=[vmem, vm...  144 us
    pallas_call x1, Pallas kernels, gather_call(): pl.pallas_call(body, in_specs=[pl.BlockSpec(memory_space=pltpu.VMEM)] * c...  104 us
    pallas_call x1, Pallas kernels, finish_call(): pl.pallas_call(body, in_specs=[hbm] + [vmem] * 7, out_specs=[vmem] * 3, o...  82 us
    pallas_call x1, Pallas kernels, ffn_call(): pl.pallas_call(body, grid_spec=pltpu.PrefetchScalarGridSpec(num_scalar_pr...  29.2 us
    pallas_call x1, Pallas kernels, attn_fwd_call(): pl.pallas_call(body, grid_spec=pltpu.PrefetchScalarGridSpec(num_scalar_pr...  25.2 us
    pallas_call x3, Pallas kernels, place_grads(): pl.pallas_call(body, in_specs=[pl.BlockSpec(memory_space=pltpu.SMEM), pl....  12.1 us
    pallas_call x1, Pallas kernels, qkv_call(): pl.pallas_call(body, grid=(n,), in_specs=[pl.BlockSpec((win, dm), lambda...  10.2 us
  transfers between devices with their start and end apart: 6, of which 0 were waited for; matrix products, arithmetic and copies ran while one was open for 3% of the time, Pallas kernels for 21%

profile of v4, /device:TPU:0, one launch (start us, length us, event | category | flops | bytes accessed | tf_op | source)
XLA Modules:
  0.0 489.1 jit_solution(17803160503610481805)
XLA Ops:
  0.7 0.9 dynamic-update-slice.8
  1.6 0.8 dynamic-update-slice.9
  2.4 0.8 dynamic-update-slice.10
  3.3 3.1 collective-permute-start.5
  6.4 2.6 collective-permute-start.4
  8.9 1.3 collective-permute-start.3
  10.3 1.5 copy.59
  11.8 2.6 collective-permute-start
  14.4 0.9 fusion.27
  15.3 0.7 collective-permute-start.1
  16.0 0.6 broadcast_in_dim.62.g_ref
  16.9 0.6 pad_add_fusion.big_ref
  17.6 0.6 pad_add_fusion.1.c_ref
  18.2 0.6 broadcast_dynamic-update-slice_fusion
  18.8 3.0 pad_maximum_fusion.refs_0_
  21.8 0.6 broadcast_in_dim.65.gain_ref
  22.4 0.9 copy.67.refs_3_.qs_ref
  23.4 0.6 broadcast_in_dim.60.refs_4_.ks_ref
  24.0 0.6 broadcast_in_dim.61.bo_ref
  24.6 0.6 broadcast_in_dim.63.b_ref
  25.2 0.6 broadcast_in_dim.64.bd_ref
  25.8 1.3 copy.69
  27.1 104.0 %shard_map.305 = (bf16[4,1024,1024]{2,1,0:T(8,128)(2,1)}, bf16[4,1024,1024]{2,1,0:T(8,128)(2,1)}, bf16[4,1024,1024]{2,1,0:T(8,128)(2,1)}) custom-call(bf16[1024,1024]{1,0:T(8,128)(2,1)} %pad_maximum_fusion.refs_0_, bf16[1024,1024]{1,0:T(8,128)(2,1)} %refs_1_.1, bf16[1024,1024]{1,0:T(8,128)(2,1)} %refs_2_.1), custom_call_target="tpu_custom_call" | custom-call | tf_op jit(solution)/shard_map/pallas_call | solution.py:553
  131.1 0.9 collective-permute-start.2
  132.1 0.6 copy.65.bq_ref
  132.7 0.6 copy.66.bv_ref
  133.3 0.6 broadcast_in_dim_reshape.3.bu_ref
  134.0 1.8 slice_add_fusion
  135.8 0.7 copy-done.8
  136.5 0.7 broadcast_in_dim.54
  137.2 3.7 concatenate.22
  140.9 0.4 convert_reduce_fusion
  141.3 0.7 fusion.2
  142.0 2.3 fusion.5
  144.3 2.3 fusion.33.n1_ref
  146.6 4.3 copy.64.x_ref
  150.8 10.2 %shard_map.306 = (bf16[4,512,256]{2,1,0:T(8,128)(2,1)}, bf16[4,1152,256]{2,1,0:T(8,128)(2,1)}, bf16[4,1152,256]{2,1,0:T(8,128)(2,1)}) custom-call(bf16[1152,1024]{1,0:T(8,128)(2,1)} %copy.64.x_ref, bf16[4,1024,1024]{2,1,0:T(8,128)(2,1)} %get-tuple-element.46.w_ref, bf16[4,1,256]{2,1,0:T(2,128)(2,1)} %copy.65.bq_ref, bf16[4,1,256]{2,1,0:T(2,128)(2,1)} %copy.66.bv_ref), custom_call_target="tpu_custom_call" | custom-call | flops 5905580032 | bytes 10747904 | tf_op jit(solution)/shard_map/pallas_call | solution.py:59
  161.0 25.2 %shard_map.307 = (bf16[4,512,256]{2,1,0:T(8,128)(2,1)}, f32[8,512,2]{2,1,0:T(8,128)}) custom-call(s32[2]{0:T(128)} %pad_add_fusion.big_ref, bf16[4,512,256]{2,1,0:T(8,128)(2,1)} %get-tuple-element.47.refs_0_.q_ref, bf16[4,1152,256]{2,1,0:T(8,128)(2,1)} %get-tuple-element.48.refs_1_.k_ref, bf16[4,1152,256]{2,1,0:T(8,128)(2,1)} %get-tuple-element.49.refs_2_.v_ref, ...), custom_call_target="tpu_custom_call" | custom-call | flops 9663676416 | bytes 6815744 | tf_op jit(solution)/shard_map/pallas_call | solution.py:120
  186.2 7.1 %shard_map.308 = (f32[512,1024]{1,0:T(8,128)}, bf16[512,1024]{1,0:T(8,128)(2,1)}) custom-call(bf16[4,512,256]{2,1,0:T(8,128)(2,1)} %get-tuple-element.50.a_ref, bf16[4,1024,1024]{2,1,0:T(8,128)(2,1)} %get-tuple-element.46.w_ref, bf16[512,1024]{1,0:T(8,128)(2,1)} %x_ref.3, bf16[1,1024]{1,0:T(2,128)(2,1)} %broadcast_in_dim.61.bo_ref, ...), custom_call_target="tpu_custom_call" | custom-call | flops 1073741824 | bytes 2097152 | tf_op jit(solution)/shard_map/pallas_call | solution.py:264
  193.2 2.5 copy.70
  195.9 0.3 multiply_reduce_fusion.2
  196.3 29.2 %shard_map.309 = (bf16[512,1024]{1,0:T(8,128)(2,1)}, f32[512,1024]{1,0:T(8,128)}, bf16[512,4096]{1,0:T(8,128)(2,1)}, bf16[512,4096]{1,0:T(8,128)(2,1)}, f32[1,4096]{1,0:T(1,128)}) custom-call(s32[1]{0:T(128)} %bitcast.core_ref, bf16[512,1024]{1,0:T(8,128)(2,1)} %get-tuple-element.51.x_ref, f32[512,1024]{1,0:T(8,128)} %get-tuple-element.52.h_ref, ...), custom_call_target="tpu_custom_call" | custom-call | flops 17179869184 | bytes 16777216 | tf_op jit(solution)/shard_map/pallas_call | solution.py:320
  225.5 3.2 multiply_reduce_fusion
  228.7 1.5 fusion.26
  230.5 1.0 copy-done
  231.6 1.5 fusion.9
  233.1 1.5 fusion.8
  234.5 1.5 fusion.7
  236.0 1.5 fusion.6
  237.5 1.3 copy.71.ghb_ref
  238.8 1.1 pad_maximum_fusion.1.g_ref
  239.9 144.5 %shard_map.310 = (bf16[8,256,512]{2,1,0:T(8,128)(2,1)}, bf16[8,256,512]{2,1,0:T(8,128)(2,1)}, bf16[1024,2048]{1,0:T(8,128)(2,1)}, bf16[2,512,512]{2,1,0:T(8,128)...) custom-call(bf16[1024,512]{1,0:T(8,128)(2,1)} %bitcast.76, ...), custom_call_target="tpu_custom_call" | custom-call | tf_op jit(solution)/shard_map/pallas_call | solution.py:881
  384.5 1.4 convert_reduce_fusion.3
  385.9 2.0 convert_reduce_fusion.1
  388.1 0.5 broadcast.72
  388.6 0.7 reduce.3
  389.5 0.6 copy-done.11
  390.1 82.0 %shard_map.311 = (bf16[8,256,512]{2,1,0:T(8,128)(2,1)}, f32[512,1024]{1,0:T(8,128)}, f32[1,12288]{1,0:T(1,128)}) custom-call(bf16[1024,2048]{1,0:T(8,128)(2,1)} %get-tuple-element.60.gp_ref, bf16[2,512,512]{2,1,0:T(8,128)(2,1)} %get-tuple-element.61.dq_ref, bf16[2,1152,512]{2,1,0:T(8,128)(2,1)} %get-tuple-element.62.dk_ref, ...), custom_call_target="tpu_custom_call" | custom-call | tf_op jit(solution)/shard_map/pallas_call | solution.py:1054
  472.2 3.5 add.102
  475.6 3.9 shard_map.312
  479.6 3.9 shard_map.313
  483.4 4.3 shard_map.314
  487.8 0.6 fusion.28
  488.4 0.6 constant_dynamic-slice_fusion.1
  (95 shorter events, 1.3 us)
Async XLA Ops:
  0.7 15.3 %copy-start.18 = (bf16[1024]{0:T(1024)(128)(2,1)S(1)}, bf16[1024]{0:T(1024)(128)(2,1)}, u32[]{:S(2)}) copy-start(bf16[1024]{0:T(1024)(128)(2,1)} %param.31) | copy-start | bytes 6148
  0.7 15.9 %copy-start.19 = (bf16[1024]{0:T(1024)(128)(2,1)S(1)}, bf16[1024]{0:T(1024)(128)(2,1)}, u32[]{:S(2)}) copy-start(bf16[1024]{0:T(1024)(128)(2,1)} %param.22) | copy-start | bytes 6148
  0.7 15.9 %copy-start.7 = (bf16[256,1024]{1,0:T(8,128)(2,1)S(1)}, bf16[256,1024]{1,0:T(8,128)(2,1)}, u32[]{:S(2)}) copy-start(bf16[256,1024]{1,0:T(8,128)(2,1)} %param.29) | copy-start | bytes 1572868
  0.7 16.8 %copy-start.20 = (s32[2048]{0:T(1024)S(1)}, s32[2048]{0:T(1024)}, u32[]{:S(2)}) copy-start(s32[2048]{0:T(1024)} %param.21) | copy-start | bytes 24580
  3.3 127.8 %collective-permute-start.5 = (bf16[1536]{0:T(1024)(128)(2,1)S(1)}, bf16[1536]{0:T(1024)(128)(2,1)S(1)}, u32[]{:S(2)}, u32[]{:S(2)}) collective-permute-start(bf16[1536]{0:T(1024)(128)(2,1)S(1)} %dynamic-update-slice.10), channel_id=1, source_target_pairs={{3,0},{0,1},{1,2},{2,3},{7,4},{4,5},{5,6},{6,7},{11,8},{8,9},{9,10... | collective-permute-start | bytes 9224 | tf_op jit(solution)/shard_map/ppermute | solution.py:1179
  6.4 125.7 %collective-permute-start.4 = (bf16[1536]{0:T(1024)(128)(2,1)S(1)}, bf16[1536]{0:T(1024)(128)(2,1)S(1)}, u32[]{:S(2)}, u32[]{:S(2)}) collective-permute-start(bf16[1536]{0:T(1024)(128)(2,1)S(1)} %dynamic-update-slice.10), channel_id=1, source_target_pairs={{2,0},{3,1},{0,2},{1,3},{6,4},{7,5},{4,6},{5,7},{10,8},{11,9},{8,1... | collective-permute-start | bytes 9224 | tf_op jit(solution)/shard_map/ppermute | solution.py:1179
  8.9 123.1 %collective-permute-start.3 = (bf16[1536]{0:T(1024)(128)(2,1)S(1)}, bf16[1536]{0:T(1024)(128)(2,1)S(1)}, u32[]{:S(2)}, u32[]{:S(2)}) collective-permute-start(bf16[1536]{0:T(1024)(128)(2,1)S(1)} %dynamic-update-slice.10), channel_id=1, source_target_pairs={{1,0},{2,1},{3,2},{0,3},{5,4},{6,5},{7,6},{4,7},{9,8},{10,9},{11,1... | collective-permute-start | bytes 9224 | tf_op jit(solution)/shard_map/ppermute | solution.py:1179
  11.8 122.2 %collective-permute-start = (bf16[512,1024]{0,1:T(8,128)(2,1)S(1)}, bf16[512,1024]{0,1:T(8,128)(2,1)}, u32[]{:S(2)}, u32[]{:S(2)}) collective-permute-start(bf16[512,1024]{0,1:T(8,128)(2,1)S(1)} %copy.59), channel_id=1, source_target_pairs={{1,0},{0,1},{5,4},{4,5},{9,8},{8,9},{13,12},{12,13},{17,16},{16,17... | collective-permute-start | bytes 3145736 | tf_op jit(solution)/shard_map/ppermute | solution.py:1172
  15.3 118.7 %collective-permute-start.1 = (bf16[64,1024]{0,1:T(8,128)(2,1)}, bf16[64,1024]{0,1:T(8,128)(2,1)S(1)}, u32[]{:S(2)}, u32[]{:S(2)}) collective-permute-start(bf16[64,1024]{0,1:T(8,128)(2,1)} %get-tuple-element.82), channel_id=1, source_target_pairs={{1,2},{2,3},{5,6},{6,7},{9,10},{10,11},{13,14},{14,15},{17,18},{18... | collective-permute-start | bytes 393224 | tf_op jit(solution)/shard_map/ppermute | solution.py:1174
  16.8 5.6 %copy-start.21 = (bf16[1024]{0:T(1024)(128)(2,1)S(1)}, bf16[1024]{0:T(1024)(128)(2,1)}, u32[]{:S(2)}) copy-start(bf16[1024]{0:T(1024)(128)(2,1)} %param.23) | copy-start | bytes 6148
  16.8 7.1 %copy-start.22 = (bf16[1024]{0:T(1024)(128)(2,1)S(1)}, bf16[1024]{0:T(1024)(128)(2,1)}, u32[]{:S(2)}) copy-start(bf16[1024]{0:T(1024)(128)(2,1)} %param.30) | copy-start | bytes 6148
  16.8 7.7 %copy-start.23 = (bf16[1024]{0:T(1024)(128)(2,1)S(1)}, bf16[1024]{0:T(1024)(128)(2,1)}, u32[]{:S(2)}) copy-start(bf16[1024]{0:T(1024)(128)(2,1)} %param.32) | copy-start | bytes 6148
  16.9 8.3 %copy-start.24 = (bf16[1024]{0:T(1024)(128)(2,1)S(1)}, bf16[1024]{0:T(1024)(128)(2,1)}, u32[]{:S(2)}) copy-start(bf16[1024]{0:T(1024)(128)(2,1)} %param.36) | copy-start | bytes 6148
  16.9 8.9 %copy-start.5 = (bf16[512,1024]{1,0:T(8,128)(2,1)S(1)}, bf16[512,1024]{1,0:T(8,128)(2,1)}, u32[]{:S(2)}) copy-start(bf16[512,1024]{1,0:T(8,128)(2,1)} %c_ref.1) | copy-start | bytes 3145732
  27.1 104.1 %copy-start.9 = (bf16[64,1024]{0,1:T(8,128)(2,1)S(1)}, bf16[64,1024]{0,1:T(8,128)(2,1)}, u32[]{:S(2)}) copy-start(bf16[64,1024]{0,1:T(8,128)(2,1)} %get-tuple-element.81) | copy-start | bytes 393220
  131.1 4.6 collective-permute-start.2
  135.8 0.7 copy-start.8
  193.2 2.5 copy-start.2
  196.2 29.2 %copy-start.3 = (f32[512,1024]{1,0:T(8,128)S(1)}, f32[512,1024]{1,0:T(8,128)}, u32[]{:S(2)}) copy-start(f32[512,1024]{1,0:T(8,128)} %get-tuple-element.52.h_ref) | copy-start | bytes 6291460
  225.4 3.3 copy-start.4
  225.4 3.2 copy-start.6
  230.2 1.4 copy-start
  384.4 4.2 copy-start.17
  384.4 4.9 %copy-start.10 = (f32[12288]{0:T(1024)S(1)}, f32[12288]{0:T(1024)}, u32[]{:S(2)}) copy-start(f32[12288]{0:T(1024)} %broadcast_dynamic-update-slice_fusion) | copy-start | bytes 147460
  384.4 4.9 %copy-start.16 = (f32[1024]{0:T(1024)S(1)}, f32[1024]{0:T(1024)}, u32[]{:S(2)}) copy-start(f32[1024]{0:T(1024)} %get-tuple-element.78) | copy-start | bytes 12292
  384.5 4.9 %copy-start.14 = (f32[1024]{0:T(1024)S(1)}, f32[1024]{0:T(1024)}, u32[]{:S(2)}) copy-start(f32[1024]{0:T(1024)} %get-tuple-element.74) | copy-start | bytes 12292
  384.5 4.9 %copy-start.13 = (f32[1024]{0:T(1024)S(1)}, f32[1024]{0:T(1024)}, u32[]{:S(2)}) copy-start(f32[1024]{0:T(1024)} %get-tuple-element.77) | copy-start | bytes 12292
  384.5 5.0 %copy-start.15 = (f32[1024]{0:T(1024)S(1)}, f32[1024]{0:T(1024)}, u32[]{:S(2)}) copy-start(f32[1024]{0:T(1024)} %get-tuple-element.80) | copy-start | bytes 12292
  389.5 0.6 copy-start.11
  390.1 82.1 %copy-start.1 = (f32[512,1024]{1,0:T(8,128)S(1)}, f32[512,1024]{1,0:T(8,128)}, u32[]{:S(2)}) copy-start(f32[512,1024]{1,0:T(8,128)} %copy-done) | copy-start | bytes 6291460
  483.4 4.3 copy-start.12

commit v5 on v4

--- a/solution.py
+++ b/solution.py
@@ -484,9 +484,8 @@
     def slot(d, kind):
         return base + (d - 1) * 9 + kind
 
-    def begin():
-        for d in (1, 2, 3):
-            wire.start(slot(d, 0), shard.at[rows(place.me)], whole.at[d, rows(place.me)], place.along(4 - d))
+    def begin(d):
+        wire.start(slot(d, 0), shard.at[rows(place.me)], whole.at[d, rows(place.me)], place.along(4 - d))
 
     def first(d):
         mine = whole.at[d, rows(place.me)]
@@ -513,55 +512,339 @@
         got = whole.at[d, rows(place.me_xy)]
         wire.start(slot(d, 8), got, got, place.core)
 
-    def finish():
+    def done(d):
         flip = 1 - 2 * place.k
+        for kind, who in ((1, place.me), (6, place.me_x), (7, place.me_y), (8, place.me_xy)):
+            wire.landed(slot(d, kind), whole.at[d, rows(who + flip)], place.core)
+
+    def drain():
         for d in (1, 2, 3):
-            for kind, who in ((1, place.me), (6, place.me_x), (7, place.me_y), (8, place.me_xy)):
-                wire.landed(slot(d, kind), whole.at[d, rows(who + flip)], place.core)
             for kind in range(9):
                 wire.sent(slot(d, kind), whole.at[d, pl.ds(0, half if kind in (4, 5) else step)])
 
-    return begin, first, second, third, finish
-
-
-def gather_call(shards):
-    count = len(shards)
-
-    def body(*refs):
-        ins, outs = refs[:count], refs[count : 2 * count]
-        send, recv, local_sem = refs[2 * count :]
+    return begin, first, second, third, done, drain
+
+
+def front_call(tokens, cot, pack, w_up, w_down, bias, small, qseg, kseg, own):
+    rows, dm = tokens.shape
+    cw = pack.shape[1] // 4
+    ffw = w_up.shape[1]
+    n = 4
+    tile = ffw // 2
+    hw = n * tile
+    win = own + rows + 2 * HALO
+    pairs = cw // PAIR
+    strip = 128
+    per = rows // strip
+    scale = HEAD_DIM**-0.5
+    length = bias.shape[1]
+    base = 6
+
+    def body(
+        tok_ref, cot_ref, pack_ref, up_ref, down_ref, small_ref, bias_ref, qs_ref, ks_ref,
+        packed, n1t, n2t, cott, ghbt, q_ref, k_ref, v_ref, a_ref, l_ref, ga_ref, act_ref, gup_ref, gbu_ref, gh_ref, o_ref, sum_ref,
+        up, down, n1, hid, n2, acc, act, gup, biases, xs, xr, ls, fs,
+    ):
         place = Place()
-        wire = Wire(send, recv, place.core)
-        copies = [pltpu.make_async_copy(ins[g], outs[g].at[0], local_sem.at[g]) for g in range(count)]
+        core, z = place.k, place.z
+        long, takes_prev, takes_next = z < 2, z >= 2, jnp.logical_and(z >= 1, z < 3)
+        swap = {"dp": place.me, "mp": lax.rem(z + 1, 2)}
+        left_dev = {"dp": place.me, "mp": lax.rem(z + 3, 4)}
+        right_dev = {"dp": place.me, "mp": lax.rem(z + 1, 4)}
+        wire = Wire(xs, xr, place.core)
+        local = [
+            pltpu.make_async_copy(src, dst, ls.at[i])
+            for i, (src, dst) in enumerate(
+                ((tok_ref, n1.at[own : own + rows]), (pack_ref, packed.at[0]), (up_ref, up.at[0]), (down_ref, down.at[0]))
+            )
+        ]
+        for c in local:
+            c.start()
         place.meet()
-        groups = [gather_steps(place, wire, g * 27, ins[g], outs[g]) for g in range(count)]
-        for begin, *_ in groups:
-            begin()
-        for c in copies:
-            c.start()
-        order = [(g, d) for g in range(count) for d in (1, 3, 2)]
-        for i in range(len(order) + 2):
+        for d in (1, 2, 3):
+            wire.start(d - 1, bias_ref, biases.at[d], place.along(4 - d))
+
+        @pl.when(long)
+        def _():
+            wire.start(3, tok_ref, n1.at[0:own], swap)
+
+        @pl.when(takes_next)
+        def _():
+            wire.start(4, tok_ref.at[rows - HALO : rows], n1.at[own - HALO : own], right_dev)
+
+        @pl.when(takes_prev)
+        def _():
+            wire.start(5, tok_ref.at[0:HALO], n1.at[own + rows : own + rows + HALO], left_dev)
+
+        groups = [
+            gather_steps(place, wire, base + 27 * g, src, dst)
+            for g, (src, dst) in enumerate(((pack_ref, packed), (up_ref, up), (down_ref, down)))
+        ]
+        items = [(0, 1), (0, 3), (0, 2), (1, 1), (2, 1), (1, 3), (2, 3), (1, 2), (2, 2)]
+        for g, d in items:
+            groups[g][0](d)
+
+        def relay(i):
             for lag in range(3):
-                if 0 <= i - lag < len(order):
-                    g, d = order[i - lag]
+                if 0 <= i - lag < len(items):
+                    g, d = items[i - lag]
                     groups[g][1 + lag](d)
-        for *_, finish in groups:
-            finish()
-        for c in copies:
+
+        def arrived(d, *which):
+            for g in which:
+                groups[g][4](d)
+
+        def turns(i, table):
+            for t, f in table.items():
+
+                @pl.when(i == t)
+                def _():
+                    f()
+
+        def shard_at(k):
+            return k + (k // 2) * (5 - 2 * k)
+
+        def strip_at(i, start=0):
+            return pl.ds(pl.multiple_of(start + i * strip, strip), strip)
+
+        row = lambda i: small_ref[i : i + 1, :]
+
+        @pl.when(takes_prev)
+        def _():
+            n1[0 : own - HALO, :] = jnp.zeros((own - HALO, dm), BF16)
+
+        @pl.when(jnp.logical_not(takes_next))
+        def _():
+            n1[own + rows : own + rows + HALO, :] = jnp.zeros((HALO, dm), BF16)
+
+        n1[own + rows + HALO :, :] = jnp.zeros((HALO, dm), BF16)
+        biases[0] = bias_ref[...]
+
+        def turn_cot(i, carry):
+            cott[:, strip_at(i)] = cot_ref[strip_at(i), :].astype(F32).T.astype(BF16)
+            return carry
+
+        lax.fori_loop(0, per, turn_cot, 0)
+
+        def norm1(i):
+            at = strip_at(i)
+            x = n1[at, :].astype(F32)
+            hat, _ = norm_rows(x)
+            val = hat * row(0) + row(1)
+            n1[at, :] = val.astype(BF16)
+            n1t[:, at] = val.T.astype(BF16)
+            return x
+
+        def norm_own(i, carry):
+            hid[strip_at(i), :] = norm1(own // strip + i) + row(4)
+            return carry
+
+        def norm_far(i, carry):
+            norm1(i)
+            return carry
+
+        local[0].wait()
+        lax.fori_loop(0, per, norm_own, 0)
+
+        @pl.when(long)
+        def _():
+            wire.landed(3, n1.at[0:own], swap)
+
+        @pl.when(takes_prev)
+        def _():
+            wire.landed(4, n1.at[own - HALO : own], left_dev)
+
+        @pl.when(takes_next)
+        def _():
+            wire.landed(5, n1.at[own + rows : own + rows + HALO], right_dev)
+
+        lax.fori_loop(0, own // strip, norm_far, 0)
+        norm1((own + rows) // strip)
+        for d in (1, 2, 3):
+            wire.landed(d - 1, biases.at[d], place.along(d))
+        for c in local[1:]:
             c.wait()
 
+        def attend(big, d, p):
+            at = pl.ds(pl.multiple_of(p * PAIR, PAIR), PAIR)
+            for qs, qn, ks, kn in blocks_of(rows, own, win, big):
+                mask = qs_ref[qs : qs + qn, :] == ks_ref[:, ks : ks + kn]
+                qq, kk, vv = q_ref[d, qs : qs + qn, at], k_ref[d, ks : ks + kn, at], v_ref[d, ks : ks + kn, at]
+                outs = []
+                for h in range(2):
+                    lanes = slice(h * HEAD_DIM, (h + 1) * HEAD_DIM)
+                    s = jnp.where(mask, dot_nt(qq[:, lanes] * BF16(scale), kk[:, lanes]), NEG)
+                    top = jnp.max(s, axis=1, keepdims=True)
+                    pr = jnp.exp(s - top)
+                    total = jnp.sum(pr, axis=1, keepdims=True)
+                    outs.append(dot_nn(pr.astype(BF16), vv[:, lanes]) / total)
+                    l_ref[d * pairs + p, qs : qs + qn, h : h + 1] = top + jnp.log(total)
+                a_ref[d, qs : qs + qn, at] = jnp.concatenate(outs, axis=1).astype(BF16)
+
+        def heads(kk, carry):
+            turns(
+                kk,
+                {
+                    0: lambda: relay(0),
+                    1: lambda: (relay(1), relay(2), relay(3), arrived(1, 0)),
+                    2: lambda: (relay(4), arrived(3, 0)),
+                    3: lambda: (relay(5), arrived(2, 0)),
+                },
+            )
+            d = shard_at(kk)
+            q_ref[d] = (dot_nn(n1[own : own + rows, :], packed[d, :, 0:cw]) + biases[d, :, 0:cw]).astype(BF16)
+            k_ref[d] = dot_nn(n1[...], packed[d, :, cw : 2 * cw]).astype(BF16)
+            v_ref[d] = (dot_nn(n1[...], packed[d, :, 2 * cw : 3 * cw]) + biases[d, :, cw : 2 * cw]).astype(BF16)
+
+            def one(p, inner):
+                @pl.when(long)
+                def _():
+                    attend(True, d, p)
+
+                @pl.when(jnp.logical_not(long))
+                def _():
+                    attend(False, d, p)
+
+                return inner
+
+            lax.fori_loop(0, pairs, one, 0)
+            hid[...] += dot_nt(a_ref[d], packed[d, :, 3 * cw : 4 * cw])
+            return carry
+
+        lax.fori_loop(0, n, heads, 0)
+        relay(6)
+
+        def norm2(i, carry):
+            at = strip_at(i)
+            hidden = hid[at, :]
+            hat, _ = norm_rows(hidden)
+            val = hat * row(2) + row(3)
+            n2[at, :] = val.astype(BF16)
+            n2t[:, at] = val.T.astype(BF16)
+            acc[at, :] = hidden + row(5)
+            return carry
+
+        lax.fori_loop(0, per, norm2, 0)
+
+        def out_copies(i, col):
+            at = pl.ds(pl.multiple_of(col, tile), tile)
+            return (
+                pltpu.make_async_copy(act.at[:, at], act_ref.at[:, at], fs.at[i]),
+                pltpu.make_async_copy(gup.at[:, at], gup_ref.at[:, at], fs.at[2 * n + i]),
+            )
+
+        def column(i):
+            return lax.rem(i, 2) * hw + shard_at(i // 2) * tile
+
+        def feed(i, carry):
+            turns(
+                i,
+                {
+                    1: lambda: relay(7),
+                    2: lambda: (relay(8), arrived(1, 1, 2)),
+                    3: lambda: relay(9),
+                    4: lambda: (relay(10), arrived(3, 1, 2)),
+                    6: lambda: arrived(2, 1, 2),
+                },
+            )
+            d = shard_at(i // 2)
+            part = lax.rem(lax.rem(i, 2) + core, 2) * tile
+            at = pl.ds(pl.multiple_of(part, tile), tile)
+            to = pl.ds(pl.multiple_of(column(i), tile), tile)
+            u = dot_nn(n2[...], up[d, :, at]) + biases[d, :, pl.ds(pl.multiple_of(2 * cw + part, PAIR), tile)]
+            cdf = 0.5 * (1.0 + lax.erf(u * 0.7071067811865476))
+            val = (u * cdf).astype(BF16)
+            slope = cdf + u * jnp.exp(-0.5 * u * u) * 0.3989422804014327
+            act[:, to] = val
+            gu = (dot_nt(cot_ref[...], down[d, at, :]) * slope).astype(BF16)
+            gup[:, to] = gu
+            gbu_ref[:, to] = jnp.sum(gu.astype(F32), axis=0, keepdims=True)
+            for c in out_copies(i, column(i)):
+                c.start()
+            acc[...] += dot_nn(val, down[d, at, :])
+            gn = dot_nt(gu, up[d, :, at])
+
+            @pl.when(i == 0)
+            def _():
+                gh_ref[...] = gn
+
+            @pl.when(i > 0)
+            def _():
+                gh_ref[...] += gn
+
+            return carry
+
+        lax.fori_loop(0, 2 * n, feed, 0)
+        sum_ref[...] = jnp.zeros_like(sum_ref)
+
+        def back2(i, carry):
+            at = strip_at(i)
+            o_ref[at, :] = acc[at, :].astype(BF16)
+            hat, inv = norm_rows(hid[at, :])
+            g = gh_ref[at, :]
+            gout = cot_ref[at, :].astype(F32)
+            gg = g * row(2)
+            first = jnp.mean(gg, axis=1, keepdims=True)
+            second = jnp.mean(gg * hat, axis=1, keepdims=True)
+            val = inv * (gg - first - hat * second) + gout
+            gh_ref[at, :] = val
+            n2[at, :] = val.astype(BF16)
+            ghbt[:, at] = val.T.astype(BF16)
+            for j, v in enumerate((val, g * hat, g, gout)):
+                sum_ref[:, j * dm : (j + 1) * dm] += jnp.sum(v, axis=0, keepdims=True)
+            return carry
+
+        lax.fori_loop(0, per, back2, 0)
+
+        def back_attn(d, carry):
+            ga_ref[d] = dot_nn(n2[...], packed[d, :, 3 * cw : 4 * cw]).astype(BF16)
+            return carry
+
+        lax.fori_loop(0, n, back_attn, 0)
+        for i in range(2 * n):
+            for c in out_copies(i, 0):
+                c.wait()
+        for group in groups:
+            group[5]()
+        for d in (1, 2, 3):
+            wire.sent(d - 1, biases.at[d])
+
+        @pl.when(long)
+        def _():
+            wire.sent(3, n1.at[0:own])
+
+        @pl.when(takes_next)
+        def _():
+            wire.sent(4, n1.at[0:HALO])
+
+        @pl.when(takes_prev)
+        def _():
+            wire.sent(5, n1.at[0:HALO])
+
+    hbm = pl.BlockSpec(memory_space=pl.ANY)
+    vmem = pl.BlockSpec(memory_space=pltpu.VMEM)
+    half = lambda *shape: jax.ShapeDtypeStruct(shape, BF16)
+    full = lambda *shape: jax.ShapeDtypeStruct(shape, F32)
+    b16 = lambda *shape: pltpu.VMEM(shape, BF16)
+    b32 = lambda *shape: pltpu.VMEM(shape, F32)
+    slots = base + 27 * 3
     return pl.pallas_call(
         body,
-        in_specs=[pl.BlockSpec(memory_space=pltpu.VMEM)] * count,
-        out_specs=[pl.BlockSpec(memory_space=pl.ANY)] * count,
-        out_shape=[jax.ShapeDtypeStruct((4,) + s.shape, s.dtype) for s in shards],
+        in_specs=[hbm, vmem, hbm, hbm, hbm, vmem, vmem, vmem, vmem],
+        out_specs=[vmem] * 11 + [hbm] * 2 + [vmem] * 4,
+        out_shape=[
+            half(n, dm, 4 * cw), half(dm, win), half(dm, rows), half(dm, rows), half(dm, rows),
+            half(n, rows, cw), half(n, win, cw), half(n, win, cw), half(n, rows, cw), full(n * pairs, rows, 2), half(n, rows, cw),
+            half(rows, 2 * hw), half(rows, 2 * hw), full(1, 2 * hw), full(rows, dm), half(rows, dm), full(1, 4 * dm),
+        ],
         scratch_shapes=[
-            pltpu.SemaphoreType.DMA((27 * count,)),
-            pltpu.SemaphoreType.DMA((27 * count,)),
-            pltpu.SemaphoreType.DMA((count,)),
+            b16(n, dm, ffw), b16(n, ffw, dm), b16(win, dm), b32(rows, dm), b16(rows, dm), b32(rows, dm),
+            b16(rows, 2 * hw), b16(rows, 2 * hw), b32(n, 1, length),
+            pltpu.SemaphoreType.DMA((slots,)), pltpu.SemaphoreType.DMA((slots,)), pltpu.SemaphoreType.DMA((4,)),
+            pltpu.SemaphoreType.DMA((4 * n,)),
         ],
-        compiler_params=pltpu.CompilerParams(collective_id=0, has_side_effects=True, vmem_limit_bytes=VMEM),
-    )(*shards)
+        compiler_params=pltpu.CompilerParams(collective_id=0, has_side_effects=True, vmem_limit_bytes=VMEM_ALL),
+    )(tokens, cot, pack, w_up, w_down, small, bias, qseg, kseg)
 
 
 class Reduce:
@@ -1168,23 +1451,6 @@
     near = -(-LONGEST // rows)
     own = (near - 1) * rows
     win = own + rows + 2 * HALO
-    halo = [
-        lax.ppermute(tokens, "mp", [((i + j) % near, i) for i in range(near)]) for j in range(1, near)
-    ]
-    before = lax.ppermute(tokens[-HALO:], "mp", [(i - 1, i) for i in range(near, mp)])
-    behind = lax.ppermute(tokens[:HALO], "mp", [(i + 1, i) for i in range(near - 1, mp - 1)])
-    small_vec = jnp.concatenate([b_query, b_value, b_up])
-    if fast:
-        vecs = [small_vec] + [
-            lax.ppermute(small_vec, "mp", [((i + d) % mp, i) for i in range(mp)]) for d in range(1, mp)
-        ]
-        vecs = jnp.stack(vecs)
-    else:
-        vecs = relative(lax.all_gather(small_vec, "mp", axis=0, tiled=False), z)
-    bq_all, bv_all = vecs[:, :cw], vecs[:, cw : 2 * cw]
-    bu_all = vecs[:, 2 * cw :].reshape(mp, 2, ffw // 2).transpose(1, 0, 2)
-    bu_all = core_first(bu_all, core, 0).reshape(mp * ffw)
-
     is_near = z < near
     seg_parts = [
         jnp.where(is_near, lax.dynamic_slice_in_dim(segments, lax.rem(z + j, near) * rows, rows), -1)
@@ -1203,44 +1469,62 @@
     info = jnp.stack([is_near.astype(jnp.int32), core]).astype(jnp.int32)
 
     pack = jnp.concatenate([w_query, w_key, w_value, w_out.T], axis=1)
+    hw = mp * ffw // 2
     if fast:
-        packed, up_all, down_all = gather_call([pack, w_up, w_down])
+        small = jnp.stack([f32(v) for v in (ln1_gain, ln1_bias, ln2_gain, ln2_bias, b_out, b_down)])
+        bias = f32(jnp.concatenate([b_query, b_value, b_up]))[None]
+        (
+            packed, n1_t, n2_t, cot_t, ghb_t, q, k, v, attn, lse, g_attn, active, g_upper, g_b_up, g_hidden, output, done
+        ) = front_call(tokens, cotangent, pack, w_up, w_down, bias, small, qseg, kseg, own)
+        done_d, done_u, gp, dq, dk, dv = back_call(
+            cot_t, active, n2_t, g_upper, ghb_t, n1_t, q, k, v, attn, g_attn, lse, qseg, kseg, own, near
+        )
+        sums = [done[0]]
     else:
+        halo = [
+            lax.ppermute(tokens, "mp", [((i + j) % near, i) for i in range(near)]) for j in range(1, near)
+        ]
+        before = lax.ppermute(tokens[-HALO:], "mp", [(i - 1, i) for i in range(near, mp)])
+        behind = lax.ppermute(tokens[:HALO], "mp", [(i + 1, i) for i in range(near - 1, mp - 1)])
+        small_vec = jnp.concatenate([b_query, b_value, b_up])
+        vecs = relative(lax.all_gather(small_vec, "mp", axis=0, tiled=False), z)
+        bq_all, bv_all = vecs[:, :cw], vecs[:, cw : 2 * cw]
+        bu_all = vecs[:, 2 * cw :].reshape(mp, 2, ffw // 2).transpose(1, 0, 2)
+        bu_all = core_first(bu_all, core, 0).reshape(mp * ffw)
+
         packed, up_all, down_all = (gather_any(w, z) for w in (pack, w_up, w_down))
 
-    far = jnp.concatenate(halo, axis=0)
-    far = jnp.concatenate([far[:-HALO], far[-HALO:] + before], axis=0)
-    tok_win = jnp.concatenate([far, tokens, behind, jnp.zeros((HALO, dm), tokens.dtype)], axis=0)
-    hat_win, inv_win = norm_rows(f32(tok_win))
-    n1w = (hat_win * f32(ln1_gain) + f32(ln1_bias)).astype(BF16)
-    q, k, v = qkv_call(n1w, packed, bq_all, bv_all, own, rows, cw)
-    attn, lse = attn_fwd_call(info, q, k, v, qseg, kseg, own)
-    hidden, n2 = out_call(attn, packed, tokens, b_out, ln2_gain, ln2_bias)
-    output, g_n2, active, g_upper, g_b_up = ffn_call(
-        info[1:], n2, hidden, cotangent, up_all, down_all, bu_all, b_down, 2
-    )
-
-    gout = f32(cotangent)
-    hat2, inv2 = norm_rows(hidden)
-
-    def norm_back(g, hat, inv, gain):
-        gg = g * gain
-        first = jnp.mean(gg, axis=1, keepdims=True)
-        second = jnp.mean(gg * hat, axis=1, keepdims=True)
-        return inv * (gg - first - hat * second), jnp.sum(g * hat, axis=0), jnp.sum(g, axis=0)
-
-    g_hidden, g_gain2, g_bias2 = norm_back(g_n2, hat2, inv2, f32(ln2_gain))
-    g_hidden = g_hidden + gout
-    ghb = g_hidden.astype(BF16)
-
-    g_attn = jnp.stack([dot_nn(ghb, packed[d, :, 3 * cw :]).astype(BF16) for d in range(mp)])
-    if fast:
-        done_d, done_u, gp, dq, dk, dv = back_call(
-            cotangent.T, active, n2.T, g_upper, ghb.T, n1w.T, q, k, v, attn, g_attn, lse, qseg, kseg, own, near
+        far = jnp.concatenate(halo, axis=0)
+        far = jnp.concatenate([far[:-HALO], far[-HALO:] + before], axis=0)
+        tok_win = jnp.concatenate([far, tokens, behind, jnp.zeros((HALO, dm), tokens.dtype)], axis=0)
+        hat_win, inv_win = norm_rows(f32(tok_win))
+        n1w = (hat_win * f32(ln1_gain) + f32(ln1_bias)).astype(BF16)
+        q, k, v = qkv_call(n1w, packed, bq_all, bv_all, own, rows, cw)
+        attn, lse = attn_fwd_call(info, q, k, v, qseg, kseg, own)
+        hidden, n2 = out_call(attn, packed, tokens, b_out, ln2_gain, ln2_bias)
+        output, g_n2, active, g_upper, g_b_up = ffn_call(
+            info[1:], n2, hidden, cotangent, up_all, down_all, bu_all, b_down, 2
         )
-    else:
+
+        gout = f32(cotangent)
+        hat2, inv2 = norm_rows(hidden)
+
+        def norm_back(g, hat, inv, gain):
+            gg = g * gain
+            first = jnp.mean(gg, axis=1, keepdims=True)
+            second = jnp.mean(gg * hat, axis=1, keepdims=True)
+            return inv * (gg - first - hat * second), jnp.sum(g * hat, axis=0), jnp.sum(g, axis=0)
+
+        g_hidden, g_gain2, g_bias2 = norm_back(g_n2, hat2, inv2, f32(ln2_gain))
+        g_hidden = g_hidden + gout
+        ghb = g_hidden.astype(BF16)
+
+        g_attn = jnp.stack([dot_nn(ghb, packed[d, :, 3 * cw :]).astype(BF16) for d in range(mp)])
         dq, dk, dv = attn_bwd_call(info, q, k, v, attn, g_attn, lse, qseg, kseg, own)
+        n1 = n1w[own : own + rows]
+        sums = [jnp.sum(g_hidden, axis=0), g_gain2, g_bias2, jnp.sum(gout, axis=0)]
     halves = dq.shape[0]
+
     def shards(v, width):
         if v.shape[0] == 2:
             v = core_first(v.reshape(2, mp, width // 2), core, 0).transpose(1, 0, 2)
@@ -1250,8 +1534,7 @@
     gbv = shards(jnp.sum(f32(dv), axis=1), cw)
     gbu = core_first(g_b_up.reshape(2, mp, ffw // 2), core, 0).transpose(1, 0, 2)
     gbu = jnp.roll(gbu.reshape(mp, ffw), z, axis=0).reshape(-1)
-    sums = [jnp.sum(g_hidden, axis=0), g_gain2, g_bias2, jnp.sum(gout, axis=0), gbq, gbv, gbu]
-    n1 = n1w[own : own + rows]
+    sums = sums + [gbq, gbv, gbu]
     if fast:
         vec = jnp.concatenate([jnp.zeros((2 * dm,), F32)] + sums)[None]
         done_p, g_in, vec = finish_call(gp, dq, dk, dv, packed, tokens, ln1_gain, vec, own)

time: 493 us -> 410 us (0.83)
  Pallas kernels: 414 us -> 384 us
  local copies, waits for them, and re-layouts: 30.2 us -> 10.4 us
  other arithmetic: 26.2 us -> 14 us
  starting transfers between devices: 11.1 us -> 0 us
  matrix products: 5.92 us -> 0 us
    pallas_call x1, Pallas kernels: 144 us -> 116 us  [back_call(): pl.pallas_call(body, in_specs=[hbm] * 6 + [vmem] * 8, out_specs=[vmem, vm...]
    ppermute x6 -> x0, starting transfers between devices: 11.1 us -> none  [the longest x3 7 us: local(): lax.ppermute(small_vec, 'mp', [((i + d) % mp, i) for i in range(mp)])]
    pallas_call x5 -> x1, Pallas kernels: 176 us -> 167 us  [front_call(): pl.pallas_call(body, in_specs=[hbm, vmem, hbm, hbm, hbm, vmem, vmem, vmem...]
    pallas_call x1, Pallas kernels: 82 us -> 89.3 us  [finish_call(): pl.pallas_call(body, in_specs=[hbm] + [vmem] * 7, out_specs=[vmem] * 3, o...]
    reduce_sum x6 -> x0, other arithmetic: 6.33 us -> none  [the longest x1 3.21 us: norm_back(): jnp.sum(g * hat, axis=0)]
    dot_general x4 -> x0, matrix products: 5.92 us -> none  [dot_nn(): lax.dot_general(a, b, (((1,), (0,)), ((), ())), preferred_element_type=F32)]
    unnamed x64 -> x28, local copies, waits for them, and re-layouts: 7.83 us -> 2.89 us
  transfers between devices with their start and end apart: 6 -> 0, of which waited for: 0 -> 0; matrix products, arithmetic and copies ran while one was open for 3% -> 0% of each run, Pallas kernels for 21% -> 0%
where the time goes in v5:
time: 410 us; the launch traced here: 409 us
  Pallas kernels  384 us (94%)
  other arithmetic  14 us (3%)
  local copies, waits for them, and re-layouts  10.4 us (3%)
    pallas_call x1, Pallas kernels, front_call(): pl.pallas_call(body, in_specs=[hbm, vmem, hbm, hbm, hbm, vmem, vmem, vmem...  167 us
    pallas_call x1, Pallas kernels, back_call(): pl.pallas_call(body, in_specs=[hbm] * 6 + [vmem] * 8, out_specs=[vmem, vm...  116 us
    pallas_call x1, Pallas kernels, finish_call(): pl.pallas_call(body, in_specs=[hbm] + [vmem] * 7, out_specs=[vmem] * 3, o...  89.3 us
    pallas_call x3, Pallas kernels, place_grads(): pl.pallas_call(body, in_specs=[pl.BlockSpec(memory_space=pltpu.SMEM), pl....  12.2 us

profile of v5, /device:TPU:0, one launch (start us, length us, event | category | flops | bytes accessed | tf_op | source)
XLA Modules:
  0.0 409.1 jit_solution(8923233301391100255)
XLA Ops:
  0.7 0.8 dynamic-slice_select_fusion
  1.5 0.8 broadcast_select_fusion
  2.4 0.1 concatenate.37
  2.4 0.6 broadcast_in_dim.26.ks_ref
  3.0 0.9 copy.37.qs_ref
  3.9 0.7 stack.41.gain_ref
  4.6 0.0 copy-start.3
  4.6 0.7 stack.42
  5.3 0.7 stack.43
  6.0 0.7 stack.44
  6.6 0.7 stack.45
  7.3 0.7 stack.46
  8.1 0.0 copy-done.3
  8.1 0.6 stack.48.small_ref
  8.7 1.2 copy.36
  9.9 0.0 copy-start.7
  10.0 0.0 copy-start.8
  10.0 0.0 copy-start.9
  10.0 3.0 pad_maximum_fusion.pack_ref
  13.0 0.0 copy-done.7
  13.0 0.0 copy-done.8
  13.0 0.0 copy-done.9
  13.0 0.6 maximum_convert_fusion.bias_ref
  13.6 166.5 %shard_map.305 = (bf16[4,1024,1024]{2,1,0:T(8,128)(2,1)}, bf16[1024,1152]{1,0:T(8,128)(2,1)}, bf16[1024,512]{1,0:T(8,128)(2,1)}, bf16[1024,512]{1,0:T(8,128)(2,1...) custom-call(bf16[512,1024]{1,0:T(8,128)(2,1)} %x_ref.1, ...), custom_call_target="tpu_custom_call" | custom-call | tf_op jit(solution)/shard_map/pallas_call | solution.py:831
  180.2 115.8 %shard_map.306 = (bf16[8,256,512]{2,1,0:T(8,128)(2,1)}, bf16[8,256,512]{2,1,0:T(8,128)(2,1)}, bf16[1024,2048]{1,0:T(8,128)(2,1)}, bf16[2,512,512]{2,1,0:T(8,128)...) custom-call(bf16[1024,512]{1,0:T(8,128)(2,1)} %get-tuple-element.49.cot_ref, ...), custom_call_target="tpu_custom_call" | custom-call | tf_op jit(solution)/shard_map/pallas_call | solution.py:1164
  296.0 0.0 copy-start.6
  296.0 0.0 copy-start.5
  296.0 1.4 convert_reduce_fusion.1
  297.4 2.0 convert_reduce_fusion
  299.5 0.0 copy-done.6
  299.6 0.5 broadcast.9
  300.1 0.0 copy-done.5
  300.1 0.7 reduce.3
  300.9 0.0 copy-start.2
  300.9 0.6 copy-done.2
  301.5 89.3 %shard_map.307 = (bf16[8,256,512]{2,1,0:T(8,128)(2,1)}, f32[512,1024]{1,0:T(8,128)}, f32[1,12288]{1,0:T(1,128)}) custom-call(bf16[1024,2048]{1,0:T(8,128)(2,1)} %get-tuple-element.61.gp_ref, bf16[2,512,512]{2,1,0:T(8,128)(2,1)} %get-tuple-element.62.dq_ref, bf16[2,1152,512]{2,1,0:T(8,128)(2,1)} %get-tuple-element.63.dk_ref, ...), custom_call_target="tpu_custom_call" | custom-call | tf_op jit(solution)/shard_map/pallas_call | solution.py:1337
  390.8 0.0 copy-start
  390.9 0.6 pad_add_fusion.c_ref
  391.4 3.9 shard_map.308
  395.4 0.0 copy-done
  395.4 3.3 add.58
  398.7 3.9 shard_map.309
  402.6 0.0 copy-start.4
  402.6 0.0 copy-start.1
  402.6 4.4 %shard_map.310 = f32[1024,1024]{1,0:T(8,128)} custom-call(s32[3]{0:T(128)} %pad_add_fusion.c_ref, bf16[8,256,512]{2,1,0:T(8,128)(2,1)} %get-tuple-element.77.f_ref), custom_call_target="tpu_custom_call" | custom-call | bytes 6291456 | tf_op jit(solution)/shard_map/pallas_call | solution.py:1388
  407.0 0.0 copy-done.4
  407.0 0.6 fusion.8
  407.6 0.6 constant_dynamic-slice_fusion.1
  408.2 0.0 copy-done.1
  408.2 1.0 copy.48
  (20 shorter events, 0.2 us)
Async XLA Ops:
  4.6 3.5 copy-start.3
  9.9 3.0 copy-start.7
  10.0 3.0 copy-start.8
  10.0 3.0 copy-start.9
  296.0 3.6 copy-start.6
  296.0 4.2 %copy-start.5 = (f32[1,4096]{1,0:T(1,128)S(1)}, f32[1,4096]{1,0:T(1,128)}, u32[]{:S(2)}) copy-start(f32[1,4096]{1,0:T(1,128)} %get-tuple-element.67) | copy-start | bytes 49156
  300.9 0.6 copy-start.2
  390.8 4.6 %copy-start = (f32[512,1024]{1,0:T(8,128)S(1)}, f32[512,1024]{1,0:T(8,128)}, u32[]{:S(2)}) copy-start(f32[512,1024]{1,0:T(8,128)} %get-tuple-element.69) | copy-start | bytes 6291460
  402.6 4.4 %copy-start.4 = (f32[1,12288]{1,0:T(1,128)S(1)}, f32[1,12288]{1,0:T(1,128)}, u32[]{:S(2)}) copy-start(f32[1,12288]{1,0:T(1,128)} %get-tuple-element.70) | copy-start | bytes 147460
  402.6 5.6 %copy-start.1 = (bf16[512,1024]{1,0:T(8,128)(2,1)S(1)}, bf16[512,1024]{1,0:T(8,128)(2,1)}, u32[]{:S(2)}) copy-start(bf16[512,1024]{1,0:T(8,128)(2,1)} %get-tuple-element.110) | copy-start | bytes 3145732

commit v6 on v5

--- a/solution.py
+++ b/solution.py
@@ -11,6 +11,7 @@
 LONGEST = 900
 HALO = 64
 PAIR = 128
+SPAN = 400
 EPS = 1e-06
 NEG = -1e30
 VMEM = 60 * 1024 * 1024
@@ -525,7 +526,7 @@
     return begin, first, second, third, done, drain
 
 
-def front_call(tokens, cot, pack, w_up, w_down, bias, small, qseg, kseg, own):
+def front_call(tokens, cot, pack, w_up, w_down, small, qseg, kseg, own):
     rows, dm = tokens.shape
     cw = pack.shape[1] // 4
     ffw = w_up.shape[1]
@@ -537,11 +538,11 @@
     strip = 128
     per = rows // strip
     scale = HEAD_DIM**-0.5
-    length = bias.shape[1]
+    length = small.shape[1] - 6 * dm
     base = 6
 
     def body(
-        tok_ref, cot_ref, pack_ref, up_ref, down_ref, small_ref, bias_ref, qs_ref, ks_ref,
+        tok_ref, cot_ref, pack_ref, up_ref, down_ref, small_ref, qs_ref, ks_ref,
         packed, n1t, n2t, cott, ghbt, q_ref, k_ref, v_ref, a_ref, l_ref, ga_ref, act_ref, gup_ref, gbu_ref, gh_ref, o_ref, sum_ref,
         up, down, n1, hid, n2, acc, act, gup, biases, xs, xr, ls, fs,
     ):
@@ -561,12 +562,17 @@
         for c in local:
             c.start()
         place.meet()
+        bias_ref = small_ref.at[:, 6 * dm : 6 * dm + length]
         for d in (1, 2, 3):
             wire.start(d - 1, bias_ref, biases.at[d], place.along(4 - d))
 
-        @pl.when(long)
+        @pl.when(z == 0)
         def _():
             wire.start(3, tok_ref, n1.at[0:own], swap)
+
+        @pl.when(z == 1)
+        def _():
+            wire.start(3, tok_ref.at[0:SPAN], n1.at[0:SPAN], swap)
 
         @pl.when(takes_next)
         def _():
@@ -580,19 +586,24 @@
             gather_steps(place, wire, base + 27 * g, src, dst)
             for g, (src, dst) in enumerate(((pack_ref, packed), (up_ref, up), (down_ref, down)))
         ]
-        items = [(0, 1), (0, 3), (0, 2), (1, 1), (2, 1), (1, 3), (2, 3), (1, 2), (2, 2)]
-        for g, d in items:
-            groups[g][0](d)
+        for g in range(3):
+            for d in (1, 2, 3):
+                groups[g][0](d)
+
+        def near_shard(i):
+            return lax.rem(4 - z + i, 3) + 1
+
+        items = [(0, 0), (0, 1), (0, 2), (1, 0), (2, 0), (1, 1), (2, 1), (1, 2), (2, 2)]
 
         def relay(i):
             for lag in range(3):
                 if 0 <= i - lag < len(items):
-                    g, d = items[i - lag]
-                    groups[g][1 + lag](d)
-
-        def arrived(d, *which):
+                    g, j = items[i - lag]
+                    groups[g][1 + lag](near_shard(j))
+
+        def arrived(j, *which):
             for g in which:
-                groups[g][4](d)
+                groups[g][4](near_shard(j))
 
         def turns(i, table):
             for t, f in table.items():
@@ -602,12 +613,16 @@
                     f()
 
         def shard_at(k):
-            return k + (k // 2) * (5 - 2 * k)
+            return near_shard(k + 2) * ((k + 3) // 4)
 
         def strip_at(i, start=0):
             return pl.ds(pl.multiple_of(start + i * strip, strip), strip)
 
-        row = lambda i: small_ref[i : i + 1, :]
+        row = lambda i: small_ref[:, i * dm : (i + 1) * dm]
+
+        @pl.when(z == 0)
+        def _():
+            n1[SPAN:own, :] = jnp.zeros((own - SPAN, dm), BF16)
 
         @pl.when(takes_prev)
         def _():
@@ -645,8 +660,15 @@
 
         local[0].wait()
         lax.fori_loop(0, per, norm_own, 0)
-
-        @pl.when(long)
+        for c in local[1:]:
+            c.wait()
+        relay(0)
+
+        @pl.when(z == 0)
+        def _():
+            wire.landed(3, n1.at[0:SPAN], swap)
+
+        @pl.when(z == 1)
         def _():
             wire.landed(3, n1.at[0:own], swap)
 
@@ -662,8 +684,7 @@
         norm1((own + rows) // strip)
         for d in (1, 2, 3):
             wire.landed(d - 1, biases.at[d], place.along(d))
-        for c in local[1:]:
-            c.wait()
+        relay(1)
 
         def attend(big, d, p):
             at = pl.ds(pl.multiple_of(p * PAIR, PAIR), PAIR)
@@ -682,15 +703,7 @@
                 a_ref[d, qs : qs + qn, at] = jnp.concatenate(outs, axis=1).astype(BF16)
 
         def heads(kk, carry):
-            turns(
-                kk,
-                {
-                    0: lambda: relay(0),
-                    1: lambda: (relay(1), relay(2), relay(3), arrived(1, 0)),
-                    2: lambda: (relay(4), arrived(3, 0)),
-                    3: lambda: (relay(5), arrived(2, 0)),
-                },
-            )
+            turns(kk, {j + 1: functools.partial(arrived, j, 0) for j in range(3)})
             d = shard_at(kk)
             q_ref[d] = (dot_nn(n1[own : own + rows, :], packed[d, :, 0:cw]) + biases[d, :, 0:cw]).astype(BF16)
             k_ref[d] = dot_nn(n1[...], packed[d, :, cw : 2 * cw]).astype(BF16)
@@ -705,6 +718,7 @@
                 def _():
                     attend(False, d, p)
 
+                turns(kk * pairs + p, {pairs * j: functools.partial(relay, 2 + j) for j in range(4)})
                 return inner
 
             lax.fori_loop(0, pairs, one, 0)
@@ -741,9 +755,10 @@
                 i,
                 {
                     1: lambda: relay(7),
-                    2: lambda: (relay(8), arrived(1, 1, 2)),
-                    3: lambda: relay(9),
-                    4: lambda: (relay(10), arrived(3, 1, 2)),
+                    2: lambda: arrived(0, 1, 2),
+                    3: lambda: relay(8),
+                    4: lambda: (arrived(1, 1, 2), relay(9)),
+                    5: lambda: relay(10),
                     6: lambda: arrived(2, 1, 2),
                 },
             )
@@ -809,9 +824,13 @@
         for d in (1, 2, 3):
             wire.sent(d - 1, biases.at[d])
 
-        @pl.when(long)
+        @pl.when(z == 0)
         def _():
             wire.sent(3, n1.at[0:own])
+
+        @pl.when(z == 1)
+        def _():
+            wire.sent(3, n1.at[0:SPAN])
 
         @pl.when(takes_next)
         def _():
@@ -830,7 +849,7 @@
     slots = base + 27 * 3
     return pl.pallas_call(
         body,
-        in_specs=[hbm, vmem, hbm, hbm, hbm, vmem, vmem, vmem, vmem],
+        in_specs=[hbm, vmem, hbm, hbm, hbm, vmem, vmem, vmem],
         out_specs=[vmem] * 11 + [hbm] * 2 + [vmem] * 4,
         out_shape=[
             half(n, dm, 4 * cw), half(dm, win), half(dm, rows), half(dm, rows), half(dm, rows),
@@ -844,7 +863,7 @@
             pltpu.SemaphoreType.DMA((4 * n,)),
         ],
         compiler_params=pltpu.CompilerParams(collective_id=0, has_side_effects=True, vmem_limit_bytes=VMEM_ALL),
-    )(tokens, cot, pack, w_up, w_down, small, bias, qseg, kseg)
+    )(tokens, cot, pack, w_up, w_down, small, qseg, kseg)
 
 
 class Reduce:
@@ -1354,45 +1373,56 @@
     )(gp, dq, dk, dv, packed, tokens, gain[None], vec)
 
 
-def place_grads(coords, done, mode):
-    _, q, w = done.shape
+def place_grads(coords, down, up, pack):
+    _, q, w = up.shape
     e = q // 2
     dm = 4 * q
     lanes = w // 4
 
-    def body(c_ref, f_ref, *outs):
-        for off in range(8):
-            y = lax.bitwise_xor(c_ref[0], off >> 2)
-            x = lax.bitwise_xor(c_ref[1], (off >> 1) & 1)
-            k = lax.bitwise_xor(c_ref[2], off & 1)
-            for part in range(2):
-                val = f_ref[off, part * e : (part + 1) * e, :].astype(F32)
-                block = x * 2 + y if part == 0 else 4 + y * 2 + x
-                rows = pl.ds(pl.multiple_of(block * e, e), e)
-                if mode == "up":
-                    outs[0][rows, pl.ds(pl.multiple_of(k * w, w), w)] = val
-                elif mode == "down":
-                    outs[0][pl.ds(pl.multiple_of(k * w, w), w), rows] = val.T
-                else:
-                    at = pl.ds(pl.multiple_of(k * lanes, lanes), lanes)
-                    for m in range(3):
-                        outs[m][rows, at] = val[:, m * lanes : (m + 1) * lanes]
-                    outs[3][at, rows] = val[:, 3 * lanes :].T
-
-    if mode == "up":
-        shapes = [(dm, 2 * w)]
-    elif mode == "down":
-        shapes = [(2 * w, dm)]
-    else:
-        shapes = [(dm, w // 2)] * 3 + [(w // 2, dm)]
+    def spot(off, part, c):
+        y = lax.bitwise_xor(c[0], off // 4)
+        x = lax.bitwise_xor(c[1], lax.rem(off // 2, 2))
+        k = lax.bitwise_xor(c[2], lax.rem(off, 2))
+        return (1 - part) * (2 * x + y) + part * (4 + 2 * y + x), k
+
+    def across(off, part, c):
+        return spot(off, part, c)
+
+    def flipped(off, part, c):
+        block, k = spot(off, part, c)
+        return k, block
+
+    def body(c_ref, d_ref, u_ref, p_ref, gd_ref, gu_ref, gq_ref, gk_ref, gv_ref, go_ref):
+        gd_ref[...] = d_ref[0].astype(F32).T
+        gu_ref[...] = u_ref[0].astype(F32)
+        val = p_ref[0].astype(F32)
+        for m, ref in enumerate((gq_ref, gk_ref, gv_ref)):
+            ref[...] = val[:, m * lanes : (m + 1) * lanes]
+        go_ref[...] = val[:, 3 * lanes :].T
+
+    piece = pl.BlockSpec((1, e, w), lambda off, part, c: (off, part, 0))
     return pl.pallas_call(
         body,
-        in_specs=[pl.BlockSpec(memory_space=pltpu.SMEM), pl.BlockSpec(memory_space=pltpu.VMEM)],
-        out_specs=[pl.BlockSpec(memory_space=pltpu.VMEM)] * len(shapes),
-        out_shape=[jax.ShapeDtypeStruct(s, F32) for s in shapes],
-        compiler_params=pltpu.CompilerParams(vmem_limit_bytes=VMEM),
-        cost_estimate=pl.CostEstimate(flops=0, bytes_accessed=12 * dm * w, transcendentals=0),
-    )(coords, done)
+        grid_spec=pltpu.PrefetchScalarGridSpec(
+            num_scalar_prefetch=1,
+            grid=(8, 2),
+            in_specs=[piece] * 3,
+            out_specs=[
+                pl.BlockSpec((w, e), flipped),
+                pl.BlockSpec((e, w), across),
+                pl.BlockSpec((e, lanes), across),
+                pl.BlockSpec((e, lanes), across),
+                pl.BlockSpec((e, lanes), across),
+                pl.BlockSpec((lanes, e), flipped),
+            ],
+        ),
+        out_shape=[
+            jax.ShapeDtypeStruct(shape, F32)
+            for shape in ((2 * w, dm), (dm, 2 * w), (dm, w // 2), (dm, w // 2), (dm, w // 2), (w // 2, dm))
+        ],
+        compiler_params=params("arbitrary", "arbitrary"),
+        cost_estimate=pl.CostEstimate(flops=0, bytes_accessed=36 * dm * w, transcendentals=0),
+    )(coords, down, up, pack)
 
 
 def relative(stack, z):
@@ -1440,7 +1470,7 @@
     ffw = w_up.shape[1]
     mp = lax.axis_size("mp")
     dp = lax.axis_size("dp")
-    fast = mp == 4 and dp == 8 and rows % 256 == 0 and cw == 2 * PAIR and rows < LONGEST <= 2 * rows
+    fast = mp == 4 and dp == 8 and rows % 256 == 0 and cw == 2 * PAIR and rows < LONGEST <= rows + SPAN <= 2 * rows
     z = lax.axis_index("mp")
     me = lax.axis_index("dp")
     core = lax.rem(me, 2)
@@ -1471,11 +1501,11 @@
     pack = jnp.concatenate([w_query, w_key, w_value, w_out.T], axis=1)
     hw = mp * ffw // 2
     if fast:
-        small = jnp.stack([f32(v) for v in (ln1_gain, ln1_bias, ln2_gain, ln2_bias, b_out, b_down)])
-        bias = f32(jnp.concatenate([b_query, b_value, b_up]))[None]
+        small = jnp.concatenate([ln1_gain, ln1_bias, ln2_gain, ln2_bias, b_out, b_down, b_query, b_value, b_up])
+        small = f32(small)[None]
         (
             packed, n1_t, n2_t, cot_t, ghb_t, q, k, v, attn, lse, g_attn, active, g_upper, g_b_up, g_hidden, output, done
-        ) = front_call(tokens, cotangent, pack, w_up, w_down, bias, small, qseg, kseg, own)
+        ) = front_call(tokens, cotangent, pack, w_up, w_down, small, qseg, kseg, own)
         done_d, done_u, gp, dq, dk, dv = back_call(
             cot_t, active, n2_t, g_upper, ghb_t, n1_t, q, k, v, attn, g_attn, lse, qseg, kseg, own, near
         )
@@ -1541,9 +1571,7 @@
         vec = vec[0]
         g_tokens = g_in + g_hidden
         coords = jnp.stack([y, x, core]).astype(jnp.int32)
-        (g_w_down,) = place_grads(coords, done_d, "down")
-        (g_w_up,) = place_grads(coords, done_u, "up")
-        g_w_query, g_w_key, g_w_value, g_w_out = place_grads(coords, done_p, "pack")
+        g_w_down, g_w_up, g_w_query, g_w_key, g_w_value, g_w_out = place_grads(coords, done_d, done_u, done_p)
     else:
         g_own, g_far, g_next = norm1_back_call(dq, dk, dv, packed, info, own)
         back = g_own

time: 410 us -> 395 us (0.963)
  Pallas kernels: 384 us -> 374 us
  local copies, waits for them, and re-layouts: 10.4 us -> 6.3 us
    pallas_call x1, Pallas kernels: 167 us -> 149 us  [front_call(): pl.pallas_call(body, in_specs=[hbm, vmem, hbm, hbm, hbm, vmem, vmem, vmem...]
    pallas_call x1, Pallas kernels: 116 us -> 127 us  [back_call(): pl.pallas_call(body, in_specs=[hbm] * 6 + [vmem] * 8, out_specs=[vmem, vm...]
    pallas_call x1, Pallas kernels: 89.3 us -> 81.9 us  [finish_call(): pl.pallas_call(body, in_specs=[hbm] + [vmem] * 7, out_specs=[vmem] * 3, o...]
    another operation x7 -> x0, local copies, waits for them, and re-layouts: 4.16 us -> none  [local(): jnp.stack([f32(v) for v in (ln1_gain, ln1_bias, ln2_gain, ln2_bias, b_out...]
    pallas_call x3 -> x1, Pallas kernels: 12.2 us -> 14.9 us  [place_grads(): pl.pallas_call(body, grid_spec=pltpu.PrefetchScalarGridSpec(num_scalar_pr...]
where the time goes in v6:
time: 395 us
  Pallas kernels  374 us (95%)
  other arithmetic  13.7 us (3%)
  local copies, waits for them, and re-layouts  6.3 us (2%)
    pallas_call x1, Pallas kernels, front_call(): pl.pallas_call(body, in_specs=[hbm, vmem, hbm, hbm, hbm, vmem, vmem, vmem...  149 us
    pallas_call x1, Pallas kernels, back_call(): pl.pallas_call(body, in_specs=[hbm] * 6 + [vmem] * 8, out_specs=[vmem, vm...  127 us
    pallas_call x1, Pallas kernels, finish_call(): pl.pallas_call(body, in_specs=[hbm] + [vmem] * 7, out_specs=[vmem] * 3, o...  81.9 us
    pallas_call x1, Pallas kernels, place_grads(): pl.pallas_call(body, grid_spec=pltpu.PrefetchScalarGridSpec(num_scalar_pr...  14.9 us

profile of v6, /device:TPU:0, one launch (start us, length us, event | category | flops | bytes accessed | tf_op | source)
XLA Modules:
  0.0 394.8 jit_solution(7238284719063663068)
XLA Ops:
  0.7 0.8 dynamic-slice_select_fusion
  1.5 0.8 broadcast_select_fusion
  2.4 0.1 concatenate.55
  2.4 0.6 broadcast_in_dim.26.ks_ref
  3.0 0.9 copy.37.qs_ref
  3.9 1.2 copy.36
  5.1 0.0 copy-start.6
  5.2 0.0 copy-start.8
  5.2 0.0 copy-start.9
  5.2 0.0 copy-start.10
  5.2 0.0 copy-start.11
  5.2 0.0 copy-start.12
  5.2 0.0 copy-start.14
  5.2 0.0 copy-start.15
  5.2 0.0 copy-start.13
  5.3 3.0 pad_maximum_fusion.pack_ref
  8.3 0.0 copy-done.6
  8.3 0.0 copy-done.8
  8.3 0.0 copy-done.9
  8.3 0.0 copy-done.10
  8.3 0.0 copy-done.11
  8.4 0.0 copy-done.12
  8.4 0.0 copy-done.14
  8.4 0.0 copy-done.15
  8.4 0.0 copy-done.13
  8.5 0.6 convert_element_type.16.small_ref
  9.1 149.4 %shard_map.305 = (bf16[4,1024,1024]{2,1,0:T(8,128)(2,1)}, bf16[1024,1152]{1,0:T(8,128)(2,1)}, bf16[1024,512]{1,0:T(8,128)(2,1)}, bf16[1024,512]{1,0:T(8,128)(2,1...) custom-call(bf16[512,1024]{1,0:T(8,128)(2,1)} %x_ref.1, ...), custom_call_target="tpu_custom_call" | custom-call | tf_op jit(solution)/shard_map/pallas_call | solution.py:850
  158.5 127.4 %shard_map.306 = (bf16[8,256,512]{2,1,0:T(8,128)(2,1)}, bf16[8,256,512]{2,1,0:T(8,128)(2,1)}, bf16[1024,2048]{1,0:T(8,128)(2,1)}, bf16[2,512,512]{2,1,0:T(8,128)...) custom-call(bf16[1024,512]{1,0:T(8,128)(2,1)} %get-tuple-element.51.cot_ref, ...), custom_call_target="tpu_custom_call" | custom-call | tf_op jit(solution)/shard_map/pallas_call | solution.py:1183
  286.0 0.0 copy-start.5
  286.0 0.0 copy-start.4
  286.0 0.0 copy-start.7
  286.0 1.4 convert_reduce_fusion.1
  287.4 2.0 convert_reduce_fusion
  289.6 0.0 copy-done.5
  289.6 0.5 broadcast.9
  290.1 0.0 copy-done.4
  290.1 0.7 reduce.3
  290.9 0.0 copy-start.2
  290.9 0.0 copy-done.7
  290.9 0.6 concatenate.45.gain_ref
  291.5 0.0 copy-done.2
  291.5 81.9 %shard_map.307 = (bf16[8,256,512]{2,1,0:T(8,128)(2,1)}, f32[512,1024]{1,0:T(8,128)}, f32[1,12288]{1,0:T(1,128)}) custom-call(bf16[1024,2048]{1,0:T(8,128)(2,1)} %get-tuple-element.63.gp_ref, bf16[2,512,512]{2,1,0:T(8,128)(2,1)} %get-tuple-element.64.dq_ref, bf16[2,1152,512]{2,1,0:T(8,128)(2,1)} %get-tuple-element.65.dk_ref, ...), custom_call_target="tpu_custom_call" | custom-call | tf_op jit(solution)/shard_map/pallas_call | solution.py:1356
  373.5 0.6 pad_add_fusion.c_ref
  374.1 0.0 copy-start
  374.1 14.9 %shard_map.308 = (f32[1024,1024]{1,0:T(8,128)}, f32[1024,1024]{1,0:T(8,128)}, f32[1024,256]{1,0:T(8,128)}, f32[1024,256]{1,0:T(8,128)}, f32[1024,256]{1,0:T(8,128)}, /*index=5*/f32[256,1024]{1,0:T(8,128)}) custom-call(s32[3]{0:T(128)} %pad_add_fusion.c_ref, bf16[8,256,512]{2,1,0:T(8,128)(2,1)} %get-tuple-element.73.d_ref, ...), custom_call_target="tpu_custom_call" | custom-call | bytes 18874368 | tf_op jit(solution)/shard_map/pallas_call | solution.py:1404
  389.0 0.0 copy-done
  389.0 0.0 copy-start.3
  389.0 0.0 copy-start.1
  389.0 3.6 add.58
  392.6 0.0 copy-done.3
  392.6 0.6 fusion.8
  393.2 0.6 constant_dynamic-slice_fusion.1
  393.8 0.0 copy-done.1
  393.8 1.0 copy.56
  (25 shorter events, 0.2 us)
Async XLA Ops:
  5.1 3.1 copy-start.6
  5.2 3.1 copy-start.8
  5.2 3.1 copy-start.9
  5.2 3.1 copy-start.10
  5.2 3.2 copy-start.11
  5.2 3.2 copy-start.12
  5.2 3.2 copy-start.14
  5.2 3.2 copy-start.15
  5.2 3.2 copy-start.13
  286.0 3.6 copy-start.5
  286.0 4.2 %copy-start.4 = (f32[1,4096]{1,0:T(1,128)S(1)}, f32[1,4096]{1,0:T(1,128)}, u32[]{:S(2)}) copy-start(f32[1,4096]{1,0:T(1,128)} %get-tuple-element.69) | copy-start | bytes 49156
  286.0 4.9 %copy-start.7 = (bf16[1024]{0:T(1024)(128)(2,1)S(1)}, bf16[1024]{0:T(1024)(128)(2,1)}, u32[]{:S(2)}) copy-start(bf16[1024]{0:T(1024)(128)(2,1)} %param.22) | copy-start | bytes 6148
  290.9 0.6 copy-start.2
  374.1 14.9 %copy-start = (f32[512,1024]{1,0:T(8,128)S(1)}, f32[512,1024]{1,0:T(8,128)}, u32[]{:S(2)}) copy-start(f32[512,1024]{1,0:T(8,128)} %get-tuple-element.71) | copy-start | bytes 6291460
  389.0 3.6 copy-start.3
  389.0 4.8 %copy-start.1 = (bf16[512,1024]{1,0:T(8,128)(2,1)S(1)}, bf16[512,1024]{1,0:T(8,128)(2,1)}, u32[]{:S(2)}) copy-start(bf16[512,1024]{1,0:T(8,128)(2,1)} %get-tuple-element.114) | copy-start | bytes 3145732

commit v7 on v6

--- a/solution.py
+++ b/solution.py
@@ -543,7 +543,7 @@
 
     def body(
         tok_ref, cot_ref, pack_ref, up_ref, down_ref, small_ref, qs_ref, ks_ref,
-        packed, n1t, n2t, cott, ghbt, q_ref, k_ref, v_ref, a_ref, l_ref, ga_ref, act_ref, gup_ref, gbu_ref, gh_ref, o_ref, sum_ref,
+        packed, n1t, n2t, cott, ghbt, q_ref, k_ref, v_ref, a_ref, l_ref, ga_ref, act_ref, gup_ref, gh_ref, o_ref, vec_ref,
         up, down, n1, hid, n2, acc, act, gup, biases, xs, xr, ls, fs,
     ):
         place = Place()
@@ -634,6 +634,8 @@
 
         n1[own + rows + HALO :, :] = jnp.zeros((HALO, dm), BF16)
         biases[0] = bias_ref[...]
+        l_ref[...] = jnp.zeros_like(l_ref)
+        vec_ref[...] = jnp.zeros_like(vec_ref)
 
         def turn_cot(i, carry):
             cott[:, strip_at(i)] = cot_ref[strip_at(i), :].astype(F32).T.astype(BF16)
@@ -699,7 +701,9 @@
                     pr = jnp.exp(s - top)
                     total = jnp.sum(pr, axis=1, keepdims=True)
                     outs.append(dot_nn(pr.astype(BF16), vv[:, lanes]) / total)
-                    l_ref[d * pairs + p, qs : qs + qn, h : h + 1] = top + jnp.log(total)
+                    lane = lax.broadcasted_iota(jnp.int32, (qn, 2 * n * pairs), 1)
+                    seen = l_ref[qs : qs + qn, :]
+                    l_ref[qs : qs + qn, :] = jnp.where(lane == (d * pairs + p) * 2 + h, top + jnp.log(total), seen)
                 a_ref[d, qs : qs + qn, at] = jnp.concatenate(outs, axis=1).astype(BF16)
 
         def heads(kk, carry):
@@ -773,7 +777,8 @@
             act[:, to] = val
             gu = (dot_nt(cot_ref[...], down[d, at, :]) * slope).astype(BF16)
             gup[:, to] = gu
-            gbu_ref[:, to] = jnp.sum(gu.astype(F32), axis=0, keepdims=True)
+            unit = 8 * dm + lax.rem(z + d, n) * ffw + part
+            vec_ref[:, pl.ds(pl.multiple_of(unit, tile), tile)] = jnp.sum(gu.astype(F32), axis=0, keepdims=True)
             for c in out_copies(i, column(i)):
                 c.start()
             acc[...] += dot_nn(val, down[d, at, :])
@@ -790,7 +795,6 @@
             return carry
 
         lax.fori_loop(0, 2 * n, feed, 0)
-        sum_ref[...] = jnp.zeros_like(sum_ref)
 
         def back2(i, carry):
             at = strip_at(i)
@@ -806,7 +810,7 @@
             n2[at, :] = val.astype(BF16)
             ghbt[:, at] = val.T.astype(BF16)
             for j, v in enumerate((val, g * hat, g, gout)):
-                sum_ref[:, j * dm : (j + 1) * dm] += jnp.sum(v, axis=0, keepdims=True)
+                vec_ref[:, (2 + j) * dm : (3 + j) * dm] += jnp.sum(v, axis=0, keepdims=True)
             return carry
 
         lax.fori_loop(0, per, back2, 0)
@@ -850,11 +854,11 @@
     return pl.pallas_call(
         body,
         in_specs=[hbm, vmem, hbm, hbm, hbm, vmem, vmem, vmem],
-        out_specs=[vmem] * 11 + [hbm] * 2 + [vmem] * 4,
+        out_specs=[vmem] * 11 + [hbm] * 2 + [vmem] * 3,
         out_shape=[
             half(n, dm, 4 * cw), half(dm, win), half(dm, rows), half(dm, rows), half(dm, rows),
-            half(n, rows, cw), half(n, win, cw), half(n, win, cw), half(n, rows, cw), full(n * pairs, rows, 2), half(n, rows, cw),
-            half(rows, 2 * hw), half(rows, 2 * hw), full(1, 2 * hw), full(rows, dm), half(rows, dm), full(1, 4 * dm),
+            half(n, rows, cw), half(n, win, cw), half(n, win, cw), half(n, rows, cw), full(rows, 2 * n * pairs), half(n, rows, cw),
+            half(rows, 2 * hw), half(rows, 2 * hw), full(rows, dm), half(rows, dm), full(1, 8 * dm + 2 * hw),
         ],
         scratch_shapes=[
             b16(n, dm, ffw), b16(n, ffw, dm), b16(win, dm), b32(rows, dm), b16(rows, dm), b32(rows, dm),
@@ -883,14 +887,29 @@
             pltpu.SemaphoreType.DMA((Reduce.SLOTS,)),
         ]
 
-    def __init__(self, place, grad, landing, scratch):
+    def __init__(self, place, grad, landing, views, zb, send, recv):
         self.place, self.g, self.f = place, grad, landing
-        self.ra1, self.rb1, self.ra2, self.rb2, self.zb = scratch[:5]
-        self.wire = Wire(scratch[5], scratch[6], place.core)
+        self.ra1, self.rb1, self.ra2, self.rb2 = views
+        self.zb = zb
+        self.wire = Wire(send, recv, place.core)
         self.q = grad.shape[0] // 4
         self.e = self.q // 2
         self.w = grad.shape[1] // 4
 
+    @staticmethod
+    def of(place, grad, landing, scratch):
+        views = [lambda d, ref=ref: ref.at[d] for ref in scratch[:4]]
+        return Reduce(place, grad, landing, views, *scratch[4:])
+
+    @staticmethod
+    def within(place, grad, landing, spare, zb, send, recv):
+        q, w = grad.shape[0] // 4, grad.shape[1] // 4
+        bounds = (0, q, 2 * q, 2 * q + q // 2, 3 * q)
+        views = [
+            lambda d, a=a, b=b: spare.at[a:b, pl.ds(pl.multiple_of(d * w, w), w)] for a, b in zip(bounds[:-1], bounds[1:])
+        ]
+        return Reduce(place, grad, landing, views, zb, send, recv)
+
     def at(self, base, big, small=None):
         start = base * 2 * self.q + big * self.q + (0 if small is None else small * self.e)
         return pl.ds(pl.multiple_of(start, self.e), self.q if small is None else self.e)
@@ -903,8 +922,8 @@
 
     def one(self, d):
         p, wire = self.place, self.wire
-        wire.start(d, self.g.at[self.at(0, 1 - p.x), self.cols(d)], self.ra1.at[d], p.by_x)
-        wire.start(4 + d, self.g.at[self.at(1, 1 - p.y), self.cols(d)], self.rb1.at[d], p.by_y)
+        wire.start(d, self.g.at[self.at(0, 1 - p.x), self.cols(d)], self.ra1(d), p.by_x)
+        wire.start(4 + d, self.g.at[self.at(1, 1 - p.y), self.cols(d)], self.rb1(d), p.by_y)
 
     def two(self, d):
         p, wire, c = self.place, self.wire, self.cols(d)
@@ -912,23 +931,23 @@
             (0, self.ra1, self.ra2, self.at(0, p.x, 1 - p.y), self.eighth(1 - p.y), p.by_x, p.by_y),
             (4, self.rb1, self.rb2, self.at(1, p.y, 1 - p.x), self.eighth(1 - p.x), p.by_y, p.by_x),
         ):
-            wire.landed(slot + d, buf.at[d], dev)
-            self.g[at, c] = (self.g[at, c].astype(F32) + buf[d, mine, :].astype(F32)).astype(BF16)
-            wire.start(8 + slot + d, self.g.at[at, c], to.at[d], nxt)
+            wire.landed(slot + d, buf(d), dev)
+            self.g[at, c] = (self.g[at, c].astype(F32) + buf(d)[mine, :].astype(F32)).astype(BF16)
+            wire.start(8 + slot + d, self.g.at[at, c], to(d), nxt)
 
     def sums(self, d):
         p, wire, c = self.place, self.wire, self.cols(d)
-        wire.landed(8 + d, self.ra2.at[d], p.by_y)
-        wire.landed(12 + d, self.rb2.at[d], p.by_x)
+        wire.landed(8 + d, self.ra2(d), p.by_y)
+        wire.landed(12 + d, self.rb2(d), p.by_x)
         up = (
             self.g[self.at(0, p.x, p.y), c].astype(F32)
-            + self.ra1[d, self.eighth(p.y), :].astype(F32)
-            + self.ra2[d].astype(F32)
+            + self.ra1(d)[self.eighth(p.y), :].astype(F32)
+            + self.ra2(d)[...].astype(F32)
         )
         low = (
             self.g[self.at(1, p.y, p.x), c].astype(F32)
-            + self.rb1[d, self.eighth(p.x), :].astype(F32)
-            + self.rb2[d].astype(F32)
+            + self.rb1(d)[self.eighth(p.x), :].astype(F32)
+            + self.rb2(d)[...].astype(F32)
         )
         return up, low
 
@@ -949,11 +968,16 @@
             wire.landed(28 + s, self.zb.at[s - 1, e : 2 * e], p.along(4 - s))
             up = up + self.zb[s - 1, 0:e].astype(F32)
             low = low + self.zb[s - 1, e : 2 * e].astype(F32)
-        self.f[0, 0:e] = up.astype(BF16)
-        self.f[0, e : 2 * e] = low.astype(BF16)
-        wire.start(20, self.f.at[0], self.f.at[2], p.by_x)
-        wire.start(21, self.f.at[0], self.f.at[4], p.by_y)
-        wire.start(22, self.f.at[0], self.f.at[1], p.core)
+        ready = self.ra1(0)
+        ready[0:e, :] = up.astype(BF16)
+        ready[e : 2 * e, :] = low.astype(BF16)
+        wire.start(20, ready, self.f.at[2], p.by_x)
+        wire.start(21, ready, self.f.at[4], p.by_y)
+        wire.start(22, ready, self.f.at[1], p.core)
+        self.keep().start()
+
+    def keep(self):
+        return pltpu.make_async_copy(self.ra1(0), self.f.at[0], self.wire.send.at[16])
 
     def four(self):
         p, wire, e = self.place, self.wire, self.e
@@ -975,10 +999,10 @@
             self.wire.landed(slot, self.f.at[to], self.place.core)
         e, sent = self.e, self.wire.sent
         for d in range(4):
-            sent(d, self.ra1.at[d])
-            sent(4 + d, self.rb1.at[d])
-            sent(8 + d, self.ra2.at[d])
-            sent(12 + d, self.rb2.at[d])
+            sent(d, self.ra1(d))
+            sent(4 + d, self.rb1(d))
+            sent(8 + d, self.ra2(d))
+            sent(12 + d, self.rb2(d))
         for d in range(1, 4):
             sent(16 + d, self.zb.at[d - 1, 0:e])
             sent(28 + d, self.zb.at[d - 1, 0:e])
@@ -986,20 +1010,10 @@
             sent(slot, self.f.at[0])
         for slot in (23, 24):
             sent(slot, self.f.at[0, 0:e])
-
-    def sweep(self):
-        return [
-            functools.partial(f, d)
-            for f, d in (
-                (self.two, 1), (self.two, 2), (self.three, 1), (self.two, 3), (self.three, 2), (self.two, 0), (self.three, 3)
-            )
-        ]
-
-    def tail(self):
-        return [self.last, self.four, self.five, self.six]
-
-
-def back_call(cot, act, n2, gup, ghb, n1w, q, k, v, attn, gattn, lse, qseg, kseg, own, near):
+        self.keep().wait()
+
+
+def back_call(cot, act, n2, gup, ghb, n1w, packed, tokens, q, k, v, attn, gattn, lse, qseg, kseg, gain, vec, own):
     n, rows, cw = q.shape
     win = k.shape[1]
     dm = cot.shape[0]
@@ -1009,16 +1023,24 @@
     pairs = cw // PAIR
     scale = HEAD_DIM**-0.5
     each = len(Reduce.scratch(dm, w))
+    length = vec.shape[1]
+    strip = 128
 
     def body(
-        cot_ref, act_ref, n2_ref, gup_ref, ghb_ref, n1_ref, q_ref, k_ref, v_ref, a_ref, g_ref, l_ref, qs_ref, ks_ref,
-        fd, fu, gp_ref, dq, dk, dv,
-        cot2, act2, n22, gup2, ghb2, n12, gd, gu, dq_o, dk_o, dv_o, at2, dkt, dvt, xs, xr, ls, *scr,
+        cot_ref, act_ref, n2_ref, gup_ref, ghb_ref, n1_ref, w_ref, x_ref,
+        q_ref, k_ref, v_ref, a_ref, g_ref, l_ref, qs_ref, ks_ref, gain_ref, vec_ref,
+        fd, fu, fp, gi_ref, sum_ref,
+        wbuf, act2, gup2, n12, gd, gu, dq_o, dk_o, dv_o, at2, dq, dk, dv, dkt, dvt,
+        far_in, prev_in, next_in, nxt, va, vr, vz, zb, ps, pr_sem, xs, xr, ls, ws, *scr,
     ):
         place = Place()
-        core = place.k
-        big_z = place.z < near
+        core, z = place.k, place.z
+        long, gives_prev, gives_next = z < 2, z >= 2, jnp.logical_and(z >= 1, z < 3)
+        swap = {"dp": place.me, "mp": lax.rem(z + 1, 2)}
+        left_dev = {"dp": place.me, "mp": lax.rem(z + 3, 4)}
+        right_dev = {"dp": place.me, "mp": lax.rem(z + 1, 4)}
         wire = Wire(xs, xr, place.core)
+        cot2, n22, ghb2 = wbuf.at[0], wbuf.at[1], wbuf.at[2]
         whole = (
             (cot_ref, cot2, rows), (n2_ref, n22, rows), (ghb_ref, ghb2, rows), (n1_ref, n12, win)
         )
@@ -1059,8 +1081,9 @@
             wire.start(6 + d, a_ref.at[d, :, theirs], at2.at[rows : 2 * rows, to], place.core)
             at2[0:rows, to] = a_ref[d, :, mine]
 
-        down = Reduce(place, gd, fd, scr[:each])
-        up = Reduce(place, gu, fu, scr[each : 2 * each])
+        down = Reduce.of(place, gd, fd, scr[:each])
+        up = Reduce.of(place, gu, fu, scr[each : 2 * each])
+        heads = Reduce.within(place, act2, fp, gup2, zb, ps, pr_sem)
 
         def make(red, grad, left, right):
             def step(i, carry):
@@ -1076,6 +1099,20 @@
         make(down, gd, cot2, act2)
         take(1, 5)
         make(up, gu, n22, gup2)
+
+        def weights(t):
+            at = lax.rem(t, 3)
+            return pltpu.make_async_copy(w_ref.at[lax.rem(t, n)], wbuf.at[at], ws.at[at])
+
+        weights(0).start()
+        weights(1).start()
+
+        def turns(i, table):
+            for t, f in table.items():
+
+                @pl.when(i == t)
+                def _():
+                    f()
 
         def work(big, d, p):
             at = pl.ds(pl.multiple_of(p * PAIR, PAIR), PAIR)
@@ -1093,7 +1130,9 @@
                 for h in range(2):
                     lanes = slice(h * HEAD_DIM, (h + 1) * HEAD_DIM)
                     qh, kh, gh = qq[:, lanes] * BF16(scale), kk[:, lanes], gg[:, lanes]
-                    s = jnp.where(mask, dot_nt(qh, kh) - l_ref[d * pairs + p, qs : qs + qn, h : h + 1], NEG)
+                    lane = lax.broadcasted_iota(jnp.int32, (qn, 2 * n * pairs), 1)
+                    picked = jnp.where(lane == (d * pairs + p) * 2 + h, l_ref[qs : qs + qn, :], 0.0)
+                    s = jnp.where(mask, dot_nt(qh, kh) - jnp.sum(picked, axis=1, keepdims=True), NEG)
                     pr = jnp.exp(s)
                     dp = dot_nt(gh, vv[:, lanes])
                     delta = jnp.sum(prod[:, lanes], axis=1, keepdims=True)
@@ -1111,36 +1150,25 @@
             dk[rel, :, to] = dkt[...].T.astype(BF16)
             dv[rel, :, to] = dvt[...].T.astype(BF16)
 
-        todo = down.sweep() + up.sweep()
-        turns = [todo[2 * i : 2 * i + 2] for i in range(n * pairs)]
-        turns[-1] = todo[2 * (n * pairs - 1) :]
-
         def head_pair(i, carry):
             d, p = i // pairs, lax.rem(i, pairs)
 
-            @pl.when(big_z)
+            @pl.when(long)
             def _():
                 work(True, d, p)
 
-            @pl.when(jnp.logical_not(big_z))
+            @pl.when(jnp.logical_not(long))
             def _():
                 work(False, d, p)
 
-            for t, steps in enumerate(turns):
-                if steps:
-
-                    @pl.when(i == t)
-                    def _():
-                        for f in steps:
-                            f()
-
+            order = [(down, 1), (down, 2), (down, 3), (down, 0), (up, 1), (up, 2)]
+            turns(i, {t + 2: functools.partial(red.two, shard) for t, (red, shard) in enumerate(order)})
             return carry
 
         lax.fori_loop(0, n * pairs, head_pair, 0)
         halves = ((dq, dq_o), (dk, dk_o), (dv, dv_o))
         for i, (src, dst) in enumerate(halves):
             wire.start(10 + i, src.at[1], dst, place.core)
-        down.last()
         take(2, 3)
         for d in range(n):
             wire.landed(6 + d, at2.at[rows : 2 * rows, d * PAIR : (d + 1) * PAIR], place.core)
@@ -1151,21 +1179,168 @@
                 act2[:, at : at + PAIR] = val[:, d * PAIR : (d + 1) * PAIR].astype(BF16)
 
         put(3, dot_nn(ghb2[...], at2[...]))
-        up.last()
-        down.four()
+        weights(2).start()
         wire.landed(10, dq_o, place.core)
         put(0, dot_nn(n12[:, own : own + rows], dq[0]) + dot_nn(n12[:, win + own : win + own + rows], dq_o[...]))
-        down.five()
-        up.four()
+        up.two(3)
         wire.landed(11, dk_o, place.core)
         put(1, dot_nn(n12[:, 0:win], dk[0]) + dot_nn(n12[:, win : 2 * win], dk_o[...]))
-        up.five()
+        up.two(0)
         wire.landed(12, dv_o, place.core)
         put(2, dot_nn(n12[:, 0:win], dv[0]) + dot_nn(n12[:, win : 2 * win], dv_o[...]))
-        out = pltpu.make_async_copy(act2, gp_ref, ls.at[6])
-        out.start()
+        for d in (1, 2, 3, 0):
+            heads.one(d)
+
+        far_out, x_buf, next_out = n12.at[0:own, 0:dm], n12.at[0:rows, dm : 2 * dm], n12.at[own : own + HALO, 0:dm]
+        tokens_in = pltpu.make_async_copy(x_ref, x_buf, ls.at[6])
+        tokens_in.start()
+
+        def dots(t, carry):
+            weights(t).wait()
+            slot = lax.rem(t, 3)
+            to = pl.ds(pl.multiple_of(lax.rem(t, n) * PAIR, PAIR), PAIR)
+
+            def weight(which, j):
+                at = which * cw + lax.rem(j + core, 2) * PAIR
+                return wbuf[slot, :, pl.ds(pl.multiple_of(at, PAIR), PAIR)]
+
+            def add(ref, val, first):
+                @pl.when(t == first)
+                def _():
+                    ref[...] = val
+
+                @pl.when(t > first)
+                def _():
+                    ref[...] += val
+
+            right = jnp.concatenate([weight(m, j) for m in (1, 2) for j in range(2)], axis=1)
+
+            @pl.when(t < n)
+            def _():
+                left = jnp.concatenate([r[j, 0:own, to] for r in (dk, dv) for j in range(2)], axis=1)
+                add(gi_ref, dot_nt(left, right), 0)
+
+            @pl.when(t >= n)
+            def _():
+                left = jnp.concatenate([r[j, own : own + rows, to] for r in (dk, dv) for j in range(2)], axis=1)
+                mine = jnp.concatenate([dq[j, :, to] for j in range(2)], axis=1)
+                other = jnp.concatenate([weight(0, j) for j in range(2)], axis=1)
+                add(gi_ref, dot_nt(left, right) + dot_nt(mine, other), n)
+                left = jnp.concatenate(
+                    [r[j, own + rows : own + rows + HALO, to] for r in (dk, dv) for j in range(2)], axis=1
+                )
+                add(nxt, dot_nt(left, right), n)
+
+            @pl.when(t < 2 * n - 3)
+            def _():
+                weights(t + 3).start()
+
+            @pl.when(t == n - 1)
+            def _():
+                far_out[...] = gi_ref[...].astype(BF16)
+
+                @pl.when(z == 0)
+                def _():
+                    wire.start(13, far_out.at[0:SPAN], far_in.at[0:SPAN], swap)
+
+                @pl.when(z == 1)
+                def _():
+                    wire.start(13, far_out, far_in, swap)
+
+                @pl.when(gives_prev)
+                def _():
+                    wire.start(14, far_out.at[own - HALO : own], prev_in, left_dev)
+
+            turns(t, {2 * i + 1: functools.partial(down.three, i + 1) for i in range(3)})
+            return carry
+
+        lax.fori_loop(0, 2 * n, dots, 0)
+        next_out[...] = nxt[...].astype(BF16)
+
+        @pl.when(gives_next)
+        def _():
+            wire.start(15, next_out, next_in, right_dev)
+
+        up.three(1)
+        up.three(2)
+        up.three(3)
+        heads.two(1)
+        heads.two(2)
+        down.last()
+        heads.two(3)
+        heads.two(0)
+        heads.three(1)
+
+        @pl.when(z == 0)
+        def _():
+            wire.landed(13, far_in, swap)
+            gi_ref[...] += far_in[...].astype(F32)
+
+        @pl.when(z == 1)
+        def _():
+            wire.landed(13, far_in.at[0:SPAN], swap)
+            gi_ref[0:SPAN, :] += far_in[0:SPAN, :].astype(F32)
+
+        @pl.when(gives_next)
+        def _():
+            wire.landed(14, prev_in, right_dev)
+            gi_ref[rows - HALO : rows, :] += prev_in[...].astype(F32)
+
+        @pl.when(gives_prev)
+        def _():
+            wire.landed(15, next_in, left_dev)
+            gi_ref[0:HALO, :] += next_in[...].astype(F32)
+
+        up.last()
+        heads.three(2)
+        heads.three(3)
+        va[0] = vec_ref[...]
+        for base, grad in ((6, dq), (7, dv)):
+            for j in range(2):
+                total = jnp.sum(grad[j].astype(F32), axis=0, keepdims=True)
+                for d in range(n):
+                    at = base * dm + lax.rem(z + d, n) * cw + lax.rem(j + core, 2) * PAIR
+                    va[0, :, pl.ds(pl.multiple_of(at, PAIR), PAIR)] = total[:, d * PAIR : (d + 1) * PAIR]
+        tokens_in.wait()
+        gains = gain_ref[...].astype(F32)
+
+        def norm(i, carry):
+            at = pl.ds(pl.multiple_of(i * strip, strip), strip)
+            hat, inv = norm_rows(x_buf[at, :].astype(F32))
+            grad = gi_ref[at, :]
+            gg = grad * gains
+            first = jnp.mean(gg, axis=1, keepdims=True)
+            second = jnp.mean(gg * hat, axis=1, keepdims=True)
+            gi_ref[at, :] = inv * (gg - first - hat * second)
+            va[0, :, 0:dm] += jnp.sum(grad * hat, axis=0, keepdims=True)
+            va[0, :, dm : 2 * dm] += jnp.sum(grad, axis=0, keepdims=True)
+            return carry
+
+        lax.fori_loop(0, rows // strip, norm, 0)
+
+        hops = (place.core, place.by_x, place.by_y)
+        between = (down.four, up.four, down.five)
+        for i, dev in enumerate(hops):
+            wire.start(16 + i, va.at[i], vr.at[i], dev)
+            between[i]()
+            wire.landed(16 + i, vr.at[i], dev)
+            if i < 2:
+                va[i + 1] = va[i] + vr[i]
+            else:
+                vz[0] = va[i] + vr[i]
+        for d in (1, 2, 3):
+            wire.start(18 + d, vz.at[0], vz.at[d], place.along(d))
+        up.five()
+        heads.last()
+        heads.four()
+        for d in (1, 2, 3):
+            wire.landed(18 + d, vz.at[d], place.along(4 - d))
+        terms = [vz[lax.rem(z - a + 4, 4)] for a in range(4)]
+        sum_ref[...] = (terms[0] + terms[1]) + (terms[2] + terms[3])
+        heads.five()
         down.six()
         up.six()
+        heads.six()
         for i in range(4):
             wire.sent(i, whole[i][0])
         for i in range(2):
@@ -1174,255 +1349,91 @@
             wire.sent(6 + d, at2.at[0:rows, 0:PAIR])
         for i in range(3):
             wire.sent(10 + i, halves[i][1])
-        out.wait()
+
+        @pl.when(z == 0)
+        def _():
+            wire.sent(13, far_in.at[0:SPAN])
+
+        @pl.when(z == 1)
+        def _():
+            wire.sent(13, far_in)
+
+        @pl.when(gives_prev)
+        def _():
+            wire.sent(14, prev_in)
+
+        @pl.when(gives_next)
+        def _():
+            wire.sent(15, next_in)
+
+        for i in range(3):
+            wire.sent(16 + i, va.at[i])
+        for d in (1, 2, 3):
+            wire.sent(18 + d, vz.at[0])
 
     hbm = pl.BlockSpec(memory_space=pl.ANY)
     vmem = pl.BlockSpec(memory_space=pltpu.VMEM)
     shaped = lambda *shape: jax.ShapeDtypeStruct(shape, BF16)
     buf = lambda *shape: pltpu.VMEM(shape, BF16)
+    wide = lambda *shape: pltpu.VMEM(shape, F32)
+    sem = lambda count: pltpu.SemaphoreType.DMA((count,))
+    q4 = dm // 4
     return pl.pallas_call(
         body,
-        in_specs=[hbm] * 6 + [vmem] * 8,
-        out_specs=[vmem, vmem, hbm, vmem, vmem, vmem],
-        out_shape=[
-            shaped(8, dm // 4, w), shaped(8, dm // 4, w), shaped(dm, hw), shaped(2, rows, half), shaped(2, win, half), shaped(2, win, half)
-        ],
+        in_specs=[hbm] * 8 + [vmem] * 10,
+        out_specs=[hbm] * 3 + [vmem] * 2,
+        out_shape=[shaped(8, q4, w)] * 3 + [jax.ShapeDtypeStruct((rows, dm), F32), jax.ShapeDtypeStruct((1, length), F32)],
         scratch_shapes=[
-            buf(dm, 2 * rows), buf(2 * rows, hw), buf(dm, 2 * rows), buf(2 * rows, hw), buf(dm, 2 * rows), buf(dm, 2 * win),
-            buf(dm, hw), buf(dm, hw), buf(rows, half), buf(win, half), buf(win, half), buf(2 * rows, half),
-            pltpu.VMEM((PAIR, win), F32), pltpu.VMEM((PAIR, win), F32),
-            pltpu.SemaphoreType.DMA((13,)), pltpu.SemaphoreType.DMA((13,)), pltpu.SemaphoreType.DMA((7,)),
+            buf(3, dm, 2 * rows), buf(2 * rows, hw), buf(2 * rows, hw), buf(dm, 2 * win), buf(dm, hw), buf(dm, hw),
+            buf(rows, half), buf(win, half), buf(win, half), buf(2 * rows, half), buf(2, rows, half), buf(2, win, half), buf(2, win, half),
+            wide(PAIR, win), wide(PAIR, win), buf(own, dm), buf(HALO, dm), buf(HALO, dm), wide(HALO, dm),
+            wide(3, 1, length), wide(3, 1, length), wide(4, 1, length), buf(3, q4, w), sem(Reduce.SLOTS), sem(Reduce.SLOTS),
+            sem(22), sem(22), sem(7), sem(3),
         ]
         + Reduce.scratch(dm, w) * 2,
         compiler_params=pltpu.CompilerParams(collective_id=1, has_side_effects=True, vmem_limit_bytes=VMEM_ALL),
-    )(cot, act, n2, gup, ghb, n1w, q, k, v, attn, gattn, lse, qseg, kseg)
-
-
-def finish_call(gp, dq, dk, dv, packed, tokens, gain, vec, own):
-    n, dm, four = packed.shape
-    cw = four // 4
-    rows = tokens.shape[0]
-    win = dk.shape[1]
-    cols = gp.shape[1]
-    w = cols // 4
-    length = vec.shape[1]
-    each = len(Reduce.scratch(dm, w))
-    strip = 128
-
-    def body(
-        gp_ref, dq_ref, dk_ref, dv_ref, w_ref, x_ref, gain_ref, vec_ref,
-        fp, gi_ref, sum_ref,
-        g, acc, far_out, next_out, far_in, prev_in, next_in, va, vr, vz, xs, xr, ls, *scr,
-    ):
-        place = Place()
-        core, z = place.k, place.z
-        load = pltpu.make_async_copy(gp_ref, g, ls)
-        load.start()
-        place.meet()
-        wire = Wire(xs, xr, place.core)
-        red = Reduce(place, g, fp, scr)
-        load.wait()
-        for d in (1, 2, 3, 0):
-            red.one(d)
-
-        def dots(d, carry):
-            def weight(which, j):
-                at = which * cw + lax.rem(j + core, 2) * PAIR
-                return w_ref[d, :, pl.ds(pl.multiple_of(at, PAIR), PAIR)]
-
-            to = pl.ds(pl.multiple_of(d * PAIR, PAIR), PAIR)
-            left = jnp.concatenate([r[j, :, to] for r in (dk_ref, dv_ref) for j in range(2)], axis=1)
-            right = jnp.concatenate([weight(m, j) for m in (1, 2) for j in range(2)], axis=1)
-            part = dot_nt(left, right)
-            left = jnp.concatenate([dq_ref[j, :, to] for j in range(2)], axis=1)
-            right = jnp.concatenate([weight(0, j) for j in range(2)], axis=1)
-            mine = dot_nt(left, right)
-
-            @pl.when(d == 0)
-            def _():
-                acc[...] = part
-
-            @pl.when(d > 0)
-            def _():
-                acc[...] += part
-
-            acc[own : own + rows, :] += mine
-            for t, f in ((2, red.sweep()[0]), (3, red.sweep()[1])):
-
-                @pl.when(d == t)
-                def _():
-                    f()
-
-            return carry
-
-        lax.fori_loop(0, n, dots, 0)
-
-        long, gives_prev, gives_next = z < 2, z >= 2, jnp.logical_and(z >= 1, z < 3)
-        swap = {"dp": place.me, "mp": lax.rem(z + 1, 2)}
-        left_dev = {"dp": place.me, "mp": lax.rem(z + 3, 4)}
-        right_dev = {"dp": place.me, "mp": lax.rem(z + 1, 4)}
-        far_out[...] = acc[0:own, :].astype(BF16)
-        next_out[...] = acc[own + rows : own + rows + HALO, :].astype(BF16)
-
-        @pl.when(long)
-        def _():
-            wire.start(0, far_out, far_in, swap)
-
-        @pl.when(gives_prev)
-        def _():
-            wire.start(1, far_out.at[own - HALO : own], prev_in, left_dev)
-
-        @pl.when(gives_next)
-        def _():
-            wire.start(2, next_out, next_in, right_dev)
-
-        for f in red.sweep()[2:]:
-            f()
-
-        @pl.when(long)
-        def _():
-            wire.landed(0, far_in, swap)
-            acc[own : own + rows, :] += far_in[...].astype(F32)
-
-        @pl.when(gives_next)
-        def _():
-            wire.landed(1, prev_in, right_dev)
-            acc[own + rows - HALO : own + rows, :] += prev_in[...].astype(F32)
-
-        @pl.when(gives_prev)
-        def _():
-            wire.landed(2, next_in, left_dev)
-            acc[own : own + HALO, :] += next_in[...].astype(F32)
-
-        va[0] = vec_ref[...]
-        va[0, :, 0 : 2 * dm] = jnp.zeros((1, 2 * dm), F32)
-        gains = gain_ref[...].astype(F32)
-
-        def norm(i, carry):
-            at = pl.ds(pl.multiple_of(i * strip, strip), strip)
-            hat, inv = norm_rows(x_ref[at, :].astype(F32))
-            back = acc[pl.ds(pl.multiple_of(own + i * strip, strip), strip), :]
-            gg = back * gains
-            first = jnp.mean(gg, axis=1, keepdims=True)
-            second = jnp.mean(gg * hat, axis=1, keepdims=True)
-            gi_ref[at, :] = inv * (gg - first - hat * second)
-            va[0, :, 0:dm] += jnp.sum(back * hat, axis=0, keepdims=True)
-            va[0, :, dm : 2 * dm] += jnp.sum(back, axis=0, keepdims=True)
-            return carry
-
-        lax.fori_loop(0, rows // strip, norm, 0)
-
-        hops = (place.core, place.by_x, place.by_y)
-        between = (red.last, red.four, red.five)
-        for i, dev in enumerate(hops):
-            wire.start(3 + i, va.at[i], vr.at[i], dev)
-            if i == 0:
-                between[0]()
-            wire.landed(3 + i, vr.at[i], dev)
-            if i < 2:
-                va[i + 1] = va[i] + vr[i]
-            else:
-                vz[0] = va[i] + vr[i]
-        for d in (1, 2, 3):
-            wire.start(5 + d, vz.at[0], vz.at[d], place.along(d))
-        between[1]()
-        between[2]()
-        for d in (1, 2, 3):
-            wire.landed(5 + d, vz.at[d], place.along(4 - d))
-        terms = [vz[lax.rem(z - a + 4, 4)] for a in range(4)]
-        sum_ref[...] = (terms[0] + terms[1]) + (terms[2] + terms[3])
-        red.six()
-
-        @pl.when(long)
-        def _():
-            wire.sent(0, far_out)
-
-        @pl.when(gives_prev)
-        def _():
-            wire.sent(1, prev_in)
-
-        @pl.when(gives_next)
-        def _():
-            wire.sent(2, next_out)
-
-        for i in range(3):
-            wire.sent(3 + i, va.at[i])
-        for d in (1, 2, 3):
-            wire.sent(5 + d, vz.at[0])
-
-    hbm = pl.BlockSpec(memory_space=pl.ANY)
-    vmem = pl.BlockSpec(memory_space=pltpu.VMEM)
-    buf = lambda *shape: pltpu.VMEM(shape, BF16)
-    return pl.pallas_call(
-        body,
-        in_specs=[hbm] + [vmem] * 7,
-        out_specs=[vmem] * 3,
-        out_shape=[
-            jax.ShapeDtypeStruct((8, dm // 4, w), BF16),
-            jax.ShapeDtypeStruct((rows, dm), F32),
-            jax.ShapeDtypeStruct((1, length), F32),
-        ],
-        scratch_shapes=[
-            buf(dm, cols), pltpu.VMEM((win, dm), F32),
-            buf(own, dm), buf(HALO, dm), buf(own, dm), buf(HALO, dm), buf(HALO, dm),
-            pltpu.VMEM((3, 1, length), F32), pltpu.VMEM((3, 1, length), F32), pltpu.VMEM((4, 1, length), F32),
-            pltpu.SemaphoreType.DMA((9,)), pltpu.SemaphoreType.DMA((9,)), pltpu.SemaphoreType.DMA(()),
-        ]
-        + Reduce.scratch(dm, w),
-        compiler_params=pltpu.CompilerParams(collective_id=2, has_side_effects=True, vmem_limit_bytes=VMEM),
-    )(gp, dq, dk, dv, packed, tokens, gain[None], vec)
-
-
-def place_grads(coords, down, up, pack):
-    _, q, w = up.shape
+    )(cot, act, n2, gup, ghb, n1w, packed, tokens, q, k, v, attn, gattn, lse, qseg, kseg, gain[None], vec)
+
+
+def place_grads(coords, done, mode):
+    _, q, w = done.shape
     e = q // 2
     dm = 4 * q
     lanes = w // 4
 
-    def spot(off, part, c):
-        y = lax.bitwise_xor(c[0], off // 4)
-        x = lax.bitwise_xor(c[1], lax.rem(off // 2, 2))
-        k = lax.bitwise_xor(c[2], lax.rem(off, 2))
-        return (1 - part) * (2 * x + y) + part * (4 + 2 * y + x), k
-
-    def across(off, part, c):
-        return spot(off, part, c)
-
-    def flipped(off, part, c):
-        block, k = spot(off, part, c)
-        return k, block
-
-    def body(c_ref, d_ref, u_ref, p_ref, gd_ref, gu_ref, gq_ref, gk_ref, gv_ref, go_ref):
-        gd_ref[...] = d_ref[0].astype(F32).T
-        gu_ref[...] = u_ref[0].astype(F32)
-        val = p_ref[0].astype(F32)
-        for m, ref in enumerate((gq_ref, gk_ref, gv_ref)):
-            ref[...] = val[:, m * lanes : (m + 1) * lanes]
-        go_ref[...] = val[:, 3 * lanes :].T
-
-    piece = pl.BlockSpec((1, e, w), lambda off, part, c: (off, part, 0))
+    def body(c_ref, f_ref, *outs):
+        for off in range(8):
+            y = lax.bitwise_xor(c_ref[0], off >> 2)
+            x = lax.bitwise_xor(c_ref[1], (off >> 1) & 1)
+            k = lax.bitwise_xor(c_ref[2], off & 1)
+            for part in range(2):
+                val = f_ref[off, part * e : (part + 1) * e, :].astype(F32)
+                block = x * 2 + y if part == 0 else 4 + y * 2 + x
+                rows = pl.ds(pl.multiple_of(block * e, e), e)
+                if mode == "up":
+                    outs[0][rows, pl.ds(pl.multiple_of(k * w, w), w)] = val
+                elif mode == "down":
+                    outs[0][pl.ds(pl.multiple_of(k * w, w), w), rows] = val.T
+                else:
+                    at = pl.ds(pl.multiple_of(k * lanes, lanes), lanes)
+                    for m in range(3):
+                        outs[m][rows, at] = val[:, m * lanes : (m + 1) * lanes]
+                    outs[3][at, rows] = val[:, 3 * lanes :].T
+
+    if mode == "up":
+        shapes = [(dm, 2 * w)]
+    elif mode == "down":
+        shapes = [(2 * w, dm)]
+    else:
+        shapes = [(dm, w // 2)] * 3 + [(w // 2, dm)]
     return pl.pallas_call(
         body,
-        grid_spec=pltpu.PrefetchScalarGridSpec(
-            num_scalar_prefetch=1,
-            grid=(8, 2),
-            in_specs=[piece] * 3,
-            out_specs=[
-                pl.BlockSpec((w, e), flipped),
-                pl.BlockSpec((e, w), across),
-                pl.BlockSpec((e, lanes), across),
-                pl.BlockSpec((e, lanes), across),
-                pl.BlockSpec((e, lanes), across),
-                pl.BlockSpec((lanes, e), flipped),
-            ],
-        ),
-        out_shape=[
-            jax.ShapeDtypeStruct(shape, F32)
-            for shape in ((2 * w, dm), (dm, 2 * w), (dm, w // 2), (dm, w // 2), (dm, w // 2), (w // 2, dm))
-        ],
-        compiler_params=params("arbitrary", "arbitrary"),
-        cost_estimate=pl.CostEstimate(flops=0, bytes_accessed=36 * dm * w, transcendentals=0),
-    )(coords, down, up, pack)
+        in_specs=[pl.BlockSpec(memory_space=pltpu.SMEM), pl.BlockSpec(memory_space=pltpu.VMEM)],
+        out_specs=[pl.BlockSpec(memory_space=pltpu.VMEM)] * len(shapes),
+        out_shape=[jax.ShapeDtypeStruct(s, F32) for s in shapes],
+        compiler_params=pltpu.CompilerParams(vmem_limit_bytes=VMEM),
+        cost_estimate=pl.CostEstimate(flops=0, bytes_accessed=12 * dm * w, transcendentals=0),
+    )(coords, done)
 
 
 def relative(stack, z):
@@ -1504,12 +1515,17 @@
         small = jnp.concatenate([ln1_gain, ln1_bias, ln2_gain, ln2_bias, b_out, b_down, b_query, b_value, b_up])
         small = f32(small)[None]
         (
-            packed, n1_t, n2_t, cot_t, ghb_t, q, k, v, attn, lse, g_attn, active, g_upper, g_b_up, g_hidden, output, done
+            packed, n1_t, n2_t, cot_t, ghb_t, q, k, v, attn, lse, g_attn, active, g_upper, g_hidden, output, vec
         ) = front_call(tokens, cotangent, pack, w_up, w_down, small, qseg, kseg, own)
-        done_d, done_u, gp, dq, dk, dv = back_call(
-            cot_t, active, n2_t, g_upper, ghb_t, n1_t, q, k, v, attn, g_attn, lse, qseg, kseg, own, near
+        done_d, done_u, done_p, g_in, vec = back_call(
+            cot_t, active, n2_t, g_upper, ghb_t, n1_t, packed, tokens, q, k, v, attn, g_attn, lse, qseg, kseg, ln1_gain, vec, own
         )
-        sums = [done[0]]
+        vec = vec[0]
+        g_tokens = g_in + g_hidden
+        coords = jnp.stack([y, x, core]).astype(jnp.int32)
+        (g_w_down,) = place_grads(coords, done_d, "down")
+        (g_w_up,) = place_grads(coords, done_u, "up")
+        g_w_query, g_w_key, g_w_value, g_w_out = place_grads(coords, done_p, "pack")
     else:
         halo = [
             lax.ppermute(tokens, "mp", [((i + j) % near, i) for i in range(near)]) for j in range(1, near)
@@ -1553,26 +1569,18 @@
         dq, dk, dv = attn_bwd_call(info, q, k, v, attn, g_attn, lse, qseg, kseg, own)
         n1 = n1w[own : own + rows]
         sums = [jnp.sum(g_hidden, axis=0), g_gain2, g_bias2, jnp.sum(gout, axis=0)]
-    halves = dq.shape[0]
-
-    def shards(v, width):
-        if v.shape[0] == 2:
-            v = core_first(v.reshape(2, mp, width // 2), core, 0).transpose(1, 0, 2)
-        return jnp.roll(v.reshape(mp, width), z, axis=0).reshape(mp * width)
-
-    gbq = shards(jnp.sum(f32(dq), axis=1), cw)
-    gbv = shards(jnp.sum(f32(dv), axis=1), cw)
-    gbu = core_first(g_b_up.reshape(2, mp, ffw // 2), core, 0).transpose(1, 0, 2)
-    gbu = jnp.roll(gbu.reshape(mp, ffw), z, axis=0).reshape(-1)
-    sums = sums + [gbq, gbv, gbu]
-    if fast:
-        vec = jnp.concatenate([jnp.zeros((2 * dm,), F32)] + sums)[None]
-        done_p, g_in, vec = finish_call(gp, dq, dk, dv, packed, tokens, ln1_gain, vec, own)
-        vec = vec[0]
-        g_tokens = g_in + g_hidden
-        coords = jnp.stack([y, x, core]).astype(jnp.int32)
-        g_w_down, g_w_up, g_w_query, g_w_key, g_w_value, g_w_out = place_grads(coords, done_d, done_u, done_p)
-    else:
+        halves = dq.shape[0]
+
+        def shards(v, width):
+            if v.shape[0] == 2:
+                v = core_first(v.reshape(2, mp, width // 2), core, 0).transpose(1, 0, 2)
+            return jnp.roll(v.reshape(mp, width), z, axis=0).reshape(mp * width)
+
+        gbq = shards(jnp.sum(f32(dq), axis=1), cw)
+        gbv = shards(jnp.sum(f32(dv), axis=1), cw)
+        gbu = core_first(g_b_up.reshape(2, mp, ffw // 2), core, 0).transpose(1, 0, 2)
+        gbu = jnp.roll(gbu.reshape(mp, ffw), z, axis=0).reshape(-1)
+        sums = sums + [gbq, gbv, gbu]
         g_own, g_far, g_next = norm1_back_call(dq, dk, dv, packed, info, own)
         back = g_own
         for j in range(1, near):

time: 395 us -> 345 us (0.87)
  Pallas kernels: 374 us -> 328 us
  other arithmetic: 13.7 us -> 9.49 us
    pallas_call x3 -> x4, Pallas kernels: 224 us -> 179 us  [the longest x1 166 us: back_call(): pl.pallas_call(body, in_specs=[hbm] * 8 + [vmem] * 10, out_specs=[hbm] *...]
where the time goes in v7:
time: 345 us; the launch traced here: 344 us
  Pallas kernels  328 us (95%)
  other arithmetic  9.49 us (3%)
  local copies, waits for them, and re-layouts  6.38 us (2%)
    pallas_call x1, Pallas kernels, back_call(): pl.pallas_call(body, in_specs=[hbm] * 8 + [vmem] * 10, out_specs=[hbm] *...  166 us
    pallas_call x1, Pallas kernels, front_call(): pl.pallas_call(body, in_specs=[hbm, vmem, hbm, hbm, hbm, vmem, vmem, vmem...  149 us
    pallas_call x3, Pallas kernels, place_grads(): pl.pallas_call(body, in_specs=[pl.BlockSpec(memory_space=pltpu.SMEM), pl....  12.3 us

profile of v7, /device:TPU:0, one launch (start us, length us, event | category | flops | bytes accessed | tf_op | source)
XLA Modules:
  0.0 344.4 jit_solution(2816879994813582066)
XLA Ops:
  0.7 0.8 dynamic-slice_select_fusion
  1.5 0.8 broadcast_select_fusion
  2.4 0.1 concatenate.45
  2.4 0.6 broadcast_in_dim.20.ks_ref
  3.0 0.9 copy.37.qs_ref
  3.9 1.2 copy.36
  5.1 0.0 copy-start.3
  5.2 0.0 copy-start.4
  5.2 0.0 copy-start.5
  5.2 0.0 copy-start.6
  5.2 0.0 copy-start.7
  5.2 0.0 copy-start.8
  5.2 0.0 copy-start.10
  5.2 0.0 copy-start.11
  5.2 0.0 copy-start.9
  5.3 3.0 pad_maximum_fusion.pack_ref
  8.3 0.0 copy-done.3
  8.3 0.0 copy-done.4
  8.3 0.0 copy-done.5
  8.3 0.0 copy-done.6
  8.3 0.0 copy-done.7
  8.4 0.0 copy-done.8
  8.4 0.0 copy-done.10
  8.4 0.0 copy-done.11
  8.4 0.0 copy-done.9
  8.5 0.6 convert_element_type.10.small_ref
  9.1 148.9 %shard_map.305 = (bf16[4,1024,1024]{2,1,0:T(8,128)(2,1)}, bf16[1024,1152]{1,0:T(8,128)(2,1)}, bf16[1024,512]{1,0:T(8,128)(2,1)}, bf16[1024,512]{1,0:T(8,128)(2,1...) custom-call(bf16[512,1024]{1,0:T(8,128)(2,1)} %x_ref.1, ...), custom_call_target="tpu_custom_call" | custom-call | tf_op jit(solution)/shard_map/pallas_call | solution.py:854
  158.0 1.3 concatenate.35.gain_ref
  159.3 166.5 %shard_map.306 = (bf16[8,256,512]{2,1,0:T(8,128)(2,1)}, bf16[8,256,512]{2,1,0:T(8,128)(2,1)}, bf16[8,256,512]{2,1,0:T(8,128)(2,1)}, f32[512,1024]{1,0:T(8,128)}, f32[1,12288]{1,0:T(1,128)}) custom-call(bf16[1024,512]{1,0:T(8,128)(2,1)} %get-tuple-element.43.cot_ref, bf16[512,4096]{1,0:T(8,128)(2,1)} %get-tuple-element.44.act_ref, ...), custom_call_target="tpu_custom_call" | custom-call | tf_op jit(solution)/shard_map/pallas_call | solution.py:1381
  325.8 0.6 pad_add_fusion.c_ref
  326.4 3.9 %shard_map.307 = (f32[1024,256]{1,0:T(8,128)}, f32[1024,256]{1,0:T(8,128)}, f32[1024,256]{1,0:T(8,128)}, f32[256,1024]{1,0:T(8,128)}) custom-call(s32[3]{0:T(128)} %pad_add_fusion.c_ref, bf16[8,256,512]{2,1,0:T(8,128)(2,1)} %get-tuple-element.60.f_ref), custom_call_target="tpu_custom_call" | custom-call | bytes 6291456 | tf_op jit(solution)/shard_map/pallas_call | solution.py:1429
  330.3 3.9 %shard_map.308 = f32[1024,1024]{1,0:T(8,128)} custom-call(s32[3]{0:T(128)} %pad_add_fusion.c_ref, bf16[8,256,512]{2,1,0:T(8,128)(2,1)} %get-tuple-element.65.f_ref), custom_call_target="tpu_custom_call" | custom-call | bytes 6291456 | tf_op jit(solution)/shard_map/pallas_call | solution.py:1429
  334.2 0.0 copy-start
  334.2 4.5 %shard_map.309 = f32[1024,1024]{1,0:T(8,128)} custom-call(s32[3]{0:T(128)} %pad_add_fusion.c_ref, bf16[8,256,512]{2,1,0:T(8,128)(2,1)} %get-tuple-element.66.f_ref), custom_call_target="tpu_custom_call" | custom-call | bytes 6291456 | tf_op jit(solution)/shard_map/pallas_call | solution.py:1429
  338.7 0.0 copy-done
  338.7 0.0 copy-start.2
  338.7 0.0 copy-start.1
  338.7 3.6 %add.39 = f32[512,1024]{1,0:T(8,128)} add(f32[512,1024]{1,0:T(8,128)} %get-tuple-element.57, f32[512,1024]{1,0:T(8,128)S(1)} %copy-done) | non-fusion elementwise | flops 524288 | bytes 6291456 | tf_op jit(solution)/shard_map/add | solution.py:1524
  342.2 0.0 copy-done.2
  342.2 0.6 fusion
  342.8 0.6 constant_dynamic-slice_fusion.1
  343.4 0.0 copy-done.1
  343.4 1.0 copy.48
  (10 shorter events, 0.1 us)
Async XLA Ops:
  5.1 3.1 copy-start.3
  5.2 3.1 copy-start.4
  5.2 3.1 copy-start.5
  5.2 3.1 copy-start.6
  5.2 3.2 copy-start.7
  5.2 3.2 copy-start.8
  5.2 3.2 copy-start.10
  5.2 3.2 copy-start.11
  5.2 3.2 copy-start.9
  334.2 4.5 %copy-start = (f32[512,1024]{1,0:T(8,128)S(1)}, f32[512,1024]{1,0:T(8,128)}, u32[]{:S(2)}) copy-start(f32[512,1024]{1,0:T(8,128)} %get-tuple-element.58) | copy-start | bytes 6291460
  338.7 3.6 %copy-start.2 = (f32[1,12288]{1,0:T(1,128)S(1)}, f32[1,12288]{1,0:T(1,128)}, u32[]{:S(2)}) copy-start(f32[1,12288]{1,0:T(1,128)} %get-tuple-element.59) | copy-start | bytes 147460
  338.7 4.8 %copy-start.1 = (bf16[512,1024]{1,0:T(8,128)(2,1)S(1)}, bf16[512,1024]{1,0:T(8,128)(2,1)}, u32[]{:S(2)}) copy-start(bf16[512,1024]{1,0:T(8,128)(2,1)} %get-tuple-element.97) | copy-start | bytes 3145732

commit v8 on v7

--- a/solution.py
+++ b/solution.py
@@ -539,12 +539,15 @@
     per = rows // strip
     scale = HEAD_DIM**-0.5
     length = small.shape[1] - 6 * dm
-    base = 6
+    give = 6
+    base = give + 3 + 3 * n
 
     def body(
         tok_ref, cot_ref, pack_ref, up_ref, down_ref, small_ref, qs_ref, ks_ref,
-        packed, n1t, n2t, cott, ghbt, q_ref, k_ref, v_ref, a_ref, l_ref, ga_ref, act_ref, gup_ref, gh_ref, o_ref, vec_ref,
-        up, down, n1, hid, n2, acc, act, gup, biases, xs, xr, ls, fs,
+        packed_out, n1t_out, n2t_out, cott_out, ghbt_out, q_out, k_out, v_out, a_out, at_out, ga_out, act_out, gup_out, gh_out,
+        l_ref, o_ref, vec_ref,
+        up, down, n1, hid, n2, acc, act, gup, biases,
+        packed, n1t, n2t, cott, ghbt, q_ref, k_ref, v_ref, a_ref, ga_ref, gh_ref, xs, xr, ls, fs, os,
     ):
         place = Place()
         core, z = place.k, place.z
@@ -620,6 +623,18 @@
 
         row = lambda i: small_ref[:, i * dm : (i + 1) * dm]
 
+        whole = [
+            (n1t, n1t_out.at[:, 0:win]), (n2t, n2t_out.at[:, 0:rows]), (cott, cott_out.at[:, 0:rows]), (ghbt, ghbt_out),
+            (q_ref, q_out), (k_ref, k_out), (v_ref, v_out), (a_ref, a_out), (ga_ref, ga_out), (gh_ref, gh_out), (packed, packed_out),
+        ]
+        leaving = [pltpu.make_async_copy(src, dst, os.at[i]) for i, (src, dst) in enumerate(whole)]
+        shared = ((n1t, n1t_out.at[:, win : 2 * win]), (n2t, n2t_out.at[:, rows : 2 * rows]), (cott, cott_out.at[:, rows : 2 * rows]))
+
+        def leave(i):
+            leaving[i].start()
+            if i < len(shared):
+                wire.start(give + i, *shared[i], place.core)
+
         @pl.when(z == 0)
         def _():
             n1[SPAN:own, :] = jnp.zeros((own - SPAN, dm), BF16)
@@ -642,6 +657,7 @@
             return carry
 
         lax.fori_loop(0, per, turn_cot, 0)
+        leave(2)
 
         def norm1(i):
             at = strip_at(i)
@@ -684,6 +700,7 @@
 
         lax.fori_loop(0, own // strip, norm_far, 0)
         norm1((own + rows) // strip)
+        leave(0)
         for d in (1, 2, 3):
             wire.landed(d - 1, biases.at[d], place.along(d))
         relay(1)
@@ -706,6 +723,15 @@
                     l_ref[qs : qs + qn, :] = jnp.where(lane == (d * pairs + p) * 2 + h, top + jnp.log(total), seen)
                 a_ref[d, qs : qs + qn, at] = jnp.concatenate(outs, axis=1).astype(BF16)
 
+        def head_lanes(d):
+            return pl.ds(pl.multiple_of(d * PAIR, PAIR), PAIR)
+
+        def half_of_attn(d):
+            mine = pl.ds(pl.multiple_of(core * PAIR, PAIR), PAIR)
+            theirs = pl.ds(pl.multiple_of((1 - core) * PAIR, PAIR), PAIR)
+            keep = pltpu.make_async_copy(a_ref.at[d, :, mine], at_out.at[0:rows, head_lanes(d)], fs.at[2 * n + d])
+            return keep, a_ref.at[d, :, theirs]
+
         def heads(kk, carry):
             turns(kk, {j + 1: functools.partial(arrived, j, 0) for j in range(3)})
             d = shard_at(kk)
@@ -727,9 +753,14 @@
 
             lax.fori_loop(0, pairs, one, 0)
             hid[...] += dot_nt(a_ref[d], packed[d, :, 3 * cw : 4 * cw])
+            halves = half_of_attn(d)
+            halves[0].start()
+            wire.start(give + 3 + d, halves[1], at_out.at[rows : 2 * rows, head_lanes(d)], place.core)
             return carry
 
         lax.fori_loop(0, n, heads, 0)
+        for i in (4, 5, 6, 7, 10):
+            leave(i)
         relay(6)
 
         def norm2(i, carry):
@@ -743,16 +774,14 @@
             return carry
 
         lax.fori_loop(0, per, norm2, 0)
-
-        def out_copies(i, col):
-            at = pl.ds(pl.multiple_of(col, tile), tile)
+        leave(1)
+
+        def kept(d):
+            at = pl.ds(pl.multiple_of(d * tile, tile), tile)
             return (
-                pltpu.make_async_copy(act.at[:, at], act_ref.at[:, at], fs.at[i]),
-                pltpu.make_async_copy(gup.at[:, at], gup_ref.at[:, at], fs.at[2 * n + i]),
+                pltpu.make_async_copy(act.at[:, at], act_out.at[0:rows, at], fs.at[d]),
+                pltpu.make_async_copy(gup.at[:, at], gup_out.at[0:rows, at], fs.at[n + d]),
             )
-
-        def column(i):
-            return lax.rem(i, 2) * hw + shard_at(i // 2) * tile
 
         def feed(i, carry):
             turns(
@@ -767,9 +796,10 @@
                 },
             )
             d = shard_at(i // 2)
-            part = lax.rem(lax.rem(i, 2) + core, 2) * tile
+            rel = 1 - lax.rem(i, 2)
+            part = lax.rem(rel + core, 2) * tile
             at = pl.ds(pl.multiple_of(part, tile), tile)
-            to = pl.ds(pl.multiple_of(column(i), tile), tile)
+            to = pl.ds(pl.multiple_of(rel * hw + d * tile, tile), tile)
             u = dot_nn(n2[...], up[d, :, at]) + biases[d, :, pl.ds(pl.multiple_of(2 * cw + part, PAIR), tile)]
             cdf = 0.5 * (1.0 + lax.erf(u * 0.7071067811865476))
             val = (u * cdf).astype(BF16)
@@ -779,8 +809,18 @@
             gup[:, to] = gu
             unit = 8 * dm + lax.rem(z + d, n) * ffw + part
             vec_ref[:, pl.ds(pl.multiple_of(unit, tile), tile)] = jnp.sum(gu.astype(F32), axis=0, keepdims=True)
-            for c in out_copies(i, column(i)):
-                c.start()
+
+            @pl.when(rel == 0)
+            def _():
+                for c in kept(d):
+                    c.start()
+
+            @pl.when(rel == 1)
+            def _():
+                theirs = pl.ds(pl.multiple_of(d * tile, tile), tile)
+                for j, (src, dst) in enumerate(((act, act_out), (gup, gup_out))):
+                    wire.start(give + 3 + (j + 1) * n + d, src.at[:, to], dst.at[rows : 2 * rows, theirs], place.core)
+
             acc[...] += dot_nn(val, down[d, at, :])
             gn = dot_nt(gu, up[d, :, at])
 
@@ -814,15 +854,29 @@
             return carry
 
         lax.fori_loop(0, per, back2, 0)
+        leave(9)
+        leave(3)
 
         def back_attn(d, carry):
             ga_ref[d] = dot_nn(n2[...], packed[d, :, 3 * cw : 4 * cw]).astype(BF16)
             return carry
 
         lax.fori_loop(0, n, back_attn, 0)
-        for i in range(2 * n):
-            for c in out_copies(i, 0):
+        leave(8)
+        for d in range(n):
+            for c in (*kept(d), half_of_attn(d)[0]):
                 c.wait()
+        for i, (src, dst) in enumerate(shared):
+            wire.landed(give + i, dst, place.core)
+            wire.sent(give + i, src)
+        for d in range(n):
+            wire.landed(give + 3 + d, at_out.at[rows : 2 * rows, d * PAIR : (d + 1) * PAIR], place.core)
+            wire.sent(give + 3 + d, at_out.at[0:rows, 0:PAIR])
+            for j, dst in enumerate((act_out, gup_out)):
+                wire.landed(give + 3 + (j + 1) * n + d, dst.at[rows : 2 * rows, d * tile : (d + 1) * tile], place.core)
+                wire.sent(give + 3 + (j + 1) * n + d, dst.at[0:rows, 0:tile])
+        for c in leaving:
+            c.wait()
         for group in groups:
             group[5]()
         for d in (1, 2, 3):
@@ -854,17 +908,20 @@
     return pl.pallas_call(
         body,
         in_specs=[hbm, vmem, hbm, hbm, hbm, vmem, vmem, vmem],
-        out_specs=[vmem] * 11 + [hbm] * 2 + [vmem] * 3,
+        out_specs=[hbm] * 14 + [vmem] * 3,
         out_shape=[
-            half(n, dm, 4 * cw), half(dm, win), half(dm, rows), half(dm, rows), half(dm, rows),
-            half(n, rows, cw), half(n, win, cw), half(n, win, cw), half(n, rows, cw), full(rows, 2 * n * pairs), half(n, rows, cw),
-            half(rows, 2 * hw), half(rows, 2 * hw), full(rows, dm), half(rows, dm), full(1, 8 * dm + 2 * hw),
+            half(n, dm, 4 * cw), half(dm, 2 * win), half(dm, 2 * rows), half(dm, 2 * rows), half(dm, rows),
+            half(n, rows, cw), half(n, win, cw), half(n, win, cw), half(n, rows, cw), half(2 * rows, n * PAIR), half(n, rows, cw),
+            half(2 * rows, hw), half(2 * rows, hw), full(rows, dm),
+            full(rows, 2 * n * pairs), half(rows, dm), full(1, 8 * dm + 2 * hw),
         ],
         scratch_shapes=[
             b16(n, dm, ffw), b16(n, ffw, dm), b16(win, dm), b32(rows, dm), b16(rows, dm), b32(rows, dm),
             b16(rows, 2 * hw), b16(rows, 2 * hw), b32(n, 1, length),
+            b16(n, dm, 4 * cw), b16(dm, win), b16(dm, rows), b16(dm, rows), b16(dm, rows),
+            b16(n, rows, cw), b16(n, win, cw), b16(n, win, cw), b16(n, rows, cw), b16(n, rows, cw), b32(rows, dm),
             pltpu.SemaphoreType.DMA((slots,)), pltpu.SemaphoreType.DMA((slots,)), pltpu.SemaphoreType.DMA((4,)),
-            pltpu.SemaphoreType.DMA((4 * n,)),
+            pltpu.SemaphoreType.DMA((3 * n,)), pltpu.SemaphoreType.DMA((11,)),
         ],
         compiler_params=pltpu.CompilerParams(collective_id=0, has_side_effects=True, vmem_limit_bytes=VMEM_ALL),
     )(tokens, cot, pack, w_up, w_down, small, qseg, kseg)
@@ -1013,11 +1070,11 @@
         self.keep().wait()
 
 
-def back_call(cot, act, n2, gup, ghb, n1w, packed, tokens, q, k, v, attn, gattn, lse, qseg, kseg, gain, vec, own):
+def back_call(cot, act, n2, gup, ghb, n1w, attn2, packed, tokens, q, k, v, attn, gattn, lse, qseg, kseg, gain, vec, own):
     n, rows, cw = q.shape
     win = k.shape[1]
     dm = cot.shape[0]
-    hw = act.shape[1] // 2
+    hw = act.shape[1]
     half = n * cw // 2
     w = hw // 4
     pairs = cw // PAIR
@@ -1027,11 +1084,11 @@
     strip = 128
 
     def body(
-        cot_ref, act_ref, n2_ref, gup_ref, ghb_ref, n1_ref, w_ref, x_ref,
-        q_ref, k_ref, v_ref, a_ref, g_ref, l_ref, qs_ref, ks_ref, gain_ref, vec_ref,
+        cot_in, act_in, n2_in, gup_in, ghb_in, n1_in, at_in, w_ref, x_ref, q_in, k_in, v_in, a_in, g_in,
+        l_ref, qs_ref, ks_ref, gain_ref, vec_ref,
         fd, fu, fp, gi_ref, sum_ref,
         wbuf, act2, gup2, n12, gd, gu, dq_o, dk_o, dv_o, at2, dq, dk, dv, dkt, dvt,
-        far_in, prev_in, next_in, nxt, va, vr, vz, zb, ps, pr_sem, xs, xr, ls, ws, *scr,
+        far_in, prev_in, next_in, nxt, va, vr, vz, zb, q_ref, k_ref, v_ref, a_ref, g_ref, ps, pr_sem, xs, xr, ls, ws, *scr,
     ):
         place = Place()
         core, z = place.k, place.z
@@ -1041,45 +1098,19 @@
         right_dev = {"dp": place.me, "mp": lax.rem(z + 1, 4)}
         wire = Wire(xs, xr, place.core)
         cot2, n22, ghb2 = wbuf.at[0], wbuf.at[1], wbuf.at[2]
-        whole = (
-            (cot_ref, cot2, rows), (n2_ref, n22, rows), (ghb_ref, ghb2, rows), (n1_ref, n12, win)
+        loads = (
+            (cot_in, cot2), (act_in, act2), (n2_in, n22), (gup_in, gup2), (q_in, q_ref), (k_in, k_ref), (v_in, v_ref),
+            (a_in, a_ref), (g_in, g_ref), (ghb_in, ghb2.at[:, 0:rows]), (n1_in, n12), (at_in, at2),
         )
-        mixed = ((act_ref, act2), (gup_ref, gup2))
-        local = [pltpu.make_async_copy(src, dst.at[:, 0:wide], ls.at[i]) for i, (src, dst, wide) in enumerate(whole)]
-        local += [pltpu.make_async_copy(src.at[:, 0:hw], dst.at[0:rows], ls.at[4 + i]) for i, (src, dst) in enumerate(mixed)]
-        for i in (0, 4, 1, 5, 2, 3):
-            local[i].start()
+        local = [pltpu.make_async_copy(src, dst, ls.at[1 + i]) for i, (src, dst) in enumerate(loads)]
+        for c in local:
+            c.start()
         place.meet()
-
-        def give_whole(i):
-            src, dst, wide = whole[i]
-            wire.start(i, src, dst.at[:, wide : 2 * wide], place.core)
-
-        def give_mixed(i):
-            src, dst = mixed[i]
-            wire.start(4 + i, src.at[:, hw : 2 * hw], dst.at[rows : 2 * rows], place.core)
+        wire.start(0, ghb_in, ghb2.at[:, rows : 2 * rows], place.core)
 
         def take(*which):
             for i in which:
                 local[i].wait()
-                if i < 4:
-                    dst, wide = whole[i][1:]
-                    wire.landed(i, dst.at[:, wide : 2 * wide], place.core)
-                else:
-                    wire.landed(i, mixed[i - 4][1].at[rows : 2 * rows], place.core)
-
-        give_whole(0)
-        give_mixed(0)
-        give_whole(1)
-        give_mixed(1)
-        give_whole(2)
-        give_whole(3)
-        for d in range(n):
-            to = slice(d * PAIR, (d + 1) * PAIR)
-            theirs = pl.ds(pl.multiple_of((1 - core) * PAIR, PAIR), PAIR)
-            mine = pl.ds(pl.multiple_of(core * PAIR, PAIR), PAIR)
-            wire.start(6 + d, a_ref.at[d, :, theirs], at2.at[rows : 2 * rows, to], place.core)
-            at2[0:rows, to] = a_ref[d, :, mine]
 
         down = Reduce.of(place, gd, fd, scr[:each])
         up = Reduce.of(place, gu, fu, scr[each : 2 * each])
@@ -1095,9 +1126,9 @@
 
             lax.fori_loop(0, 4, step, 0)
 
-        take(0, 4)
+        take(0, 1)
         make(down, gd, cot2, act2)
-        take(1, 5)
+        take(2, 3)
         make(up, gu, n22, gup2)
 
         def weights(t):
@@ -1165,13 +1196,13 @@
             turns(i, {t + 2: functools.partial(red.two, shard) for t, (red, shard) in enumerate(order)})
             return carry
 
+        take(4, 5, 6, 7, 8)
         lax.fori_loop(0, n * pairs, head_pair, 0)
         halves = ((dq, dq_o), (dk, dk_o), (dv, dv_o))
         for i, (src, dst) in enumerate(halves):
             wire.start(10 + i, src.at[1], dst, place.core)
-        take(2, 3)
-        for d in range(n):
-            wire.landed(6 + d, at2.at[rows : 2 * rows, d * PAIR : (d + 1) * PAIR], place.core)
+        take(9, 10, 11)
+        wire.landed(0, ghb2.at[:, rows : 2 * rows], place.core)
 
         def put(m, val):
             for d in range(n):
@@ -1192,7 +1223,7 @@
             heads.one(d)
 
         far_out, x_buf, next_out = n12.at[0:own, 0:dm], n12.at[0:rows, dm : 2 * dm], n12.at[own : own + HALO, 0:dm]
-        tokens_in = pltpu.make_async_copy(x_ref, x_buf, ls.at[6])
+        tokens_in = pltpu.make_async_copy(x_ref, x_buf, ls.at[0])
         tokens_in.start()
 
         def dots(t, carry):
@@ -1341,12 +1372,7 @@
         down.six()
         up.six()
         heads.six()
-        for i in range(4):
-            wire.sent(i, whole[i][0])
-        for i in range(2):
-            wire.sent(4 + i, act2.at[0:rows])
-        for d in range(n):
-            wire.sent(6 + d, at2.at[0:rows, 0:PAIR])
+        wire.sent(0, ghb2.at[:, 0:rows])
         for i in range(3):
             wire.sent(10 + i, halves[i][1])
 
@@ -1380,19 +1406,20 @@
     q4 = dm // 4
     return pl.pallas_call(
         body,
-        in_specs=[hbm] * 8 + [vmem] * 10,
+        in_specs=[hbm] * 14 + [vmem] * 5,
         out_specs=[hbm] * 3 + [vmem] * 2,
         out_shape=[shaped(8, q4, w)] * 3 + [jax.ShapeDtypeStruct((rows, dm), F32), jax.ShapeDtypeStruct((1, length), F32)],
         scratch_shapes=[
             buf(3, dm, 2 * rows), buf(2 * rows, hw), buf(2 * rows, hw), buf(dm, 2 * win), buf(dm, hw), buf(dm, hw),
             buf(rows, half), buf(win, half), buf(win, half), buf(2 * rows, half), buf(2, rows, half), buf(2, win, half), buf(2, win, half),
             wide(PAIR, win), wide(PAIR, win), buf(own, dm), buf(HALO, dm), buf(HALO, dm), wide(HALO, dm),
-            wide(3, 1, length), wide(3, 1, length), wide(4, 1, length), buf(3, q4, w), sem(Reduce.SLOTS), sem(Reduce.SLOTS),
-            sem(22), sem(22), sem(7), sem(3),
+            wide(3, 1, length), wide(3, 1, length), wide(4, 1, length), buf(3, q4, w),
+            buf(n, rows, cw), buf(n, win, cw), buf(n, win, cw), buf(n, rows, cw), buf(n, rows, cw),
+            sem(Reduce.SLOTS), sem(Reduce.SLOTS), sem(22), sem(22), sem(13), sem(3),
         ]
         + Reduce.scratch(dm, w) * 2,
         compiler_params=pltpu.CompilerParams(collective_id=1, has_side_effects=True, vmem_limit_bytes=VMEM_ALL),
-    )(cot, act, n2, gup, ghb, n1w, packed, tokens, q, k, v, attn, gattn, lse, qseg, kseg, gain[None], vec)
+    )(cot, act, n2, gup, ghb, n1w, attn2, packed, tokens, q, k, v, attn, gattn, lse, qseg, kseg, gain[None], vec)
 
 
 def place_grads(coords, done, mode):
@@ -1515,10 +1542,10 @@
         small = jnp.concatenate([ln1_gain, ln1_bias, ln2_gain, ln2_bias, b_out, b_down, b_query, b_value, b_up])
         small = f32(small)[None]
         (
-            packed, n1_t, n2_t, cot_t, ghb_t, q, k, v, attn, lse, g_attn, active, g_upper, g_hidden, output, vec
+            packed, n1_t, n2_t, cot_t, ghb_t, q, k, v, attn, attn_2, g_attn, active, g_upper, g_hidden, lse, output, vec
         ) = front_call(tokens, cotangent, pack, w_up, w_down, small, qseg, kseg, own)
         done_d, done_u, done_p, g_in, vec = back_call(
-            cot_t, active, n2_t, g_upper, ghb_t, n1_t, packed, tokens, q, k, v, attn, g_attn, lse, qseg, kseg, ln1_gain, vec, own
+            cot_t, active, n2_t, g_upper, ghb_t, n1_t, attn_2, packed, tokens, q, k, v, attn, g_attn, lse, qseg, kseg, ln1_gain, vec, own
         )
         vec = vec[0]
         g_tokens = g_in + g_hidden

time: 345 us -> 329 us (0.954)
  Pallas kernels: 328 us -> 312 us
    pallas_call x1, Pallas kernels: 166 us -> 156 us  [back_call(): pl.pallas_call(body, in_specs=[hbm] * 14 + [vmem] * 5, out_specs=[hbm] *...]
    pallas_call x1, Pallas kernels: 149 us -> 144 us  [front_call(): pl.pallas_call(body, in_specs=[hbm, vmem, hbm, hbm, hbm, vmem, vmem, vmem...]
where the time goes in v8:
time: 329 us; the launch traced here: 328 us
  Pallas kernels  312 us (95%)
  other arithmetic  9.49 us (3%)
  local copies, waits for them, and re-layouts  6.38 us (2%)
    pallas_call x1, Pallas kernels, back_call(): pl.pallas_call(body, in_specs=[hbm] * 14 + [vmem] * 5, out_specs=[hbm] *...  156 us
    pallas_call x1, Pallas kernels, front_call(): pl.pallas_call(body, in_specs=[hbm, vmem, hbm, hbm, hbm, vmem, vmem, vmem...  144 us
    pallas_call x3, Pallas kernels, place_grads(): pl.pallas_call(body, in_specs=[pl.BlockSpec(memory_space=pltpu.SMEM), pl....  12.3 us

profile of v8, /device:TPU:0, one launch (start us, length us, event | category | flops | bytes accessed | tf_op | source)
XLA Modules:
  0.0 328.5 jit_solution(8109484559185949000)
XLA Ops:
  0.7 0.8 dynamic-slice_select_fusion
  1.5 0.8 broadcast_select_fusion
  2.4 0.1 concatenate.45
  2.4 0.6 broadcast_in_dim.20.ks_ref
  3.0 0.9 copy.37.qs_ref
  3.9 1.2 copy.36
  5.1 0.0 copy-start.3
  5.2 0.0 copy-start.4
  5.2 0.0 copy-start.5
  5.2 0.0 copy-start.6
  5.2 0.0 copy-start.7
  5.2 0.0 copy-start.8
  5.2 0.0 copy-start.10
  5.2 0.0 copy-start.11
  5.2 0.0 copy-start.9
  5.3 3.0 pad_maximum_fusion.pack_ref
  8.3 0.0 copy-done.3
  8.3 0.0 copy-done.4
  8.3 0.0 copy-done.5
  8.3 0.0 copy-done.6
  8.3 0.0 copy-done.7
  8.4 0.0 copy-done.8
  8.4 0.0 copy-done.10
  8.4 0.0 copy-done.11
  8.4 0.0 copy-done.9
  8.5 0.6 convert_element_type.10.small_ref
  9.1 143.9 %shard_map.305 = (bf16[4,1024,1024]{2,1,0:T(8,128)(2,1)}, bf16[1024,2304]{1,0:T(8,128)(2,1)}, bf16[1024,1024]{1,0:T(8,128)(2,1)}, bf16[1024,1024]{1,0:T(8,128)(2...) custom-call(bf16[512,1024]{1,0:T(8,128)(2,1)} %x_ref.1, ...), custom_call_target="tpu_custom_call" | custom-call | tf_op jit(solution)/shard_map/pallas_call | solution.py:908
  153.0 1.3 concatenate.35.gain_ref
  154.3 155.5 %shard_map.306 = (bf16[8,256,512]{2,1,0:T(8,128)(2,1)}, bf16[8,256,512]{2,1,0:T(8,128)(2,1)}, bf16[8,256,512]{2,1,0:T(8,128)(2,1)}, f32[512,1024]{1,0:T(8,128)}, f32[1,12288]{1,0:T(1,128)}) custom-call(bf16[1024,1024]{1,0:T(8,128)(2,1)} %get-tuple-element.44.cot_in, bf16[1024,2048]{1,0:T(8,128)(2,1)} %get-tuple-element.45.act_in, ...), custom_call_target="tpu_custom_call" | custom-call | tf_op jit(solution)/shard_map/pallas_call | solution.py:1407
  309.9 0.6 pad_add_fusion.c_ref
  310.5 3.9 %shard_map.307 = (f32[1024,256]{1,0:T(8,128)}, f32[1024,256]{1,0:T(8,128)}, f32[1024,256]{1,0:T(8,128)}, f32[256,1024]{1,0:T(8,128)}) custom-call(s32[3]{0:T(128)} %pad_add_fusion.c_ref, bf16[8,256,512]{2,1,0:T(8,128)(2,1)} %get-tuple-element.62.f_ref), custom_call_target="tpu_custom_call" | custom-call | bytes 6291456 | tf_op jit(solution)/shard_map/pallas_call | solution.py:1456
  314.4 3.9 %shard_map.308 = f32[1024,1024]{1,0:T(8,128)} custom-call(s32[3]{0:T(128)} %pad_add_fusion.c_ref, bf16[8,256,512]{2,1,0:T(8,128)(2,1)} %get-tuple-element.67.f_ref), custom_call_target="tpu_custom_call" | custom-call | bytes 6291456 | tf_op jit(solution)/shard_map/pallas_call | solution.py:1456
  318.3 0.0 copy-start
  318.3 4.5 %shard_map.309 = f32[1024,1024]{1,0:T(8,128)} custom-call(s32[3]{0:T(128)} %pad_add_fusion.c_ref, bf16[8,256,512]{2,1,0:T(8,128)(2,1)} %get-tuple-element.68.f_ref), custom_call_target="tpu_custom_call" | custom-call | bytes 6291456 | tf_op jit(solution)/shard_map/pallas_call | solution.py:1456
  322.7 0.0 copy-done
  322.7 0.0 copy-start.2
  322.7 0.0 copy-start.1
  322.8 3.6 %add.39 = f32[512,1024]{1,0:T(8,128)} add(f32[512,1024]{1,0:T(8,128)} %get-tuple-element.59, f32[512,1024]{1,0:T(8,128)S(1)} %copy-done) | non-fusion elementwise | flops 524288 | bytes 6291456 | tf_op jit(solution)/shard_map/add | solution.py:1551
  326.3 0.0 copy-done.2
  326.3 0.6 fusion
  326.9 0.6 constant_dynamic-slice_fusion.1
  327.5 0.0 copy-done.1
  327.5 1.0 copy.48
  (10 shorter events, 0.1 us)
Async XLA Ops:
  5.1 3.1 copy-start.3
  5.2 3.1 copy-start.4
  5.2 3.1 copy-start.5
  5.2 3.1 copy-start.6
  5.2 3.2 copy-start.7
  5.2 3.2 copy-start.8
  5.2 3.2 copy-start.10
  5.2 3.2 copy-start.11
  5.2 3.2 copy-start.9
  318.3 4.5 %copy-start = (f32[512,1024]{1,0:T(8,128)S(1)}, f32[512,1024]{1,0:T(8,128)}, u32[]{:S(2)}) copy-start(f32[512,1024]{1,0:T(8,128)} %get-tuple-element.60) | copy-start | bytes 6291460
  322.7 3.6 %copy-start.2 = (f32[1,12288]{1,0:T(1,128)S(1)}, f32[1,12288]{1,0:T(1,128)}, u32[]{:S(2)}) copy-start(f32[1,12288]{1,0:T(1,128)} %get-tuple-element.61) | copy-start | bytes 147460
  322.7 4.8 %copy-start.1 = (bf16[512,1024]{1,0:T(8,128)(2,1)S(1)}, bf16[512,1024]{1,0:T(8,128)(2,1)}, u32[]{:S(2)}) copy-start(bf16[512,1024]{1,0:T(8,128)(2,1)} %get-tuple-element.99) | copy-start | bytes 3145732

commit v9 on v8

--- a/solution.py
+++ b/solution.py
@@ -483,14 +483,45 @@
         return pl.ds(pl.multiple_of(who * step + at, half), size)
 
     def slot(d, kind):
-        return base + (d - 1) * 9 + kind
-
-    def begin(d):
-        wire.start(slot(d, 0), shard.at[rows(place.me)], whole.at[d, rows(place.me)], place.along(4 - d))
+        return base + (d - 1) * 10 + kind
+
+    lower, upper = place.along(3), place.along(1)
+
+    def begin():
+        mine = shard.at[rows(place.me)]
+
+        @pl.when(place.z > 0)
+        def _():
+            wire.start(slot(1, 0), mine, whole.at[1, rows(place.me)], lower)
+
+        @pl.when(place.z < 3)
+        def _():
+            wire.start(slot(3, 0), mine, whole.at[3, rows(place.me)], upper)
+
+    def goes_down(d):
+        return jnp.logical_and(place.z + d < 4, place.z > 0)
+
+    def goes_up(d):
+        return jnp.logical_and(place.z + d > 3, place.z < 3)
+
+    def onward(src, dst, d, to, dev):
+        pltpu.make_async_remote_copy(
+            src_ref=src, dst_ref=dst, send_sem=wire.send.at[slot(d, 9)], recv_sem=wire.recv.at[slot(to, 0)],
+            device_id=dev, device_id_type=MESH,
+        ).start()
 
     def first(d):
         mine = whole.at[d, rows(place.me)]
         wire.landed(slot(d, 0), mine, place.along(d))
+
+        @pl.when(goes_down(d))
+        def _():
+            onward(mine, whole.at[d + 1, rows(place.me)], d, d + 1, lower)
+
+        @pl.when(goes_up(d))
+        def _():
+            onward(mine, whole.at[d - 1, rows(place.me)], d, d - 1, upper)
+
         wire.start(slot(d, 2), mine, mine, place.by_x)
         wire.start(slot(d, 3), mine, mine, place.by_y)
         wire.start(slot(d, 1), mine, mine, place.core)
@@ -519,9 +550,24 @@
             wire.landed(slot(d, kind), whole.at[d, rows(who + flip)], place.core)
 
     def drain():
+        piece = whole.at[0, pl.ds(0, step)]
+
+        @pl.when(place.z > 0)
+        def _():
+            wire.sent(slot(1, 0), piece)
+
+        @pl.when(place.z < 3)
+        def _():
+            wire.sent(slot(3, 0), piece)
+
         for d in (1, 2, 3):
-            for kind in range(9):
-                wire.sent(slot(d, kind), whole.at[d, pl.ds(0, half if kind in (4, 5) else step)])
+
+            @pl.when(jnp.logical_or(goes_down(d), goes_up(d)))
+            def _():
+                wire.sent(slot(d, 9), piece)
+
+            for kind in range(1, 9):
+                wire.sent(slot(d, kind), whole.at[0, pl.ds(0, half if kind in (4, 5) else step)])
 
     return begin, first, second, third, done, drain
 
@@ -569,32 +615,29 @@
         for d in (1, 2, 3):
             wire.start(d - 1, bias_ref, biases.at[d], place.along(4 - d))
 
-        @pl.when(z == 0)
-        def _():
-            wire.start(3, tok_ref, n1.at[0:own], swap)
-
-        @pl.when(z == 1)
-        def _():
-            wire.start(3, tok_ref.at[0:SPAN], n1.at[0:SPAN], swap)
-
-        @pl.when(takes_next)
-        def _():
-            wire.start(4, tok_ref.at[rows - HALO : rows], n1.at[own - HALO : own], right_dev)
-
-        @pl.when(takes_prev)
-        def _():
-            wire.start(5, tok_ref.at[0:HALO], n1.at[own + rows : own + rows + HALO], left_dev)
-
         groups = [
-            gather_steps(place, wire, base + 27 * g, src, dst)
+            gather_steps(place, wire, base + 30 * g, src, dst)
             for g, (src, dst) in enumerate(((pack_ref, packed), (up_ref, up), (down_ref, down)))
         ]
-        for g in range(3):
-            for d in (1, 2, 3):
-                groups[g][0](d)
+        groups[0][0]()
+
+        @pl.when(z == 0)
+        def _():
+            wire.start(3, tok_ref, n1.at[0:own], swap)
+
+        @pl.when(takes_next)
+        def _():
+            wire.start(4, tok_ref.at[rows - HALO : rows], n1.at[own - HALO : own], right_dev)
+
+        @pl.when(takes_prev)
+        def _():
+            wire.start(5, tok_ref.at[0:HALO], n1.at[own + rows : own + rows + HALO], left_dev)
 
         def near_shard(i):
-            return lax.rem(4 - z + i, 3) + 1
+            upper, odd = z // 2, lax.rem(z, 2)
+            place_z = (1 + 3 * odd) * (1 + 15 * upper)
+            place_i = 1 + 255 * i + (i * (i - 1) // 2) * 65025
+            return lax.rem(7053045 // (place_z * place_i), 4)
 
         items = [(0, 0), (0, 1), (0, 2), (1, 0), (2, 0), (1, 1), (2, 1), (1, 2), (2, 2)]
 
@@ -616,7 +659,7 @@
                     f()
 
         def shard_at(k):
-            return near_shard(k + 2) * ((k + 3) // 4)
+            return near_shard(lax.rem(k + 2, 3)) * ((k + 3) // 4)
 
         def strip_at(i, start=0):
             return pl.ds(pl.multiple_of(start + i * strip, strip), strip)
@@ -681,6 +724,15 @@
         for c in local[1:]:
             c.wait()
         relay(0)
+        relay(1)
+        relay(2)
+
+        @pl.when(z == 1)
+        def _():
+            wire.start(3, tok_ref.at[0:SPAN], n1.at[0:SPAN], swap)
+
+        groups[1][0]()
+        groups[2][0]()
 
         @pl.when(z == 0)
         def _():
@@ -703,7 +755,7 @@
         leave(0)
         for d in (1, 2, 3):
             wire.landed(d - 1, biases.at[d], place.along(d))
-        relay(1)
+        relay(3)
 
         def attend(big, d, p):
             at = pl.ds(pl.multiple_of(p * PAIR, PAIR), PAIR)
@@ -748,7 +800,7 @@
                 def _():
                     attend(False, d, p)
 
-                turns(kk * pairs + p, {pairs * j: functools.partial(relay, 2 + j) for j in range(4)})
+                turns(kk * pairs + p, {pairs * j: functools.partial(relay, 4 + j) for j in range(4)})
                 return inner
 
             lax.fori_loop(0, pairs, one, 0)
@@ -761,7 +813,6 @@
         lax.fori_loop(0, n, heads, 0)
         for i in (4, 5, 6, 7, 10):
             leave(i)
-        relay(6)
 
         def norm2(i, carry):
             at = strip_at(i)
@@ -787,9 +838,7 @@
             turns(
                 i,
                 {
-                    1: lambda: relay(7),
-                    2: lambda: arrived(0, 1, 2),
-                    3: lambda: relay(8),
+                    2: lambda: (arrived(0, 1, 2), relay(8)),
                     4: lambda: (arrived(1, 1, 2), relay(9)),
                     5: lambda: relay(10),
                     6: lambda: arrived(2, 1, 2),
@@ -904,7 +953,7 @@
     full = lambda *shape: jax.ShapeDtypeStruct(shape, F32)
     b16 = lambda *shape: pltpu.VMEM(shape, BF16)
     b32 = lambda *shape: pltpu.VMEM(shape, F32)
-    slots = base + 27 * 3
+    slots = base + 30 * 3
     return pl.pallas_call(
         body,
         in_specs=[hbm, vmem, hbm, hbm, hbm, vmem, vmem, vmem],
@@ -1422,45 +1471,87 @@
     )(cot, act, n2, gup, ghb, n1w, attn2, packed, tokens, q, k, v, attn, gattn, lse, qseg, kseg, gain[None], vec)
 
 
-def place_grads(coords, done, mode):
-    _, q, w = done.shape
+def place_grads(coords, down, up, pack, g_in, g_hidden):
+    _, q, w = up.shape
     e = q // 2
     dm = 4 * q
     lanes = w // 4
-
-    def body(c_ref, f_ref, *outs):
-        for off in range(8):
-            y = lax.bitwise_xor(c_ref[0], off >> 2)
-            x = lax.bitwise_xor(c_ref[1], (off >> 1) & 1)
-            k = lax.bitwise_xor(c_ref[2], off & 1)
-            for part in range(2):
-                val = f_ref[off, part * e : (part + 1) * e, :].astype(F32)
-                block = x * 2 + y if part == 0 else 4 + y * 2 + x
-                rows = pl.ds(pl.multiple_of(block * e, e), e)
-                if mode == "up":
-                    outs[0][rows, pl.ds(pl.multiple_of(k * w, w), w)] = val
-                elif mode == "down":
-                    outs[0][pl.ds(pl.multiple_of(k * w, w), w), rows] = val.T
-                else:
-                    at = pl.ds(pl.multiple_of(k * lanes, lanes), lanes)
-                    for m in range(3):
-                        outs[m][rows, at] = val[:, m * lanes : (m + 1) * lanes]
-                    outs[3][at, rows] = val[:, 3 * lanes :].T
-
-    if mode == "up":
-        shapes = [(dm, 2 * w)]
-    elif mode == "down":
-        shapes = [(2 * w, dm)]
-    else:
-        shapes = [(dm, w // 2)] * 3 + [(w // 2, dm)]
+    rows = g_in.shape[0]
+    shapes = [(rows, dm), (2 * w, dm), (dm, 2 * w), (dm, w // 2), (dm, w // 2), (dm, w // 2), (w // 2, dm)]
+    count = len(shapes)
+    strip = 128
+
+    def body(c_ref, *refs):
+        ins, outs, bufs, more = refs[:5], refs[5 : 5 + count], refs[5 + count : 5 + 2 * count], refs[5 + 2 * count :]
+        d_buf, u_buf, p_buf, h_buf, ls, os = more
+        pieces = (d_buf, u_buf, p_buf)
+        loads = [
+            pltpu.make_async_copy(src, dst, ls.at[i])
+            for i, (src, dst) in enumerate(zip(ins, (*pieces, bufs[0], h_buf)))
+        ]
+        stores = [pltpu.make_async_copy(bufs[i], outs[i], os.at[i]) for i in range(count)]
+        for i in (1, 3, 4, 0, 2):
+            loads[i].start()
+
+        def spread(ref, put):
+            def one(off, carry):
+                y = lax.rem(c_ref[0] + off // 4, 2)
+                x = lax.rem(c_ref[1] + lax.rem(off // 2, 2), 2)
+                k = lax.rem(c_ref[2] + lax.rem(off, 2), 2)
+                for part, block in enumerate((2 * x + y, 4 + 2 * y + x)):
+                    val = ref[off, part * e : (part + 1) * e, :].astype(F32)
+                    put(val, pl.ds(pl.multiple_of(block * e, e), e), k)
+                return carry
+
+            lax.fori_loop(0, 8, one, 0)
+
+        def put_up(val, at, k):
+            bufs[2][at, pl.ds(pl.multiple_of(k * w, w), w)] = val
+
+        def put_down(val, at, k):
+            bufs[1][pl.ds(pl.multiple_of(k * w, w), w), at] = val.T
+
+        def put_pack(val, at, k):
+            half = pl.ds(pl.multiple_of(k * lanes, lanes), lanes)
+            for m in range(3):
+                bufs[3 + m][at, half] = val[:, m * lanes : (m + 1) * lanes]
+            bufs[6][half, at] = val[:, 3 * lanes :].T
+
+        loads[1].wait()
+        spread(u_buf, put_up)
+        stores[2].start()
+        loads[3].wait()
+        loads[4].wait()
+
+        def add(i, carry):
+            at = pl.ds(pl.multiple_of(i * strip, strip), strip)
+            bufs[0][at, :] += h_buf[at, :]
+            return carry
+
+        lax.fori_loop(0, rows // strip, add, 0)
+        stores[0].start()
+        loads[0].wait()
+        spread(d_buf, put_down)
+        stores[1].start()
+        loads[2].wait()
+        spread(p_buf, put_pack)
+        for i in range(3, count):
+            stores[i].start()
+        for c in stores:
+            c.wait()
+
+    hbm = pl.BlockSpec(memory_space=pl.ANY)
     return pl.pallas_call(
         body,
-        in_specs=[pl.BlockSpec(memory_space=pltpu.SMEM), pl.BlockSpec(memory_space=pltpu.VMEM)],
-        out_specs=[pl.BlockSpec(memory_space=pltpu.VMEM)] * len(shapes),
-        out_shape=[jax.ShapeDtypeStruct(s, F32) for s in shapes],
+        in_specs=[pl.BlockSpec(memory_space=pltpu.SMEM)] + [hbm] * 5,
+        out_specs=[hbm] * count,
+        out_shape=[jax.ShapeDtypeStruct(shape, F32) for shape in shapes],
+        scratch_shapes=[pltpu.VMEM(shape, F32) for shape in shapes]
+        + [pltpu.VMEM((8, q, w), BF16)] * 3
+        + [pltpu.VMEM((rows, dm), F32), pltpu.SemaphoreType.DMA((5,)), pltpu.SemaphoreType.DMA((count,))],
         compiler_params=pltpu.CompilerParams(vmem_limit_bytes=VMEM),
-        cost_estimate=pl.CostEstimate(flops=0, bytes_accessed=12 * dm * w, transcendentals=0),
-    )(coords, done)
+        cost_estimate=pl.CostEstimate(flops=0, bytes_accessed=36 * dm * w, transcendentals=0),
+    )(coords, down, up, pack, g_in, g_hidden)
 
 
 def relative(stack, z):
@@ -1548,11 +1639,10 @@
             cot_t, active, n2_t, g_upper, ghb_t, n1_t, attn_2, packed, tokens, q, k, v, attn, g_attn, lse, qseg, kseg, ln1_gain, vec, own
         )
         vec = vec[0]
-        g_tokens = g_in + g_hidden
         coords = jnp.stack([y, x, core]).astype(jnp.int32)
-        (g_w_down,) = place_grads(coords, done_d, "down")
-        (g_w_up,) = place_grads(coords, done_u, "up")
-        g_w_query, g_w_key, g_w_value, g_w_out = place_grads(coords, done_p, "pack")
+        g_tokens, g_w_down, g_w_up, g_w_query, g_w_key, g_w_value, g_w_out = place_grads(
+            coords, done_d, done_u, done_p, g_in, g_hidden
+        )
     else:
         halo = [
             lax.ppermute(tokens, "mp", [((i + j) % near, i) for i in range(near)]) for j in range(1, near)

time: 329 us -> 309 us (0.939)
  Pallas kernels: 312 us -> 296 us
  other arithmetic: 9.49 us -> 5.93 us
    pallas_call x1, Pallas kernels: 144 us -> 130 us  [front_call(): pl.pallas_call(body, in_specs=[hbm, vmem, hbm, hbm, hbm, vmem, vmem, vmem...]
    add x1 -> x0, other arithmetic: 3.56 us -> none  [local(): g_tokens = g_in + g_hidden]
    pallas_call x3 -> x1, Pallas kernels: 12.3 us -> 10.1 us  [place_grads(): pl.pallas_call(body, in_specs=[pl.BlockSpec(memory_space=pltpu.SMEM)] + [...]
where the time goes in v9:
time: 309 us
  Pallas kernels  296 us (96%)
  local copies, waits for them, and re-layouts  6.38 us (2%)
  other arithmetic  5.93 us (2%)
    pallas_call x1, Pallas kernels, back_call(): pl.pallas_call(body, in_specs=[hbm] * 14 + [vmem] * 5, out_specs=[hbm] *...  156 us
    pallas_call x1, Pallas kernels, front_call(): pl.pallas_call(body, in_specs=[hbm, vmem, hbm, hbm, hbm, vmem, vmem, vmem...  130 us
    pallas_call x1, Pallas kernels, place_grads(): pl.pallas_call(body, in_specs=[pl.BlockSpec(memory_space=pltpu.SMEM)] + [...  10.1 us

profile of v9, /device:TPU:0, one launch (start us, length us, event | category | flops | bytes accessed | tf_op | source)
XLA Modules:
  0.0 309.0 jit_solution(13684204262468222646)
XLA Ops:
  0.7 0.8 dynamic-slice_select_fusion
  1.5 0.8 broadcast_select_fusion
  2.4 0.1 concatenate.45
  2.4 0.6 broadcast_in_dim.20.ks_ref
  3.0 0.9 copy.37.qs_ref
  3.9 1.2 copy.36
  5.1 0.0 copy-start.2
  5.2 0.0 copy-start.3
  5.2 0.0 copy-start.4
  5.2 0.0 copy-start.5
  5.2 0.0 copy-start.6
  5.2 0.0 copy-start.7
  5.2 0.0 copy-start.9
  5.2 0.0 copy-start.10
  5.2 0.0 copy-start.8
  5.3 3.0 pad_maximum_fusion.pack_ref
  8.3 0.0 copy-done.2
  8.3 0.0 copy-done.3
  8.3 0.0 copy-done.4
  8.3 0.0 copy-done.5
  8.3 0.0 copy-done.6
  8.4 0.0 copy-done.7
  8.4 0.0 copy-done.9
  8.4 0.0 copy-done.10
  8.4 0.0 copy-done.8
  8.5 0.6 convert_element_type.10.small_ref
  9.1 129.6 %shard_map.305 = (bf16[4,1024,1024]{2,1,0:T(8,128)(2,1)}, bf16[1024,2304]{1,0:T(8,128)(2,1)}, bf16[1024,1024]{1,0:T(8,128)(2,1)}, bf16[1024,1024]{1,0:T(8,128)(2...) custom-call(bf16[512,1024]{1,0:T(8,128)(2,1)} %x_ref.1, ...), custom_call_target="tpu_custom_call" | custom-call | tf_op jit(solution)/shard_map/pallas_call | solution.py:957
  138.7 1.3 concatenate.35.gain_ref
  140.0 156.1 %shard_map.306 = (bf16[8,256,512]{2,1,0:T(8,128)(2,1)}, bf16[8,256,512]{2,1,0:T(8,128)(2,1)}, bf16[8,256,512]{2,1,0:T(8,128)(2,1)}, f32[512,1024]{1,0:T(8,128)}, f32[1,12288]{1,0:T(1,128)}) custom-call(bf16[1024,1024]{1,0:T(8,128)(2,1)} %get-tuple-element.47.cot_in, bf16[1024,2048]{1,0:T(8,128)(2,1)} %get-tuple-element.48.act_in, ...), custom_call_target="tpu_custom_call" | custom-call | tf_op jit(solution)/shard_map/pallas_call | solution.py:1456
  296.2 0.6 pad_add_fusion.c_ref
  296.8 0.0 copy-start.1
  296.8 0.0 copy-start
  296.8 10.1 %shard_map.307 = (f32[512,1024]{1,0:T(8,128)}, f32[1024,1024]{1,0:T(8,128)}, f32[1024,1024]{1,0:T(8,128)}, f32[1024,256]{1,0:T(8,128)}, f32[1024,256]{1,0:T(8,12...) custom-call(s32[3]{0:T(128)} %pad_add_fusion.c_ref, bf16[8,256,512]{2,1,0:T(8,128)(2,1)} %get-tuple-element.62.refs_0_, ...), custom_call_target="tpu_custom_call" | custom-call | bytes 18874368 | tf_op jit(solution)/shard_map/pallas_call | solution.py:1544
  306.8 0.0 copy-done.1
  306.9 0.6 fusion
  307.5 0.6 constant_dynamic-slice_fusion.1
  308.0 0.0 copy-done
  308.0 1.0 copy.48
  (10 shorter events, 0.1 us)
Async XLA Ops:
  5.1 3.1 %copy-start.2 = (bf16[1024]{0:T(1024)(128)(2,1)S(1)}, bf16[1024]{0:T(1024)(128)(2,1)}, u32[]{:S(2)}) copy-start(bf16[1024]{0:T(1024)(128)(2,1)} %param.20) | copy-start | bytes 6148
  5.2 3.1 %copy-start.3 = (bf16[1024]{0:T(1024)(128)(2,1)S(1)}, bf16[1024]{0:T(1024)(128)(2,1)}, u32[]{:S(2)}) copy-start(bf16[1024]{0:T(1024)(128)(2,1)} %param.21) | copy-start | bytes 6148
  5.2 3.1 %copy-start.4 = (bf16[1024]{0:T(1024)(128)(2,1)S(1)}, bf16[1024]{0:T(1024)(128)(2,1)}, u32[]{:S(2)}) copy-start(bf16[1024]{0:T(1024)(128)(2,1)} %param.29) | copy-start | bytes 6148
  5.2 3.1 %copy-start.5 = (bf16[1024]{0:T(1024)(128)(2,1)S(1)}, bf16[1024]{0:T(1024)(128)(2,1)}, u32[]{:S(2)}) copy-start(bf16[1024]{0:T(1024)(128)(2,1)} %param.30) | copy-start | bytes 6148
  5.2 3.2 %copy-start.6 = (bf16[1024]{0:T(1024)(128)(2,1)S(1)}, bf16[1024]{0:T(1024)(128)(2,1)}, u32[]{:S(2)}) copy-start(bf16[1024]{0:T(1024)(128)(2,1)} %param.28) | copy-start | bytes 6148
  5.2 3.2 %copy-start.7 = (bf16[1024]{0:T(1024)(128)(2,1)S(1)}, bf16[1024]{0:T(1024)(128)(2,1)}, u32[]{:S(2)}) copy-start(bf16[1024]{0:T(1024)(128)(2,1)} %param.34) | copy-start | bytes 6148
  5.2 3.2 %copy-start.9 = (bf16[256]{0:T(256)(128)(2,1)S(1)}, bf16[256]{0:T(256)(128)(2,1)}, u32[]{:S(2)}) copy-start(bf16[256]{0:T(256)(128)(2,1)} %param.23) | copy-start | bytes 1540
  5.2 3.2 %copy-start.10 = (bf16[256]{0:T(256)(128)(2,1)S(1)}, bf16[256]{0:T(256)(128)(2,1)}, u32[]{:S(2)}) copy-start(bf16[256]{0:T(256)(128)(2,1)} %param.26) | copy-start | bytes 1540
  5.2 3.2 %copy-start.8 = (bf16[1024]{0:T(1024)(128)(2,1)S(1)}, bf16[1024]{0:T(1024)(128)(2,1)}, u32[]{:S(2)}) copy-start(bf16[1024]{0:T(1024)(128)(2,1)} %param.32) | copy-start | bytes 6148
  296.8 10.1 %copy-start.1 = (f32[1,12288]{1,0:T(1,128)S(1)}, f32[1,12288]{1,0:T(1,128)}, u32[]{:S(2)}) copy-start(f32[1,12288]{1,0:T(1,128)} %get-tuple-element.68) | copy-start | bytes 147460
  296.8 11.3 %copy-start = (bf16[512,1024]{1,0:T(8,128)(2,1)S(1)}, bf16[512,1024]{1,0:T(8,128)(2,1)}, u32[]{:S(2)}) copy-start(bf16[512,1024]{1,0:T(8,128)(2,1)} %get-tuple-element.105) | copy-start | bytes 3145732

commit v10 on v9

--- a/solution.py
+++ b/solution.py
@@ -1119,7 +1119,7 @@
         self.keep().wait()
 
 
-def back_call(cot, act, n2, gup, ghb, n1w, attn2, packed, tokens, q, k, v, attn, gattn, lse, qseg, kseg, gain, vec, own):
+def back_call(cot, act, n2, gup, ghb, n1w, attn2, packed, tokens, q, k, v, attn, gattn, lse, qseg, kseg, small, vec, own):
     n, rows, cw = q.shape
     win = k.shape[1]
     dm = cot.shape[0]
@@ -1382,7 +1382,7 @@
                     at = base * dm + lax.rem(z + d, n) * cw + lax.rem(j + core, 2) * PAIR
                     va[0, :, pl.ds(pl.multiple_of(at, PAIR), PAIR)] = total[:, d * PAIR : (d + 1) * PAIR]
         tokens_in.wait()
-        gains = gain_ref[...].astype(F32)
+        gains = gain_ref[:, 0:dm]
 
         def norm(i, carry):
             at = pl.ds(pl.multiple_of(i * strip, strip), strip)
@@ -1468,7 +1468,7 @@
         ]
         + Reduce.scratch(dm, w) * 2,
         compiler_params=pltpu.CompilerParams(collective_id=1, has_side_effects=True, vmem_limit_bytes=VMEM_ALL),
-    )(cot, act, n2, gup, ghb, n1w, attn2, packed, tokens, q, k, v, attn, gattn, lse, qseg, kseg, gain[None], vec)
+    )(cot, act, n2, gup, ghb, n1w, attn2, packed, tokens, q, k, v, attn, gattn, lse, qseg, kseg, small, vec)
 
 
 def place_grads(coords, down, up, pack, g_in, g_hidden):
@@ -1636,7 +1636,7 @@
             packed, n1_t, n2_t, cot_t, ghb_t, q, k, v, attn, attn_2, g_attn, active, g_upper, g_hidden, lse, output, vec
         ) = front_call(tokens, cotangent, pack, w_up, w_down, small, qseg, kseg, own)
         done_d, done_u, done_p, g_in, vec = back_call(
-            cot_t, active, n2_t, g_upper, ghb_t, n1_t, attn_2, packed, tokens, q, k, v, attn, g_attn, lse, qseg, kseg, ln1_gain, vec, own
+            cot_t, active, n2_t, g_upper, ghb_t, n1_t, attn_2, packed, tokens, q, k, v, attn, g_attn, lse, qseg, kseg, small, vec, own
         )
         vec = vec[0]
         coords = jnp.stack([y, x, core]).astype(jnp.int32)

time: 309 us -> 314 us (1.016)
  local copies, waits for them, and re-layouts: 6.38 us -> 11.1 us
    unnamed x32 -> x14, local copies, waits for them, and re-layouts: 2.36 us -> 7.69 us
where the time goes in v10:
time: 314 us
  Pallas kernels  296 us (94%)
  local copies, waits for them, and re-layouts  11.1 us (4%)
  other arithmetic  5.9 us (2%)
    pallas_call x1, Pallas kernels, back_call(): pl.pallas_call(body, in_specs=[hbm] * 14 + [vmem] * 5, out_specs=[hbm] *...  156 us
    pallas_call x1, Pallas kernels, front_call(): pl.pallas_call(body, in_specs=[hbm, vmem, hbm, hbm, hbm, vmem, vmem, vmem...  130 us
    pallas_call x1, Pallas kernels, place_grads(): pl.pallas_call(body, in_specs=[pl.BlockSpec(memory_space=pltpu.SMEM)] + [...  10.1 us
    unnamed x14, local copies, waits for them, and re-layouts  7.69 us

profile of v10, /device:TPU:0, one launch (start us, length us, event | category | flops | bytes accessed | tf_op | source)
XLA Modules:
  0.0 313.6 jit_solution(8846306244553819731)
XLA Ops:
  0.7 0.8 dynamic-slice_select_fusion
  1.5 0.8 broadcast_select_fusion
  2.4 0.1 concatenate.45
  2.4 0.6 broadcast_in_dim.19.ks_ref
  3.0 0.9 copy.37.qs_ref
  3.9 0.7 constant_dynamic-update-slice_fusion.8
  4.6 0.7 constant_dynamic-update-slice_fusion.7
  5.3 0.7 constant_dynamic-update-slice_fusion.6
  6.0 0.7 constant_dynamic-update-slice_fusion.5
  6.7 0.7 constant_dynamic-update-slice_fusion.4
  7.3 0.7 constant_dynamic-update-slice_fusion.3
  8.0 0.7 constant_dynamic-update-slice_fusion.2
  8.7 0.7 constant_dynamic-update-slice_fusion.1
  9.4 0.7 constant_dynamic-update-slice_fusion
  10.1 0.6 convert_element_type.10.small_ref.gain_ref
  10.7 1.2 copy.36
  11.9 3.0 pad_maximum_fusion.pack_ref
  14.9 129.6 %shard_map.305 = (bf16[4,1024,1024]{2,1,0:T(8,128)(2,1)}, bf16[1024,2304]{1,0:T(8,128)(2,1)}, bf16[1024,1024]{1,0:T(8,128)(2,1)}, bf16[1024,1024]{1,0:T(8,128)(2...) custom-call(bf16[512,1024]{1,0:T(8,128)(2,1)} %x_ref.1, ...), custom_call_target="tpu_custom_call" | custom-call | tf_op jit(solution)/shard_map/pallas_call | solution.py:957
  144.5 156.2 %shard_map.306 = (bf16[8,256,512]{2,1,0:T(8,128)(2,1)}, bf16[8,256,512]{2,1,0:T(8,128)(2,1)}, bf16[8,256,512]{2,1,0:T(8,128)(2,1)}, f32[512,1024]{1,0:T(8,128)}, f32[1,12288]{1,0:T(1,128)}) custom-call(bf16[1024,1024]{1,0:T(8,128)(2,1)} %get-tuple-element.47.cot_in, bf16[1024,2048]{1,0:T(8,128)(2,1)} %get-tuple-element.48.act_in, ...), custom_call_target="tpu_custom_call" | custom-call | tf_op jit(solution)/shard_map/pallas_call | solution.py:1456
  300.8 0.6 pad_add_fusion.c_ref
  301.3 0.0 copy-start.1
  301.3 0.0 copy-start
  301.3 10.1 %shard_map.307 = (f32[512,1024]{1,0:T(8,128)}, f32[1024,1024]{1,0:T(8,128)}, f32[1024,1024]{1,0:T(8,128)}, f32[1024,256]{1,0:T(8,128)}, f32[1024,256]{1,0:T(8,12...) custom-call(s32[3]{0:T(128)} %pad_add_fusion.c_ref, bf16[8,256,512]{2,1,0:T(8,128)(2,1)} %get-tuple-element.62.refs_0_, ...), custom_call_target="tpu_custom_call" | custom-call | bytes 18874368 | tf_op jit(solution)/shard_map/pallas_call | solution.py:1544
  311.4 0.0 copy-done.1
  311.4 0.6 fusion
  312.1 0.6 constant_dynamic-slice_fusion.1
  312.6 0.0 copy-done
  312.6 1.0 copy.48
  (1 shorter events, 0.0 us)
Async XLA Ops:
  301.3 10.1 %copy-start.1 = (f32[1,12288]{1,0:T(1,128)S(1)}, f32[1,12288]{1,0:T(1,128)}, u32[]{:S(2)}) copy-start(f32[1,12288]{1,0:T(1,128)} %get-tuple-element.68) | copy-start | bytes 147460
  301.3 11.3 %copy-start = (bf16[512,1024]{1,0:T(8,128)(2,1)S(1)}, bf16[512,1024]{1,0:T(8,128)(2,1)}, u32[]{:S(2)}) copy-start(bf16[512,1024]{1,0:T(8,128)(2,1)} %get-tuple-element.105) | copy-start | bytes 3145732
